TPU v7x, 256 devices: a whole 4x4x8 slice. The times are simulated.
256 devices in a mesh: sub: 8 (over z), row: 2 (over core), col: 16 (over y, x).
Axes of the slice: x: 4, y: 4, z: 8, core: 2. Of those that a mesh axis runs over, the one named last changes fastest.
Arguments:
- factor_cols: bfloat16 [8, 2, 2048, 4096], P('sub', None, 'col', 'row'), may hold values from -0.09375 to 0.09375
- block_pattern: int32 [8, 16, 16], P('sub'), may hold values 0 or 1
- diag_inverse: float32 [8, 4096, 2048], P('sub', ('row', 'col')), may hold values from -1 to 2
- coupling_cols: bfloat16 [8, 2, 2048, 1024], P('sub', 'row', 'col'), may hold values from -0.09375 to 0.09375
- separator_rows: int32 [8, 1024], P('sub'), may hold values from 0 to 1535, as said below
- root_inverse: float32 [1536, 1536], P('col'), may hold values from -1 to 2
- right_side: float32 [8, 4096, 128], P('sub', 'row'), may hold values from -6 to 6
- root_right: float32 [1536, 128], P('col'), may hold values from -6 to 6
Outputs:
- solution: float32 [8, 4096, 128], P('sub', ('row', 'col'))
- root_solution: float32 [1536, 128], P('col')
Inputs may be any that keep to these rules, and one draw needn't show every extreme that they name: `separator_rows`: within one section the 1024 entries are distinct.
All inputs are finite; a program needn't handle non-finite values. No bound on the sum of `block_pattern` on one device may be relied on, other than what follows from the above.
Results may differ from a plain program's by a relative error of at most 0.003.
Values may be sent and summed in bfloat16 or wider, within the bound.
No kernel may reach another device: no remote copies, remote signals or barrier semaphores. Data moves between devices by JAX's collectives and lax.ppermute only.
A program may use at most 64 MiB of HBM per device.

v0:
```python
import jax
import jax.numpy as jnp
from jax import lax
from jax.sharding import PartitionSpec as P

BLOCK = 256
SEPARATOR = 1536


precise = lax.Precision.HIGHEST
first_axes = (((0,), (0,)), ((), ()))


def spread(block, axis, source):
    block = jnp.where(lax.axis_index(axis) == source, block, jnp.zeros_like(block))
    return lax.psum(block, axis)


def shards(
    factor_cols,
    block_pattern,
    diag_inverse,
    coupling_cols,
    separator_rows,
    root_inverse,
    right_side,
    root_right,
):
    factor = factor_cols[0]
    table = block_pattern[0]
    inverse = diag_inverse[0]
    couple_own = coupling_cols[0, 0]
    right_rows = right_side[0]
    rows_sep = separator_rows[0]
    panel_count, col_width, panel_rows = factor.shape
    sources = right_rows.shape[1]
    block_count = table.shape[1]
    row_id = lax.axis_index("row")
    col_id = lax.axis_index("col")
    sub_id = lax.axis_index("sub")
    own_blocks = lax.dynamic_slice_in_dim(
        table, row_id * (panel_rows // BLOCK), panel_rows // BLOCK, 0
    ).astype(jnp.float32)
    row_mask = jnp.repeat(own_blocks, BLOCK, axis=0)
    col_pos = (
        jnp.arange(panel_count)[:, None] * panel_rows
        + col_id * col_width
        + jnp.arange(col_width)[None, :]
    )
    selector = (jnp.arange(block_count)[:, None, None] == (col_pos // BLOCK)[None]).astype(
        jnp.float32
    )
    pattern_mask = jnp.einsum("in,nqj->qji", row_mask, selector)
    below_mask = (jnp.arange(panel_count) < row_id).astype(jnp.float32)[:, None, None]
    masked = factor * (pattern_mask * below_mask).astype(jnp.bfloat16)
    zero_panel = jnp.zeros((panel_rows, sources), jnp.float32)
    zero_share = jnp.zeros((col_width, sources), jnp.float32)

    def forward(current, carried):
        accumulated, solved = carried
        panel_total = lax.psum(accumulated, "col")
        solved = lax.cond(
            row_id == current,
            lambda values: jnp.dot(
                inverse, right_rows - values, precision=precise, preferred_element_type=jnp.float32
            ),
            lambda values: solved,
            panel_total,
        )
        received = spread(solved.astype(jnp.bfloat16), "row", current)
        factor_now = lax.dynamic_index_in_dim(masked, current, 0, keepdims=False)
        accumulated = accumulated + lax.dot_general(
            factor_now, received, first_axes, preferred_element_type=jnp.float32
        )
        return (accumulated, solved)

    accumulated, solved = lax.fori_loop(0, panel_count, forward, (zero_panel, zero_share))
    own_low = solved.astype(jnp.bfloat16)
    sep_partial = lax.dot_general(
        couple_own, own_low, first_axes, preferred_element_type=jnp.float32
    )
    onehot = (jnp.arange(SEPARATOR)[:, None] == rows_sep[None, :]).astype(jnp.float32)
    mapped = jnp.dot(onehot, sep_partial, precision=precise, preferred_element_type=jnp.float32)
    share_rows = root_inverse.shape[0]
    slice_start = col_id * share_rows
    first_device = ((sub_id == 0) & (row_id == 0)).astype(jnp.float32)
    own_rows = (
        lax.dynamic_slice_in_dim(-mapped, slice_start, share_rows, 0) + first_device * root_right
    )
    root_term = lax.dynamic_update_slice_in_dim(-mapped, own_rows, slice_start, 0)
    root_rhs = lax.psum(root_term, ("sub", "row", "col"))
    root_half = jnp.dot(
        root_inverse, root_rhs, precision=precise, preferred_element_type=jnp.float32
    )
    root_part = lax.psum_scatter(
        lax.dot_general(
            root_inverse,
            root_half,
            first_axes,
            precision=precise,
            preferred_element_type=jnp.float32,
        ),
        "col",
        scatter_dimension=0,
        tiled=True,
    )
    root_full = lax.all_gather(root_part.astype(jnp.bfloat16), "col", axis=0, tiled=True).astype(
        root_part.dtype
    )
    picked = lax.dot_general(
        onehot, root_full, first_axes, precision=precise, preferred_element_type=jnp.float32
    ).astype(jnp.bfloat16)
    couple_back = jnp.dot(couple_own, picked, preferred_element_type=jnp.float32)

    def backward(counter, carried):
        finished, panel_low = carried
        current = panel_count - 1 - counter
        factor_now = lax.dynamic_index_in_dim(masked, current, 0, keepdims=False)
        contribution = jnp.dot(factor_now, panel_low, preferred_element_type=jnp.float32)
        own_couple = couple_back * (row_id == current).astype(jnp.float32)
        summed = lax.psum(contribution + own_couple, "row")
        partial_value = lax.cond(
            row_id == current,
            lambda values: lax.dot_general(
                inverse,
                solved - values,
                first_axes,
                precision=precise,
                preferred_element_type=jnp.float32,
            ),
            lambda values: zero_panel,
            summed,
        )
        value = lax.psum_scatter(partial_value, "col", scatter_dimension=0, tiled=True)
        whole_low = lax.all_gather(value.astype(jnp.bfloat16), "col", axis=0, tiled=True)
        active = row_id == current
        finished = jnp.where(active, value, finished)
        panel_low = jnp.where(active, whole_low, panel_low)
        return (finished, panel_low)

    finished, panel_low = lax.fori_loop(
        0, panel_count, backward, (zero_share, zero_panel.astype(jnp.bfloat16))
    )
    return (finished[None], root_part)


def solution(mesh):
    return jax.shard_map(
        shards,
        mesh=mesh,
        in_specs=(
            P("sub", None, "col", "row"),
            P("sub", None, None),
            P("sub", ("row", "col"), None),
            P("sub", "row", "col", None),
            P("sub", None),
            P("col", None),
            P("sub", "row", None),
            P("col", None),
        ),
        out_specs=(P("sub", ("row", "col"), None), P("col", None)),
        check_vma=False,
    )
```

profile of v0, /device:TPU:1, one launch (start us, length us, event | category | flops | bytes accessed | tf_op | source)
XLA Modules:
  0.0 880.4 jit_solution(2642969435639359948)
XLA Ops:
  8.0 0.7 convert_bitcast_fusion
  8.8 0.1 copy.21
  8.9 0.1 broadcast_in_dim.25
  9.0 0.1 and_select_fusion
  9.1 2.8 fusion.15
  11.9 223.4 %while.37 = (s32[]{:T(128)}, f32[2048,128]{1,0:T(8,128)}, f32[128,128]{0,1:T(8,128)S(1)}, bf16[2,128,2048]{2,1,0:T(8,128)(2,1)}, s32[]{:T(128)}, /*index=5*/f32[...) while((s32[]{:T(128)}, f32[2048,128]{1,0:T(8,128)}, ...), condition=%wide.region_5.6_spmd.clone, body=%wide.region_0.5_spmd.clone.sunk | while | flops 470859776 | bytes 18612512 | solution.py:77
  11.9 0.0 all-reduce.6.cloned.1.call-start
  12.0 1.1 broadcast_select_fusion.7
  13.1 0.0 all-reduce.6.cloned.1.call-update
  13.1 102.7 %all-reduce.6.cloned.1.call-done = f32[2048,128]{1,0:T(8,128)} async-done(((f32[2048,128]{1,0:T(8,128)}), f32[2048,128]{1,0:T(8,128)}) %all-reduce.6.cloned.1.call-update) | async-done | bytes 1048592 | tf_op jit(solution)/shard_map/while/body/eval_jaxpr/psum | solution.py:61
  115.9 8.9 %psum.51 = bf16[128,128]{0,1:T(8,128)(2,1)S(1)} all-reduce(bf16[128,128]{0,1:T(8,128)(2,1)S(1)} %convert_select_fusion.2), channel_id=1, replica_groups=mesh['sub'=8,'row'=2,'col'=16] {'row'}, use_global_device_ids=true, to_apply=%region_4.4 | all-reduce | flops 16384 | bytes 65536 | tf_op jit(solution)/shard_map/while/body/eval_jaxpr/psum | solution.py:16
  124.8 2.4 convolution_add_fusion.4
  127.1 2.3 broadcast_select_fusion.7
  129.4 0.0 all-reduce.6.cloned.1.call-update
  129.5 96.6 %all-reduce.6.cloned.1.call-done = f32[2048,128]{1,0:T(8,128)} async-done(((f32[2048,128]{1,0:T(8,128)}), f32[2048,128]{1,0:T(8,128)}) %all-reduce.6.cloned.1.call-update) | async-done | bytes 1048592 | tf_op jit(solution)/shard_map/while/body/eval_jaxpr/psum | solution.py:61
  226.0 3.5 conditional.7
  226.0 3.5 convolution_bitcast_fusion.1
  229.5 3.4 psum.51
  233.0 2.4 convolution_add_fusion.4
  235.3 0.2 fusion.19
  235.6 2.9 fusion.16
  238.5 0.9 copy-done.5
  239.4 0.0 all-reduce.4.cloned.1.call-update
  239.5 0.0 reduce-scatter.5.cloned.1.call-start
  239.5 252.9 %all-reduce.4.cloned.1.call-done = f32[1536,128]{1,0:T(8,128)} async-done(((f32[1536,128]{1,0:T(8,128)}), f32[1536,128]{1,0:T(8,128)}) %all-reduce.4.cloned.1.call-update) | async-done | bytes 786448 | tf_op jit(solution)/shard_map/psum | solution.py:91
  492.4 1.9 fusion.24
  494.3 0.8 convolution_bitcast_fusion.2
  495.1 1.2 copy.27
  496.3 0.0 reduce-scatter.5.cloned.1.call-update
  496.3 0.1 copy.24
  496.4 76.2 %reduce-scatter.5.cloned.1.call-done = f32[96,128]{1,0:T(8,128)} async-done(((f32[1536,128]{1,0:T(8,128)}), f32[96,128]{1,0:T(8,128)}) %reduce-scatter.5.cloned.1.call-update) | async-done | bytes 49168 | tf_op jit(solution)/shard_map/reduce_scatter | solution.py:95
  572.6 0.8 convert_element_type.87
  573.5 17.5 %all_gather.13 = bf16[1536,128]{1,0:T(8,128)(2,1)S(1)} all-gather(bf16[96,128]{1,0:T(8,128)(2,1)S(1)} %convert_element_type.87), channel_id=1, replica_groups=mesh['sub'=8,'row'=2,'col'=16] {'col'}, dimensions={0}, use_global_device_ids=true | all-gather | bytes 417792 | tf_op jit(solution)/shard_map/all_gather | solution.py:107
  590.9 1.8 fusion.17
  592.8 0.3 convolution_bitcast_fusion.3
  593.0 0.1 copy.23
  593.1 279.1 %while.38 = (s32[]{:T(128)}, f32[128,128]{0,1:T(8,128)S(1)}, bf16[2048,128]{0,1:T(8,128)(2,1)S(1)}, s32[]{:T(128)}, bf16[2,128,2048]{2,1,0:T(8,128)(2,1)}, /*ind...) while((s32[]{:T(128)}, f32[128,128]{0,1:T(8,128)S(1)}, ...), condition=%wide.region_13.14_spmd.clone, body=%wide.region_8.13_spmd.clone.sunk | while | flops 470663168 | bytes 13697360 | solution.py:141
  593.1 0.0 all-reduce.8.cloned.1.call-start
  593.2 2.0 convolution_add_fusion.5
  595.2 0.0 all-reduce.8.cloned.1.call-update
  595.2 0.0 reduce-scatter.7.cloned.1.call-start
  595.3 37.9 %all-reduce.8.cloned.1.call-done = f32[128,128]{1,0:T(8,128)} async-done(((f32[128,128]{1,0:T(8,128)}), f32[128,128]{1,0:T(8,128)}) %all-reduce.8.cloned.1.call-update) | async-done | bytes 65552 | tf_op jit(solution)/shard_map/while/body/eval_jaxpr/psum | solution.py:121
  633.1 1.9 conditional.8
  633.1 1.9 convolution_bitcast_fusion
  635.0 1.0 copy-done.3
  636.0 0.0 reduce-scatter.7.cloned.1.call-update
  636.0 77.7 %reduce-scatter.7.cloned.1.call-done = f32[128,128]{0,1:T(8,128)} async-done(((f32[2048,128]{0,1:T(8,128)}), f32[128,128]{0,1:T(8,128)}) %reduce-scatter.7.cloned.1.call-update) | async-done | bytes 65552 | tf_op jit(solution)/shard_map/while/body/eval_jaxpr/reduce_scatter | solution.py:134
  713.8 0.9 fusion.43
  714.7 18.0 %all_gather.16 = bf16[2048,128]{0,1:T(8,128)(2,1)S(1)} all-gather(bf16[128,128]{0,1:T(8,128)(2,1)S(1)} %get-tuple-element.583), channel_id=1, replica_groups=mesh['sub'=8,'row'=2,'col'=16] {'col'}, dimensions={0}, use_global_device_ids=true | all-gather | bytes 557056 | tf_op jit(solution)/shard_map/while/body/eval_jaxpr/all_gather | solution.py:135
  732.7 0.2 broadcast_select_fusion.9
  732.9 0.0 all-reduce.8.cloned.1.call-start
  733.0 2.0 convolution_add_fusion.5
  735.0 0.0 all-reduce.8.cloned.1.call-update
  735.0 0.0 reduce-scatter.7.cloned.1.call-start
  735.1 37.3 %all-reduce.8.cloned.1.call-done = f32[128,128]{1,0:T(8,128)} async-done(((f32[128,128]{1,0:T(8,128)}), f32[128,128]{1,0:T(8,128)}) %all-reduce.8.cloned.1.call-update) | async-done | bytes 65552 | tf_op jit(solution)/shard_map/while/body/eval_jaxpr/psum | solution.py:121
  772.4 0.1 conditional.8
  772.4 0.1 broadcast_in_dim.1
  772.5 1.0 copy-done.3
  773.5 0.0 reduce-scatter.7.cloned.1.call-update
  773.6 79.5 %reduce-scatter.7.cloned.1.call-done = f32[128,128]{0,1:T(8,128)} async-done(((f32[2048,128]{0,1:T(8,128)}), f32[128,128]{0,1:T(8,128)}) %reduce-scatter.7.cloned.1.call-update) | async-done | bytes 65552 | tf_op jit(solution)/shard_map/while/body/eval_jaxpr/reduce_scatter | solution.py:134
  853.0 0.9 fusion.43
  854.0 18.0 %all_gather.16 = bf16[2048,128]{0,1:T(8,128)(2,1)S(1)} all-gather(bf16[128,128]{0,1:T(8,128)(2,1)S(1)} %get-tuple-element.583), channel_id=1, replica_groups=mesh['sub'=8,'row'=2,'col'=16] {'col'}, dimensions={0}, use_global_device_ids=true | all-gather | bytes 557056 | tf_op jit(solution)/shard_map/while/body/eval_jaxpr/all_gather | solution.py:135
  872.0 0.2 broadcast_select_fusion.9
  872.2 0.7 copy.25
  (30 shorter events, 0.1 us)
Async XLA Ops:
  8.0 484.4 %copy-start = (f32[96,1536]{1,0:T(8,128)S(1)}, f32[96,1536]{1,0:T(8,128)}, u32[]{:S(2)}) copy-start(f32[96,1536]{1,0:T(8,128)} %param.21) | copy-start | bytes 1769476
  9.1 2.8 copy-start.2
  11.9 223.4 %copy-start.4 = (bf16[1,1,128,1024]{3,2,1,0:T(8,128)(2,1)S(1)}, bf16[1,1,128,1024]{3,2,1,0:T(8,128)(2,1)}, u32[]{:S(2)}) copy-start(bf16[1,1,128,1024]{3,2,1,0:T(8,128)(2,1)} %param.19) | copy-start | bytes 786436
  11.9 223.6 %copy-start.7 = (s32[1,1024]{1,0:T(1,128)S(1)}, s32[1,1024]{1,0:T(1,128)}, u32[]{:S(2)}) copy-start(s32[1,1024]{1,0:T(1,128)} %param.20) | copy-start | bytes 12292
  11.9 103.9 %all-reduce.6.cloned.1.call-start = ((), (), s32[]{:S(2)}) async-start(), calls=%async_computation.4 | async-start | bytes 2097152 | tf_op jit(solution)/shard_map/while/body/eval_jaxpr/psum | solution.py:61
  115.8 8.9 %copy-start.1 = (f32[2048,128]{1,0:T(8,128)S(1)}, f32[2048,128]{1,0:T(8,128)}, u32[]{:S(2)}) copy-start(f32[2048,128]{1,0:T(8,128)} %broadcast_select_fusion.7) | copy-start | bytes 3145732 | tf_op jit(solution)/shard_map/while
  127.1 98.9 %all-reduce.6.cloned.1.call-start = ((), (), s32[]{:S(2)}) async-start(), calls=%async_computation.4 | async-start | bytes 2097152 | tf_op jit(solution)/shard_map/while/body/eval_jaxpr/psum | solution.py:61
  226.0 6.9 copy-start.1
  235.3 257.1 %all-reduce.4.cloned.1.call-start = ((), (), s32[]{:S(2)}) async-start(), calls=%async_computation.2 | async-start | bytes 1572864 | tf_op jit(solution)/shard_map/psum | solution.py:91
  235.6 2.9 copy-start.6
  238.5 0.9 copy-start.5
  239.5 333.2 %reduce-scatter.5.cloned.1.call-start = ((), (), s32[]{:S(2)}) async-start(), calls=%async_computation.3 | async-start | bytes 835584 | tf_op jit(solution)/shard_map/reduce_scatter | solution.py:95
  593.1 40.0 %all-reduce.8.cloned.1.call-start = ((), (), s32[]{:S(2)}) async-start(), calls=%async_computation.5 | async-start | bytes 131072 | tf_op jit(solution)/shard_map/while/body/eval_jaxpr/psum | solution.py:121
  595.2 118.5 %reduce-scatter.7.cloned.1.call-start = ((), (), s32[]{:S(2)}) async-start(), calls=%async_computation.6 | async-start | bytes 1114112 | tf_op jit(solution)/shard_map/while/body/eval_jaxpr/reduce_scatter | solution.py:134
  635.0 1.0 copy-start.3
  732.9 39.5 %all-reduce.8.cloned.1.call-start = ((), (), s32[]{:S(2)}) async-start(), calls=%async_computation.5 | async-start | bytes 131072 | tf_op jit(solution)/shard_map/while/body/eval_jaxpr/psum | solution.py:121
  735.0 118.0 %reduce-scatter.7.cloned.1.call-start = ((), (), s32[]{:S(2)}) async-start(), calls=%async_computation.6 | async-start | bytes 1114112 | tf_op jit(solution)/shard_map/while/body/eval_jaxpr/reduce_scatter | solution.py:134
  772.5 1.0 copy-start.3
Sparse Core Ops, SparseCore 0:
  16.4 99.4 all-reduce.5
  131.6 94.4 all-reduce.5
  597.3 35.8 all-reduce.7
  636.9 76.8 reduce-scatter.6
  736.8 35.6 all-reduce.7
  776.2 76.8 reduce-scatter.6
Sparse Core Ops, SparseCore 1:
  241.2 251.1 all-reduce.3
  496.7 75.9 reduce-scatter.4
where the time goes:
time: 888 us; the launch traced here: 880 us
  waiting for transfers between devices  761 us (86%)
  blocking collectives  65.9 us (7%)
  matrix products  24.7 us (3%)
  between operations  15.7 us (2%)
    psum x1, waiting for transfers between devices, shards(): root_rhs = lax.psum(root_term, ('sub', 'row', 'col'))  253 us
    psum x2, waiting for transfers between devices, forward(): panel_total = lax.psum(accumulated, 'col')  199 us
    reduce_scatter x2, waiting for transfers between devices, backward(): lax.psum_scatter(partial_value, 'col', scatter_dimension=0, tiled=True)  157 us
    reduce_scatter x1, waiting for transfers between devices, shards(): lax.psum_scatter(lax.dot_general(root_inverse, root_half, first_axes, pre...  76.2 us
    psum x2, waiting for transfers between devices, backward(): summed = lax.psum(contribution + own_couple, 'row')  75.2 us
    all_gather x2, blocking collectives, backward(): lax.all_gather(value.astype(jnp.bfloat16), 'col', axis=0, tiled=True)  36 us
  transfers between devices with their start and end apart: 8, of which 8 were waited for; matrix products, arithmetic and copies ran while one was open for 0% of the time, Pallas kernels for 0%

commit v1 on v0

v1 whole, which is shorter than its diff:
```python
import jax
import jax.numpy as jnp
from jax import lax
from jax.sharding import PartitionSpec as P

BLOCK = 256
PANEL = 2048
SEPARATOR = 1536
COLS = 16
SUBS = 8

f32 = jnp.float32
bf16 = jnp.bfloat16
fine = lax.Precision.HIGH
first_axes = (((0,), (0,)), ((), ()))


def mul(left, right, **kw):
    return jnp.dot(left, right, preferred_element_type=f32, **kw)


def mul_t(left, right, **kw):
    return lax.dot_general(left, right, first_axes, preferred_element_type=f32, **kw)


def sum_scatter(partial, axes, count):
    parts = partial.reshape(count, -1, partial.shape[-1])
    return lax.all_to_all(parts, axes, 0, 0).astype(f32).sum(0)


def gather(chunk, axes, count):
    spread = jnp.broadcast_to(chunk[None], (count,) + chunk.shape)
    return lax.all_to_all(spread, axes, 0, 0)


def shards(
    factor_cols,
    block_pattern,
    diag_inverse,
    coupling_cols,
    separator_rows,
    root_inverse,
    right_side,
    root_right,
):
    table = block_pattern[0]
    inverse = diag_inverse[0]
    couple = coupling_cols[0, 0]
    rows_sep = separator_rows[0]
    row_id = lax.axis_index("row")
    col_id = lax.axis_index("col")
    sources = right_side.shape[-1]

    blocks = lax.dynamic_slice(table, (PANEL // BLOCK, col_id // 2), (PANEL // BLOCK, 1))
    lower = factor_cols[0, 0] * jnp.repeat(blocks[:, 0], BLOCK)[None, :].astype(bf16)

    onehot = (rows_sep[:, None] == jnp.arange(SEPARATOR)[None, :]).astype(bf16)
    couple_sep = mul(couple, onehot).astype(bf16)

    own = mul(inverse, right_side[0], precision=fine)
    first_low = lax.ppermute(own.astype(bf16), "row", [(0, 1)])
    total = sum_scatter(mul_t(lower, first_low).astype(bf16), "col", COLS)
    total = gather(total.astype(bf16), "col", COLS).reshape(PANEL, sources)
    solved = own - mul(inverse, total.astype(f32), precision=fine)

    updates = sum_scatter(mul_t(couple_sep, solved.astype(bf16)), ("col", "row"), COLS * 2)
    updates = gather(updates, "sub", SUBS).sum(0)
    half = updates.shape[0]
    rhs = lax.dynamic_slice_in_dim(root_right, row_id * half, half, 0) - updates
    rhs = gather(rhs, ("col", "row"), COLS * 2).reshape(SEPARATOR, sources)
    root_half = mul(root_inverse, rhs, precision=fine)
    root_part = sum_scatter(mul_t(root_inverse, root_half, precision=fine), "col", COLS)
    root_full = gather(root_part.astype(bf16), "col", COLS).reshape(SEPARATOR, sources)

    value = solved - mul(couple_sep, root_full)
    value = sum_scatter(mul_t(inverse, value, precision=fine), "col", COLS)
    later_low = gather(value.astype(bf16), "col", COLS).reshape(PANEL, sources)
    terms = lax.ppermute(mul(lower, later_low), "row", [(1, 0)])
    value = value - sum_scatter(mul_t(inverse, terms, precision=fine), "col", COLS)
    return value[None], root_part


def solution(mesh):
    return jax.shard_map(
        shards,
        mesh=mesh,
        in_specs=(
            P("sub", None, "col", "row"),
            P("sub", None, None),
            P("sub", ("row", "col"), None),
            P("sub", "row", "col", None),
            P("sub", None),
            P("col", None),
            P("sub", "row", None),
            P("col", None),
        ),
        out_specs=(P("sub", ("row", "col"), None), P("col", None)),
        check_vma=False,
    )
```

time: 888 us -> 189 us (0.21)
  waiting for transfers between devices: 761 us -> 21.9 us
  blocking collectives: 65.9 us -> 134 us
  starting transfers between devices: 0.26 us -> 19.3 us
  matrix products: 24.7 us -> 6.8 us
  between operations: 15.7 us -> 0.94 us
    psum x5 -> x0, waiting for transfers between devices: 527 us -> none  [the longest x1 253 us: shards(): root_rhs = lax.psum(root_term, ('sub', 'row', 'col'))]
    reduce_scatter x3 -> x0, waiting for transfers between devices: 233 us -> none  [the longest x2 157 us: backward(): lax.psum_scatter(partial_value, 'col', scatter_dimension=0, tiled=True)]
    all_to_all x0 -> x8, blocking collectives: none -> 134 us  [the longest x5 90.2 us: sum_scatter(): return lax.all_to_all(parts, axes, 0, 0).astype(f32).sum(0)]
    all_gather x3 -> x0, blocking collectives: 53.5 us -> none  [the longest x2 36 us: backward(): lax.all_gather(value.astype(jnp.bfloat16), 'col', axis=0, tiled=True)]
    dot_general x13 -> x11, matrix products: 24.7 us -> 6.8 us  [the longest x6 4.5 us: mul(): return jnp.dot(left, right, preferred_element_type=f32, **kw)]
    all_to_all x0 -> x2, waiting for transfers between devices: none -> 17.4 us  [gather(): return lax.all_to_all(spread, axes, 0, 0)]
    psum x2 -> x0, blocking collectives: 12.3 us -> none  [spread(): return lax.psum(block, axis)]
    all_to_all x0 -> x2, starting transfers between devices: none -> 11.8 us  [gather(): return lax.all_to_all(spread, axes, 0, 0)]
  transfers between devices with their start and end apart: 8 -> 4, of which waited for: 8 -> 4; matrix products, arithmetic and copies ran while one was open for 0% -> 1% of each run, Pallas kernels for 0% -> 0%
where the time goes in v1:
time: 189 us; the launch traced here: 188 us
  blocking collectives  134 us (71%)
  waiting for transfers between devices  21.9 us (12%)
  starting transfers between devices  19.3 us (10%)
  matrix products  6.8 us (4%)
  local copies, waits for them, and re-layouts  4.4 us (2%)
    all_to_all x5, blocking collectives, sum_scatter(): return lax.all_to_all(parts, axes, 0, 0).astype(f32).sum(0)  90.2 us
    all_to_all x3, blocking collectives, gather(): return lax.all_to_all(spread, axes, 0, 0)  44.2 us
    all_to_all x2, waiting for transfers between devices, gather(): return lax.all_to_all(spread, axes, 0, 0)  17.4 us
    all_to_all x2, starting transfers between devices, gather(): return lax.all_to_all(spread, axes, 0, 0)  11.8 us
    ppermute x1, starting transfers between devices, shards(): terms = lax.ppermute(mul(lower, later_low), 'row', [(1, 0)])  6.21 us
    dot_general x6, matrix products, mul(): return jnp.dot(left, right, preferred_element_type=f32, **kw)  4.5 us
  transfers between devices with their start and end apart: 4, of which 4 were waited for; matrix products, arithmetic and copies ran while one was open for 1% of the time, Pallas kernels for 0%

profile of v1, /device:TPU:1, one launch (start us, length us, event | category | flops | bytes accessed | tf_op | source)
XLA Modules:
  0.0 188.2 jit_solution(7016343400806508268)
XLA Ops:
  0.6 0.0 copy-start
  0.6 0.0 copy-start.6
  0.7 0.0 copy-start.2
  0.7 1.2 copy-done
  1.9 1.8 fusion.25
  3.7 1.3 collective-permute-start
  5.0 0.0 copy-done.6
  5.0 0.2 fusion.24
  5.2 0.1 broadcast_bitcast_fusion
  5.3 3.6 %collective-permute-done = bf16[128,128]{1,0:T(8,128)(2,1)S(1)} collective-permute-done((bf16[128,128]{1,0:T(8,128)(2,1)S(1)}, bf16[128,128]{1,0:T(8,128)(2,1)S(1)}, u32[]{:S(2)}, u32[]{:S(2)}) %collective-permute-start) | collective-permute-done | bytes 32800 | tf_op jit(solution)/shard_map/ppermute | solution.py:61
  8.9 0.0 copy-done.2
  8.9 0.3 convolution_convert_fusion
  9.3 16.2 %all_to_all.50 = bf16[16,128,128]{2,1,0:T(8,128)(2,1)S(1)} all-to-all(bf16[16,128,128]{2,1,0:T(8,128)(2,1)S(1)} %bitcast.74), channel_id=1, replica_groups=mesh['sub'=8,'row'=2,'col'=16] {'col'}, dimensions={0} | all-to-all | bytes 1048576 | tf_op jit(solution)/shard_map/all_to_all | solution.py:28
  25.4 0.0 copy-start.7
  25.4 0.0 copy-start.8
  25.4 0.1 reduce_sum.57
  25.5 0.9 broadcast_in_dim.13
  26.4 3.6 %all-to-all-start.1 = ((bf16[16,128,128]{2,1,0:T(8,128)(2,1)}), bf16[16,128,128]{2,1,0:T(8,128)(2,1)S(1)}, u32[]{:S(2)}, u32[]{:S(2)}) async-start(bf16[16,128,128]{2,1,0:T(8,128)(2,1)} %broadcast_in_dim.13), calls=%async_computation.1 | async-start | bytes 1048576 | tf_op jit(solution)/shard_map/all_to_all | solution.py:33
  30.0 0.0 copy-done.7
  30.0 0.0 copy-done.8
  30.0 1.2 fusion.4
  31.3 8.8 %all-to-all-done.1 = bf16[16,128,128]{2,1,0:T(8,128)(2,1)S(1)} async-done(((bf16[16,128,128]{2,1,0:T(8,128)(2,1)}), bf16[16,128,128]{2,1,0:T(8,128)(2,1)S(1)}, u32[]{:S(2)}, u32[]{:S(2)}) %all-to-all-start.1) | async-done | bytes 524320 | tf_op jit(solution)/shard_map/all_to_all | solution.py:33
  40.1 0.4 fusion.7
  40.5 0.2 fusion.22
  40.8 19.6 %all_to_all.51 = f32[32,48,128]{2,1,0:T(8,128)S(1)} all-to-all(f32[32,48,128]{2,1,0:T(8,128)S(1)} %bitcast.71), channel_id=1, replica_groups=mesh['sub'=8,'row'=2,'col'=16] {'col','row'}, dimensions={0} | all-to-all | bytes 1572864 | tf_op jit(solution)/shard_map/all_to_all | solution.py:28
  60.3 0.0 copy-start.5
  60.3 0.1 reduce_sum.58
  60.4 0.7 broadcast_in_dim.14
  61.1 8.2 %all-to-all-start.3 = ((f32[8,48,128]{2,1,0:T(8,128)}), f32[8,48,128]{2,1,0:T(8,128)S(1)}, u32[]{:S(2)}, u32[]{:S(2)}) async-start(f32[8,48,128]{2,1,0:T(8,128)} %broadcast_in_dim.14), calls=%async_computation.3 | async-start | bytes 393216 | tf_op jit(solution)/shard_map/all_to_all | solution.py:33
  69.3 8.6 %all-to-all-done.3 = f32[8,48,128]{2,1,0:T(8,128)S(1)} async-done(((f32[8,48,128]{2,1,0:T(8,128)}), f32[8,48,128]{2,1,0:T(8,128)S(1)}, u32[]{:S(2)}, u32[]{:S(2)}) %all-to-all-start.3) | async-done | bytes 196640 | tf_op jit(solution)/shard_map/all_to_all | solution.py:33
  77.9 0.0 copy-done.5
  77.9 0.0 copy-start.1
  77.9 0.1 broadcast_in_dim.15
  78.0 20.7 %all_to_all.52 = f32[32,48,128]{2,1,0:T(8,128)S(1)} all-to-all(f32[32,48,128]{2,1,0:T(8,128)S(1)} %broadcast_in_dim.15), channel_id=1, replica_groups=mesh['sub'=8,'row'=2,'col'=16] {'col','row'}, dimensions={0} | all-to-all | bytes 1572864 | tf_op jit(solution)/shard_map/all_to_all | solution.py:33
  98.7 0.0 copy-done.1
  98.7 0.4 fusion.26
  99.2 0.5 convolution_bitcast_fusion
  99.7 0.3 copy.22
  99.9 17.4 %all_to_all.53 = f32[16,96,128]{2,1,0:T(8,128)S(1)} all-to-all(f32[16,96,128]{2,1,0:T(8,128)S(1)} %bitcast.70), channel_id=1, replica_groups=mesh['sub'=8,'row'=2,'col'=16] {'col'}, dimensions={0} | all-to-all | bytes 1572864 | tf_op jit(solution)/shard_map/all_to_all | solution.py:28
  117.4 0.0 copy-start.4
  117.4 0.1 broadcast_in_dim.16
  117.4 11.7 %all_to_all.54 = bf16[16,96,128]{2,1,0:T(8,128)(2,1)S(1)} all-to-all(bf16[16,96,128]{2,1,0:T(8,128)(2,1)S(1)} %broadcast_in_dim.16), channel_id=1, replica_groups=mesh['sub'=8,'row'=2,'col'=16] {'col'}, dimensions={0} | all-to-all | bytes 786432 | tf_op jit(solution)/shard_map/all_to_all | solution.py:33
  129.2 0.3 convolution_subtract_fusion
  129.5 0.0 copy-done.4
  129.5 0.6 convolution_bitcast_fusion.2
  130.1 0.1 copy.38
  130.2 18.0 %all_to_all.55 = f32[16,128,128]{1,2,0:T(8,128)S(1)} all-to-all(f32[16,128,128]{1,2,0:T(8,128)S(1)} %bitcast.68), channel_id=1, replica_groups=mesh['sub'=8,'row'=2,'col'=16] {'col'}, dimensions={0} | all-to-all | bytes 2097152 | tf_op jit(solution)/shard_map/all_to_all | solution.py:28
  148.2 0.1 reduce_sum.61
  148.3 0.0 copy-start.3
  148.3 0.1 copy.25
  148.4 0.1 broadcast_in_dim.17
  148.5 11.7 %all_to_all.56 = bf16[16,128,128]{2,1,0:T(8,128)(2,1)S(1)} all-to-all(bf16[16,128,128]{2,1,0:T(8,128)(2,1)S(1)} %broadcast_in_dim.17), channel_id=1, replica_groups=mesh['sub'=8,'row'=2,'col'=16] {'col'}, dimensions={0} | all-to-all | bytes 1048576 | tf_op jit(solution)/shard_map/all_to_all | solution.py:33
  160.3 0.0 copy-done.3
  160.3 0.3 fusion.14
  160.6 6.2 %collective-permute-start.1 = (f32[128,128]{1,0:T(8,128)S(1)}, f32[128,128]{1,0:T(8,128)S(1)}, u32[]{:S(2)}, u32[]{:S(2)}) collective-permute-start(f32[128,128]{1,0:T(8,128)S(1)} %fusion.14), channel_id=1, source_target_pairs={{16,0},{17,1},{18,2},{19,3},{20,4},{21,5},{22,6},{23,7},{24,8},{25... | collective-permute-start | bytes 196616 | tf_op jit(solution)/shard_map/ppermute | solution.py:78
  166.8 0.9 collective-permute-done.1
  167.7 0.6 convolution_bitcast_fusion.1
  168.3 0.1 copy.37
  168.4 19.0 %all_to_all.57 = f32[16,128,128]{1,2,0:T(8,128)S(1)} all-to-all(f32[16,128,128]{1,2,0:T(8,128)S(1)} %bitcast.69), channel_id=1, replica_groups=mesh['sub'=8,'row'=2,'col'=16] {'col'}, dimensions={0} | all-to-all | bytes 2097152 | tf_op jit(solution)/shard_map/all_to_all | solution.py:28
  187.4 0.1 reduce_sum.62
  187.5 0.7 copy.28
  (7 shorter events, 0.1 us)
Async XLA Ops:
  0.6 1.2 copy-start
  0.6 4.4 %copy-start.6 = (s32[1,16,16]{2,1,0:T(8,128)S(1)}, s32[1,16,16]{2,1,0:T(8,128)}, u32[]{:S(2)}) copy-start(s32[1,16,16]{2,1,0:T(8,128)} %param.9) | copy-start | bytes 3076
  0.7 8.3 %copy-start.2 = (bf16[1,2,128,2048]{3,2,1,0:T(8,128)(2,1)S(1)}, bf16[1,2,128,2048]{3,2,1,0:T(8,128)(2,1)}, u32[]{:S(2)}) copy-start(bf16[1,2,128,2048]{3,2,1,0:T(8,128)(2,1)} %param.8) | copy-start | bytes 3145732
  3.7 5.2 %collective-permute-start = (bf16[128,128]{1,0:T(8,128)(2,1)S(1)}, bf16[128,128]{1,0:T(8,128)(2,1)S(1)}, u32[]{:S(2)}, u32[]{:S(2)}) collective-permute-start(bf16[128,128]{1,0:T(8,128)(2,1)S(1)} %get-tuple-element.6), channel_id=1, source_target_pairs={{0,16},{1,17},{2,18},{3,19},{4,20},{5,21},{6,22},{7,23},{8,24},{9,... | collective-permute-start | bytes 98312 | tf_op jit(solution)/shard_map/ppermute | solution.py:61
  25.4 4.6 %copy-start.7 = (bf16[1,1,128,1024]{3,2,1,0:T(8,128)(2,1)S(1)}, bf16[1,1,128,1024]{3,2,1,0:T(8,128)(2,1)}, u32[]{:S(2)}) copy-start(bf16[1,1,128,1024]{3,2,1,0:T(8,128)(2,1)} %param.11) | copy-start | bytes 786436
  25.4 4.6 %copy-start.8 = (s32[1,1024]{1,0:T(1,128)S(1)}, s32[1,1024]{1,0:T(1,128)}, u32[]{:S(2)}) copy-start(s32[1,1024]{1,0:T(1,128)} %param.12) | copy-start | bytes 12292
  26.4 13.7 %all-to-all-start.1 = ((bf16[16,128,128]{2,1,0:T(8,128)(2,1)}), bf16[16,128,128]{2,1,0:T(8,128)(2,1)S(1)}, u32[]{:S(2)}, u32[]{:S(2)}) async-start(bf16[16,128,128]{2,1,0:T(8,128)(2,1)} %broadcast_in_dim.13), calls=%async_computation.1 | async-start | bytes 1048576 | tf_op jit(solution)/shard_map/all_to_all | solution.py:33
  60.3 17.6 %copy-start.5 = (f32[96,128]{1,0:T(8,128)S(1)}, f32[96,128]{1,0:T(8,128)}, u32[]{:S(2)}) copy-start(f32[96,128]{1,0:T(8,128)} %param.15) | copy-start | bytes 147460
  61.1 16.8 %all-to-all-start.3 = ((f32[8,48,128]{2,1,0:T(8,128)}), f32[8,48,128]{2,1,0:T(8,128)S(1)}, u32[]{:S(2)}, u32[]{:S(2)}) async-start(f32[8,48,128]{2,1,0:T(8,128)} %broadcast_in_dim.14), calls=%async_computation.3 | async-start | bytes 393216 | tf_op jit(solution)/shard_map/all_to_all | solution.py:33
  77.9 20.8 %copy-start.1 = (f32[96,1536]{1,0:T(8,128)S(1)}, f32[96,1536]{1,0:T(8,128)}, u32[]{:S(2)}) copy-start(f32[96,1536]{1,0:T(8,128)} %param.13) | copy-start | bytes 1769476
  117.4 12.1 %copy-start.4 = (f32[96,128]{1,0:T(8,128)}, f32[96,128]{1,0:T(8,128)S(1)}, u32[]{:S(2)}) copy-start(f32[96,128]{1,0:T(8,128)S(1)} %reduce_sum.60) | copy-start | bytes 147460
  148.3 12.0 %copy-start.3 = (bf16[1,2,128,2048]{3,2,1,0:T(8,128)(2,1)S(1)}, bf16[1,2,128,2048]{3,2,1,0:T(8,128)(2,1)}, u32[]{:S(2)}) copy-start(bf16[1,2,128,2048]{3,2,1,0:T(8,128)(2,1)} %param.8) | copy-start | bytes 3145732
  160.6 7.1 %collective-permute-start.1 = (f32[128,128]{1,0:T(8,128)S(1)}, f32[128,128]{1,0:T(8,128)S(1)}, u32[]{:S(2)}, u32[]{:S(2)}) collective-permute-start(f32[128,128]{1,0:T(8,128)S(1)} %fusion.14), channel_id=1, source_target_pairs={{16,0},{17,1},{18,2},{19,3},{20,4},{21,5},{22,6},{23,7},{24,8},{25... | collective-permute-start | bytes 196616 | tf_op jit(solution)/shard_map/ppermute | solution.py:78

commit v2 on v1

--- a/solution.py
+++ b/solution.py
@@ -25,7 +25,11 @@
 
 def sum_scatter(partial, axes, count):
     parts = partial.reshape(count, -1, partial.shape[-1])
-    return lax.all_to_all(parts, axes, 0, 0).astype(f32).sum(0)
+    here = lax.axis_index(axes)
+    own = lax.dynamic_index_in_dim(parts, here, 0)
+    others = lax.all_to_all(parts.astype(bf16), axes, 0, 0).astype(f32)
+    index = lax.broadcasted_iota(jnp.int32, (count, 1, 1), 0)
+    return jnp.where(index == here, own, others).sum(0)
 
 
 def gather(chunk, axes, count):
@@ -54,8 +58,39 @@
     blocks = lax.dynamic_slice(table, (PANEL // BLOCK, col_id // 2), (PANEL // BLOCK, 1))
     lower = factor_cols[0, 0] * jnp.repeat(blocks[:, 0], BLOCK)[None, :].astype(bf16)
 
-    onehot = (rows_sep[:, None] == jnp.arange(SEPARATOR)[None, :]).astype(bf16)
-    couple_sep = mul(couple, onehot).astype(bf16)
+    share = root_inverse.shape[0]
+    half = SEPARATOR // 2
+    lane = lax.broadcasted_iota(jnp.int32, root_inverse.shape, 1)
+    line = lax.broadcasted_iota(jnp.int32, root_inverse.shape, 0) + col_id * share
+    on_diag = lane == line
+    diag = jnp.where(on_diag, root_inverse, 0.0).sum(1, keepdims=True)
+    pieces = []
+    rest = diag
+    for _ in range(3):
+        pieces.append(lax.reduce_precision(rest, 8, 7))
+        rest = rest - pieces[-1]
+    off = lax.dynamic_slice_in_dim(jnp.where(on_diag, 0.0, root_inverse), row_id * half, half, 1)
+    packed = jnp.concatenate([off] + pieces + [jnp.zeros((share, 125), f32)], 1).astype(bf16)
+    packed = lax.all_gather(packed, "col", axis=0, tiled=True)
+
+    onehot = (jnp.arange(SEPARATOR)[:, None] == rows_sep[None, :]).astype(bf16)
+    couple_sep = lax.dot_general(
+        onehot, couple, (((1,), (1,)), ((), ())), preferred_element_type=f32
+    ).astype(bf16)
+    width = couple.shape[0]
+
+    piece = share // 2
+    pairs = [
+        (core * COLS + chip, (chip // 8) * COLS + 2 * (chip % 8) + core)
+        for core in range(2)
+        for chip in range(COLS)
+    ]
+    root_rows = lax.ppermute(
+        lax.dynamic_slice_in_dim(root_right, row_id * piece, piece, 0), ("row", "col"), pairs
+    )
+
+    swap = [(0, 1), (1, 0)]
+    other_sep = lax.ppermute(couple_sep, "row", swap)
 
     own = mul(inverse, right_side[0], precision=fine)
     first_low = lax.ppermute(own.astype(bf16), "row", [(0, 1)])
@@ -63,16 +98,30 @@
     total = gather(total.astype(bf16), "col", COLS).reshape(PANEL, sources)
     solved = own - mul(inverse, total.astype(f32), precision=fine)
 
-    updates = sum_scatter(mul_t(couple_sep, solved.astype(bf16)), ("col", "row"), COLS * 2)
+    updates = sum_scatter(mul(couple_sep, solved.astype(bf16)), ("row", "col"), COLS * 2)
+    packed, _ = lax.optimization_barrier((packed, updates))
+    off_half = packed[:, :half]
+    diag_all = packed[:, half : half + 3].astype(f32).sum(1, keepdims=True)
+
+    own_rows = (
+        jnp.arange(SEPARATOR)[:, None] == (col_id * share + jnp.arange(share))[None, :]
+    ).astype(bf16)
+    wanted = jnp.concatenate([couple_sep, other_sep, own_rows], 1)
+    mine = lax.dynamic_slice_in_dim(wanted, row_id * half, half, 0)
+    part = mul(off_half, mine)
+    sent = jnp.concatenate([part[:, width : 2 * width], part[:, :width], part[:, 2 * width :]], 1)
+    inner = wanted * diag_all + part + lax.ppermute(sent.astype(bf16), "row", swap).astype(f32)
+    outer = mul_t(off_half, inner.astype(bf16)) + lax.dynamic_slice_in_dim(
+        diag_all * inner, row_id * half, half, 0
+    )
+
     updates = gather(updates, "sub", SUBS).sum(0)
-    half = updates.shape[0]
-    rhs = lax.dynamic_slice_in_dim(root_right, row_id * half, half, 0) - updates
-    rhs = gather(rhs, ("col", "row"), COLS * 2).reshape(SEPARATOR, sources)
-    root_half = mul(root_inverse, rhs, precision=fine)
-    root_part = sum_scatter(mul_t(root_inverse, root_half, precision=fine), "col", COLS)
-    root_full = gather(root_part.astype(bf16), "col", COLS).reshape(SEPARATOR, sources)
+    rhs = gather(root_rows - updates, "col", COLS).reshape(half, sources)
+    applied = mul_t(outer, rhs, precision=fine)
+    theirs = lax.ppermute(applied[width:], "row", swap)
+    value = solved - (applied[:width] + theirs[:width])
+    root_part = applied[2 * width :] + theirs[width:]
 
-    value = solved - mul(couple_sep, root_full)
     value = sum_scatter(mul_t(inverse, value, precision=fine), "col", COLS)
     later_low = gather(value.astype(bf16), "col", COLS).reshape(PANEL, sources)
     terms = lax.ppermute(mul(lower, later_low), "row", [(1, 0)])

time: 189 us -> 178 us (0.942)
  blocking collectives: 134 us -> 13.4 us
  waiting for transfers between devices: 21.9 us -> 70.8 us
  starting transfers between devices: 19.3 us -> 46.4 us
  other arithmetic: 0.54 us -> 15.3 us
  between operations: 0.94 us -> 14.5 us
  matrix products: 6.8 us -> 10.8 us
    all_to_all x5 -> x0, blocking collectives: 90.2 us -> none  [sum_scatter(): return lax.all_to_all(parts, axes, 0, 0).astype(f32).sum(0)]
    all_to_all x0 -> x4, waiting for transfers between devices: none -> 44.1 us  [sum_scatter(): others = lax.all_to_all(parts.astype(bf16), axes, 0, 0).astype(f32)]
    all_to_all x3 -> x1, blocking collectives: 44.2 us -> 13.4 us  [gather(): return lax.all_to_all(spread, axes, 0, 0)]
    all_to_all x0 -> x4, starting transfers between devices: none -> 19.2 us  [sum_scatter(): others = lax.all_to_all(parts.astype(bf16), axes, 0, 0).astype(f32)]
    ppermute x0 -> x4, starting transfers between devices: none -> 6.77 us  [the longest x1 2.39 us: shards(): lax.ppermute(lax.dynamic_slice_in_dim(root_right, row_id * piece, piece,...]
    all_to_all x2 -> x3, starting transfers between devices: 11.8 us -> 15 us  [gather(): return lax.all_to_all(spread, axes, 0, 0)]
    reduce_sum x5 -> x6, other arithmetic: 0.3 us -> 3.27 us  [the longest x1 1.44 us: shards(): diag = jnp.where(on_diag, root_inverse, 0.0).sum(1, keepdims=True)]
    convert_element_type x1 -> x4, other arithmetic: 0.01 us -> 2.71 us  [the longest x3 2.6 us: sum_scatter(): others = lax.all_to_all(parts.astype(bf16), axes, 0, 0).astype(f32)]
  transfers between devices with their start and end apart: 4 -> 14, of which waited for: 4 -> 11; matrix products, arithmetic and copies ran while one was open for 1% -> 10% of each run, Pallas kernels for 0% -> 0%
where the time goes in v2:
time: 178 us; the launch traced here: 177 us
  waiting for transfers between devices  70.8 us (40%)
  starting transfers between devices  46.4 us (26%)
  other arithmetic  15.3 us (9%)
  between operations  14.5 us (8%)
  blocking collectives  13.4 us (8%)
  matrix products  10.8 us (6%)
  local copies, waits for them, and re-layouts  5.65 us (3%)
    all_to_all x4, waiting for transfers between devices, sum_scatter(): others = lax.all_to_all(parts.astype(bf16), axes, 0, 0).astype(f32)  44.1 us
    all_to_all x4, starting transfers between devices, sum_scatter(): others = lax.all_to_all(parts.astype(bf16), axes, 0, 0).astype(f32)  19.2 us
    all_to_all x3, waiting for transfers between devices, gather(): return lax.all_to_all(spread, axes, 0, 0)  18.8 us
    all_to_all x3, starting transfers between devices, gather(): return lax.all_to_all(spread, axes, 0, 0)  15 us
    all_to_all x1, blocking collectives, gather(): return lax.all_to_all(spread, axes, 0, 0)  13.4 us
    dot_general x5, matrix products, mul_t(): lax.dot_general(left, right, first_axes, preferred_element_type=f32, **kw)  4.96 us
    dot_general x5, matrix products, mul(): return jnp.dot(left, right, preferred_element_type=f32, **kw)  4.43 us
    ppermute x1, starting transfers between devices, shards(): terms = lax.ppermute(mul(lower, later_low), 'row', [(1, 0)])  4.07 us
  transfers between devices with their start and end apart: 14, of which 11 were waited for; matrix products, arithmetic and copies ran while one was open for 10% of the time, Pallas kernels for 0%

profile of v2, /device:TPU:1, one launch (start us, length us, event | category | flops | bytes accessed | tf_op | source)
XLA Modules:
  0.0 176.8 jit_solution(4978491470423951681)
XLA Ops:
  7.3 0.1 iota_compare_fusion.5
  7.4 1.4 select_reduce_fusion.4
  9.3 1.0 fusion.25
  10.3 0.8 concatenate.11
  11.1 0.6 fusion.39
  11.8 1.3 collective-permute-start
  13.1 0.2 fusion.35
  13.4 3.6 %collective-permute-done = bf16[128,128]{1,0:T(8,128)(2,1)S(1)} collective-permute-done((bf16[128,128]{1,0:T(8,128)(2,1)S(1)}, bf16[128,128]{1,0:T(8,128)(2,1)S(1)}, u32[]{:S(2)}, u32[]{:S(2)}) %collective-permute-start) | collective-permute-done | bytes 32800 | tf_op jit(solution)/shard_map/ppermute | solution.py:96
  17.0 1.1 convolution_convert_fusion
  18.1 5.6 %all-to-all-start = ((bf16[16,128,128]{2,1,0:T(8,128)(2,1)}), bf16[16,128,128]{2,1,0:T(8,128)(2,1)S(1)}, u32[]{:S(2)}, u32[]{:S(2)}) async-start(bf16[16,128,128]{2,1,0:T(8,128)(2,1)} %bitcast.3), calls=%async_computation | async-start | bytes 1048576 | tf_op jit(solution)/shard_map/all_to_all | solution.py:30
  23.8 0.8 bitcast_convert_fusion
  24.5 10.8 %all-to-all-done = bf16[16,128,128]{2,1,0:T(8,128)(2,1)S(1)} async-done(((bf16[16,128,128]{2,1,0:T(8,128)(2,1)}), bf16[16,128,128]{2,1,0:T(8,128)(2,1)S(1)}, u32[]{:S(2)}, u32[]{:S(2)}) %all-to-all-start) | async-done | bytes 524320 | tf_op jit(solution)/shard_map/all_to_all | solution.py:30
  35.3 0.2 select_reduce_fusion.2
  35.5 0.9 broadcast_in_dim.112
  36.4 3.6 %all-to-all-start.1 = ((bf16[16,128,128]{2,1,0:T(8,128)(2,1)}), bf16[16,128,128]{2,1,0:T(8,128)(2,1)S(1)}, u32[]{:S(2)}, u32[]{:S(2)}) async-start(bf16[16,128,128]{2,1,0:T(8,128)(2,1)} %broadcast_in_dim.112), calls=%async_computation.1 | async-start | bytes 1048576 | tf_op jit(solution)/shard_map/all_to_all | solution.py:37
  40.0 1.4 fusion.2
  41.5 1.9 %collective-permute-start.1 = (bf16[1536,128]{0,1:T(8,128)(2,1)S(1)}, bf16[1536,128]{0,1:T(8,128)(2,1)S(1)}, u32[]{:S(2)}, u32[]{:S(2)}) collective-permute-start(bf16[1536,128]{0,1:T(8,128)(2,1)S(1)} %fusion.2), channel_id=1, source_target_pairs={{0,16},{16,0},{1,17},{17,1},{2,18},{18,2},{3,19},{19,3},{4,20},{20... | collective-permute-start | bytes 1179656 | tf_op jit(solution)/shard_map/ppermute | solution.py:93
  43.5 6.3 %all-to-all-done.1 = bf16[16,128,128]{2,1,0:T(8,128)(2,1)S(1)} async-done(((bf16[16,128,128]{2,1,0:T(8,128)(2,1)}), bf16[16,128,128]{2,1,0:T(8,128)(2,1)S(1)}, u32[]{:S(2)}, u32[]{:S(2)}) %all-to-all-start.1) | async-done | bytes 524320 | tf_op jit(solution)/shard_map/all_to_all | solution.py:37
  49.8 0.4 fusion.10
  50.3 0.3 fusion.32
  50.6 0.8 convert_element_type.92
  51.4 6.3 %all-to-all-start.2 = ((bf16[32,48,128]{2,1,0:T(8,128)(2,1)}), bf16[32,48,128]{2,1,0:T(8,128)(2,1)S(1)}, u32[]{:S(2)}, u32[]{:S(2)}) async-start(bf16[32,48,128]{2,1,0:T(8,128)(2,1)} %convert_element_type.92), calls=%async_computation.2 | async-start | bytes 786432 | tf_op jit(solution)/shard_map/all_to_all | solution.py:30
  57.7 1.1 pad_maximum_fusion
  58.8 12.1 %all-to-all-done.2 = bf16[32,48,128]{2,1,0:T(8,128)(2,1)S(1)} async-done(((bf16[32,48,128]{2,1,0:T(8,128)(2,1)}), bf16[32,48,128]{2,1,0:T(8,128)(2,1)S(1)}, u32[]{:S(2)}, u32[]{:S(2)}) %all-to-all-start.2) | async-done | bytes 393248 | tf_op jit(solution)/shard_map/all_to_all | solution.py:30
  70.9 0.1 select_reduce_fusion.3
  71.1 2.4 %all-gather.2.cloned.1.call-done = bf16[1536,896]{1,0:T(8,128)(2,1)} async-done(((bf16[96,896]{1,0:T(8,128)(2,1)}), bf16[1536,896]{1,0:T(8,128)(2,1)}) %all-gather.2.cloned.1.call-update) | async-done | bytes 2752528 | tf_op jit(solution)/shard_map/all_gather | solution.py:74
  73.4 2.8 %fusion.40 = (bf16[1536,352]{0,1:T(8,128)(2,1)S(1)}, f32[1536,352]{0,1:T(8,128)S(1)}) fusion(bf16[1536,352]{0,1:T(8,128)(2,1)} %pad_maximum_fusion, s32[]{:T(128)S(6)} %select_n.55, bf16[1536,896]{1,0:T(8,128)(2,1)} %all-gather.2.cloned.1.call-done), kind=kOutput, calls=%fused_computation.73 | convolution fusion | flops 831012864 | bytes 6144004 | tf_op jit(solution)/shard_map/dot_general | solution.py:19
  76.3 1.1 pad_maximum_fusion.1
  77.4 0.6 collective-permute-start.2
  78.0 0.7 broadcast_in_dim.118
  78.7 7.3 %all-to-all-start.3 = ((f32[8,48,128]{2,1,0:T(8,128)}), f32[8,48,128]{2,1,0:T(8,128)}, u32[]{:S(2)}, u32[]{:S(2)}) async-start(f32[8,48,128]{2,1,0:T(8,128)} %broadcast_in_dim.118), calls=%async_computation.3 | async-start | bytes 393216 | tf_op jit(solution)/shard_map/all_to_all | solution.py:37
  86.0 0.7 constant_dynamic-slice_fusion
  86.7 2.4 %collective-permute-start.3 = (f32[48,128]{1,0:T(8,128)S(1)}, f32[48,128]{1,0:T(8,128)}, u32[]{:S(2)}, u32[]{:S(2)}) collective-permute-start(f32[48,128]{1,0:T(8,128)S(1)} %constant_dynamic-slice_fusion), channel_id=1, source_target_pairs={{0,0},{1,2},{2,4},{3,6},{4,8},{5,10},{6,12},{7,14},{8,16},{9,18},{... | collective-permute-start | bytes 73736 | tf_op jit(solution)/shard_map/ppermute | solution.py:88
  89.1 7.8 %all-to-all-done.3 = f32[8,48,128]{2,1,0:T(8,128)} async-done(((f32[8,48,128]{2,1,0:T(8,128)}), f32[8,48,128]{2,1,0:T(8,128)}, u32[]{:S(2)}, u32[]{:S(2)}) %all-to-all-start.3) | async-done | bytes 196640 | tf_op jit(solution)/shard_map/all_to_all | solution.py:37
  96.9 0.9 reduce_sum.70
  97.8 0.7 sub.56
  98.6 0.8 broadcast_in_dim.119
  99.4 4.2 %all-to-all-start.4 = ((f32[16,48,128]{2,1,0:T(8,128)}), f32[16,48,128]{2,1,0:T(8,128)}, u32[]{:S(2)}, u32[]{:S(2)}) async-start(f32[16,48,128]{2,1,0:T(8,128)} %broadcast_in_dim.119), calls=%async_computation.4 | async-start | bytes 786432 | tf_op jit(solution)/shard_map/all_to_all | solution.py:37
  103.6 1.2 convert_reduce_fusion
  104.8 2.0 %convert_add_fusion = f32[1536,352]{0,1:T(8,128)S(1)} fusion(bf16[1536,352]{0,1:T(8,128)(2,1)} %collective-permute-done.2, f32[1536,352]{0,1:T(8,128)S(1)} %get-tuple-element.12, f32[1536]{0:T(1024)S(1)} %convert_reduce_fusion, bf16[1536,96]{0,1:T(8,128)(2,1)S(1)} %fusion.18, bf16[1536,128]{0,1:T(8,128)(2,1)} %copy-done.3, bf16[1536,128]{0,1:T(8,128)(2,1)} %copy-done.2), kind=kLoop, calls=%fused_computation.7 | loop fusion | flops 5406720 | bytes 6494208 | tf_op jit(solution)/shard_map/add | solution.py:113
  106.9 0.3 copy-done.1
  107.2 1.0 fusion.7
  108.2 4.7 %all-to-all-done.4 = f32[16,48,128]{2,1,0:T(8,128)} async-done(((f32[16,48,128]{2,1,0:T(8,128)}), f32[16,48,128]{2,1,0:T(8,128)}, u32[]{:S(2)}, u32[]{:S(2)}) %all-to-all-start.4) | async-done | bytes 393248 | tf_op jit(solution)/shard_map/all_to_all | solution.py:37
  112.9 1.6 fusion.41
  114.5 1.8 %collective-permute-start.4 = (f32[224,128]{1,0:T(8,128)S(1)}, f32[224,128]{1,0:T(8,128)S(1)}, u32[]{:S(2)}, u32[]{:S(2)}) collective-permute-start(f32[224,128]{1,0:T(8,128)S(1)} %slice.51), channel_id=1, source_target_pairs={{0,16},{16,0},{1,17},{17,1},{2,18},{18,2},{3,19},{19,3},{4,20},{20... | collective-permute-start | bytes 344072 | tf_op jit(solution)/shard_map/ppermute | solution.py:121
  116.3 1.0 collective-permute-done.4
  117.3 0.6 convolution_bitcast_fusion.1
  117.9 0.3 copy.33
  118.3 0.9 convert_element_type.99
  119.2 3.7 %all-to-all-start.5 = ((bf16[16,128,128]{2,1,0:T(8,128)(2,1)}), bf16[16,128,128]{2,1,0:T(8,128)(2,1)S(1)}, u32[]{:S(2)}, u32[]{:S(2)}) async-start(bf16[16,128,128]{2,1,0:T(8,128)(2,1)} %convert_element_type.99), calls=%async_computation.5 | async-start | bytes 1048576 | tf_op jit(solution)/shard_map/all_to_all | solution.py:30
  122.9 10.9 %all-to-all-done.5 = bf16[16,128,128]{2,1,0:T(8,128)(2,1)S(1)} async-done(((bf16[16,128,128]{2,1,0:T(8,128)(2,1)}), bf16[16,128,128]{2,1,0:T(8,128)(2,1)S(1)}, u32[]{:S(2)}, u32[]{:S(2)}) %all-to-all-start.5) | async-done | bytes 524320 | tf_op jit(solution)/shard_map/all_to_all | solution.py:30
  133.8 0.2 select_reduce_fusion.1
  134.1 13.4 %all_to_all.40 = bf16[16,128,128]{2,1,0:T(8,128)(2,1)S(1)} all-to-all(bf16[16,128,128]{2,1,0:T(8,128)(2,1)S(1)} %broadcast_in_dim.122), channel_id=1, replica_groups=mesh['sub'=8,'row'=2,'col'=16] {'col'}, dimensions={0} | all-to-all | bytes 1048576 | tf_op jit(solution)/shard_map/all_to_all | solution.py:37
  147.5 0.3 fusion.20
  147.8 4.1 %collective-permute-start.5 = (f32[128,128]{1,0:T(8,128)S(1)}, f32[128,128]{1,0:T(8,128)S(1)}, u32[]{:S(2)}, u32[]{:S(2)}) collective-permute-start(f32[128,128]{1,0:T(8,128)S(1)} %fusion.20), channel_id=1, source_target_pairs={{16,0},{17,1},{18,2},{19,3},{20,4},{21,5},{22,6},{23,7},{24,8},{25... | collective-permute-start | bytes 196616 | tf_op jit(solution)/shard_map/ppermute | solution.py:127
  151.9 0.9 collective-permute-done.5
  152.8 0.6 convolution_bitcast_fusion
  153.4 0.3 copy.34
  153.7 0.9 convert_element_type.102
  154.6 3.6 %all-to-all-start.7 = ((bf16[16,128,128]{2,1,0:T(8,128)(2,1)}), bf16[16,128,128]{2,1,0:T(8,128)(2,1)S(1)}, u32[]{:S(2)}, u32[]{:S(2)}) async-start(bf16[16,128,128]{2,1,0:T(8,128)(2,1)} %convert_element_type.102), calls=%async_computation.7 | async-start | bytes 1048576 | tf_op jit(solution)/shard_map/all_to_all | solution.py:30
  158.2 0.6 slice_add_fusion.1
  158.8 10.3 %all-to-all-done.7 = bf16[16,128,128]{2,1,0:T(8,128)(2,1)S(1)} async-done(((bf16[16,128,128]{2,1,0:T(8,128)(2,1)}), bf16[16,128,128]{2,1,0:T(8,128)(2,1)S(1)}, u32[]{:S(2)}, u32[]{:S(2)}) %all-to-all-start.7) | async-done | bytes 524320 | tf_op jit(solution)/shard_map/all_to_all | solution.py:30
  169.2 0.2 select_reduce_fusion
  169.3 0.6 subtract_bitcast_fusion
  (56 shorter events, 1.0 us)
Async XLA Ops:
  7.2 3.9 %copy-start = (f32[1,128,2048]{2,1,0:T(8,128)S(1)}, f32[1,128,2048]{2,1,0:T(8,128)}, u32[]{:S(2)}) copy-start(f32[1,128,2048]{2,1,0:T(8,128)} %param.10) | copy-start | bytes 3145732
  7.2 3.9 %copy-start.4 = (f32[1,2048,128]{2,1,0:T(8,128)S(1)}, f32[1,2048,128]{2,1,0:T(8,128)}, u32[]{:S(2)}) copy-start(f32[1,2048,128]{2,1,0:T(8,128)} %param.14) | copy-start | bytes 3145732
  7.2 5.9 %copy-start.13 = (s32[1,16,16]{2,1,0:T(8,128)S(1)}, s32[1,16,16]{2,1,0:T(8,128)}, u32[]{:S(2)}) copy-start(s32[1,16,16]{2,1,0:T(8,128)} %param.9) | copy-start | bytes 3076
  7.2 9.8 %copy-start.7 = (bf16[1,2,128,2048]{3,2,1,0:T(8,128)(2,1)S(1)}, bf16[1,2,128,2048]{3,2,1,0:T(8,128)(2,1)}, u32[]{:S(2)}) copy-start(bf16[1,2,128,2048]{3,2,1,0:T(8,128)(2,1)} %param.8) | copy-start | bytes 3145732
  7.2 66.2 %all-gather.2.cloned.1.call-start = ((), (), s32[]{:S(2)}) async-start(), calls=%async_computation.8 | async-start | bytes 2924544 | tf_op jit(solution)/shard_map/all_gather | solution.py:74
  11.8 5.2 %collective-permute-start = (bf16[128,128]{1,0:T(8,128)(2,1)S(1)}, bf16[128,128]{1,0:T(8,128)(2,1)S(1)}, u32[]{:S(2)}, u32[]{:S(2)}) collective-permute-start(bf16[128,128]{1,0:T(8,128)(2,1)S(1)} %get-tuple-element.9), channel_id=1, source_target_pairs={{0,16},{1,17},{2,18},{3,19},{4,20},{5,21},{6,22},{7,23},{8,24},{9,... | collective-permute-start | bytes 98312 | tf_op jit(solution)/shard_map/ppermute | solution.py:96
  13.4 4.8 %copy-start.9 = (bf16[1,2,8,128]{3,1,2,0:T(2,128)(2,1)}, bf16[1,2,8,128]{3,1,2,0:T(2,128)(2,1)S(1)}, u32[]{:S(2)}) copy-start(bf16[1,2,8,128]{3,1,2,0:T(2,128)(2,1)S(1)} %copy.35) | copy-start | bytes 12292
  17.0 23.0 %copy-start.15 = (s32[1,1024]{1,0:T(1,128)S(1)}, s32[1,1024]{1,0:T(1,128)}, u32[]{:S(2)}) copy-start(s32[1,1024]{1,0:T(1,128)} %param.12) | copy-start | bytes 12292
  18.1 21.9 %copy-start.14 = (bf16[1,1,128,1024]{3,2,1,0:T(8,128)(2,1)S(1)}, bf16[1,1,128,1024]{3,2,1,0:T(8,128)(2,1)}, u32[]{:S(2)}) copy-start(bf16[1,1,128,1024]{3,2,1,0:T(8,128)(2,1)} %param.11) | copy-start | bytes 786436
  18.1 17.2 %all-to-all-start = ((bf16[16,128,128]{2,1,0:T(8,128)(2,1)}), bf16[16,128,128]{2,1,0:T(8,128)(2,1)S(1)}, u32[]{:S(2)}, u32[]{:S(2)}) async-start(bf16[16,128,128]{2,1,0:T(8,128)(2,1)} %bitcast.3), calls=%async_computation | async-start | bytes 1048576 | tf_op jit(solution)/shard_map/all_to_all | solution.py:30
  23.7 16.2 %copy-start.11 = (pred[16]{0:T(512)(128)(4,1)}, pred[16]{0:T(512)(128)(4,1)S(1)}, u32[]{:S(2)}) copy-start(pred[16]{0:T(512)(128)(4,1)S(1)} %iota_compare_fusion.7) | copy-start | bytes 52
  36.4 13.4 %all-to-all-start.1 = ((bf16[16,128,128]{2,1,0:T(8,128)(2,1)}), bf16[16,128,128]{2,1,0:T(8,128)(2,1)S(1)}, u32[]{:S(2)}, u32[]{:S(2)}) async-start(bf16[16,128,128]{2,1,0:T(8,128)(2,1)} %broadcast_in_dim.112), calls=%async_computation.1 | async-start | bytes 1048576 | tf_op jit(solution)/shard_map/all_to_all | solution.py:37
  41.5 16.2 %copy-start.2 = (bf16[1536,128]{0,1:T(8,128)(2,1)}, bf16[1536,128]{0,1:T(8,128)(2,1)S(1)}, u32[]{:S(2)}) copy-start(bf16[1536,128]{0,1:T(8,128)(2,1)S(1)} %fusion.2) | copy-start | bytes 1179652
  41.5 16.2 %collective-permute-start.1 = (bf16[1536,128]{0,1:T(8,128)(2,1)S(1)}, bf16[1536,128]{0,1:T(8,128)(2,1)S(1)}, u32[]{:S(2)}, u32[]{:S(2)}) collective-permute-start(bf16[1536,128]{0,1:T(8,128)(2,1)S(1)} %fusion.2), channel_id=1, source_target_pairs={{0,16},{16,0},{1,17},{17,1},{2,18},{18,2},{3,19},{19,3},{4,20},{20... | collective-permute-start | bytes 1179656 | tf_op jit(solution)/shard_map/ppermute | solution.py:93
  50.3 1.1 copy-start.5
  51.4 19.5 %all-to-all-start.2 = ((bf16[32,48,128]{2,1,0:T(8,128)(2,1)}), bf16[32,48,128]{2,1,0:T(8,128)(2,1)S(1)}, u32[]{:S(2)}, u32[]{:S(2)}) async-start(bf16[32,48,128]{2,1,0:T(8,128)(2,1)} %convert_element_type.92), calls=%async_computation.2 | async-start | bytes 786432 | tf_op jit(solution)/shard_map/all_to_all | solution.py:30
  57.7 13.4 %copy-start.3 = (bf16[1536,128]{0,1:T(8,128)(2,1)}, bf16[1536,128]{0,1:T(8,128)(2,1)S(1)}, u32[]{:S(2)}) copy-start(bf16[1536,128]{0,1:T(8,128)(2,1)S(1)} %collective-permute-done.1) | copy-start | bytes 1179652
  77.4 27.5 %collective-permute-start.2 = (bf16[1536,352]{0,1:T(8,128)(2,1)}, bf16[1536,352]{0,1:T(8,128)(2,1)}, u32[]{:S(2)}, u32[]{:S(2)}) collective-permute-start(bf16[1536,352]{0,1:T(8,128)(2,1)} %pad_maximum_fusion.1), channel_id=1, source_target_pairs={{0,16},{16,0},{1,17},{17,1},{2,18},{18,2},{3,19},{19,3},{4,20},{20... | collective-permute-start | bytes 3244040 | tf_op jit(solution)/shard_map/ppermute | solution.py:113
  78.7 18.2 %all-to-all-start.3 = ((f32[8,48,128]{2,1,0:T(8,128)}), f32[8,48,128]{2,1,0:T(8,128)}, u32[]{:S(2)}, u32[]{:S(2)}) async-start(f32[8,48,128]{2,1,0:T(8,128)} %broadcast_in_dim.118), calls=%async_computation.3 | async-start | bytes 393216 | tf_op jit(solution)/shard_map/all_to_all | solution.py:37
  86.7 11.1 %collective-permute-start.3 = (f32[48,128]{1,0:T(8,128)S(1)}, f32[48,128]{1,0:T(8,128)}, u32[]{:S(2)}, u32[]{:S(2)}) collective-permute-start(f32[48,128]{1,0:T(8,128)S(1)} %constant_dynamic-slice_fusion), channel_id=1, source_target_pairs={{0,0},{1,2},{2,4},{3,6},{4,8},{5,10},{6,12},{7,14},{8,16},{9,18},{... | collective-permute-start | bytes 73736 | tf_op jit(solution)/shard_map/ppermute | solution.py:88
  99.4 13.5 %all-to-all-start.4 = ((f32[16,48,128]{2,1,0:T(8,128)}), f32[16,48,128]{2,1,0:T(8,128)}, u32[]{:S(2)}, u32[]{:S(2)}) async-start(f32[16,48,128]{2,1,0:T(8,128)} %broadcast_in_dim.119), calls=%async_computation.4 | async-start | bytes 786432 | tf_op jit(solution)/shard_map/all_to_all | solution.py:37
  104.8 2.3 %copy-start.1 = (bf16[1536,896]{1,0:T(8,128)(2,1)S(1)}, bf16[1536,896]{1,0:T(8,128)(2,1)}, u32[]{:S(2)}) copy-start(bf16[1536,896]{1,0:T(8,128)(2,1)} %all-gather.2.cloned.1.call-done) | copy-start | bytes 8257540
  107.2 10.1 %copy-start.6 = (f32[128,128]{1,0:T(8,128)S(1)}, f32[128,128]{1,0:T(8,128)}, u32[]{:S(2)}) copy-start(f32[128,128]{1,0:T(8,128)} %copy-done.5) | copy-start | bytes 196612
  114.5 2.8 %collective-permute-start.4 = (f32[224,128]{1,0:T(8,128)S(1)}, f32[224,128]{1,0:T(8,128)S(1)}, u32[]{:S(2)}, u32[]{:S(2)}) collective-permute-start(f32[224,128]{1,0:T(8,128)S(1)} %slice.51), channel_id=1, source_target_pairs={{0,16},{16,0},{1,17},{17,1},{2,18},{18,2},{3,19},{19,3},{4,20},{20... | collective-permute-start | bytes 344072 | tf_op jit(solution)/shard_map/ppermute | solution.py:121
  117.9 15.9 %copy-start.12 = (pred[16]{0:T(512)(128)(4,1)S(1)}, pred[16]{0:T(512)(128)(4,1)}, u32[]{:S(2)}) copy-start(pred[16]{0:T(512)(128)(4,1)} %copy-done.11) | copy-start | bytes 52
  119.2 28.3 %copy-start.10 = (bf16[1,2,8,128]{3,1,2,0:T(2,128)(2,1)S(1)}, bf16[1,2,8,128]{3,1,2,0:T(2,128)(2,1)}, u32[]{:S(2)}) copy-start(bf16[1,2,8,128]{3,1,2,0:T(2,128)(2,1)} %copy-done.9) | copy-start | bytes 12292
  119.2 14.7 %all-to-all-start.5 = ((bf16[16,128,128]{2,1,0:T(8,128)(2,1)}), bf16[16,128,128]{2,1,0:T(8,128)(2,1)S(1)}, u32[]{:S(2)}, u32[]{:S(2)}) async-start(bf16[16,128,128]{2,1,0:T(8,128)(2,1)} %convert_element_type.99), calls=%async_computation.5 | async-start | bytes 1048576 | tf_op jit(solution)/shard_map/all_to_all | solution.py:30
  122.9 24.6 %copy-start.8 = (bf16[1,2,128,2048]{3,2,1,0:T(8,128)(2,1)S(1)}, bf16[1,2,128,2048]{3,2,1,0:T(8,128)(2,1)}, u32[]{:S(2)}) copy-start(bf16[1,2,128,2048]{3,2,1,0:T(8,128)(2,1)} %param.8) | copy-start | bytes 3145732
  147.8 5.0 %collective-permute-start.5 = (f32[128,128]{1,0:T(8,128)S(1)}, f32[128,128]{1,0:T(8,128)S(1)}, u32[]{:S(2)}, u32[]{:S(2)}) collective-permute-start(f32[128,128]{1,0:T(8,128)S(1)} %fusion.20), channel_id=1, source_target_pairs={{16,0},{17,1},{18,2},{19,3},{20,4},{21,5},{22,6},{23,7},{24,8},{25... | collective-permute-start | bytes 196616 | tf_op jit(solution)/shard_map/ppermute | solution.py:127
  154.6 14.6 %all-to-all-start.7 = ((bf16[16,128,128]{2,1,0:T(8,128)(2,1)}), bf16[16,128,128]{2,1,0:T(8,128)(2,1)S(1)}, u32[]{:S(2)}, u32[]{:S(2)}) async-start(bf16[16,128,128]{2,1,0:T(8,128)(2,1)} %convert_element_type.102), calls=%async_computation.7 | async-start | bytes 1048576 | tf_op jit(solution)/shard_map/all_to_all | solution.py:30
Sparse Core Ops, SparseCore 0:
  11.2 62.1 all-gather.1

commit v3 on v2

--- a/solution.py
+++ b/solution.py
@@ -21,6 +21,29 @@
 
 def mul_t(left, right, **kw):
     return lax.dot_general(left, right, first_axes, preferred_element_type=f32, **kw)
+
+
+def split3(value):
+    pieces = []
+    for _ in range(3):
+        pieces.append(lax.reduce_precision(value, 8, 7))
+        value = value - pieces[-1]
+    return pieces
+
+
+def plane(step_y, step_x, source=1, target=1):
+    return [
+        (
+            source * COLS + 4 * y + x,
+            target * COLS + 4 * ((y + step_y) % 4) + (x + step_x) % 4,
+        )
+        for y in range(4)
+        for x in range(4)
+    ]
+
+
+def send(value, pairs):
+    return lax.ppermute(value, ("row", "col"), pairs)
 
 
 def sum_scatter(partial, axes, count):
@@ -55,8 +78,36 @@
     col_id = lax.axis_index("col")
     sources = right_side.shape[-1]
 
+    own = mul(inverse, right_side[0], precision=fine)
+    own_low = own.astype(bf16)
+
     blocks = lax.dynamic_slice(table, (PANEL // BLOCK, col_id // 2), (PANEL // BLOCK, 1))
     lower = factor_cols[0, 0] * jnp.repeat(blocks[:, 0], BLOCK)[None, :].astype(bf16)
+    width = lower.shape[0]
+    square = lax.dynamic_slice_in_dim(inverse, col_id * width, width, 1)
+    line = lax.broadcasted_iota(jnp.int32, inverse.shape, 0) + col_id * width
+    apart = jnp.where(lax.broadcasted_iota(jnp.int32, inverse.shape, 1) == line, 0.0, inverse)
+    diag = jnp.where(jnp.eye(width, dtype=bool), square, 0.0).sum(0, keepdims=True)
+    rest = jnp.concatenate(split3(diag) + [jnp.zeros((13, width), f32)], 0)
+    rest = jnp.pad(rest, ((0, 0), (0, PANEL - width)))
+    apart = jnp.concatenate([apart, rest], 0).astype(bf16)
+    lowers = jnp.concatenate([lower] + [send(lower, plane(-k, 0)) for k in (1, 2, 3)], 0)
+    first = jnp.concatenate([send(own_low, plane(-k, 0, 0, 1)) for k in range(4)], 0)
+    aparts = [apart] + [send(apart, plane(0, -k)) for k in (1, 2, 3)]
+    elim = []
+    for k in range(4):
+        chip = col_id // 4 * 4 + (col_id + k) % 4
+        rows = lax.dynamic_slice_in_dim(lowers, chip * width, width, 1).astype(f32)
+        scale = aparts[k][width : width + 3, :width].astype(f32).sum(0, keepdims=True)
+        off = lax.dot_general(
+            lowers, aparts[k][:width], (((1,), (1,)), ((), ())), preferred_element_type=f32
+        )
+        elim.append(off + rows * scale)
+    elim = jnp.concatenate(elim, 1)
+    terms = mul_t(elim, first.astype(f32), precision=fine)
+    solved = own - terms[:width]
+    for k in (1, 2, 3):
+        solved = solved - send(terms[k * width : (k + 1) * width], plane(0, k))
 
     share = root_inverse.shape[0]
     half = SEPARATOR // 2
@@ -64,20 +115,23 @@
     line = lax.broadcasted_iota(jnp.int32, root_inverse.shape, 0) + col_id * share
     on_diag = lane == line
     diag = jnp.where(on_diag, root_inverse, 0.0).sum(1, keepdims=True)
-    pieces = []
-    rest = diag
-    for _ in range(3):
-        pieces.append(lax.reduce_precision(rest, 8, 7))
-        rest = rest - pieces[-1]
+    pieces = split3(diag)
     off = lax.dynamic_slice_in_dim(jnp.where(on_diag, 0.0, root_inverse), row_id * half, half, 1)
     packed = jnp.concatenate([off] + pieces + [jnp.zeros((share, 125), f32)], 1).astype(bf16)
-    packed = lax.all_gather(packed, "col", axis=0, tiled=True)
+    packed, _ = lax.optimization_barrier((packed, lowers))
+    for step_y, step_x, place in ((0, 1, col_id % 4), (1, 0, col_id // 4)):
+        whole = jnp.zeros((4,) + packed.shape, bf16)
+        for k in range(4):
+            pairs = [(i % COLS, j % COLS) for i, j in plane(-k * step_y, -k * step_x)]
+            piece = lax.ppermute(packed, "col", pairs) if k else packed
+            whole = lax.dynamic_update_slice_in_dim(whole, piece[None], (place + k) % 4, 0)
+        packed = whole
+    packed = packed.reshape(SEPARATOR, half + 128)
 
     onehot = (jnp.arange(SEPARATOR)[:, None] == rows_sep[None, :]).astype(bf16)
     couple_sep = lax.dot_general(
         onehot, couple, (((1,), (1,)), ((), ())), preferred_element_type=f32
     ).astype(bf16)
-    width = couple.shape[0]
 
     piece = share // 2
     pairs = [
@@ -91,12 +145,6 @@
 
     swap = [(0, 1), (1, 0)]
     other_sep = lax.ppermute(couple_sep, "row", swap)
-
-    own = mul(inverse, right_side[0], precision=fine)
-    first_low = lax.ppermute(own.astype(bf16), "row", [(0, 1)])
-    total = sum_scatter(mul_t(lower, first_low).astype(bf16), "col", COLS)
-    total = gather(total.astype(bf16), "col", COLS).reshape(PANEL, sources)
-    solved = own - mul(inverse, total.astype(f32), precision=fine)
 
     updates = sum_scatter(mul(couple_sep, solved.astype(bf16)), ("row", "col"), COLS * 2)
     packed, _ = lax.optimization_barrier((packed, updates))
@@ -122,10 +170,13 @@
     value = solved - (applied[:width] + theirs[:width])
     root_part = applied[2 * width :] + theirs[width:]
 
+    later = jnp.concatenate([value] + [send(value, plane(0, -k)) for k in (1, 2, 3)], 0)
+    terms = mul(elim, later, precision=fine)
+    taken = terms[:width]
+    for k in (1, 2, 3):
+        taken = taken + send(terms[k * width : (k + 1) * width], plane(k, 0))
+    value = value - lax.ppermute(taken, "row", [(1, 0)])
     value = sum_scatter(mul_t(inverse, value, precision=fine), "col", COLS)
-    later_low = gather(value.astype(bf16), "col", COLS).reshape(PANEL, sources)
-    terms = lax.ppermute(mul(lower, later_low), "row", [(1, 0)])
-    value = value - sum_scatter(mul_t(inverse, terms, precision=fine), "col", COLS)
     return value[None], root_part
 
 

time: 178 us -> 204 us (1.15)
  starting transfers between devices: 46.4 us -> 90.9 us
  waiting for transfers between devices: 70.8 us -> 53.9 us
  blocking collectives: 13.4 us -> 0 us
  local copies, waits for them, and re-layouts: 5.65 us -> 18.5 us
  between operations: 14.5 us -> 1.75 us
  matrix products: 10.8 us -> 18 us
  other arithmetic: 15.3 us -> 19.3 us
    ppermute x2 -> x26, starting transfers between devices: 5.37 us -> 59.2 us  [the longest x19 50.1 us: send(): return lax.ppermute(value, ('row', 'col'), pairs)]
    all_to_all x4 -> x2, waiting for transfers between devices: 44.1 us -> 9.85 us  [sum_scatter(): others = lax.all_to_all(parts.astype(bf16), axes, 0, 0).astype(f32)]
    ppermute x2 -> x26, waiting for transfers between devices: 4.5 us -> 32.9 us  [the longest x6 24.6 us: shards(): piece = lax.ppermute(packed, 'col', pairs) if k else packed]
    all_to_all x1 -> x0, blocking collectives: 13.4 us -> none  [gather(): return lax.all_to_all(spread, axes, 0, 0)]
    dynamic_update_slice x0 -> x8, local copies, waits for them, and re-layouts: none -> 9.62 us  [shards(): lax.dynamic_update_slice_in_dim(whole, piece[None], (place + k) % 4, 0)]
    all_to_all x4 -> x2, starting transfers between devices: 19.2 us -> 10 us  [sum_scatter(): others = lax.all_to_all(parts.astype(bf16), axes, 0, 0).astype(f32)]
    all_to_all x3 -> x2, waiting for transfers between devices: 18.8 us -> 10.2 us  [gather(): return lax.all_to_all(spread, axes, 0, 0)]
    dot_general x0 -> x4, matrix products: none -> 3.99 us  [shards(): lax.dot_general(lowers, aparts[k][:width], (((1,), (1,)), ((), ())), pref...]
  transfers between devices with their start and end apart: 14 -> 34, of which waited for: 11 -> 12; matrix products, arithmetic and copies ran while one was open for 10% -> 21% of each run, Pallas kernels for 0% -> 0%
where the time goes in v3:
time: 204 us; the launch traced here: 202 us
  starting transfers between devices  90.9 us (45%)
  waiting for transfers between devices  53.9 us (26%)
  other arithmetic  19.3 us (9%)
  local copies, waits for them, and re-layouts  18.5 us (9%)
  matrix products  18 us (9%)
    ppermute x19, starting transfers between devices, send(): return lax.ppermute(value, ('row', 'col'), pairs)  50.1 us
    ppermute x6, waiting for transfers between devices, shards(): piece = lax.ppermute(packed, 'col', pairs) if k else packed  24.6 us
    all_to_all x2, starting transfers between devices, gather(): return lax.all_to_all(spread, axes, 0, 0)  13.8 us
    all_to_all x2, waiting for transfers between devices, gather(): return lax.all_to_all(spread, axes, 0, 0)  10.2 us
    all_to_all x2, starting transfers between devices, sum_scatter(): others = lax.all_to_all(parts.astype(bf16), axes, 0, 0).astype(f32)  10 us
    all_to_all x2, waiting for transfers between devices, sum_scatter(): others = lax.all_to_all(parts.astype(bf16), axes, 0, 0).astype(f32)  9.85 us
    dynamic_update_slice x8, local copies, waits for them, and re-layouts, shards(): lax.dynamic_update_slice_in_dim(whole, piece[None], (place + k) % 4, 0)  9.62 us
    ppermute x6, starting transfers between devices, shards(): piece = lax.ppermute(packed, 'col', pairs) if k else packed  7.83 us
  transfers between devices with their start and end apart: 34, of which 12 were waited for; matrix products, arithmetic and copies ran while one was open for 21% of the time, Pallas kernels for 0%

profile of v3, /device:TPU:1, one launch (start us, length us, event | category | flops | bytes accessed | tf_op | source)
XLA Modules:
  0.0 202.3 jit_solution(16933158070594317612)
XLA Ops:
  0.7 1.0 fusion.54
  1.8 1.1 slice.85
  3.5 5.5 %collective-permute-start = (bf16[128,2048]{0,1:T(8,128)(2,1)S(1)}, bf16[128,2048]{0,1:T(8,128)(2,1)}, u32[]{:S(2)}, u32[]{:S(2)}) collective-permute-start(bf16[128,2048]{0,1:T(8,128)(2,1)S(1)} %bitcast_multiply_fusion), channel_id=1, source_target_pairs={{16,28},{17,29},{18,30},{19,31},{20,16},{21,17},{22,18},{23,19},{2... | collective-permute-start | bytes 1572872 | tf_op jit(solution)/shard_map/ppermute | solution.py:46
  9.0 2.3 %collective-permute-start.1 = (bf16[128,2048]{0,1:T(8,128)(2,1)S(1)}, bf16[128,2048]{0,1:T(8,128)(2,1)}, u32[]{:S(2)}, u32[]{:S(2)}) collective-permute-start(bf16[128,2048]{0,1:T(8,128)(2,1)S(1)} %bitcast_multiply_fusion), channel_id=1, source_target_pairs={{16,24},{17,25},{18,26},{19,27},{20,28},{21,29},{22,30},{23,31},{2... | collective-permute-start | bytes 1572872 | tf_op jit(solution)/shard_map/ppermute | solution.py:46
  11.2 2.6 %collective-permute-start.2 = (bf16[128,2048]{0,1:T(8,128)(2,1)S(1)}, bf16[128,2048]{0,1:T(8,128)(2,1)}, u32[]{:S(2)}, u32[]{:S(2)}) collective-permute-start(bf16[128,2048]{0,1:T(8,128)(2,1)S(1)} %bitcast_multiply_fusion), channel_id=1, source_target_pairs={{16,20},{17,21},{18,22},{19,23},{20,24},{21,25},{22,26},{23,27},{2... | collective-permute-start | bytes 1572872 | tf_op jit(solution)/shard_map/ppermute | solution.py:46
  15.1 4.4 %collective-permute-start.3 = (bf16[144,2048]{1,0:T(8,128)(2,1)}, bf16[144,2048]{1,0:T(8,128)(2,1)}, u32[]{:S(2)}, u32[]{:S(2)}) collective-permute-start(bf16[144,2048]{1,0:T(8,128)(2,1)} %fusion.20), channel_id=1, source_target_pairs={{16,19},{17,16},{18,17},{19,18},{20,23},{21,20},{22,21},{23,22},{2... | collective-permute-start | bytes 1769480 | tf_op jit(solution)/shard_map/ppermute | solution.py:46
  19.5 2.4 %collective-permute-start.4 = (bf16[144,2048]{1,0:T(8,128)(2,1)}, bf16[144,2048]{1,0:T(8,128)(2,1)}, u32[]{:S(2)}, u32[]{:S(2)}) collective-permute-start(bf16[144,2048]{1,0:T(8,128)(2,1)} %fusion.20), channel_id=1, source_target_pairs={{16,18},{17,19},{18,16},{19,17},{20,22},{21,23},{22,20},{23,21},{2... | collective-permute-start | bytes 1769480 | tf_op jit(solution)/shard_map/ppermute | solution.py:46
  22.1 1.3 select_reduce_fusion.2
  24.0 1.3 fusion.65
  25.2 1.0 fusion.26
  26.3 2.4 %fusion.2 = bf16[1536,128]{0,1:T(8,128)(2,1)S(1)} fusion(s32[1024]{0:T(1024)S(1)} %bitcast.90, bf16[1,1,128,1024]{3,2,1,0:T(8,128)(2,1)} %param.11), kind=kOutput, calls=%fused_computation.3 | convolution fusion | flops 404422656 | bytes 659456 | tf_op jit(solution)/shard_map/dot_general | solution.py:132
  30.3 2.5 %collective-permute-start.5 = (bf16[144,2048]{1,0:T(8,128)(2,1)}, bf16[144,2048]{1,0:T(8,128)(2,1)S(1)}, u32[]{:S(2)}, u32[]{:S(2)}) collective-permute-start(bf16[144,2048]{1,0:T(8,128)(2,1)} %fusion.20), channel_id=1, source_target_pairs={{16,17},{17,18},{18,19},{19,16},{20,21},{21,22},{22,23},{23,20},{2... | collective-permute-start | bytes 1769480 | tf_op jit(solution)/shard_map/ppermute | solution.py:46
  32.8 1.3 collective-permute-start.6
  34.1 1.3 collective-permute-start.7
  35.4 1.6 pad_maximum_fusion
  37.5 1.3 collective-permute-start.8
  39.5 1.3 collective-permute-start.9
  42.3 2.2 %collective-permute-start.19 = (bf16[1536,128]{0,1:T(8,128)(2,1)S(1)}, bf16[1536,128]{0,1:T(8,128)(2,1)}, u32[]{:S(2)}, u32[]{:S(2)}) collective-permute-start(bf16[1536,128]{0,1:T(8,128)(2,1)S(1)} %fusion.2), channel_id=1, source_target_pairs={{0,16},{16,0},{1,17},{17,1},{2,18},{18,2},{3,19},{19,3},{4,20},{20... | collective-permute-start | bytes 1179656 | tf_op jit(solution)/shard_map/ppermute | solution.py:147
  44.6 1.5 convolution_add_fusion.2
  46.1 1.6 convolution_add_fusion.1
  48.2 2.2 %collective-permute-start.13 = (bf16[96,896]{1,0:T(8,128)(2,1)}, bf16[96,896]{1,0:T(8,128)(2,1)}, u32[]{:S(2)}, u32[]{:S(2)}) collective-permute-start(bf16[96,896]{1,0:T(8,128)(2,1)} %concatenate.40), channel_id=1, source_target_pairs={{0,3},{1,0},{2,1},{3,2},{4,7},{5,4},{6,5},{7,6},{8,11},{9,8},{10,9... | collective-permute-start | bytes 516104 | tf_op jit(solution)/shard_map/ppermute | solution.py:126
  50.9 1.9 collective-permute-start.10
  52.8 3.1 %collective-permute-start.11 = (f32[128,128]{1,0:T(8,128)S(1)}, f32[128,128]{1,0:T(8,128)S(1)}, u32[]{:S(2)}, u32[]{:S(2)}) collective-permute-start(f32[128,128]{1,0:T(8,128)S(1)} %get-tuple-element.17), channel_id=1, source_target_pairs={{16,18},{17,19},{18,16},{19,17},{20,22},{21,23},{22,20},{23,21},{2... | collective-permute-start | bytes 196616 | tf_op jit(solution)/shard_map/ppermute | solution.py:46
  55.9 4.0 %collective-permute-start.12 = (f32[128,128]{1,0:T(8,128)S(1)}, f32[128,128]{1,0:T(8,128)S(1)}, u32[]{:S(2)}, u32[]{:S(2)}) collective-permute-start(f32[128,128]{1,0:T(8,128)S(1)} %get-tuple-element.16), channel_id=1, source_target_pairs={{16,19},{17,16},{18,17},{19,18},{20,23},{21,20},{22,21},{23,22},{2... | collective-permute-start | bytes 196616 | tf_op jit(solution)/shard_map/ppermute | solution.py:46
  60.0 0.9 bitcast_dynamic-update-slice_fusion.7
  60.9 1.8 collective-permute-start.14
  63.9 6.3 %all-to-all-start = ((bf16[32,48,128]{2,1,0:T(8,128)(2,1)}), bf16[32,48,128]{2,1,0:T(8,128)(2,1)}, u32[]{:S(2)}, u32[]{:S(2)}) async-start(bf16[32,48,128]{2,1,0:T(8,128)(2,1)} %convert_element_type.96), calls=%async_computation | async-start | bytes 786432 | tf_op jit(solution)/shard_map/all_to_all | solution.py:53
  70.2 0.9 bitcast_dynamic-update-slice_fusion.6
  71.2 0.9 bitcast_dynamic-update-slice_fusion.5
  72.2 0.9 bitcast_dynamic-update-slice_fusion.4
  73.1 2.7 %collective-permute-start.16 = (bf16[4,96,896]{2,1,0:T(8,128)(2,1)S(1)}, bf16[4,96,896]{2,1,0:T(8,128)(2,1)}, u32[]{:S(2)}, u32[]{:S(2)}) collective-permute-start(bf16[4,96,896]{2,1,0:T(8,128)(2,1)S(1)} %bitcast_dynamic-update-slice_fusion.4), channel_id=1, source_target_pairs={{0,12},{1,13},{2,14},{3,15},{4,0},{5,1},{6,2},{7,3},{8,4},{9,5},{1... | collective-permute-start | bytes 2064392 | tf_op jit(solution)/shard_map/ppermute | solution.py:126
  75.8 2.1 %pad_maximum_fusion.1 = bf16[1536,352]{0,1:T(8,128)(2,1)} fusion(bf16[1536,96]{0,1:T(8,128)(2,1)S(1)} %fusion.21, bf16[1536,128]{0,1:T(8,128)(2,1)} %collective-permute-done.19, bf16[1536,128]{0,1:T(8,128)(2,1)S(1)} %fusion.2), kind=kLoop, calls=%fused_computation.18 | loop fusion | flops 3244032 | bytes 2162688 | tf_op jit(solution)/shard_map/concatenate | solution.py:157
  79.0 1.8 broadcast_in_dim.119
  81.7 1.1 select_reduce_fusion.1
  82.8 9.9 %collective-permute-done.16 = bf16[4,96,896]{2,1,0:T(8,128)(2,1)} collective-permute-done((bf16[4,96,896]{2,1,0:T(8,128)(2,1)S(1)}, bf16[4,96,896]{2,1,0:T(8,128)(2,1)}, u32[]{:S(2)}, u32[]{:S(2)}) %collective-permute-start.16) | collective-permute-done | bytes 688160 | tf_op jit(solution)/shard_map/ppermute | solution.py:126
  92.8 2.0 %bitcast_dynamic-update-slice_fusion.2 = bf16[4,4,96,896]{3,2,1,0:T(8,128)(2,1)} fusion(bf16[4,4,96,896]{3,2,1,0:T(8,128)(2,1)} %bitcast_dynamic-update-slice_fusion.3, s32[]{:T(128)S(6)} %select_n.174, bf16[4,96,896]{2,1,0:T(8,128)(2,1)} %collective-permute-done.16), kind=kLoop, calls=%fused_computation.36 | loop fusion | bytes 1376260 | tf_op jit(solution)/shard_map/dynamic_update_slice | solution.py:127
  94.8 1.1 collective-permute-done.17
  95.9 2.0 bitcast_dynamic-update-slice_fusion.1
  97.9 13.6 %collective-permute-done.18 = bf16[4,96,896]{2,1,0:T(8,128)(2,1)S(1)} collective-permute-done((bf16[4,96,896]{2,1,0:T(8,128)(2,1)S(1)}, bf16[4,96,896]{2,1,0:T(8,128)(2,1)S(1)}, u32[]{:S(2)}, u32[]{:S(2)}) %collective-permute-start.18) | collective-permute-done | bytes 688160 | tf_op jit(solution)/shard_map/ppermute | solution.py:126
  112.4 2.7 %fusion.66 = (bf16[1536,352]{0,1:T(8,128)(2,1)S(1)}, f32[1536,352]{0,1:T(8,128)S(1)}) fusion(bf16[1536,352]{0,1:T(8,128)(2,1)S(1)} %copy-done.4, s32[]{:T(128)S(6)} %select_n.161, bf16[1536,896]{1,0:T(8,128)(2,1)} %bitcast.14), kind=kOutput, calls=%fused_computation.123 | convolution fusion | flops 831012864 | bytes 6144004 | tf_op jit(solution)/shard_map/dot_general | solution.py:19
  115.2 1.1 pad_maximum_fusion.2
  117.4 8.2 %all-to-all-start.1 = ((f32[8,48,128]{2,1,0:T(8,128)}), f32[8,48,128]{2,1,0:T(8,128)}, u32[]{:S(2)}, u32[]{:S(2)}) async-start(f32[8,48,128]{2,1,0:T(8,128)} %broadcast_in_dim.134), calls=%async_computation.1 | async-start | bytes 393216 | tf_op jit(solution)/shard_map/all_to_all | solution.py:60
  126.3 3.3 %collective-permute-start.21 = (f32[48,128]{1,0:T(8,128)S(1)}, f32[48,128]{1,0:T(8,128)}, u32[]{:S(2)}, u32[]{:S(2)}) collective-permute-start(f32[48,128]{1,0:T(8,128)S(1)} %constant_dynamic-slice_fusion.1), channel_id=1, source_target_pairs={{0,0},{1,2},{2,4},{3,6},{4,8},{5,10},{6,12},{7,14},{8,16},{9,18},{... | collective-permute-start | bytes 73736 | tf_op jit(solution)/shard_map/ppermute | solution.py:142
  129.6 6.9 %all-to-all-done.1 = f32[8,48,128]{2,1,0:T(8,128)} async-done(((f32[8,48,128]{2,1,0:T(8,128)}), f32[8,48,128]{2,1,0:T(8,128)}, u32[]{:S(2)}, u32[]{:S(2)}) %all-to-all-start.1) | async-done | bytes 196640 | tf_op jit(solution)/shard_map/all_to_all | solution.py:60
  139.0 5.6 %all-to-all-start.2 = ((f32[16,48,128]{2,1,0:T(8,128)}), f32[16,48,128]{2,1,0:T(8,128)}, u32[]{:S(2)}, u32[]{:S(2)}) async-start(f32[16,48,128]{2,1,0:T(8,128)} %broadcast_in_dim.135), calls=%async_computation.2 | async-start | bytes 786432 | tf_op jit(solution)/shard_map/all_to_all | solution.py:60
  144.6 1.2 convert_reduce_fusion
  145.9 1.9 convert_add_fusion
  147.8 2.8 %fusion.7 = f32[768,352]{0,1:T(8,128)S(1)} fusion(bf16[1536,896]{1,0:T(8,128)(2,1)} %bitcast.14, f32[1536,352]{0,1:T(8,128)S(1)} %convert_add_fusion, s32[]{:T(128)S(6)} %select_n.161, f32[768]{0:T(1024)S(1)} %dynamic-slice.2), kind=kOutput, calls=%fused_computation.10 | convolution fusion | flops 831553536 | bytes 6688772 | tf_op jit(solution)/shard_map/dot_general | solution.py:23
  150.6 3.4 %all-to-all-done.2 = f32[16,48,128]{2,1,0:T(8,128)} async-done(((f32[16,48,128]{2,1,0:T(8,128)}), f32[16,48,128]{2,1,0:T(8,128)}, u32[]{:S(2)}, u32[]{:S(2)}) %all-to-all-start.2) | async-done | bytes 393248 | tf_op jit(solution)/shard_map/all_to_all | solution.py:60
  153.9 1.6 fusion.67
  155.5 1.9 collective-permute-start.22
  157.4 1.0 collective-permute-done.22
  158.4 2.2 %collective-permute-start.23 = (f32[128,128]{1,0:T(8,128)S(1)}, f32[128,128]{1,0:T(8,128)S(1)}, u32[]{:S(2)}, u32[]{:S(2)}) collective-permute-start(f32[128,128]{1,0:T(8,128)S(1)} %fusion.44), channel_id=1, source_target_pairs={{16,19},{17,16},{18,17},{19,18},{20,23},{21,20},{22,21},{23,22},{2... | collective-permute-start | bytes 196616 | tf_op jit(solution)/shard_map/ppermute | solution.py:46
  160.6 3.7 %collective-permute-start.24 = (f32[128,128]{1,0:T(8,128)S(1)}, f32[128,128]{1,0:T(8,128)S(1)}, u32[]{:S(2)}, u32[]{:S(2)}) collective-permute-start(f32[128,128]{1,0:T(8,128)S(1)} %fusion.44), channel_id=1, source_target_pairs={{16,18},{17,19},{18,16},{19,17},{20,22},{21,23},{22,20},{23,21},{2... | collective-permute-start | bytes 196616 | tf_op jit(solution)/shard_map/ppermute | solution.py:46
  164.3 1.9 collective-permute-start.25
  167.1 3.4 %collective-permute-done.25 = f32[128,128]{1,0:T(8,128)S(1)} collective-permute-done((f32[128,128]{1,0:T(8,128)S(1)}, f32[128,128]{1,0:T(8,128)S(1)}, u32[]{:S(2)}, u32[]{:S(2)}) %collective-permute-start.25) | collective-permute-done | bytes 65568 | tf_op jit(solution)/shard_map/ppermute | solution.py:46
  170.6 1.9 fusion.18
  172.5 1.9 collective-permute-start.26
  174.5 3.7 %collective-permute-start.27 = (f32[128,128]{1,0:T(8,128)S(1)}, f32[128,128]{1,0:T(8,128)S(1)}, u32[]{:S(2)}, u32[]{:S(2)}) collective-permute-start(f32[128,128]{1,0:T(8,128)S(1)} %get-tuple-element.14), channel_id=1, source_target_pairs={{16,24},{17,25},{18,26},{19,27},{20,28},{21,29},{22,30},{23,31},{2... | collective-permute-start | bytes 196616 | tf_op jit(solution)/shard_map/ppermute | solution.py:46
  178.1 2.8 %collective-permute-start.28 = (f32[128,128]{1,0:T(8,128)S(1)}, f32[128,128]{1,0:T(8,128)S(1)}, u32[]{:S(2)}, u32[]{:S(2)}) collective-permute-start(f32[128,128]{1,0:T(8,128)S(1)} %get-tuple-element.13), channel_id=1, source_target_pairs={{16,28},{17,29},{18,30},{19,31},{20,16},{21,17},{22,18},{23,19},{2... | collective-permute-start | bytes 196616 | tf_op jit(solution)/shard_map/ppermute | solution.py:46
  181.0 2.2 %collective-permute-done.28 = f32[128,128]{1,0:T(8,128)S(1)} collective-permute-done((f32[128,128]{1,0:T(8,128)S(1)}, f32[128,128]{1,0:T(8,128)S(1)}, u32[]{:S(2)}, u32[]{:S(2)}) %collective-permute-start.28) | collective-permute-done | bytes 65568 | tf_op jit(solution)/shard_map/ppermute | solution.py:46
  183.2 1.3 collective-permute-start.29
  186.9 3.8 %all-to-all-start.3 = ((bf16[16,128,128]{1,2,0:T(8,128)(2,1)}), bf16[16,128,128]{1,2,0:T(8,128)(2,1)S(1)}, u32[]{:S(2)}, u32[]{:S(2)}) async-start(bf16[16,128,128]{1,2,0:T(8,128)(2,1)} %bitcast_convert_fusion), calls=%async_computation.3 | async-start | bytes 1048576 | tf_op jit(solution)/shard_map/all_to_all | solution.py:53
  191.6 9.8 %all-to-all-done.3 = bf16[16,128,128]{1,2,0:T(8,128)(2,1)S(1)} async-done(((bf16[16,128,128]{1,2,0:T(8,128)(2,1)}), bf16[16,128,128]{1,2,0:T(8,128)(2,1)S(1)}, u32[]{:S(2)}, u32[]{:S(2)}) %all-to-all-start.3) | async-done | bytes 524320 | tf_op jit(solution)/shard_map/all_to_all | solution.py:53
  (124 shorter events, 21.5 us)
Async XLA Ops:
  0.6 23.3 %copy-start = (f32[1,2048,128]{2,1,0:T(8,128)S(1)}, f32[1,2048,128]{2,1,0:T(8,128)}, u32[]{:S(2)}) copy-start(f32[1,2048,128]{2,1,0:T(8,128)} %param.14) | copy-start | bytes 3145732
  0.6 13.2 %copy-start.1 = (f32[1,128,2048]{2,1,0:T(8,128)S(1)}, f32[1,128,2048]{2,1,0:T(8,128)}, u32[]{:S(2)}) copy-start(f32[1,128,2048]{2,1,0:T(8,128)} %param.10) | copy-start | bytes 3145732
  3.5 26.8 %collective-permute-start = (bf16[128,2048]{0,1:T(8,128)(2,1)S(1)}, bf16[128,2048]{0,1:T(8,128)(2,1)}, u32[]{:S(2)}, u32[]{:S(2)}) collective-permute-start(bf16[128,2048]{0,1:T(8,128)(2,1)S(1)} %bitcast_multiply_fusion), channel_id=1, source_target_pairs={{16,28},{17,29},{18,30},{19,31},{20,16},{21,17},{22,18},{23,19},{2... | collective-permute-start | bytes 1572872 | tf_op jit(solution)/shard_map/ppermute | solution.py:46
  9.0 23.9 %collective-permute-start.1 = (bf16[128,2048]{0,1:T(8,128)(2,1)S(1)}, bf16[128,2048]{0,1:T(8,128)(2,1)}, u32[]{:S(2)}, u32[]{:S(2)}) collective-permute-start(bf16[128,2048]{0,1:T(8,128)(2,1)S(1)} %bitcast_multiply_fusion), channel_id=1, source_target_pairs={{16,24},{17,25},{18,26},{19,27},{20,28},{21,29},{22,30},{23,31},{2... | collective-permute-start | bytes 1572872 | tf_op jit(solution)/shard_map/ppermute | solution.py:46
  11.2 22.9 %collective-permute-start.2 = (bf16[128,2048]{0,1:T(8,128)(2,1)S(1)}, bf16[128,2048]{0,1:T(8,128)(2,1)}, u32[]{:S(2)}, u32[]{:S(2)}) collective-permute-start(bf16[128,2048]{0,1:T(8,128)(2,1)S(1)} %bitcast_multiply_fusion), channel_id=1, source_target_pairs={{16,20},{17,21},{18,22},{19,23},{20,24},{21,25},{22,26},{23,27},{2... | collective-permute-start | bytes 1572872 | tf_op jit(solution)/shard_map/ppermute | solution.py:46
  14.2 12.0 %copy-start.18 = (s32[1,1024]{1,0:T(1,128)S(1)}, s32[1,1024]{1,0:T(1,128)}, u32[]{:S(2)}) copy-start(s32[1,1024]{1,0:T(1,128)} %param.12) | copy-start | bytes 12292
  15.1 22.4 %collective-permute-start.3 = (bf16[144,2048]{1,0:T(8,128)(2,1)}, bf16[144,2048]{1,0:T(8,128)(2,1)}, u32[]{:S(2)}, u32[]{:S(2)}) collective-permute-start(bf16[144,2048]{1,0:T(8,128)(2,1)} %fusion.20), channel_id=1, source_target_pairs={{16,19},{17,16},{18,17},{19,18},{20,23},{21,20},{22,21},{23,22},{2... | collective-permute-start | bytes 1769480 | tf_op jit(solution)/shard_map/ppermute | solution.py:46
  19.5 20.0 %collective-permute-start.4 = (bf16[144,2048]{1,0:T(8,128)(2,1)}, bf16[144,2048]{1,0:T(8,128)(2,1)}, u32[]{:S(2)}, u32[]{:S(2)}) collective-permute-start(bf16[144,2048]{1,0:T(8,128)(2,1)} %fusion.20), channel_id=1, source_target_pairs={{16,18},{17,19},{18,16},{19,17},{20,22},{21,23},{22,20},{23,21},{2... | collective-permute-start | bytes 1769480 | tf_op jit(solution)/shard_map/ppermute | solution.py:46
  26.2 2.8 %copy-start.17 = (bf16[96,1]{0,1:T(2,128)(2,1)S(1)}, bf16[96,1]{0,1:T(2,128)(2,1)}, u32[]{:S(2)}) copy-start(bf16[96,1]{0,1:T(2,128)(2,1)} %get-tuple-element.20) | copy-start | bytes 580
  26.3 2.9 %copy-start.16 = (bf16[96,1]{0,1:T(2,128)(2,1)S(1)}, bf16[96,1]{0,1:T(2,128)(2,1)}, u32[]{:S(2)}) copy-start(bf16[96,1]{0,1:T(2,128)(2,1)} %get-tuple-element.19) | copy-start | bytes 580
  26.3 3.0 %copy-start.15 = (bf16[96,1]{0,1:T(2,128)(2,1)S(1)}, bf16[96,1]{0,1:T(2,128)(2,1)}, u32[]{:S(2)}) copy-start(bf16[96,1]{0,1:T(2,128)(2,1)} %get-tuple-element.18) | copy-start | bytes 580
  28.7 47.1 %copy-start.3 = (bf16[1536,128]{0,1:T(8,128)(2,1)}, bf16[1536,128]{0,1:T(8,128)(2,1)S(1)}, u32[]{:S(2)}) copy-start(bf16[1536,128]{0,1:T(8,128)(2,1)S(1)} %fusion.2) | copy-start | bytes 1179652
  30.3 12.0 %collective-permute-start.5 = (bf16[144,2048]{1,0:T(8,128)(2,1)}, bf16[144,2048]{1,0:T(8,128)(2,1)S(1)}, u32[]{:S(2)}, u32[]{:S(2)}) collective-permute-start(bf16[144,2048]{1,0:T(8,128)(2,1)} %fusion.20), channel_id=1, source_target_pairs={{16,17},{17,18},{18,19},{19,16},{20,21},{21,22},{22,23},{23,20},{2... | collective-permute-start | bytes 1769480 | tf_op jit(solution)/shard_map/ppermute | solution.py:46
  32.8 15.4 %collective-permute-start.6 = (bf16[128,128]{1,0:T(8,128)(2,1)S(1)}, bf16[128,128]{1,0:T(8,128)(2,1)S(1)}, u32[]{:S(2)}, u32[]{:S(2)}) collective-permute-start(bf16[128,128]{1,0:T(8,128)(2,1)S(1)} %get-tuple-element.24), channel_id=1, source_target_pairs={{0,16},{1,17},{2,18},{3,19},{4,20},{5,21},{6,22},{7,23},{8,24},{9,... | collective-permute-start | bytes 98312 | tf_op jit(solution)/shard_map/ppermute | solution.py:46
  34.1 16.2 %collective-permute-start.7 = (bf16[128,128]{1,0:T(8,128)(2,1)S(1)}, bf16[128,128]{1,0:T(8,128)(2,1)S(1)}, u32[]{:S(2)}, u32[]{:S(2)}) collective-permute-start(bf16[128,128]{1,0:T(8,128)(2,1)S(1)} %get-tuple-element.24), channel_id=1, source_target_pairs={{0,28},{1,29},{2,30},{3,31},{4,16},{5,17},{6,18},{7,19},{8,20},{9,... | collective-permute-start | bytes 98312 | tf_op jit(solution)/shard_map/ppermute | solution.py:46
  37.5 12.9 %copy-start.8 = (f32[512,128]{0,1:T(8,128)}, f32[512,128]{0,1:T(8,128)S(1)}, u32[]{:S(2)}) copy-start(f32[512,128]{0,1:T(8,128)S(1)} %convolution_add_fusion.3) | copy-start | bytes 786436
  37.5 12.9 %collective-permute-start.8 = (bf16[128,128]{1,0:T(8,128)(2,1)S(1)}, bf16[128,128]{1,0:T(8,128)(2,1)S(1)}, u32[]{:S(2)}, u32[]{:S(2)}) collective-permute-start(bf16[128,128]{1,0:T(8,128)(2,1)S(1)} %get-tuple-element.24), channel_id=1, source_target_pairs={{0,24},{1,25},{2,26},{3,27},{4,28},{5,29},{6,30},{7,31},{8,16},{9,... | collective-permute-start | bytes 98312 | tf_op jit(solution)/shard_map/ppermute | solution.py:46
  39.5 10.9 %collective-permute-start.9 = (bf16[128,128]{1,0:T(8,128)(2,1)S(1)}, bf16[128,128]{1,0:T(8,128)(2,1)S(1)}, u32[]{:S(2)}, u32[]{:S(2)}) collective-permute-start(bf16[128,128]{1,0:T(8,128)(2,1)S(1)} %get-tuple-element.24), channel_id=1, source_target_pairs={{0,20},{1,21},{2,22},{3,23},{4,24},{5,25},{6,26},{7,27},{8,28},{9,... | collective-permute-start | bytes 98312 | tf_op jit(solution)/shard_map/ppermute | solution.py:46
  42.3 33.5 %collective-permute-start.19 = (bf16[1536,128]{0,1:T(8,128)(2,1)S(1)}, bf16[1536,128]{0,1:T(8,128)(2,1)}, u32[]{:S(2)}, u32[]{:S(2)}) collective-permute-start(bf16[1536,128]{0,1:T(8,128)(2,1)S(1)} %fusion.2), channel_id=1, source_target_pairs={{0,16},{16,0},{1,17},{17,1},{2,18},{18,2},{3,19},{19,3},{4,20},{20... | collective-permute-start | bytes 1179656 | tf_op jit(solution)/shard_map/ppermute | solution.py:147
  46.1 4.3 %copy-start.10 = (f32[512,128]{0,1:T(8,128)}, f32[512,128]{0,1:T(8,128)S(1)}, u32[]{:S(2)}) copy-start(f32[512,128]{0,1:T(8,128)S(1)} %convolution_add_fusion.2) | copy-start | bytes 786436
  47.7 3.2 %copy-start.12 = (f32[512,128]{0,1:T(8,128)}, f32[512,128]{0,1:T(8,128)S(1)}, u32[]{:S(2)}) copy-start(f32[512,128]{0,1:T(8,128)S(1)} %convolution_add_fusion.1) | copy-start | bytes 786436
  48.2 15.0 %copy-start.14 = (f32[512,128]{0,1:T(8,128)}, f32[512,128]{0,1:T(8,128)S(1)}, u32[]{:S(2)}) copy-start(f32[512,128]{0,1:T(8,128)S(1)} %convolution_add_fusion) | copy-start | bytes 786436
  48.2 14.6 %copy-start.7 = (f32[128,128]{1,0:T(8,128)S(1)}, f32[128,128]{1,0:T(8,128)}, u32[]{:S(2)}) copy-start(f32[128,128]{1,0:T(8,128)} %get-tuple-element.25) | copy-start | bytes 196612
  48.2 22.0 %collective-permute-start.13 = (bf16[96,896]{1,0:T(8,128)(2,1)}, bf16[96,896]{1,0:T(8,128)(2,1)}, u32[]{:S(2)}, u32[]{:S(2)}) collective-permute-start(bf16[96,896]{1,0:T(8,128)(2,1)} %concatenate.40), channel_id=1, source_target_pairs={{0,3},{1,0},{2,1},{3,2},{4,7},{5,4},{6,5},{7,6},{8,11},{9,8},{10,9... | collective-permute-start | bytes 516104 | tf_op jit(solution)/shard_map/ppermute | solution.py:126
  50.9 10.1 %collective-permute-start.10 = (f32[128,128]{1,0:T(8,128)S(1)}, f32[128,128]{1,0:T(8,128)S(1)}, u32[]{:S(2)}, u32[]{:S(2)}) collective-permute-start(f32[128,128]{1,0:T(8,128)S(1)} %get-tuple-element.15), channel_id=1, source_target_pairs={{16,17},{17,18},{18,19},{19,16},{20,21},{21,22},{22,23},{23,20},{2... | collective-permute-start | bytes 196616 | tf_op jit(solution)/shard_map/ppermute | solution.py:46
  52.8 10.0 %collective-permute-start.11 = (f32[128,128]{1,0:T(8,128)S(1)}, f32[128,128]{1,0:T(8,128)S(1)}, u32[]{:S(2)}, u32[]{:S(2)}) collective-permute-start(f32[128,128]{1,0:T(8,128)S(1)} %get-tuple-element.17), channel_id=1, source_target_pairs={{16,18},{17,19},{18,16},{19,17},{20,22},{21,23},{22,20},{23,21},{2... | collective-permute-start | bytes 196616 | tf_op jit(solution)/shard_map/ppermute | solution.py:46
  55.9 6.8 %collective-permute-start.12 = (f32[128,128]{1,0:T(8,128)S(1)}, f32[128,128]{1,0:T(8,128)S(1)}, u32[]{:S(2)}, u32[]{:S(2)}) collective-permute-start(f32[128,128]{1,0:T(8,128)S(1)} %get-tuple-element.16), channel_id=1, source_target_pairs={{16,19},{17,16},{18,17},{19,18},{20,23},{21,20},{22,21},{23,22},{2... | collective-permute-start | bytes 196616 | tf_op jit(solution)/shard_map/ppermute | solution.py:46
  60.9 10.2 %collective-permute-start.14 = (bf16[96,896]{1,0:T(8,128)(2,1)}, bf16[96,896]{1,0:T(8,128)(2,1)}, u32[]{:S(2)}, u32[]{:S(2)}) collective-permute-start(bf16[96,896]{1,0:T(8,128)(2,1)} %concatenate.40), channel_id=1, source_target_pairs={{0,2},{1,3},{2,0},{3,1},{4,6},{5,7},{6,4},{7,5},{8,10},{9,11},{10,... | collective-permute-start | bytes 516104 | tf_op jit(solution)/shard_map/ppermute | solution.py:126
  62.8 9.4 %collective-permute-start.15 = (bf16[96,896]{1,0:T(8,128)(2,1)}, bf16[96,896]{1,0:T(8,128)(2,1)}, u32[]{:S(2)}, u32[]{:S(2)}) collective-permute-start(bf16[96,896]{1,0:T(8,128)(2,1)} %concatenate.40), channel_id=1, source_target_pairs={{0,1},{1,2},{2,3},{3,0},{4,5},{5,6},{6,7},{7,4},{8,9},{9,10},{10,1... | collective-permute-start | bytes 516104 | tf_op jit(solution)/shard_map/ppermute | solution.py:126
  62.8 15.1 %copy-start.5 = (f32[128,128]{1,0:T(8,128)}, f32[128,128]{1,0:T(8,128)S(1)}, u32[]{:S(2)}) copy-start(f32[128,128]{1,0:T(8,128)S(1)} %fusion.47) | copy-start | bytes 196612
  63.9 17.7 %all-to-all-start = ((bf16[32,48,128]{2,1,0:T(8,128)(2,1)}), bf16[32,48,128]{2,1,0:T(8,128)(2,1)}, u32[]{:S(2)}, u32[]{:S(2)}) async-start(bf16[32,48,128]{2,1,0:T(8,128)(2,1)} %convert_element_type.96), calls=%async_computation | async-start | bytes 786432 | tf_op jit(solution)/shard_map/all_to_all | solution.py:53
  73.1 19.7 %collective-permute-start.16 = (bf16[4,96,896]{2,1,0:T(8,128)(2,1)S(1)}, bf16[4,96,896]{2,1,0:T(8,128)(2,1)}, u32[]{:S(2)}, u32[]{:S(2)}) collective-permute-start(bf16[4,96,896]{2,1,0:T(8,128)(2,1)S(1)} %bitcast_dynamic-update-slice_fusion.4), channel_id=1, source_target_pairs={{0,12},{1,13},{2,14},{3,15},{4,0},{5,1},{6,2},{7,3},{8,4},{9,5},{1... | collective-permute-start | bytes 2064392 | tf_op jit(solution)/shard_map/ppermute | solution.py:126
  77.9 18.0 %collective-permute-start.17 = (bf16[4,96,896]{2,1,0:T(8,128)(2,1)S(1)}, bf16[4,96,896]{2,1,0:T(8,128)(2,1)}, u32[]{:S(2)}, u32[]{:S(2)}) collective-permute-start(bf16[4,96,896]{2,1,0:T(8,128)(2,1)S(1)} %bitcast_dynamic-update-slice_fusion.4), channel_id=1, source_target_pairs={{0,8},{1,9},{2,10},{3,11},{4,12},{5,13},{6,14},{7,15},{8,0},{9,1},... | collective-permute-start | bytes 2064392 | tf_op jit(solution)/shard_map/ppermute | solution.py:126
  78.4 33.1 %collective-permute-start.18 = (bf16[4,96,896]{2,1,0:T(8,128)(2,1)S(1)}, bf16[4,96,896]{2,1,0:T(8,128)(2,1)S(1)}, u32[]{:S(2)}, u32[]{:S(2)}) collective-permute-start(bf16[4,96,896]{2,1,0:T(8,128)(2,1)S(1)} %bitcast_dynamic-update-slice_fusion.4), channel_id=1, source_target_pairs={{0,4},{1,5},{2,6},{3,7},{4,8},{5,9},{6,10},{7,11},{8,12},{9,13},{1... | collective-permute-start | bytes 2064392 | tf_op jit(solution)/shard_map/ppermute | solution.py:126
  82.8 29.6 %copy-start.4 = (bf16[1536,352]{0,1:T(8,128)(2,1)S(1)}, bf16[1536,352]{0,1:T(8,128)(2,1)}, u32[]{:S(2)}) copy-start(bf16[1536,352]{0,1:T(8,128)(2,1)} %pad_maximum_fusion.1) | copy-start | bytes 3244036
  116.2 29.6 %collective-permute-start.20 = (bf16[1536,352]{0,1:T(8,128)(2,1)}, bf16[1536,352]{0,1:T(8,128)(2,1)}, u32[]{:S(2)}, u32[]{:S(2)}) collective-permute-start(bf16[1536,352]{0,1:T(8,128)(2,1)} %pad_maximum_fusion.2), channel_id=1, source_target_pairs={{0,16},{16,0},{1,17},{17,1},{2,18},{18,2},{3,19},{19,3},{4,20},{20... | collective-permute-start | bytes 3244040 | tf_op jit(solution)/shard_map/ppermute | solution.py:161
  117.4 19.1 %all-to-all-start.1 = ((f32[8,48,128]{2,1,0:T(8,128)}), f32[8,48,128]{2,1,0:T(8,128)}, u32[]{:S(2)}, u32[]{:S(2)}) async-start(f32[8,48,128]{2,1,0:T(8,128)} %broadcast_in_dim.134), calls=%async_computation.1 | async-start | bytes 393216 | tf_op jit(solution)/shard_map/all_to_all | solution.py:60
  126.3 11.1 %collective-permute-start.21 = (f32[48,128]{1,0:T(8,128)S(1)}, f32[48,128]{1,0:T(8,128)}, u32[]{:S(2)}, u32[]{:S(2)}) collective-permute-start(f32[48,128]{1,0:T(8,128)S(1)} %constant_dynamic-slice_fusion.1), channel_id=1, source_target_pairs={{0,0},{1,2},{2,4},{3,6},{4,8},{5,10},{6,12},{7,14},{8,16},{9,18},{... | collective-permute-start | bytes 73736 | tf_op jit(solution)/shard_map/ppermute | solution.py:142
  139.0 14.9 %all-to-all-start.2 = ((f32[16,48,128]{2,1,0:T(8,128)}), f32[16,48,128]{2,1,0:T(8,128)}, u32[]{:S(2)}, u32[]{:S(2)}) async-start(f32[16,48,128]{2,1,0:T(8,128)} %broadcast_in_dim.135), calls=%async_computation.2 | async-start | bytes 786432 | tf_op jit(solution)/shard_map/all_to_all | solution.py:60
  147.8 10.6 %copy-start.6 = (f32[128,128]{1,0:T(8,128)S(1)}, f32[128,128]{1,0:T(8,128)}, u32[]{:S(2)}) copy-start(f32[128,128]{1,0:T(8,128)} %copy-done.5) | copy-start | bytes 196612
  147.8 22.8 %copy-start.9 = (f32[512,128]{0,1:T(8,128)S(1)}, f32[512,128]{0,1:T(8,128)}, u32[]{:S(2)}) copy-start(f32[512,128]{0,1:T(8,128)} %copy-done.8) | copy-start | bytes 786436
  147.8 22.8 %copy-start.11 = (f32[512,128]{0,1:T(8,128)S(1)}, f32[512,128]{0,1:T(8,128)}, u32[]{:S(2)}) copy-start(f32[512,128]{0,1:T(8,128)} %copy-done.10) | copy-start | bytes 786436
  147.8 22.8 %copy-start.13 = (f32[512,128]{0,1:T(8,128)S(1)}, f32[512,128]{0,1:T(8,128)}, u32[]{:S(2)}) copy-start(f32[512,128]{0,1:T(8,128)} %copy-done.12) | copy-start | bytes 786436
  155.5 29.9 %copy-start.2 = (f32[1,128,2048]{2,1,0:T(8,128)S(1)}, f32[1,128,2048]{2,1,0:T(8,128)}, u32[]{:S(2)}) copy-start(f32[1,128,2048]{2,1,0:T(8,128)} %param.10) | copy-start | bytes 3145732
  155.5 2.9 %collective-permute-start.22 = (f32[224,128]{1,0:T(8,128)S(1)}, f32[224,128]{1,0:T(8,128)S(1)}, u32[]{:S(2)}, u32[]{:S(2)}) collective-permute-start(f32[224,128]{1,0:T(8,128)S(1)} %slice.125), channel_id=1, source_target_pairs={{0,16},{16,0},{1,17},{17,1},{2,18},{18,2},{3,19},{19,3},{4,20},{20... | collective-permute-start | bytes 344072 | tf_op jit(solution)/shard_map/ppermute | solution.py:169
  158.4 7.8 %collective-permute-start.23 = (f32[128,128]{1,0:T(8,128)S(1)}, f32[128,128]{1,0:T(8,128)S(1)}, u32[]{:S(2)}, u32[]{:S(2)}) collective-permute-start(f32[128,128]{1,0:T(8,128)S(1)} %fusion.44), channel_id=1, source_target_pairs={{16,19},{17,16},{18,17},{19,18},{20,23},{21,20},{22,21},{23,22},{2... | collective-permute-start | bytes 196616 | tf_op jit(solution)/shard_map/ppermute | solution.py:46
  160.6 6.5 %collective-permute-start.24 = (f32[128,128]{1,0:T(8,128)S(1)}, f32[128,128]{1,0:T(8,128)S(1)}, u32[]{:S(2)}, u32[]{:S(2)}) collective-permute-start(f32[128,128]{1,0:T(8,128)S(1)} %fusion.44), channel_id=1, source_target_pairs={{16,18},{17,19},{18,16},{19,17},{20,22},{21,23},{22,20},{23,21},{2... | collective-permute-start | bytes 196616 | tf_op jit(solution)/shard_map/ppermute | solution.py:46
  164.3 6.2 %collective-permute-start.25 = (f32[128,128]{1,0:T(8,128)S(1)}, f32[128,128]{1,0:T(8,128)S(1)}, u32[]{:S(2)}, u32[]{:S(2)}) collective-permute-start(f32[128,128]{1,0:T(8,128)S(1)} %fusion.44), channel_id=1, source_target_pairs={{16,17},{17,18},{18,19},{19,16},{20,21},{21,22},{22,23},{23,20},{2... | collective-permute-start | bytes 196616 | tf_op jit(solution)/shard_map/ppermute | solution.py:46
  172.5 8.4 %collective-permute-start.26 = (f32[128,128]{1,0:T(8,128)S(1)}, f32[128,128]{1,0:T(8,128)S(1)}, u32[]{:S(2)}, u32[]{:S(2)}) collective-permute-start(f32[128,128]{1,0:T(8,128)S(1)} %get-tuple-element.12), channel_id=1, source_target_pairs={{16,20},{17,21},{18,22},{19,23},{20,24},{21,25},{22,26},{23,27},{2... | collective-permute-start | bytes 196616 | tf_op jit(solution)/shard_map/ppermute | solution.py:46
  174.5 6.5 %collective-permute-start.27 = (f32[128,128]{1,0:T(8,128)S(1)}, f32[128,128]{1,0:T(8,128)S(1)}, u32[]{:S(2)}, u32[]{:S(2)}) collective-permute-start(f32[128,128]{1,0:T(8,128)S(1)} %get-tuple-element.14), channel_id=1, source_target_pairs={{16,24},{17,25},{18,26},{19,27},{20,28},{21,29},{22,30},{23,31},{2... | collective-permute-start | bytes 196616 | tf_op jit(solution)/shard_map/ppermute | solution.py:46
  178.1 5.1 %collective-permute-start.28 = (f32[128,128]{1,0:T(8,128)S(1)}, f32[128,128]{1,0:T(8,128)S(1)}, u32[]{:S(2)}, u32[]{:S(2)}) collective-permute-start(f32[128,128]{1,0:T(8,128)S(1)} %get-tuple-element.13), channel_id=1, source_target_pairs={{16,28},{17,29},{18,30},{19,31},{20,16},{21,17},{22,18},{23,19},{2... | collective-permute-start | bytes 196616 | tf_op jit(solution)/shard_map/ppermute | solution.py:46
  183.2 2.2 %collective-permute-start.29 = (f32[128,128]{1,0:T(8,128)S(1)}, f32[128,128]{1,0:T(8,128)S(1)}, u32[]{:S(2)}, u32[]{:S(2)}) collective-permute-start(f32[128,128]{1,0:T(8,128)S(1)} %fusion.43), channel_id=1, source_target_pairs={{16,0},{17,1},{18,2},{19,3},{20,4},{21,5},{22,6},{23,7},{24,8},{25... | collective-permute-start | bytes 196616 | tf_op jit(solution)/shard_map/ppermute | solution.py:178
  186.9 14.5 %all-to-all-start.3 = ((bf16[16,128,128]{1,2,0:T(8,128)(2,1)}), bf16[16,128,128]{1,2,0:T(8,128)(2,1)S(1)}, u32[]{:S(2)}, u32[]{:S(2)}) async-start(bf16[16,128,128]{1,2,0:T(8,128)(2,1)} %bitcast_convert_fusion), calls=%async_computation.3 | async-start | bytes 1048576 | tf_op jit(solution)/shard_map/all_to_all | solution.py:53

commit v4 on v2

--- a/solution.py
+++ b/solution.py
@@ -21,6 +21,24 @@
 
 def mul_t(left, right, **kw):
     return lax.dot_general(left, right, first_axes, preferred_element_type=f32, **kw)
+
+
+def split3(value):
+    pieces = []
+    for _ in range(3):
+        pieces.append(lax.reduce_precision(value, 8, 7))
+        value = value - pieces[-1]
+    return pieces
+
+
+def after(value, other):
+    return lax.optimization_barrier((value, other))[0]
+
+
+def plane(step_y, step_x):
+    return [
+        (4 * y + x, 4 * ((y + step_y) % 4) + (x + step_x) % 4) for y in range(4) for x in range(4)
+    ]
 
 
 def sum_scatter(partial, axes, count):
@@ -54,30 +72,42 @@
     row_id = lax.axis_index("row")
     col_id = lax.axis_index("col")
     sources = right_side.shape[-1]
+    col_y, col_x = col_id // 4, col_id % 4
 
     blocks = lax.dynamic_slice(table, (PANEL // BLOCK, col_id // 2), (PANEL // BLOCK, 1))
     lower = factor_cols[0, 0] * jnp.repeat(blocks[:, 0], BLOCK)[None, :].astype(bf16)
+    width = lower.shape[0]
+
+    own = mul(inverse, right_side[0], precision=fine)
+    first_low = lax.ppermute(own.astype(bf16), "row", [(0, 1)])
+    partial = mul_t(lower, first_low).astype(bf16)
+    total = lax.all_to_all(partial.reshape(COLS, width, sources), "col", 0, 0)
+    total = total.astype(f32).sum(0).astype(bf16)
+    solved = own - mul(inverse, gather(total, "col", COLS).reshape(PANEL, sources).astype(f32), precision=fine)
 
     share = root_inverse.shape[0]
     half = SEPARATOR // 2
+    root_inverse = after(root_inverse, partial)
     lane = lax.broadcasted_iota(jnp.int32, root_inverse.shape, 1)
     line = lax.broadcasted_iota(jnp.int32, root_inverse.shape, 0) + col_id * share
     on_diag = lane == line
     diag = jnp.where(on_diag, root_inverse, 0.0).sum(1, keepdims=True)
-    pieces = []
-    rest = diag
-    for _ in range(3):
-        pieces.append(lax.reduce_precision(rest, 8, 7))
-        rest = rest - pieces[-1]
+    pieces = split3(diag)
     off = lax.dynamic_slice_in_dim(jnp.where(on_diag, 0.0, root_inverse), row_id * half, half, 1)
     packed = jnp.concatenate([off] + pieces + [jnp.zeros((share, 125), f32)], 1).astype(bf16)
-    packed = lax.all_gather(packed, "col", axis=0, tiled=True)
+    for step_y, step_x, place, dep in ((0, 1, col_x, partial), (1, 0, col_y, total)):
+        packed = after(packed, dep)
+        whole = jnp.zeros((4,) + packed.shape, bf16)
+        for k in range(4):
+            piece = lax.ppermute(packed, "col", plane(-k * step_y, -k * step_x)) if k else packed
+            whole = lax.dynamic_update_slice_in_dim(whole, piece[None], (place + k) % 4, 0)
+        packed = whole
+    packed = packed.reshape(SEPARATOR, half + 128)
 
     onehot = (jnp.arange(SEPARATOR)[:, None] == rows_sep[None, :]).astype(bf16)
     couple_sep = lax.dot_general(
         onehot, couple, (((1,), (1,)), ((), ())), preferred_element_type=f32
     ).astype(bf16)
-    width = couple.shape[0]
 
     piece = share // 2
     pairs = [
@@ -92,14 +122,12 @@
     swap = [(0, 1), (1, 0)]
     other_sep = lax.ppermute(couple_sep, "row", swap)
 
-    own = mul(inverse, right_side[0], precision=fine)
-    first_low = lax.ppermute(own.astype(bf16), "row", [(0, 1)])
-    total = sum_scatter(mul_t(lower, first_low).astype(bf16), "col", COLS)
-    total = gather(total.astype(bf16), "col", COLS).reshape(PANEL, sources)
-    solved = own - mul(inverse, total.astype(f32), precision=fine)
+    updates = mul(couple_sep, solved.astype(bf16)).astype(bf16).reshape(COLS * 2, -1, sources)
+    updates = lax.all_to_all(updates, ("row", "col"), 0, 0).astype(f32).sum(0)
+    updates = gather(updates, "sub", SUBS).sum(0)
+    rhs = gather(root_rows - updates, "col", COLS).reshape(half, sources)
 
-    updates = sum_scatter(mul(couple_sep, solved.astype(bf16)), ("row", "col"), COLS * 2)
-    packed, _ = lax.optimization_barrier((packed, updates))
+    packed = after(packed, updates)
     off_half = packed[:, :half]
     diag_all = packed[:, half : half + 3].astype(f32).sum(1, keepdims=True)
 
@@ -115,8 +143,6 @@
         diag_all * inner, row_id * half, half, 0
     )
 
-    updates = gather(updates, "sub", SUBS).sum(0)
-    rhs = gather(root_rows - updates, "col", COLS).reshape(half, sources)
     applied = mul_t(outer, rhs, precision=fine)
     theirs = lax.ppermute(applied[width:], "row", swap)
     value = solved - (applied[:width] + theirs[:width])

time: 178 us -> 189 us (1.062)
  starting transfers between devices: 46.4 us -> 68.5 us
  local copies, waits for them, and re-layouts: 5.65 us -> 21.6 us
  between operations: 14.5 us -> 1.27 us
  waiting for transfers between devices: 70.8 us -> 58.9 us
  other arithmetic: 15.3 us -> 7.09 us
  matrix products: 10.8 us -> 17.2 us
    all_to_all x0 -> x2, starting transfers between devices: none -> 23.7 us  [the longest x1 17.6 us: shards(): updates = lax.all_to_all(updates, ('row', 'col'), 0, 0).astype(f32).sum(0)]
    all_to_all x4 -> x2, waiting for transfers between devices: 44.1 us -> 20.8 us  [sum_scatter(): others = lax.all_to_all(parts.astype(bf16), axes, 0, 0).astype(f32)]
    all_to_all x0 -> x2, waiting for transfers between devices: none -> 19.1 us  [the longest x1 10.6 us: shards(): updates = lax.all_to_all(updates, ('row', 'col'), 0, 0).astype(f32).sum(0)]
    all_to_all x4 -> x2, starting transfers between devices: 19.2 us -> 7.14 us  [sum_scatter(): others = lax.all_to_all(parts.astype(bf16), axes, 0, 0).astype(f32)]
    dynamic_update_slice x0 -> x8, local copies, waits for them, and re-layouts: none -> 10.7 us  [shards(): lax.dynamic_update_slice_in_dim(whole, piece[None], (place + k) % 4, 0)]
    ppermute x0 -> x6, starting transfers between devices: none -> 6.04 us  [shards(): lax.ppermute(packed, 'col', plane(-k * step_y, -k * step_x))]
    all_to_all x3, waiting for transfers between devices: 18.8 us -> 13.8 us  [gather(): return lax.all_to_all(spread, axes, 0, 0)]
    dot_general x5, matrix products: 4.43 us -> 8.09 us  [mul(): return jnp.dot(left, right, preferred_element_type=f32, **kw)]
  transfers between devices with their start and end apart: 14 -> 19, of which waited for: 11 -> 10; matrix products, arithmetic and copies ran while one was open for 10% -> 16% of each run, Pallas kernels for 0% -> 0%
where the time goes in v4:
time: 189 us; the launch traced here: 188 us
  starting transfers between devices  68.5 us (36%)
  waiting for transfers between devices  58.9 us (31%)
  local copies, waits for them, and re-layouts  21.6 us (11%)
  matrix products  17.2 us (9%)
  blocking collectives  13.4 us (7%)
  other arithmetic  7.09 us (4%)
    all_to_all x2, waiting for transfers between devices, sum_scatter(): others = lax.all_to_all(parts.astype(bf16), axes, 0, 0).astype(f32)  20.8 us
    all_to_all x1, starting transfers between devices, shards(): updates = lax.all_to_all(updates, ('row', 'col'), 0, 0).astype(f32).sum(0)  17.6 us
    all_to_all x3, starting transfers between devices, gather(): return lax.all_to_all(spread, axes, 0, 0)  16.3 us
    all_to_all x3, waiting for transfers between devices, gather(): return lax.all_to_all(spread, axes, 0, 0)  13.8 us
    all_to_all x1, blocking collectives, gather(): return lax.all_to_all(spread, axes, 0, 0)  13.4 us
    dynamic_update_slice x8, local copies, waits for them, and re-layouts, shards(): lax.dynamic_update_slice_in_dim(whole, piece[None], (place + k) % 4, 0)  10.7 us
    all_to_all x1, waiting for transfers between devices, shards(): updates = lax.all_to_all(updates, ('row', 'col'), 0, 0).astype(f32).sum(0)  10.6 us
    all_to_all x1, waiting for transfers between devices, shards(): total = lax.all_to_all(partial.reshape(COLS, width, sources), 'col', 0, 0)  8.45 us
  transfers between devices with their start and end apart: 19, of which 10 were waited for; matrix products, arithmetic and copies ran while one was open for 16% of the time, Pallas kernels for 0%

profile of v4, /device:TPU:1, one launch (start us, length us, event | category | flops | bytes accessed | tf_op | source)
XLA Modules:
  0.0 188.0 jit_solution(6448175701345525346)
XLA Ops:
  0.7 1.2 copy-done
  1.9 2.5 %fusion.40 = (bf16[128,128]{1,0:T(8,128)(2,1)S(1)}, f32[128,128]{1,0:T(8,128)}) fusion(f32[1,2048,128]{2,1,0:T(8,128)} %param.14, f32[1,128,2048]{2,1,0:T(8,128)S(1)} %copy-done), kind=kOutput, calls=%fused_computation.78 | convolution fusion | flops 201342976 | bytes 2195456 | tf_op jit(solution)/shard_map/dot_general | solution.py:19
  4.3 1.3 collective-permute-start
  5.6 1.4 fusion.2
  7.1 3.3 %collective-permute-start.7 = (bf16[1536,128]{0,1:T(8,128)(2,1)S(1)}, bf16[1536,128]{0,1:T(8,128)(2,1)S(1)}, u32[]{:S(2)}, u32[]{:S(2)}) collective-permute-start(bf16[1536,128]{0,1:T(8,128)(2,1)S(1)} %fusion.2), channel_id=1, source_target_pairs={{0,16},{16,0},{1,17},{17,1},{2,18},{18,2},{3,19},{19,3},{4,20},{20... | collective-permute-start | bytes 1179656 | tf_op jit(solution)/shard_map/ppermute | solution.py:123
  11.2 2.2 %convolution_convert_fusion.1 = bf16[2048,128]{1,0:T(8,128)(2,1)} fusion(bf16[128,128]{1,0:T(8,128)(2,1)S(1)} %collective-permute-done, bf16[1,2,128,2048]{3,2,1,0:T(8,128)(2,1)} %param.8, bf16[2048]{0:T(1024)(128)(2,1)S(1)} %bitcast.101), kind=kOutput, calls=%fused_computation.5 | convolution fusion | flops 67633152 | bytes 1085440 | tf_op jit(solution)/shard_map/dot_general | solution.py:23
  14.0 0.8 concatenate.11
  14.8 1.2 collective-permute-start.1
  16.0 0.5 collective-permute-start.2
  16.5 0.6 collective-permute-start.3
  17.1 6.1 %all-to-all-start = ((bf16[16,128,128]{2,1,0:T(8,128)(2,1)}), bf16[16,128,128]{2,1,0:T(8,128)(2,1)S(1)}, u32[]{:S(2)}, u32[]{:S(2)}) async-start(bf16[16,128,128]{2,1,0:T(8,128)(2,1)} %bitcast.3), calls=%async_computation | async-start | bytes 1048576 | tf_op jit(solution)/shard_map/all_to_all | solution.py:84
  23.3 0.9 bitcast_dynamic-update-slice_fusion.7
  24.3 0.9 bitcast_dynamic-update-slice_fusion.6
  25.2 0.9 bitcast_dynamic-update-slice_fusion.5
  26.2 8.4 %all-to-all-done = bf16[16,128,128]{2,1,0:T(8,128)(2,1)S(1)} async-done(((bf16[16,128,128]{2,1,0:T(8,128)(2,1)}), bf16[16,128,128]{2,1,0:T(8,128)(2,1)S(1)}, u32[]{:S(2)}, u32[]{:S(2)}) %all-to-all-start) | async-done | bytes 524320 | tf_op jit(solution)/shard_map/all_to_all | solution.py:84
  34.7 0.9 broadcast_in_dim.102
  35.6 3.7 %all-to-all-start.1 = ((bf16[16,128,128]{2,1,0:T(8,128)(2,1)}), bf16[16,128,128]{2,1,0:T(8,128)(2,1)S(1)}, u32[]{:S(2)}, u32[]{:S(2)}) async-start(bf16[16,128,128]{2,1,0:T(8,128)(2,1)} %broadcast_in_dim.102), calls=%async_computation.1 | async-start | bytes 1048576 | tf_op jit(solution)/shard_map/all_to_all | solution.py:55
  39.3 0.9 bitcast_dynamic-update-slice_fusion.4
  40.3 1.1 pad_maximum_fusion
  41.4 2.6 %collective-permute-start.4 = (bf16[4,96,896]{2,1,0:T(8,128)(2,1)S(1)}, bf16[4,96,896]{2,1,0:T(8,128)(2,1)}, u32[]{:S(2)}, u32[]{:S(2)}) collective-permute-start(bf16[4,96,896]{2,1,0:T(8,128)(2,1)S(1)} %bitcast_dynamic-update-slice_fusion.4), channel_id=1, source_target_pairs={{0,12},{1,13},{2,14},{3,15},{4,0},{5,1},{6,2},{7,3},{8,4},{9,5},{1... | collective-permute-start | bytes 2064392 | tf_op jit(solution)/shard_map/ppermute | solution.py:102
  43.9 0.6 collective-permute-start.5
  44.5 0.6 collective-permute-start.6
  45.1 4.3 %all-to-all-done.1 = bf16[16,128,128]{2,1,0:T(8,128)(2,1)S(1)} async-done(((bf16[16,128,128]{2,1,0:T(8,128)(2,1)}), bf16[16,128,128]{2,1,0:T(8,128)(2,1)S(1)}, u32[]{:S(2)}, u32[]{:S(2)}) %all-to-all-start.1) | async-done | bytes 524320 | tf_op jit(solution)/shard_map/all_to_all | solution.py:55
  49.4 0.4 fusion.10
  49.9 1.1 convolution_convert_fusion
  50.9 17.6 %all-to-all-start.2 = ((bf16[32,48,128]{2,1,0:T(8,128)(2,1)}), bf16[32,48,128]{2,1,0:T(8,128)(2,1)S(1)}, u32[]{:S(2)}, u32[]{:S(2)}) async-start(bf16[32,48,128]{2,1,0:T(8,128)(2,1)} %bitcast.18), calls=%async_computation.2 | async-start | bytes 786432 | tf_op jit(solution)/shard_map/all_to_all | solution.py:126
  68.6 1.8 broadcast_in_dim.103
  70.3 0.9 bitcast_dynamic-update-slice_fusion.3
  71.2 2.0 %bitcast_dynamic-update-slice_fusion.2 = bf16[4,4,96,896]{3,2,1,0:T(8,128)(2,1)} fusion(bf16[4,4,96,896]{3,2,1,0:T(8,128)(2,1)} %bitcast_dynamic-update-slice_fusion.3, s32[]{:T(128)S(6)} %select_n.119, bf16[4,96,896]{2,1,0:T(8,128)(2,1)} %collective-permute-done.4), kind=kLoop, calls=%fused_computation.34 | loop fusion | bytes 1376260 | tf_op jit(solution)/shard_map/dynamic_update_slice | solution.py:103
  73.3 10.6 %all-to-all-done.2 = bf16[32,48,128]{2,1,0:T(8,128)(2,1)S(1)} async-done(((bf16[32,48,128]{2,1,0:T(8,128)(2,1)}), bf16[32,48,128]{2,1,0:T(8,128)(2,1)S(1)}, u32[]{:S(2)}, u32[]{:S(2)}) %all-to-all-start.2) | async-done | bytes 393248 | tf_op jit(solution)/shard_map/all_to_all | solution.py:126
  84.0 0.7 broadcast_in_dim.115
  84.7 8.2 %all-to-all-start.3 = ((f32[8,48,128]{2,1,0:T(8,128)}), f32[8,48,128]{2,1,0:T(8,128)S(1)}, u32[]{:S(2)}, u32[]{:S(2)}) async-start(f32[8,48,128]{2,1,0:T(8,128)} %broadcast_in_dim.115), calls=%async_computation.3 | async-start | bytes 393216 | tf_op jit(solution)/shard_map/all_to_all | solution.py:55
  92.9 2.0 %bitcast_dynamic-update-slice_fusion.1 = bf16[4,4,96,896]{3,2,1,0:T(8,128)(2,1)} fusion(bf16[4,4,96,896]{3,2,1,0:T(8,128)(2,1)} %bitcast_dynamic-update-slice_fusion.2, s32[]{:T(128)S(6)} %select_n.121, bf16[4,96,896]{2,1,0:T(8,128)(2,1)} %collective-permute-done.5), kind=kLoop, calls=%fused_computation.33 | loop fusion | bytes 1376260 | tf_op jit(solution)/shard_map/dynamic_update_slice | solution.py:103
  94.9 2.0 %bitcast_dynamic-update-slice_fusion = bf16[4,4,96,896]{3,2,1,0:T(8,128)(2,1)} fusion(bf16[4,4,96,896]{3,2,1,0:T(8,128)(2,1)} %bitcast_dynamic-update-slice_fusion.1, s32[]{:T(128)S(6)} %select_n.123, bf16[4,96,896]{2,1,0:T(8,128)(2,1)} %collective-permute-done.6), kind=kLoop, calls=%fused_computation.32 | loop fusion | bytes 1376260 | tf_op jit(solution)/shard_map/dynamic_update_slice | solution.py:103
  96.9 5.2 %all-to-all-done.3 = f32[8,48,128]{2,1,0:T(8,128)S(1)} async-done(((f32[8,48,128]{2,1,0:T(8,128)}), f32[8,48,128]{2,1,0:T(8,128)S(1)}, u32[]{:S(2)}, u32[]{:S(2)}) %all-to-all-start.3) | async-done | bytes 196640 | tf_op jit(solution)/shard_map/all_to_all | solution.py:55
  102.1 2.8 %fusion.41 = (bf16[1536,352]{0,1:T(8,128)(2,1)S(1)}, f32[1536,352]{0,1:T(8,128)S(1)}) fusion(bf16[1536,352]{0,1:T(8,128)(2,1)} %pad_maximum_fusion, s32[]{:T(128)S(6)} %select_n.104, bf16[1536,896]{1,0:T(8,128)(2,1)} %bitcast.15), kind=kOutput, calls=%fused_computation.79 | convolution fusion | flops 831012864 | bytes 6144004 | tf_op jit(solution)/shard_map/dot_general | solution.py:19
  105.0 1.1 pad_maximum_fusion.1
  106.1 2.2 %collective-permute-start.8 = (bf16[1536,352]{0,1:T(8,128)(2,1)}, bf16[1536,352]{0,1:T(8,128)(2,1)}, u32[]{:S(2)}, u32[]{:S(2)}) collective-permute-start(bf16[1536,352]{0,1:T(8,128)(2,1)} %pad_maximum_fusion.1), channel_id=1, source_target_pairs={{0,16},{16,0},{1,17},{17,1},{2,18},{18,2},{3,19},{19,3},{4,20},{20... | collective-permute-start | bytes 3244040 | tf_op jit(solution)/shard_map/ppermute | solution.py:141
  108.3 0.7 constant_dynamic-slice_fusion.2
  109.0 2.2 %collective-permute-start.9 = (f32[48,128]{1,0:T(8,128)S(1)}, f32[48,128]{1,0:T(8,128)S(1)}, u32[]{:S(2)}, u32[]{:S(2)}) collective-permute-start(f32[48,128]{1,0:T(8,128)S(1)} %constant_dynamic-slice_fusion.2), channel_id=1, source_target_pairs={{0,0},{1,2},{2,4},{3,6},{4,8},{5,10},{6,12},{7,14},{8,16},{9,18},{... | collective-permute-start | bytes 73736 | tf_op jit(solution)/shard_map/ppermute | solution.py:118
  111.2 1.2 convert_reduce_fusion
  112.5 3.4 %collective-permute-done.9 = f32[48,128]{1,0:T(8,128)S(1)} collective-permute-done((f32[48,128]{1,0:T(8,128)S(1)}, f32[48,128]{1,0:T(8,128)S(1)}, u32[]{:S(2)}, u32[]{:S(2)}) %collective-permute-start.9) | collective-permute-done | bytes 24608 | tf_op jit(solution)/shard_map/ppermute | solution.py:118
  115.8 0.8 broadcast_in_dim.116
  116.7 4.4 %all-to-all-start.4 = ((f32[16,48,128]{2,1,0:T(8,128)}), f32[16,48,128]{2,1,0:T(8,128)}, u32[]{:S(2)}, u32[]{:S(2)}) async-start(f32[16,48,128]{2,1,0:T(8,128)} %broadcast_in_dim.116), calls=%async_computation.4 | async-start | bytes 786432 | tf_op jit(solution)/shard_map/all_to_all | solution.py:55
  121.1 1.9 convert_add_fusion
  123.0 2.7 %fusion.7 = f32[768,352]{0,1:T(8,128)S(1)} fusion(bf16[1536,896]{1,0:T(8,128)(2,1)} %bitcast.15, f32[1536,352]{0,1:T(8,128)S(1)} %convert_add_fusion, s32[]{:T(128)S(6)} %select_n.104, f32[768]{0:T(1024)S(1)} %dynamic-slice.1), kind=kOutput, calls=%fused_computation.11 | convolution fusion | flops 831553536 | bytes 6688772 | tf_op jit(solution)/shard_map/dot_general | solution.py:23
  125.7 4.3 %all-to-all-done.4 = f32[16,48,128]{2,1,0:T(8,128)} async-done(((f32[16,48,128]{2,1,0:T(8,128)}), f32[16,48,128]{2,1,0:T(8,128)}, u32[]{:S(2)}, u32[]{:S(2)}) %all-to-all-start.4) | async-done | bytes 393248 | tf_op jit(solution)/shard_map/all_to_all | solution.py:55
  130.0 1.6 fusion.42
  131.6 2.3 %collective-permute-start.10 = (f32[224,128]{1,0:T(8,128)S(1)}, f32[224,128]{1,0:T(8,128)S(1)}, u32[]{:S(2)}, u32[]{:S(2)}) collective-permute-start(f32[224,128]{1,0:T(8,128)S(1)} %slice.51), channel_id=1, source_target_pairs={{0,16},{16,0},{1,17},{17,1},{2,18},{18,2},{3,19},{19,3},{4,20},{20... | collective-permute-start | bytes 344072 | tf_op jit(solution)/shard_map/ppermute | solution.py:147
  133.9 1.0 collective-permute-done.10
  134.9 0.6 fusion.16
  135.5 0.9 bitcast_convert_fusion.1
  136.4 3.6 %all-to-all-start.5 = ((bf16[16,128,128]{1,2,0:T(8,128)(2,1)}), bf16[16,128,128]{1,2,0:T(8,128)(2,1)S(1)}, u32[]{:S(2)}, u32[]{:S(2)}) async-start(bf16[16,128,128]{1,2,0:T(8,128)(2,1)} %bitcast_convert_fusion.1), calls=%async_computation.5 | async-start | bytes 1048576 | tf_op jit(solution)/shard_map/all_to_all | solution.py:48
  140.2 10.7 %all-to-all-done.5 = bf16[16,128,128]{1,2,0:T(8,128)(2,1)S(1)} async-done(((bf16[16,128,128]{1,2,0:T(8,128)(2,1)}), bf16[16,128,128]{1,2,0:T(8,128)(2,1)S(1)}, u32[]{:S(2)}, u32[]{:S(2)}) %all-to-all-start.5) | async-done | bytes 524320 | tf_op jit(solution)/shard_map/all_to_all | solution.py:48
  151.4 13.4 %all_to_all.40 = bf16[16,128,128]{2,1,0:T(8,128)(2,1)S(1)} all-to-all(bf16[16,128,128]{2,1,0:T(8,128)(2,1)S(1)} %broadcast_in_dim.119), channel_id=1, replica_groups=mesh['sub'=8,'row'=2,'col'=16] {'col'}, dimensions={0} | all-to-all | bytes 1048576 | tf_op jit(solution)/shard_map/all_to_all | solution.py:55
  164.7 1.3 fusion.22
  166.0 4.1 %collective-permute-start.11 = (f32[128,128]{1,0:T(8,128)S(1)}, f32[128,128]{1,0:T(8,128)S(1)}, u32[]{:S(2)}, u32[]{:S(2)}) collective-permute-start(f32[128,128]{1,0:T(8,128)S(1)} %fusion.22), channel_id=1, source_target_pairs={{16,0},{17,1},{18,2},{19,3},{20,4},{21,5},{22,6},{23,7},{24,8},{25... | collective-permute-start | bytes 196616 | tf_op jit(solution)/shard_map/ppermute | solution.py:153
  170.1 0.9 collective-permute-done.11
  171.0 0.6 fusion.14
  171.6 0.9 bitcast_convert_fusion
  172.5 3.6 %all-to-all-start.7 = ((bf16[16,128,128]{1,2,0:T(8,128)(2,1)}), bf16[16,128,128]{1,2,0:T(8,128)(2,1)S(1)}, u32[]{:S(2)}, u32[]{:S(2)}) async-start(bf16[16,128,128]{1,2,0:T(8,128)(2,1)} %bitcast_convert_fusion), calls=%async_computation.7 | async-start | bytes 1048576 | tf_op jit(solution)/shard_map/all_to_all | solution.py:48
  176.1 0.6 slice_add_fusion.1
  177.0 10.1 %all-to-all-done.7 = bf16[16,128,128]{1,2,0:T(8,128)(2,1)S(1)} async-done(((bf16[16,128,128]{1,2,0:T(8,128)(2,1)}), bf16[16,128,128]{1,2,0:T(8,128)(2,1)S(1)}, u32[]{:S(2)}, u32[]{:S(2)}) %all-to-all-start.7) | async-done | bytes 524320 | tf_op jit(solution)/shard_map/all_to_all | solution.py:48
  187.3 0.7 copy.33
  (61 shorter events, 2.7 us)
Async XLA Ops:
  0.6 1.2 copy-start
  0.6 5.0 %copy-start.9 = (s32[1,1024]{1,0:T(1,128)S(1)}, s32[1,1024]{1,0:T(1,128)}, u32[]{:S(2)}) copy-start(s32[1,1024]{1,0:T(1,128)} %param.12) | copy-start | bytes 12292
  0.7 5.0 %copy-start.8 = (bf16[1,1,128,1024]{3,2,1,0:T(8,128)(2,1)S(1)}, bf16[1,1,128,1024]{3,2,1,0:T(8,128)(2,1)}, u32[]{:S(2)}) copy-start(bf16[1,1,128,1024]{3,2,1,0:T(8,128)(2,1)} %param.11) | copy-start | bytes 786436
  4.3 6.9 %collective-permute-start = (bf16[128,128]{1,0:T(8,128)(2,1)S(1)}, bf16[128,128]{1,0:T(8,128)(2,1)S(1)}, u32[]{:S(2)}, u32[]{:S(2)}) collective-permute-start(bf16[128,128]{1,0:T(8,128)(2,1)S(1)} %get-tuple-element.19), channel_id=1, source_target_pairs={{0,16},{1,17},{2,18},{3,19},{4,20},{5,21},{6,22},{7,23},{8,24},{9,... | collective-permute-start | bytes 98312 | tf_op jit(solution)/shard_map/ppermute | solution.py:82
  5.6 5.1 %copy-start.7 = (s32[1,16,16]{2,1,0:T(8,128)S(1)}, s32[1,16,16]{2,1,0:T(8,128)}, u32[]{:S(2)}) copy-start(s32[1,16,16]{2,1,0:T(8,128)} %param.9) | copy-start | bytes 3076
  7.1 42.8 %copy-start.1 = (bf16[1536,128]{0,1:T(8,128)(2,1)}, bf16[1536,128]{0,1:T(8,128)(2,1)S(1)}, u32[]{:S(2)}) copy-start(bf16[1536,128]{0,1:T(8,128)(2,1)S(1)} %fusion.2) | copy-start | bytes 1179652
  7.1 6.3 %copy-start.3 = (f32[96,1536]{1,0:T(8,128)S(1)}, f32[96,1536]{1,0:T(8,128)}, u32[]{:S(2)}) copy-start(f32[96,1536]{1,0:T(8,128)} %param.13) | copy-start | bytes 1769476
  7.1 33.1 %collective-permute-start.7 = (bf16[1536,128]{0,1:T(8,128)(2,1)S(1)}, bf16[1536,128]{0,1:T(8,128)(2,1)S(1)}, u32[]{:S(2)}, u32[]{:S(2)}) collective-permute-start(bf16[1536,128]{0,1:T(8,128)(2,1)S(1)} %fusion.2), channel_id=1, source_target_pairs={{0,16},{16,0},{1,17},{17,1},{2,18},{18,2},{3,19},{19,3},{4,20},{20... | collective-permute-start | bytes 1179656 | tf_op jit(solution)/shard_map/ppermute | solution.py:123
  14.8 9.4 %collective-permute-start.1 = (bf16[96,896]{1,0:T(8,128)(2,1)}, bf16[96,896]{1,0:T(8,128)(2,1)}, u32[]{:S(2)}, u32[]{:S(2)}) collective-permute-start(bf16[96,896]{1,0:T(8,128)(2,1)} %concatenate.11), channel_id=1, source_target_pairs={{0,3},{1,0},{2,1},{3,2},{4,7},{5,4},{6,5},{7,6},{8,11},{9,8},{10,9... | collective-permute-start | bytes 516104 | tf_op jit(solution)/shard_map/ppermute | solution.py:102
  16.0 9.2 %collective-permute-start.2 = (bf16[96,896]{1,0:T(8,128)(2,1)}, bf16[96,896]{1,0:T(8,128)(2,1)}, u32[]{:S(2)}, u32[]{:S(2)}) collective-permute-start(bf16[96,896]{1,0:T(8,128)(2,1)} %concatenate.11), channel_id=1, source_target_pairs={{0,2},{1,3},{2,0},{3,1},{4,6},{5,7},{6,4},{7,5},{8,10},{9,11},{10,... | collective-permute-start | bytes 516104 | tf_op jit(solution)/shard_map/ppermute | solution.py:102
  16.5 22.8 %collective-permute-start.3 = (bf16[96,896]{1,0:T(8,128)(2,1)}, bf16[96,896]{1,0:T(8,128)(2,1)}, u32[]{:S(2)}, u32[]{:S(2)}) collective-permute-start(bf16[96,896]{1,0:T(8,128)(2,1)} %concatenate.11), channel_id=1, source_target_pairs={{0,1},{1,2},{2,3},{3,0},{4,5},{5,6},{6,7},{7,4},{8,9},{9,10},{10,1... | collective-permute-start | bytes 516104 | tf_op jit(solution)/shard_map/ppermute | solution.py:102
  17.1 17.5 %all-to-all-start = ((bf16[16,128,128]{2,1,0:T(8,128)(2,1)}), bf16[16,128,128]{2,1,0:T(8,128)(2,1)S(1)}, u32[]{:S(2)}, u32[]{:S(2)}) async-start(bf16[16,128,128]{2,1,0:T(8,128)(2,1)} %bitcast.3), calls=%async_computation | async-start | bytes 1048576 | tf_op jit(solution)/shard_map/all_to_all | solution.py:84
  34.7 14.7 %copy-start.6 = (f32[128,128]{1,0:T(8,128)S(1)}, f32[128,128]{1,0:T(8,128)}, u32[]{:S(2)}) copy-start(f32[128,128]{1,0:T(8,128)} %get-tuple-element.20) | copy-start | bytes 196612
  35.6 13.8 %all-to-all-start.1 = ((bf16[16,128,128]{2,1,0:T(8,128)(2,1)}), bf16[16,128,128]{2,1,0:T(8,128)(2,1)S(1)}, u32[]{:S(2)}, u32[]{:S(2)}) async-start(bf16[16,128,128]{2,1,0:T(8,128)(2,1)} %broadcast_in_dim.102), calls=%async_computation.1 | async-start | bytes 1048576 | tf_op jit(solution)/shard_map/all_to_all | solution.py:55
  40.3 54.6 %copy-start.2 = (bf16[1536,128]{0,1:T(8,128)(2,1)}, bf16[1536,128]{0,1:T(8,128)(2,1)S(1)}, u32[]{:S(2)}) copy-start(bf16[1536,128]{0,1:T(8,128)(2,1)S(1)} %collective-permute-done.7) | copy-start | bytes 1179652
  41.4 29.9 %collective-permute-start.4 = (bf16[4,96,896]{2,1,0:T(8,128)(2,1)S(1)}, bf16[4,96,896]{2,1,0:T(8,128)(2,1)}, u32[]{:S(2)}, u32[]{:S(2)}) collective-permute-start(bf16[4,96,896]{2,1,0:T(8,128)(2,1)S(1)} %bitcast_dynamic-update-slice_fusion.4), channel_id=1, source_target_pairs={{0,12},{1,13},{2,14},{3,15},{4,0},{5,1},{6,2},{7,3},{8,4},{9,5},{1... | collective-permute-start | bytes 2064392 | tf_op jit(solution)/shard_map/ppermute | solution.py:102
  43.9 48.9 %collective-permute-start.5 = (bf16[4,96,896]{2,1,0:T(8,128)(2,1)S(1)}, bf16[4,96,896]{2,1,0:T(8,128)(2,1)}, u32[]{:S(2)}, u32[]{:S(2)}) collective-permute-start(bf16[4,96,896]{2,1,0:T(8,128)(2,1)S(1)} %bitcast_dynamic-update-slice_fusion.4), channel_id=1, source_target_pairs={{0,8},{1,9},{2,10},{3,11},{4,12},{5,13},{6,14},{7,15},{8,0},{9,1},... | collective-permute-start | bytes 2064392 | tf_op jit(solution)/shard_map/ppermute | solution.py:102
  44.5 50.4 %collective-permute-start.6 = (bf16[4,96,896]{2,1,0:T(8,128)(2,1)S(1)}, bf16[4,96,896]{2,1,0:T(8,128)(2,1)}, u32[]{:S(2)}, u32[]{:S(2)}) collective-permute-start(bf16[4,96,896]{2,1,0:T(8,128)(2,1)S(1)} %bitcast_dynamic-update-slice_fusion.4), channel_id=1, source_target_pairs={{0,4},{1,5},{2,6},{3,7},{4,8},{5,9},{6,10},{7,11},{8,12},{9,13},{1... | collective-permute-start | bytes 2064392 | tf_op jit(solution)/shard_map/ppermute | solution.py:102
  49.9 20.5 %copy-start.4 = (f32[128,128]{1,0:T(8,128)}, f32[128,128]{1,0:T(8,128)S(1)}, u32[]{:S(2)}) copy-start(f32[128,128]{1,0:T(8,128)S(1)} %fusion.10) | copy-start | bytes 196612
  50.9 33.0 %all-to-all-start.2 = ((bf16[32,48,128]{2,1,0:T(8,128)(2,1)}), bf16[32,48,128]{2,1,0:T(8,128)(2,1)S(1)}, u32[]{:S(2)}, u32[]{:S(2)}) async-start(bf16[32,48,128]{2,1,0:T(8,128)(2,1)} %bitcast.18), calls=%async_computation.2 | async-start | bytes 786432 | tf_op jit(solution)/shard_map/all_to_all | solution.py:126
  84.7 17.4 %all-to-all-start.3 = ((f32[8,48,128]{2,1,0:T(8,128)}), f32[8,48,128]{2,1,0:T(8,128)S(1)}, u32[]{:S(2)}, u32[]{:S(2)}) async-start(f32[8,48,128]{2,1,0:T(8,128)} %broadcast_in_dim.115), calls=%async_computation.3 | async-start | bytes 393216 | tf_op jit(solution)/shard_map/all_to_all | solution.py:55
  106.1 15.0 %collective-permute-start.8 = (bf16[1536,352]{0,1:T(8,128)(2,1)}, bf16[1536,352]{0,1:T(8,128)(2,1)}, u32[]{:S(2)}, u32[]{:S(2)}) collective-permute-start(bf16[1536,352]{0,1:T(8,128)(2,1)} %pad_maximum_fusion.1), channel_id=1, source_target_pairs={{0,16},{16,0},{1,17},{17,1},{2,18},{18,2},{3,19},{19,3},{4,20},{20... | collective-permute-start | bytes 3244040 | tf_op jit(solution)/shard_map/ppermute | solution.py:141
  109.0 6.8 %collective-permute-start.9 = (f32[48,128]{1,0:T(8,128)S(1)}, f32[48,128]{1,0:T(8,128)S(1)}, u32[]{:S(2)}, u32[]{:S(2)}) collective-permute-start(f32[48,128]{1,0:T(8,128)S(1)} %constant_dynamic-slice_fusion.2), channel_id=1, source_target_pairs={{0,0},{1,2},{2,4},{3,6},{4,8},{5,10},{6,12},{7,14},{8,16},{9,18},{... | collective-permute-start | bytes 73736 | tf_op jit(solution)/shard_map/ppermute | solution.py:118
  116.7 13.3 %all-to-all-start.4 = ((f32[16,48,128]{2,1,0:T(8,128)}), f32[16,48,128]{2,1,0:T(8,128)}, u32[]{:S(2)}, u32[]{:S(2)}) async-start(f32[16,48,128]{2,1,0:T(8,128)} %broadcast_in_dim.116), calls=%async_computation.4 | async-start | bytes 786432 | tf_op jit(solution)/shard_map/all_to_all | solution.py:55
  123.0 11.9 %copy-start.5 = (f32[128,128]{1,0:T(8,128)S(1)}, f32[128,128]{1,0:T(8,128)}, u32[]{:S(2)}) copy-start(f32[128,128]{1,0:T(8,128)} %copy-done.4) | copy-start | bytes 196612
  131.6 3.3 %collective-permute-start.10 = (f32[224,128]{1,0:T(8,128)S(1)}, f32[224,128]{1,0:T(8,128)S(1)}, u32[]{:S(2)}, u32[]{:S(2)}) collective-permute-start(f32[224,128]{1,0:T(8,128)S(1)} %slice.51), channel_id=1, source_target_pairs={{0,16},{16,0},{1,17},{17,1},{2,18},{18,2},{3,19},{19,3},{4,20},{20... | collective-permute-start | bytes 344072 | tf_op jit(solution)/shard_map/ppermute | solution.py:147
  136.4 14.5 %all-to-all-start.5 = ((bf16[16,128,128]{1,2,0:T(8,128)(2,1)}), bf16[16,128,128]{1,2,0:T(8,128)(2,1)S(1)}, u32[]{:S(2)}, u32[]{:S(2)}) async-start(bf16[16,128,128]{1,2,0:T(8,128)(2,1)} %bitcast_convert_fusion.1), calls=%async_computation.5 | async-start | bytes 1048576 | tf_op jit(solution)/shard_map/all_to_all | solution.py:48
  166.0 5.0 %collective-permute-start.11 = (f32[128,128]{1,0:T(8,128)S(1)}, f32[128,128]{1,0:T(8,128)S(1)}, u32[]{:S(2)}, u32[]{:S(2)}) collective-permute-start(f32[128,128]{1,0:T(8,128)S(1)} %fusion.22), channel_id=1, source_target_pairs={{16,0},{17,1},{18,2},{19,3},{20,4},{21,5},{22,6},{23,7},{24,8},{25... | collective-permute-start | bytes 196616 | tf_op jit(solution)/shard_map/ppermute | solution.py:153
  172.5 14.6 %all-to-all-start.7 = ((bf16[16,128,128]{1,2,0:T(8,128)(2,1)}), bf16[16,128,128]{1,2,0:T(8,128)(2,1)S(1)}, u32[]{:S(2)}, u32[]{:S(2)}) async-start(bf16[16,128,128]{1,2,0:T(8,128)(2,1)} %bitcast_convert_fusion), calls=%async_computation.7 | async-start | bytes 1048576 | tf_op jit(solution)/shard_map/all_to_all | solution.py:48

commit v5 on v1

--- a/solution.py
+++ b/solution.py
@@ -23,9 +23,17 @@
     return lax.dot_general(left, right, first_axes, preferred_element_type=f32, **kw)
 
 
+def after(value, other):
+    return lax.optimization_barrier((value, other))[0]
+
+
 def sum_scatter(partial, axes, count):
     parts = partial.reshape(count, -1, partial.shape[-1])
-    return lax.all_to_all(parts, axes, 0, 0).astype(f32).sum(0)
+    here = lax.axis_index(axes)
+    own = lax.dynamic_index_in_dim(parts, here, 0)
+    others = lax.all_to_all(parts.astype(bf16), axes, 0, 0).astype(f32)
+    index = lax.broadcasted_iota(jnp.int32, (count, 1, 1), 0)
+    return jnp.where(index == here, own, others).sum(0)
 
 
 def gather(chunk, axes, count):
@@ -50,29 +58,58 @@
     row_id = lax.axis_index("row")
     col_id = lax.axis_index("col")
     sources = right_side.shape[-1]
+    band_id = lax.axis_index(("sub", "row"))
 
     blocks = lax.dynamic_slice(table, (PANEL // BLOCK, col_id // 2), (PANEL // BLOCK, 1))
     lower = factor_cols[0, 0] * jnp.repeat(blocks[:, 0], BLOCK)[None, :].astype(bf16)
-
-    onehot = (rows_sep[:, None] == jnp.arange(SEPARATOR)[None, :]).astype(bf16)
-    couple_sep = mul(couple, onehot).astype(bf16)
+    width = lower.shape[0]
 
     own = mul(inverse, right_side[0], precision=fine)
     first_low = lax.ppermute(own.astype(bf16), "row", [(0, 1)])
-    total = sum_scatter(mul_t(lower, first_low).astype(bf16), "col", COLS)
-    total = gather(total.astype(bf16), "col", COLS).reshape(PANEL, sources)
+    partial = mul_t(lower, first_low).astype(bf16)
+    total = lax.all_to_all(partial.reshape(COLS, width, sources), "col", 0, 0)
+    total = total.astype(f32).sum(0).astype(bf16)
+
+    share = root_inverse.shape[0]
+    band = SEPARATOR // (2 * SUBS)
+    root_inverse = after(root_inverse, partial)
+    gram = mul_t(
+        root_inverse,
+        lax.dynamic_slice_in_dim(root_inverse, band_id * band, band, 1),
+        precision=fine,
+    ).reshape(COLS, share, band)
+    own_gram = lax.dynamic_index_in_dim(gram, col_id, 0)
+    gram = jnp.pad(gram.astype(bf16), ((0, 0), (0, 0), (0, sources - band)))
+
+    both = jnp.concatenate([jnp.broadcast_to(total[None], (COLS,) + total.shape), gram], 1)
+    both = lax.all_to_all(both, "col", 0, 0)
+    total = both[:, :width].reshape(PANEL, sources)
     solved = own - mul(inverse, total.astype(f32), precision=fine)
+    chips = lax.broadcasted_iota(jnp.int32, (COLS, 1, 1), 0)
+    gram = jnp.where(chips == col_id, own_gram, both[:, width:, :band].astype(f32)).sum(0)
 
-    updates = sum_scatter(mul_t(couple_sep, solved.astype(bf16)), ("col", "row"), COLS * 2)
-    updates = gather(updates, "sub", SUBS).sum(0)
-    half = updates.shape[0]
-    rhs = lax.dynamic_slice_in_dim(root_right, row_id * half, half, 0) - updates
-    rhs = gather(rhs, ("col", "row"), COLS * 2).reshape(SEPARATOR, sources)
-    root_half = mul(root_inverse, rhs, precision=fine)
-    root_part = sum_scatter(mul_t(root_inverse, root_half, precision=fine), "col", COLS)
+    onehot = (jnp.arange(SEPARATOR)[:, None] == rows_sep[None, :]).astype(bf16)
+    couple_sep = lax.dot_general(
+        onehot, couple, (((1,), (1,)), ((), ())), preferred_element_type=f32
+    ).astype(bf16)
+
+    updates = mul(couple_sep, solved.astype(bf16)).astype(bf16).reshape(2 * SUBS, band, sources)
+    updates = lax.all_to_all(updates, ("sub", "row"), 0, 0).astype(f32).sum(0)
+    here = (band_id == col_id).astype(f32)
+    rhs = gather(here * root_right - updates, "col", COLS).sum(0)
+    applied = mul(gram, rhs, precision=fine)
+    half = share // 2
+    kept = lax.dynamic_slice_in_dim(applied, row_id * half, half, 0)
+    sent = lax.dynamic_slice_in_dim(applied, (1 - row_id) * half, half, 0)
+    swap = [(0, 1), (1, 0)]
+    kept = gather(kept + lax.ppermute(sent, "row", swap), "sub", SUBS).sum(0)
+    other = lax.ppermute(kept, "row", swap)
+    root_part = jnp.where(
+        row_id == 0, jnp.concatenate([kept, other], 0), jnp.concatenate([other, kept], 0)
+    )
     root_full = gather(root_part.astype(bf16), "col", COLS).reshape(SEPARATOR, sources)
+    value = solved - mul_t(couple_sep, root_full)
 
-    value = solved - mul(couple_sep, root_full)
     value = sum_scatter(mul_t(inverse, value, precision=fine), "col", COLS)
     later_low = gather(value.astype(bf16), "col", COLS).reshape(PANEL, sources)
     terms = lax.ppermute(mul(lower, later_low), "row", [(1, 0)])

time: 189 us -> 174 us (0.921)
  blocking collectives: 134 us -> 37.4 us
  waiting for transfers between devices: 21.9 us -> 78.8 us
  starting transfers between devices: 19.3 us -> 39.4 us
  other arithmetic: 0.54 us -> 2.69 us
    all_to_all x5 -> x0, blocking collectives: 90.2 us -> none  [sum_scatter(): return lax.all_to_all(parts, axes, 0, 0).astype(f32).sum(0)]
    all_to_all x0 -> x5, waiting for transfers between devices: none -> 57.8 us  [the longest x2 20.5 us: sum_scatter(): others = lax.all_to_all(parts.astype(bf16), axes, 0, 0).astype(f32)]
    all_to_all x0 -> x5, starting transfers between devices: none -> 27.6 us  [the longest x1 11.2 us: shards(): updates = lax.all_to_all(updates, ('sub', 'row'), 0, 0).astype(f32).sum(0)]
    all_to_all x2 -> x1, starting transfers between devices: 11.8 us -> 3.61 us  [gather(): return lax.all_to_all(spread, axes, 0, 0)]
    all_to_all x3, blocking collectives: 44.2 us -> 37.4 us  [gather(): return lax.all_to_all(spread, axes, 0, 0)]
    all_to_all x2 -> x1, waiting for transfers between devices: 17.4 us -> 14.7 us  [gather(): return lax.all_to_all(spread, axes, 0, 0)]
    dot_general x6 -> x5, matrix products: 4.5 us -> 3.72 us  [mul(): return jnp.dot(left, right, preferred_element_type=f32, **kw)]
  transfers between devices with their start and end apart: 4 -> 10, of which waited for: 4 -> 10; matrix products, arithmetic and copies ran while one was open for 1% -> 2% of each run, Pallas kernels for 0% -> 0%
where the time goes in v5:
time: 174 us; the launch traced here: 173 us
  waiting for transfers between devices  78.8 us (45%)
  starting transfers between devices  39.4 us (23%)
  blocking collectives  37.4 us (21%)
  matrix products  8.41 us (5%)
  local copies, waits for them, and re-layouts  5.77 us (3%)
  other arithmetic  2.69 us (2%)
    all_to_all x3, blocking collectives, gather(): return lax.all_to_all(spread, axes, 0, 0)  37.4 us
    all_to_all x2, waiting for transfers between devices, sum_scatter(): others = lax.all_to_all(parts.astype(bf16), axes, 0, 0).astype(f32)  20.5 us
    all_to_all x1, waiting for transfers between devices, gather(): return lax.all_to_all(spread, axes, 0, 0)  14.7 us
    all_to_all x1, waiting for transfers between devices, shards(): updates = lax.all_to_all(updates, ('sub', 'row'), 0, 0).astype(f32).sum(0)  14.5 us
    all_to_all x1, waiting for transfers between devices, shards(): both = lax.all_to_all(both, 'col', 0, 0)  12.8 us
    all_to_all x1, starting transfers between devices, shards(): updates = lax.all_to_all(updates, ('sub', 'row'), 0, 0).astype(f32).sum(0)  11.2 us
    all_to_all x1, waiting for transfers between devices, shards(): total = lax.all_to_all(partial.reshape(COLS, width, sources), 'col', 0, 0)  9.98 us
    all_to_all x2, starting transfers between devices, sum_scatter(): others = lax.all_to_all(parts.astype(bf16), axes, 0, 0).astype(f32)  7.14 us
  transfers between devices with their start and end apart: 10, of which 10 were waited for; matrix products, arithmetic and copies ran while one was open for 2% of the time, Pallas kernels for 0%

profile of v5, /device:TPU:1, one launch (start us, length us, event | category | flops | bytes accessed | tf_op | source)
XLA Modules:
  0.0 173.5 jit_solution(16972184739072038828)
XLA Ops:
  0.6 0.0 copy-start
  0.7 0.0 copy-start.6
  0.7 1.2 copy-done
  1.9 1.8 %fusion.28 = (bf16[128,128]{1,0:T(8,128)(2,1)S(1)}, f32[128,128]{1,0:T(8,128)S(1)}) fusion(f32[1,2048,128]{2,1,0:T(8,128)} %param.14, f32[1,128,2048]{2,1,0:T(8,128)S(1)} %copy-done), kind=kOutput, calls=%fused_computation.52 | convolution fusion | flops 201342976 | bytes 2195456 | tf_op jit(solution)/shard_map/dot_general | solution.py:19
  3.7 1.3 collective-permute-start
  5.0 0.2 fusion.25
  5.2 0.1 broadcast_bitcast_fusion
  5.3 3.6 %collective-permute-done = bf16[128,128]{1,0:T(8,128)(2,1)S(1)} collective-permute-done((bf16[128,128]{1,0:T(8,128)(2,1)S(1)}, bf16[128,128]{1,0:T(8,128)(2,1)S(1)}, u32[]{:S(2)}, u32[]{:S(2)}) %collective-permute-start) | collective-permute-done | bytes 32800 | tf_op jit(solution)/shard_map/ppermute | solution.py:68
  8.9 1.1 convolution_convert_fusion.1
  10.1 5.5 %all-to-all-start = ((bf16[16,128,128]{2,1,0:T(8,128)(2,1)}), bf16[16,128,128]{2,1,0:T(8,128)(2,1)S(1)}, u32[]{:S(2)}, u32[]{:S(2)}) async-start(bf16[16,128,128]{2,1,0:T(8,128)(2,1)} %bitcast.3), calls=%async_computation | async-start | bytes 1048576 | tf_op jit(solution)/shard_map/all_to_all | solution.py:70
  15.6 0.8 fusion.22
  16.4 0.1 convert_element_type.79
  16.5 10.0 %all-to-all-done = bf16[16,128,128]{2,1,0:T(8,128)(2,1)S(1)} async-done(((bf16[16,128,128]{2,1,0:T(8,128)(2,1)}), bf16[16,128,128]{2,1,0:T(8,128)(2,1)S(1)}, u32[]{:S(2)}, u32[]{:S(2)}) %all-to-all-start) | async-done | bytes 524320 | tf_op jit(solution)/shard_map/all_to_all | solution.py:70
  26.4 0.1 reduce_sum.66
  26.5 0.1 broadcast_in_dim.83
  26.6 1.1 fusion.13
  27.7 3.8 %all-to-all-start.1 = ((bf16[16,224,128]{2,1,0:T(8,128)(2,1)}), bf16[16,224,128]{2,1,0:T(8,128)(2,1)S(1)}, u32[]{:S(2)}, u32[]{:S(2)}) async-start(bf16[16,224,128]{2,1,0:T(8,128)(2,1)} %fusion.13), calls=%async_computation.1 | async-start | bytes 1835008 | tf_op jit(solution)/shard_map/all_to_all | solution.py:85
  31.5 1.2 fusion.2
  32.7 12.8 %all-to-all-done.1 = bf16[16,224,128]{2,1,0:T(8,128)(2,1)S(1)} async-done(((bf16[16,224,128]{2,1,0:T(8,128)(2,1)}), bf16[16,224,128]{2,1,0:T(8,128)(2,1)S(1)}, u32[]{:S(2)}, u32[]{:S(2)}) %all-to-all-start.1) | async-done | bytes 917536 | tf_op jit(solution)/shard_map/all_to_all | solution.py:85
  45.5 0.4 fusion.4
  45.9 0.0 copy-start.4
  46.0 0.0 copy-start.8
  46.0 1.0 convolution_convert_fusion
  47.0 11.2 %all-to-all-start.2 = ((bf16[16,96,128]{2,1,0:T(8,128)(2,1)}), bf16[16,96,128]{2,1,0:T(8,128)(2,1)S(1)}, u32[]{:S(2)}, u32[]{:S(2)}) async-start(bf16[16,96,128]{2,1,0:T(8,128)(2,1)} %bitcast.9), calls=%async_computation.2 | async-start | bytes 786432 | tf_op jit(solution)/shard_map/all_to_all | solution.py:97
  58.2 14.5 %all-to-all-done.2 = bf16[16,96,128]{2,1,0:T(8,128)(2,1)S(1)} async-done(((bf16[16,96,128]{2,1,0:T(8,128)(2,1)}), bf16[16,96,128]{2,1,0:T(8,128)(2,1)S(1)}, u32[]{:S(2)}, u32[]{:S(2)}) %all-to-all-start.2) | async-done | bytes 393248 | tf_op jit(solution)/shard_map/all_to_all | solution.py:97
  72.8 0.1 convert_reduce_fusion
  72.8 0.0 copy-done.8
  72.9 1.0 broadcast_in_dim.87
  73.8 3.6 %all-to-all-start.3 = ((f32[16,96,128]{2,1,0:T(8,128)}), f32[16,96,128]{2,1,0:T(8,128)S(1)}, u32[]{:S(2)}, u32[]{:S(2)}) async-start(f32[16,96,128]{2,1,0:T(8,128)} %broadcast_in_dim.87), calls=%async_computation.3 | async-start | bytes 1572864 | tf_op jit(solution)/shard_map/all_to_all | solution.py:41
  77.5 0.2 select_reduce_fusion.2
  77.7 14.7 %all-to-all-done.3 = f32[16,96,128]{2,1,0:T(8,128)S(1)} async-done(((f32[16,96,128]{2,1,0:T(8,128)}), f32[16,96,128]{2,1,0:T(8,128)S(1)}, u32[]{:S(2)}, u32[]{:S(2)}) %all-to-all-start.3) | async-done | bytes 786464 | tf_op jit(solution)/shard_map/all_to_all | solution.py:41
  92.4 0.2 fusion.29
  92.6 0.5 collective-permute-start.1
  93.1 0.8 collective-permute-done.1
  94.0 12.7 %all_to_all.45 = f32[8,48,128]{2,1,0:T(8,128)S(1)} all-to-all(f32[8,48,128]{2,1,0:T(8,128)S(1)} %broadcast_in_dim.88), channel_id=1, replica_groups=mesh['sub'=8,'row'=2,'col'=16] {'sub'}, dimensions={0} | all-to-all | bytes 393216 | tf_op jit(solution)/shard_map/all_to_all | solution.py:41
  106.7 1.3 collective-permute-start.2
  108.0 0.8 collective-permute-done.2
  108.9 0.6 fusion.27
  109.5 0.1 broadcast_in_dim.89
  109.6 12.3 %all_to_all.46 = bf16[16,96,128]{2,1,0:T(8,128)(2,1)S(1)} all-to-all(bf16[16,96,128]{2,1,0:T(8,128)(2,1)S(1)} %broadcast_in_dim.89), channel_id=1, replica_groups=mesh['sub'=8,'row'=2,'col'=16] {'col'}, dimensions={0} | all-to-all | bytes 786432 | tf_op jit(solution)/shard_map/all_to_all | solution.py:41
  121.9 0.0 copy-done.2
  121.9 0.3 convolution_subtract_fusion
  122.2 0.6 fusion.9
  122.8 0.9 bitcast_convert_fusion.1
  123.7 3.6 %all-to-all-start.6 = ((bf16[16,128,128]{1,2,0:T(8,128)(2,1)}), bf16[16,128,128]{1,2,0:T(8,128)(2,1)S(1)}, u32[]{:S(2)}, u32[]{:S(2)}) async-start(bf16[16,128,128]{1,2,0:T(8,128)(2,1)} %bitcast_convert_fusion.1), calls=%async_computation.6 | async-start | bytes 1048576 | tf_op jit(solution)/shard_map/all_to_all | solution.py:34
  127.3 0.2 copy.40
  127.5 0.1 constant_dynamic-slice_fusion.1
  127.5 9.8 %all-to-all-done.6 = bf16[16,128,128]{1,2,0:T(8,128)(2,1)S(1)} async-done(((bf16[16,128,128]{1,2,0:T(8,128)(2,1)}), bf16[16,128,128]{1,2,0:T(8,128)(2,1)S(1)}, u32[]{:S(2)}, u32[]{:S(2)}) %all-to-all-start.6) | async-done | bytes 524320 | tf_op jit(solution)/shard_map/all_to_all | solution.py:34
  137.4 0.2 select_reduce_fusion.1
  137.5 0.0 copy-start.7
  137.6 0.1 copy.29
  137.7 0.1 broadcast_in_dim.92
  137.8 12.4 %all_to_all.47 = bf16[16,128,128]{2,1,0:T(8,128)(2,1)S(1)} all-to-all(bf16[16,128,128]{2,1,0:T(8,128)(2,1)S(1)} %broadcast_in_dim.92), channel_id=1, replica_groups=mesh['sub'=8,'row'=2,'col'=16] {'col'}, dimensions={0} | all-to-all | bytes 1048576 | tf_op jit(solution)/shard_map/all_to_all | solution.py:41
  150.2 0.3 fusion.14
  150.5 5.1 %collective-permute-start.3 = (f32[128,128]{1,0:T(8,128)S(1)}, f32[128,128]{1,0:T(8,128)S(1)}, u32[]{:S(2)}, u32[]{:S(2)}) collective-permute-start(f32[128,128]{1,0:T(8,128)S(1)} %fusion.14), channel_id=1, source_target_pairs={{16,0},{17,1},{18,2},{19,3},{20,4},{21,5},{22,6},{23,7},{24,8},{25... | collective-permute-start | bytes 196616 | tf_op jit(solution)/shard_map/ppermute | solution.py:115
  155.6 0.9 collective-permute-done.3
  156.5 0.6 fusion.7
  157.1 0.9 bitcast_convert_fusion
  158.0 3.6 %all-to-all-start.8 = ((bf16[16,128,128]{1,2,0:T(8,128)(2,1)}), bf16[16,128,128]{1,2,0:T(8,128)(2,1)S(1)}, u32[]{:S(2)}, u32[]{:S(2)}) async-start(bf16[16,128,128]{1,2,0:T(8,128)(2,1)} %bitcast_convert_fusion), calls=%async_computation.8 | async-start | bytes 1048576 | tf_op jit(solution)/shard_map/all_to_all | solution.py:34
  161.6 0.2 copy.41
  161.8 0.1 constant_dynamic-slice_fusion
  161.8 10.7 %all-to-all-done.8 = bf16[16,128,128]{1,2,0:T(8,128)(2,1)S(1)} async-done(((bf16[16,128,128]{1,2,0:T(8,128)(2,1)}), bf16[16,128,128]{1,2,0:T(8,128)(2,1)S(1)}, u32[]{:S(2)}, u32[]{:S(2)}) %all-to-all-start.8) | async-done | bytes 524320 | tf_op jit(solution)/shard_map/all_to_all | solution.py:34
  172.5 0.2 select_reduce_fusion
  172.7 0.7 copy.32
  (28 shorter events, 0.2 us)
Async XLA Ops:
  0.6 1.2 copy-start
  0.6 4.4 %copy-start.9 = (s32[1,16,16]{2,1,0:T(8,128)S(1)}, s32[1,16,16]{2,1,0:T(8,128)}, u32[]{:S(2)}) copy-start(s32[1,16,16]{2,1,0:T(8,128)} %param.9) | copy-start | bytes 3076
  0.7 8.3 %copy-start.6 = (bf16[1,2,128,2048]{3,2,1,0:T(8,128)(2,1)S(1)}, bf16[1,2,128,2048]{3,2,1,0:T(8,128)(2,1)}, u32[]{:S(2)}) copy-start(bf16[1,2,128,2048]{3,2,1,0:T(8,128)(2,1)} %param.8) | copy-start | bytes 3145732
  3.7 5.2 %collective-permute-start = (bf16[128,128]{1,0:T(8,128)(2,1)S(1)}, bf16[128,128]{1,0:T(8,128)(2,1)S(1)}, u32[]{:S(2)}, u32[]{:S(2)}) collective-permute-start(bf16[128,128]{1,0:T(8,128)(2,1)S(1)} %get-tuple-element.10), channel_id=1, source_target_pairs={{0,16},{1,17},{2,18},{3,19},{4,20},{5,21},{6,22},{7,23},{8,24},{9,... | collective-permute-start | bytes 98312 | tf_op jit(solution)/shard_map/ppermute | solution.py:68
  8.9 6.6 %copy-start.3 = (f32[96,1536]{1,0:T(8,128)S(1)}, f32[96,1536]{1,0:T(8,128)}, u32[]{:S(2)}) copy-start(f32[96,1536]{1,0:T(8,128)} %param.13) | copy-start | bytes 1769476
  10.1 16.4 %all-to-all-start = ((bf16[16,128,128]{2,1,0:T(8,128)(2,1)}), bf16[16,128,128]{2,1,0:T(8,128)(2,1)S(1)}, u32[]{:S(2)}, u32[]{:S(2)}) async-start(bf16[16,128,128]{2,1,0:T(8,128)(2,1)} %bitcast.3), calls=%async_computation | async-start | bytes 1048576 | tf_op jit(solution)/shard_map/all_to_all | solution.py:70
  27.7 3.8 %copy-start.10 = (bf16[1,1,128,1024]{3,2,1,0:T(8,128)(2,1)S(1)}, bf16[1,1,128,1024]{3,2,1,0:T(8,128)(2,1)}, u32[]{:S(2)}) copy-start(bf16[1,1,128,1024]{3,2,1,0:T(8,128)(2,1)} %param.11) | copy-start | bytes 786436
  27.7 3.8 %copy-start.11 = (s32[1,1024]{1,0:T(1,128)S(1)}, s32[1,1024]{1,0:T(1,128)}, u32[]{:S(2)}) copy-start(s32[1,1024]{1,0:T(1,128)} %param.12) | copy-start | bytes 12292
  27.7 17.8 %all-to-all-start.1 = ((bf16[16,224,128]{2,1,0:T(8,128)(2,1)}), bf16[16,224,128]{2,1,0:T(8,128)(2,1)S(1)}, u32[]{:S(2)}, u32[]{:S(2)}) async-start(bf16[16,224,128]{2,1,0:T(8,128)(2,1)} %fusion.13), calls=%async_computation.1 | async-start | bytes 1835008 | tf_op jit(solution)/shard_map/all_to_all | solution.py:85
  32.7 13.3 %copy-start.1 = (bf16[1536,128]{1,0:T(8,128)(2,1)}, bf16[1536,128]{1,0:T(8,128)(2,1)S(1)}, u32[]{:S(2)}) copy-start(bf16[1536,128]{1,0:T(8,128)(2,1)S(1)} %fusion.2) | copy-start | bytes 1179652
  45.9 1.0 copy-start.4
  46.0 26.9 %copy-start.8 = (f32[96,128]{1,0:T(8,128)S(1)}, f32[96,128]{1,0:T(8,128)}, u32[]{:S(2)}) copy-start(f32[96,128]{1,0:T(8,128)} %param.15) | copy-start | bytes 147460
  47.0 25.8 %all-to-all-start.2 = ((bf16[16,96,128]{2,1,0:T(8,128)(2,1)}), bf16[16,96,128]{2,1,0:T(8,128)(2,1)S(1)}, u32[]{:S(2)}, u32[]{:S(2)}) async-start(bf16[16,96,128]{2,1,0:T(8,128)(2,1)} %bitcast.9), calls=%async_computation.2 | async-start | bytes 786432 | tf_op jit(solution)/shard_map/all_to_all | solution.py:97
  73.8 18.6 %all-to-all-start.3 = ((f32[16,96,128]{2,1,0:T(8,128)}), f32[16,96,128]{2,1,0:T(8,128)S(1)}, u32[]{:S(2)}, u32[]{:S(2)}) async-start(f32[16,96,128]{2,1,0:T(8,128)} %broadcast_in_dim.87), calls=%async_computation.3 | async-start | bytes 1572864 | tf_op jit(solution)/shard_map/all_to_all | solution.py:41
  92.6 1.3 collective-permute-start.1
  93.9 27.9 %copy-start.2 = (bf16[1536,128]{1,0:T(8,128)(2,1)S(1)}, bf16[1536,128]{1,0:T(8,128)(2,1)}, u32[]{:S(2)}) copy-start(bf16[1536,128]{1,0:T(8,128)(2,1)} %copy-done.1) | copy-start | bytes 1179652
  93.9 27.9 %copy-start.5 = (f32[128,128]{1,0:T(8,128)S(1)}, f32[128,128]{1,0:T(8,128)}, u32[]{:S(2)}) copy-start(f32[128,128]{1,0:T(8,128)} %copy-done.4) | copy-start | bytes 196612
  106.7 2.2 %collective-permute-start.2 = (f32[48,128]{1,0:T(8,128)S(1)}, f32[48,128]{1,0:T(8,128)S(1)}, u32[]{:S(2)}, u32[]{:S(2)}) collective-permute-start(f32[48,128]{1,0:T(8,128)S(1)} %reduce_sum.70), channel_id=1, source_target_pairs={{0,16},{16,0},{1,17},{17,1},{2,18},{18,2},{3,19},{19,3},{4,20},{20... | collective-permute-start | bytes 73736 | tf_op jit(solution)/shard_map/ppermute | solution.py:106
  123.7 13.7 %all-to-all-start.6 = ((bf16[16,128,128]{1,2,0:T(8,128)(2,1)}), bf16[16,128,128]{1,2,0:T(8,128)(2,1)S(1)}, u32[]{:S(2)}, u32[]{:S(2)}) async-start(bf16[16,128,128]{1,2,0:T(8,128)(2,1)} %bitcast_convert_fusion.1), calls=%async_computation.6 | async-start | bytes 1048576 | tf_op jit(solution)/shard_map/all_to_all | solution.py:34
  137.5 12.7 %copy-start.7 = (bf16[1,2,128,2048]{3,2,1,0:T(8,128)(2,1)S(1)}, bf16[1,2,128,2048]{3,2,1,0:T(8,128)(2,1)}, u32[]{:S(2)}) copy-start(bf16[1,2,128,2048]{3,2,1,0:T(8,128)(2,1)} %param.8) | copy-start | bytes 3145732
  150.5 6.0 %collective-permute-start.3 = (f32[128,128]{1,0:T(8,128)S(1)}, f32[128,128]{1,0:T(8,128)S(1)}, u32[]{:S(2)}, u32[]{:S(2)}) collective-permute-start(f32[128,128]{1,0:T(8,128)S(1)} %fusion.14), channel_id=1, source_target_pairs={{16,0},{17,1},{18,2},{19,3},{20,4},{21,5},{22,6},{23,7},{24,8},{25... | collective-permute-start | bytes 196616 | tf_op jit(solution)/shard_map/ppermute | solution.py:115
  158.0 14.6 %all-to-all-start.8 = ((bf16[16,128,128]{1,2,0:T(8,128)(2,1)}), bf16[16,128,128]{1,2,0:T(8,128)(2,1)S(1)}, u32[]{:S(2)}, u32[]{:S(2)}) async-start(bf16[16,128,128]{1,2,0:T(8,128)(2,1)} %bitcast_convert_fusion), calls=%async_computation.8 | async-start | bytes 1048576 | tf_op jit(solution)/shard_map/all_to_all | solution.py:34

commit v6 on v5

--- a/solution.py
+++ b/solution.py
@@ -12,6 +12,8 @@
 f32 = jnp.float32
 bf16 = jnp.bfloat16
 fine = lax.Precision.HIGH
+along_x = [[4 * y + x for x in range(4)] for y in range(4)]
+along_y = [[4 * y + x for y in range(4)] for x in range(4)]
 first_axes = (((0,), (0,)), ((), ()))
 
 
@@ -25,6 +27,20 @@
 
 def after(value, other):
     return lax.optimization_barrier((value, other))[0]
+
+
+def send(value, step_y, step_x):
+    pairs = [
+        (COLS + 4 * y + x, COLS + 4 * ((y + step_y) % 4) + (x + step_x) % 4)
+        for y in range(4)
+        for x in range(4)
+    ]
+    return lax.ppermute(value, ("row", "col"), pairs)
+
+
+def twice(product, low, value):
+    high = lax.reduce_precision(value, 8, 7)
+    return product(low, high.astype(bf16)) + product(low, (value - high).astype(bf16))
 
 
 def sum_scatter(partial, axes, count):
@@ -58,7 +74,8 @@
     row_id = lax.axis_index("row")
     col_id = lax.axis_index("col")
     sources = right_side.shape[-1]
-    band_id = lax.axis_index(("sub", "row"))
+    col_y, col_x = col_id // 4, col_id % 4
+    band_id = lax.axis_index(("row", "sub"))
 
     blocks = lax.dynamic_slice(table, (PANEL // BLOCK, col_id // 2), (PANEL // BLOCK, 1))
     lower = factor_cols[0, 0] * jnp.repeat(blocks[:, 0], BLOCK)[None, :].astype(bf16)
@@ -88,32 +105,52 @@
     chips = lax.broadcasted_iota(jnp.int32, (COLS, 1, 1), 0)
     gram = jnp.where(chips == col_id, own_gram, both[:, width:, :band].astype(f32)).sum(0)
 
+    flipped = lax.optimization_barrier(after(inverse, partial).T)
+    flipped_own = lax.dynamic_slice_in_dim(flipped, col_id * width, width, 0)
     onehot = (jnp.arange(SEPARATOR)[:, None] == rows_sep[None, :]).astype(bf16)
     couple_sep = lax.dot_general(
         onehot, couple, (((1,), (1,)), ((), ())), preferred_element_type=f32
     ).astype(bf16)
 
-    updates = mul(couple_sep, solved.astype(bf16)).astype(bf16).reshape(2 * SUBS, band, sources)
-    updates = lax.all_to_all(updates, ("sub", "row"), 0, 0).astype(f32).sum(0)
+    swap = [(0, 1), (1, 0)]
+    updates = mul(couple_sep, solved.astype(bf16)).reshape(2, SUBS * band, sources)
+    sent = lax.dynamic_index_in_dim(updates, 1 - row_id, 0, False)
+    updates = lax.dynamic_index_in_dim(updates, row_id, 0, False)
+    updates = sum_scatter(updates + lax.ppermute(sent, "row", swap), "sub", SUBS)
     here = (band_id == col_id).astype(f32)
     rhs = gather(here * root_right - updates, "col", COLS).sum(0)
+    panels = [after(inverse, total).astype(bf16)]
+    panels = jnp.concatenate(panels + [send(panels[0], 0, -k) for k in (1, 2, 3)], 0)
+    rhs = after(rhs, panels)
+    lowers = [after(lower, updates)]
+    lowers = jnp.concatenate(lowers + [send(lowers[0], -k, 0) for k in (1, 2, 3)], 0)
     applied = mul(gram, rhs, precision=fine)
     half = share // 2
     kept = lax.dynamic_slice_in_dim(applied, row_id * half, half, 0)
     sent = lax.dynamic_slice_in_dim(applied, (1 - row_id) * half, half, 0)
-    swap = [(0, 1), (1, 0)]
     kept = gather(kept + lax.ppermute(sent, "row", swap), "sub", SUBS).sum(0)
     other = lax.ppermute(kept, "row", swap)
     root_part = jnp.where(
         row_id == 0, jnp.concatenate([kept, other], 0), jnp.concatenate([other, kept], 0)
     )
     root_full = gather(root_part.astype(bf16), "col", COLS).reshape(SEPARATOR, sources)
-    value = solved - mul_t(couple_sep, root_full)
+    value = solved - mul_t(couple_sep, after(root_full, lowers))
 
-    value = sum_scatter(mul_t(inverse, value, precision=fine), "col", COLS)
-    later_low = gather(value.astype(bf16), "col", COLS).reshape(PANEL, sources)
-    terms = lax.ppermute(mul(lower, later_low), "row", [(1, 0)])
-    value = value - sum_scatter(mul_t(inverse, terms, precision=fine), "col", COLS)
+    later = lax.all_to_all(
+        jnp.broadcast_to(value[None], (4,) + value.shape), "col", 0, 0, axis_index_groups=along_x
+    )
+    later = [lax.dynamic_index_in_dim(later, (col_x + k) % 4, 0, False) for k in range(4)]
+    later = twice(mul_t, panels, jnp.concatenate(later, 0))
+    terms = twice(mul, lowers, later).reshape(4, width, sources)
+    chips = lax.broadcasted_iota(jnp.int32, (4, 1, 1), 0)
+    terms = sum(jnp.where(chips == (col_y + k) % 4, terms[k], 0.0) for k in range(4))
+    taken = lax.all_to_all(terms, "col", 0, 0, axis_index_groups=along_y).sum(0)
+    value = value - lax.ppermute(taken, "row", [(1, 0)])
+
+    shares = mul(flipped, value, precision=fine).astype(bf16).reshape(COLS, width, sources)
+    shares = lax.all_to_all(shares, "col", 0, 0).astype(f32)
+    chips = lax.broadcasted_iota(jnp.int32, (COLS, 1, 1), 0)
+    value = jnp.where(chips == col_id, mul(flipped_own, value, precision=fine), shares).sum(0)
     return value[None], root_part
 
 

time: 174 us -> 182 us (1.046)
  blocking collectives: 37.4 us -> 7.92 us
  starting transfers between devices: 39.4 us -> 67 us
  waiting for transfers between devices: 78.8 us -> 60.1 us
  local copies, waits for them, and re-layouts: 5.77 us -> 18 us
  other arithmetic: 2.69 us -> 12.1 us
  matrix products: 8.41 us -> 14.2 us
    all_to_all x3 -> x1, blocking collectives: 37.4 us -> 7.92 us  [shards(): taken = lax.all_to_all(terms, 'col', 0, 0, axis_index_groups=along_y).sum(0)]
    all_to_all x2 -> x1, waiting for transfers between devices: 20.5 us -> 0.22 us  [sum_scatter(): others = lax.all_to_all(parts.astype(bf16), axes, 0, 0).astype(f32)]
    ppermute x1 -> x8, starting transfers between devices: 5.07 us -> 23.7 us  [the longest x6 15.3 us: send(): return lax.ppermute(value, ('row', 'col'), pairs)]
    all_to_all x1 -> x3, starting transfers between devices: 3.61 us -> 14.5 us  [gather(): return lax.all_to_all(spread, axes, 0, 0)]
    unnamed x29 -> x39, local copies, waits for them, and re-layouts: 2.44 us -> 11.1 us
    all_to_all x1 -> x2, starting transfers between devices: 11.2 us -> 7.16 us  [the longest x1 3.58 us: shards(): lax.all_to_all(jnp.broadcast_to(value[None], (4,) + value.shape), 'col',...]
    ppermute x1 -> x8, waiting for transfers between devices: 0.88 us -> 3.77 us  [the longest x1 1.69 us: shards(): lax.ppermute(sent, 'row', swap)]
    ppermute x1, starting transfers between devices: 0.47 us -> 3.01 us  [shards(): kept = gather(kept + lax.ppermute(sent, 'row', swap), 'sub', SUBS).sum(0)]
  transfers between devices with their start and end apart: 10 -> 19, of which waited for: 10 -> 13; matrix products, arithmetic and copies ran while one was open for 2% -> 12% of each run, Pallas kernels for 0% -> 0%
where the time goes in v6:
time: 182 us; the launch traced here: 180 us
  starting transfers between devices  67 us (37%)
  waiting for transfers between devices  60.1 us (33%)
  local copies, waits for them, and re-layouts  18 us (10%)
  matrix products  14.2 us (8%)
  other arithmetic  12.1 us (7%)
  blocking collectives  7.92 us (4%)
    all_to_all x3, waiting for transfers between devices, gather(): return lax.all_to_all(spread, axes, 0, 0)  15.9 us
    ppermute x6, starting transfers between devices, send(): return lax.ppermute(value, ('row', 'col'), pairs)  15.3 us
    all_to_all x3, starting transfers between devices, gather(): return lax.all_to_all(spread, axes, 0, 0)  14.5 us
    all_to_all x1, waiting for transfers between devices, shards(): both = lax.all_to_all(both, 'col', 0, 0)  11.7 us
    unnamed x39, local copies, waits for them, and re-layouts  11.1 us
    all_to_all x1, waiting for transfers between devices, shards(): shares = lax.all_to_all(shares, 'col', 0, 0).astype(f32)  10.7 us
    all_to_all x1, waiting for transfers between devices, shards(): total = lax.all_to_all(partial.reshape(COLS, width, sources), 'col', 0, 0)  8.91 us
    all_to_all x1, starting transfers between devices, sum_scatter(): others = lax.all_to_all(parts.astype(bf16), axes, 0, 0).astype(f32)  8.19 us
  transfers between devices with their start and end apart: 19, of which 13 were waited for; matrix products, arithmetic and copies ran while one was open for 12% of the time, Pallas kernels for 0%

profile of v6, /device:TPU:1, one launch (start us, length us, event | category | flops | bytes accessed | tf_op | source)
XLA Modules:
  0.0 180.4 jit_solution(12962565787665975477)
XLA Ops:
  0.7 1.2 copy-done
  1.9 1.9 %fusion.32 = (bf16[128,128]{1,0:T(8,128)(2,1)S(1)}, f32[128,128]{1,0:T(8,128)S(1)}) fusion(f32[1,2048,128]{2,1,0:T(8,128)S(1)} %copy-done, f32[1,128,2048]{2,1,0:T(8,128)} %param.10), kind=kOutput, calls=%fused_computation.73 | convolution fusion | flops 201342976 | bytes 2195456 | tf_op jit(solution)/shard_map/dot_general | solution.py:21
  3.7 1.3 collective-permute-start
  5.4 3.6 %collective-permute-done = bf16[128,128]{1,0:T(8,128)(2,1)S(1)} collective-permute-done((bf16[128,128]{1,0:T(8,128)(2,1)S(1)}, bf16[128,128]{1,0:T(8,128)(2,1)S(1)}, u32[]{:S(2)}, u32[]{:S(2)}) %collective-permute-start) | collective-permute-done | bytes 32800 | tf_op jit(solution)/shard_map/ppermute | solution.py:85
  8.9 1.1 convolution_convert_fusion.1
  10.1 5.5 %all-to-all-start = ((bf16[16,128,128]{2,1,0:T(8,128)(2,1)}), bf16[16,128,128]{2,1,0:T(8,128)(2,1)S(1)}, u32[]{:S(2)}, u32[]{:S(2)}) async-start(bf16[16,128,128]{2,1,0:T(8,128)(2,1)} %bitcast.4), calls=%async_computation | async-start | bytes 1048576 | tf_op jit(solution)/shard_map/all_to_all | solution.py:87
  15.6 1.9 %fusion.17 = f32[1536,96]{1,0:T(8,128)S(1)} fusion(f32[96,1536]{1,0:T(8,128)} %param.13, s32[]{:T(128)S(6)} %select_n.129), kind=kOutput, calls=%fused_computation.44 | convolution fusion | flops 84934656 | bytes 1228804 | tf_op jit(solution)/shard_map/reshape | solution.py:97
  17.6 8.9 %all-to-all-done = bf16[16,128,128]{2,1,0:T(8,128)(2,1)S(1)} async-done(((bf16[16,128,128]{2,1,0:T(8,128)(2,1)}), bf16[16,128,128]{2,1,0:T(8,128)(2,1)S(1)}, u32[]{:S(2)}, u32[]{:S(2)}) %all-to-all-start) | async-done | bytes 524320 | tf_op jit(solution)/shard_map/all_to_all | solution.py:87
  26.7 1.0 fusion.8
  27.7 3.6 %all-to-all-start.1 = ((bf16[16,224,128]{2,1,0:T(8,128)(2,1)}), bf16[16,224,128]{2,1,0:T(8,128)(2,1)S(1)}, u32[]{:S(2)}, u32[]{:S(2)}) async-start(bf16[16,224,128]{2,1,0:T(8,128)(2,1)} %fusion.8), calls=%async_computation.1 | async-start | bytes 1835008 | tf_op jit(solution)/shard_map/all_to_all | solution.py:102
  31.4 2.2 %fusion.2 = bf16[1536,128]{1,0:T(8,128)(2,1)S(1)} fusion(s32[1024]{0:T(1024)S(1)} %bitcast.76, bf16[1,1,128,1024]{3,2,1,0:T(8,128)(2,1)} %param.11), kind=kOutput, calls=%fused_computation.4 | convolution fusion | flops 404422656 | bytes 659456 | tf_op jit(solution)/shard_map/dot_general | solution.py:111
  33.6 11.7 %all-to-all-done.1 = bf16[16,224,128]{2,1,0:T(8,128)(2,1)S(1)} async-done(((bf16[16,224,128]{2,1,0:T(8,128)(2,1)}), bf16[16,224,128]{2,1,0:T(8,128)(2,1)S(1)}, u32[]{:S(2)}, u32[]{:S(2)}) %all-to-all-start.1) | async-done | bytes 917536 | tf_op jit(solution)/shard_map/all_to_all | solution.py:102
  46.1 0.9 copy-done.6
  47.0 0.8 dynamic-slice_bitcast_fusion
  47.8 2.8 %collective-permute-start.1 = (f32[768,128]{1,0:T(8,128)}, f32[768,128]{1,0:T(8,128)}, u32[]{:S(2)}, u32[]{:S(2)}) collective-permute-start(f32[768,128]{1,0:T(8,128)} %dynamic-slice_bitcast_fusion), channel_id=1, source_target_pairs={{0,16},{16,0},{1,17},{17,1},{2,18},{18,2},{3,19},{19,3},{4,20},{20... | collective-permute-start | bytes 1179656 | tf_op jit(solution)/shard_map/ppermute | solution.py:119
  50.5 1.7 collective-permute-done.1
  52.2 1.2 bitcast_add_fusion
  53.4 0.7 convert_element_type.86
  54.1 8.2 %all-to-all-start.2 = ((bf16[8,96,128]{2,1,0:T(8,128)(2,1)}), bf16[8,96,128]{2,1,0:T(8,128)(2,1)}, u32[]{:S(2)}, u32[]{:S(2)}) async-start(bf16[8,96,128]{2,1,0:T(8,128)(2,1)} %convert_element_type.86), calls=%async_computation.2 | async-start | bytes 393216 | tf_op jit(solution)/shard_map/all_to_all | solution.py:50
  62.3 0.9 convert_element_type.88
  63.1 2.1 %collective-permute-start.4 = (bf16[128,2048]{1,0:T(8,128)(2,1)}, bf16[128,2048]{1,0:T(8,128)(2,1)S(1)}, u32[]{:S(2)}, u32[]{:S(2)}) collective-permute-start(bf16[128,2048]{1,0:T(8,128)(2,1)} %convert_element_type.88), channel_id=1, source_target_pairs={{16,17},{17,18},{18,19},{19,16},{20,21},{21,22},{22,23},{23,20},{2... | collective-permute-start | bytes 1572872 | tf_op jit(solution)/shard_map/ppermute | solution.py:38
  65.3 3.0 %collective-permute-start.3 = (bf16[128,2048]{1,0:T(8,128)(2,1)}, bf16[128,2048]{1,0:T(8,128)(2,1)S(1)}, u32[]{:S(2)}, u32[]{:S(2)}) collective-permute-start(bf16[128,2048]{1,0:T(8,128)(2,1)} %convert_element_type.88), channel_id=1, source_target_pairs={{16,18},{17,19},{18,16},{19,17},{20,22},{21,23},{22,20},{23,21},{2... | collective-permute-start | bytes 1572872 | tf_op jit(solution)/shard_map/ppermute | solution.py:38
  68.3 3.3 %collective-permute-start.2 = (bf16[128,2048]{1,0:T(8,128)(2,1)}, bf16[128,2048]{1,0:T(8,128)(2,1)}, u32[]{:S(2)}, u32[]{:S(2)}) collective-permute-start(bf16[128,2048]{1,0:T(8,128)(2,1)} %convert_element_type.88), channel_id=1, source_target_pairs={{16,19},{17,16},{18,17},{19,18},{20,23},{21,20},{22,21},{23,22},{2... | collective-permute-start | bytes 1572872 | tf_op jit(solution)/shard_map/ppermute | solution.py:38
  71.8 1.0 select_reduce_fusion.2
  72.8 0.8 multiply_subtract_fusion
  73.7 1.0 broadcast_in_dim.137
  74.6 4.3 %all-to-all-start.3 = ((f32[16,96,128]{2,1,0:T(8,128)}), f32[16,96,128]{2,1,0:T(8,128)}, u32[]{:S(2)}, u32[]{:S(2)}) async-start(f32[16,96,128]{2,1,0:T(8,128)} %broadcast_in_dim.137), calls=%async_computation.3 | async-start | bytes 1572864 | tf_op jit(solution)/shard_map/all_to_all | solution.py:57
  78.9 0.8 dynamic-slice_bitcast_fusion.6
  80.1 0.8 copy-done.12
  80.9 0.8 copy-done.13
  81.7 1.0 collective-permute-done.2
  82.7 1.8 pad_maximum_fusion
  84.5 6.8 %all-to-all-done.3 = f32[16,96,128]{2,1,0:T(8,128)} async-done(((f32[16,96,128]{2,1,0:T(8,128)}), f32[16,96,128]{2,1,0:T(8,128)}, u32[]{:S(2)}, u32[]{:S(2)}) %all-to-all-start.3) | async-done | bytes 786464 | tf_op jit(solution)/shard_map/all_to_all | solution.py:57
  91.3 1.2 reduce_sum.69
  92.7 3.0 %collective-permute-start.5 = (f32[48,128]{1,0:T(8,128)S(1)}, f32[48,128]{1,0:T(8,128)S(1)}, u32[]{:S(2)}, u32[]{:S(2)}) collective-permute-start(f32[48,128]{1,0:T(8,128)S(1)} %constant_dynamic-slice_fusion), channel_id=1, source_target_pairs={{0,16},{16,0},{1,17},{17,1},{2,18},{18,2},{3,19},{19,3},{4,20},{20... | collective-permute-start | bytes 73736 | tf_op jit(solution)/shard_map/ppermute | solution.py:131
  95.7 2.5 %collective-permute-start.7 = (bf16[128,2048]{1,0:T(8,128)(2,1)}, bf16[128,2048]{1,0:T(8,128)(2,1)}, u32[]{:S(2)}, u32[]{:S(2)}) collective-permute-start(bf16[128,2048]{1,0:T(8,128)(2,1)} %copy-done.4), channel_id=1, source_target_pairs={{16,28},{17,29},{18,30},{19,31},{20,16},{21,17},{22,18},{23,19},{2... | collective-permute-start | bytes 1572872 | tf_op jit(solution)/shard_map/ppermute | solution.py:38
  98.9 5.1 %all-to-all-start.4 = ((f32[8,48,128]{2,1,0:T(8,128)}), f32[8,48,128]{2,1,0:T(8,128)S(1)}, u32[]{:S(2)}, u32[]{:S(2)}) async-start(f32[8,48,128]{2,1,0:T(8,128)} %broadcast_in_dim.138), calls=%async_computation.4 | async-start | bytes 393216 | tf_op jit(solution)/shard_map/all_to_all | solution.py:57
  104.0 1.9 %collective-permute-start.8 = (bf16[128,2048]{1,0:T(8,128)(2,1)}, bf16[128,2048]{1,0:T(8,128)(2,1)}, u32[]{:S(2)}, u32[]{:S(2)}) collective-permute-start(bf16[128,2048]{1,0:T(8,128)(2,1)} %copy-done.4), channel_id=1, source_target_pairs={{16,24},{17,25},{18,26},{19,27},{20,28},{21,29},{22,30},{23,31},{2... | collective-permute-start | bytes 1572872 | tf_op jit(solution)/shard_map/ppermute | solution.py:38
  105.9 2.5 %collective-permute-start.9 = (bf16[128,2048]{1,0:T(8,128)(2,1)}, bf16[128,2048]{1,0:T(8,128)(2,1)}, u32[]{:S(2)}, u32[]{:S(2)}) collective-permute-start(bf16[128,2048]{1,0:T(8,128)(2,1)} %copy-done.4), channel_id=1, source_target_pairs={{16,20},{17,21},{18,22},{19,23},{20,24},{21,25},{22,26},{23,27},{2... | collective-permute-start | bytes 1572872 | tf_op jit(solution)/shard_map/ppermute | solution.py:38
  108.4 1.9 %constant_dynamic-update-slice_fusion.3 = bf16[512,2048]{1,0:T(8,128)(2,1)} fusion(bf16[128,2048]{1,0:T(8,128)(2,1)} %copy-done.4), kind=kLoop, calls=%fused_computation.54 | loop fusion | bytes 1048576
  110.4 3.2 %all-to-all-done.4 = f32[8,48,128]{2,1,0:T(8,128)S(1)} async-done(((f32[8,48,128]{2,1,0:T(8,128)}), f32[8,48,128]{2,1,0:T(8,128)S(1)}, u32[]{:S(2)}, u32[]{:S(2)}) %all-to-all-start.4) | async-done | bytes 196640 | tf_op jit(solution)/shard_map/all_to_all | solution.py:57
  114.2 2.0 %constant_dynamic-update-slice_fusion.2 = bf16[512,2048]{1,0:T(8,128)(2,1)} fusion(bf16[512,2048]{1,0:T(8,128)(2,1)} %constant_dynamic-update-slice_fusion.3, bf16[128,2048]{1,0:T(8,128)(2,1)} %collective-permute-done.7), kind=kLoop, calls=%fused_computation.53 | loop fusion | bytes 1048576
  116.1 1.4 fusion.30
  117.6 0.8 broadcast_in_dim.139
  118.4 5.2 %all-to-all-start.5 = ((bf16[16,96,128]{2,1,0:T(8,128)(2,1)}), bf16[16,96,128]{2,1,0:T(8,128)(2,1)}, u32[]{:S(2)}, u32[]{:S(2)}) async-start(bf16[16,96,128]{2,1,0:T(8,128)(2,1)} %broadcast_in_dim.139), calls=%async_computation.5 | async-start | bytes 786432 | tf_op jit(solution)/shard_map/all_to_all | solution.py:57
  123.6 1.9 %constant_dynamic-update-slice_fusion.1 = bf16[512,2048]{1,0:T(8,128)(2,1)} fusion(bf16[512,2048]{1,0:T(8,128)(2,1)} %constant_dynamic-update-slice_fusion.2, bf16[128,2048]{1,0:T(8,128)(2,1)} %collective-permute-done.8), kind=kLoop, calls=%fused_computation.52 | loop fusion | bytes 1048576
  125.5 1.9 %constant_dynamic-update-slice_fusion = bf16[512,2048]{1,0:T(8,128)(2,1)} fusion(bf16[512,2048]{1,0:T(8,128)(2,1)} %constant_dynamic-update-slice_fusion.1, bf16[128,2048]{1,0:T(8,128)(2,1)} %collective-permute-done.9), kind=kLoop, calls=%fused_computation.51 | loop fusion | bytes 1048576 | tf_op jit(solution)/shard_map/concatenate | solution.py:126
  127.4 5.9 %all-to-all-done.5 = bf16[16,96,128]{2,1,0:T(8,128)(2,1)} async-done(((bf16[16,96,128]{2,1,0:T(8,128)(2,1)}), bf16[16,96,128]{2,1,0:T(8,128)(2,1)}, u32[]{:S(2)}, u32[]{:S(2)}) %all-to-all-start.5) | async-done | bytes 393248 | tf_op jit(solution)/shard_map/all_to_all | solution.py:57
  133.2 1.3 convolution_subtract_fusion
  135.2 0.7 broadcast_in_dim.141
  135.9 3.6 %all-to-all-start.6 = ((f32[4,128,128]{2,1,0:T(8,128)}), f32[4,128,128]{2,1,0:T(8,128)S(1)}, u32[]{:S(2)}, u32[]{:S(2)}) async-start(f32[4,128,128]{2,1,0:T(8,128)} %broadcast_in_dim.141), calls=%async_computation.6 | async-start | bytes 524288 | tf_op jit(solution)/shard_map/all_to_all | solution.py:139
  139.5 5.3 %all-to-all-done.6 = f32[4,128,128]{2,1,0:T(8,128)S(1)} async-done(((f32[4,128,128]{2,1,0:T(8,128)}), f32[4,128,128]{2,1,0:T(8,128)S(1)}, u32[]{:S(2)}, u32[]{:S(2)}) %all-to-all-start.6) | async-done | bytes 262176 | tf_op jit(solution)/shard_map/all_to_all | solution.py:139
  144.8 0.7 fusion.13
  145.6 0.7 convolution_add_fusion
  146.3 0.8 copy-done.3
  147.2 0.7 fusion.9
  147.9 0.7 convolution_add_fusion.1
  148.8 7.9 %all_to_all.45 = f32[4,128,128]{2,1,0:T(8,128)S(1)} all-to-all(f32[4,128,128]{2,1,0:T(8,128)S(1)} %select_add_fusion), channel_id=1, replica_groups={{0,4,8,12},{1,5,9,13},{2,6,10,14},{3,7,11,15},{16,20,24,28},{17,21,25,2..., dimensions={0} | all-to-all | bytes 524288 | tf_op jit(solution)/shard_map/all_to_all | solution.py:147
  156.7 5.7 %collective-permute-start.10 = (f32[128,128]{1,0:T(8,128)S(1)}, f32[128,128]{1,0:T(8,128)S(1)}, u32[]{:S(2)}, u32[]{:S(2)}) collective-permute-start(f32[128,128]{1,0:T(8,128)S(1)} %reduce_sum.71), channel_id=1, source_target_pairs={{16,0},{17,1},{18,2},{19,3},{20,4},{21,5},{22,6},{23,7},{24,8},{25... | collective-permute-start | bytes 196616 | tf_op jit(solution)/shard_map/ppermute | solution.py:148
  162.4 0.9 collective-permute-done.10
  163.3 1.8 convolution_convert_fusion
  165.1 3.6 %all-to-all-start.8 = ((bf16[16,128,128]{2,1,0:T(8,128)(2,1)}), bf16[16,128,128]{2,1,0:T(8,128)(2,1)S(1)}, u32[]{:S(2)}, u32[]{:S(2)}) async-start(bf16[16,128,128]{2,1,0:T(8,128)(2,1)} %bitcast.20), calls=%async_computation.8 | async-start | bytes 1048576 | tf_op jit(solution)/shard_map/all_to_all | solution.py:151
  168.9 10.7 %all-to-all-done.8 = bf16[16,128,128]{2,1,0:T(8,128)(2,1)S(1)} async-done(((bf16[16,128,128]{2,1,0:T(8,128)(2,1)}), bf16[16,128,128]{2,1,0:T(8,128)(2,1)S(1)}, u32[]{:S(2)}, u32[]{:S(2)}) %all-to-all-start.8) | async-done | bytes 524320 | tf_op jit(solution)/shard_map/all_to_all | solution.py:151
  179.6 0.8 select_reduce_fusion
  (64 shorter events, 4.5 us)
Async XLA Ops:
  0.6 1.2 copy-start
  0.6 4.4 %copy-start.15 = (s32[1,16,16]{2,1,0:T(8,128)S(1)}, s32[1,16,16]{2,1,0:T(8,128)}, u32[]{:S(2)}) copy-start(s32[1,16,16]{2,1,0:T(8,128)} %param.9) | copy-start | bytes 3076
  0.7 4.7 %copy-start.14 = (bf16[1,2,128,2048]{3,2,1,0:T(8,128)(2,1)S(1)}, bf16[1,2,128,2048]{3,2,1,0:T(8,128)(2,1)}, u32[]{:S(2)}) copy-start(bf16[1,2,128,2048]{3,2,1,0:T(8,128)(2,1)} %param.8) | copy-start | bytes 3145732
  3.7 5.2 %collective-permute-start = (bf16[128,128]{1,0:T(8,128)(2,1)S(1)}, bf16[128,128]{1,0:T(8,128)(2,1)S(1)}, u32[]{:S(2)}, u32[]{:S(2)}) collective-permute-start(bf16[128,128]{1,0:T(8,128)(2,1)S(1)} %get-tuple-element.24), channel_id=1, source_target_pairs={{0,16},{1,17},{2,18},{3,19},{4,20},{5,21},{6,22},{7,23},{8,24},{9,... | collective-permute-start | bytes 98312 | tf_op jit(solution)/shard_map/ppermute | solution.py:85
  5.4 12.2 %copy-start.4 = (bf16[128,2048]{1,0:T(8,128)(2,1)}, bf16[128,2048]{1,0:T(8,128)(2,1)S(1)}, u32[]{:S(2)}) copy-start(bf16[128,2048]{1,0:T(8,128)(2,1)S(1)} %bitcast_multiply_fusion) | copy-start | bytes 1572868
  10.1 16.4 %all-to-all-start = ((bf16[16,128,128]{2,1,0:T(8,128)(2,1)}), bf16[16,128,128]{2,1,0:T(8,128)(2,1)S(1)}, u32[]{:S(2)}, u32[]{:S(2)}) async-start(bf16[16,128,128]{2,1,0:T(8,128)(2,1)} %bitcast.4), calls=%async_computation | async-start | bytes 1048576 | tf_op jit(solution)/shard_map/all_to_all | solution.py:87
  17.5 10.2 %copy-start.5 = (f32[1536,96]{1,0:T(8,128)}, f32[1536,96]{1,0:T(8,128)S(1)}, u32[]{:S(2)}) copy-start(f32[1536,96]{1,0:T(8,128)S(1)} %fusion.17) | copy-start | bytes 1769476
  26.5 4.8 %copy-start.16 = (s32[1,1024]{1,0:T(1,128)S(1)}, s32[1,1024]{1,0:T(1,128)}, u32[]{:S(2)}) copy-start(s32[1,1024]{1,0:T(1,128)} %param.12) | copy-start | bytes 12292
  27.7 17.6 %all-to-all-start.1 = ((bf16[16,224,128]{2,1,0:T(8,128)(2,1)}), bf16[16,224,128]{2,1,0:T(8,128)(2,1)S(1)}, u32[]{:S(2)}, u32[]{:S(2)}) async-start(bf16[16,224,128]{2,1,0:T(8,128)(2,1)} %fusion.8), calls=%async_computation.1 | async-start | bytes 1835008 | tf_op jit(solution)/shard_map/all_to_all | solution.py:102
  31.3 14.0 %copy-start.1 = (f32[1,128,2048]{2,1,0:T(8,128)S(1)}, f32[1,128,2048]{2,1,0:T(8,128)}, u32[]{:S(2)}) copy-start(f32[1,128,2048]{2,1,0:T(8,128)} %param.10) | copy-start | bytes 3145732
  33.6 14.2 %copy-start.7 = (bf16[1536,128]{1,0:T(8,128)(2,1)}, bf16[1536,128]{1,0:T(8,128)(2,1)S(1)}, u32[]{:S(2)}) copy-start(bf16[1536,128]{1,0:T(8,128)(2,1)S(1)} %fusion.2) | copy-start | bytes 1179652
  45.8 8.3 %copy-start.11 = (f32[128,128]{1,0:T(8,128)}, f32[128,128]{1,0:T(8,128)S(1)}, u32[]{:S(2)}) copy-start(f32[128,128]{1,0:T(8,128)S(1)} %fusion.4) | copy-start | bytes 196612
  46.1 0.9 copy-start.6
  47.8 4.5 %collective-permute-start.1 = (f32[768,128]{1,0:T(8,128)}, f32[768,128]{1,0:T(8,128)}, u32[]{:S(2)}, u32[]{:S(2)}) collective-permute-start(f32[768,128]{1,0:T(8,128)} %dynamic-slice_bitcast_fusion), channel_id=1, source_target_pairs={{0,16},{16,0},{1,17},{17,1},{2,18},{18,2},{3,19},{19,3},{4,20},{20... | collective-permute-start | bytes 1179656 | tf_op jit(solution)/shard_map/ppermute | solution.py:119
  54.1 17.7 %all-to-all-start.2 = ((bf16[8,96,128]{2,1,0:T(8,128)(2,1)}), bf16[8,96,128]{2,1,0:T(8,128)(2,1)}, u32[]{:S(2)}, u32[]{:S(2)}) async-start(bf16[8,96,128]{2,1,0:T(8,128)(2,1)} %convert_element_type.86), calls=%async_computation.2 | async-start | bytes 393216 | tf_op jit(solution)/shard_map/all_to_all | solution.py:50
  63.1 17.0 %collective-permute-start.4 = (bf16[128,2048]{1,0:T(8,128)(2,1)}, bf16[128,2048]{1,0:T(8,128)(2,1)S(1)}, u32[]{:S(2)}, u32[]{:S(2)}) collective-permute-start(bf16[128,2048]{1,0:T(8,128)(2,1)} %convert_element_type.88), channel_id=1, source_target_pairs={{16,17},{17,18},{18,19},{19,16},{20,21},{21,22},{22,23},{23,20},{2... | collective-permute-start | bytes 1572872 | tf_op jit(solution)/shard_map/ppermute | solution.py:38
  65.3 14.8 %collective-permute-start.3 = (bf16[128,2048]{1,0:T(8,128)(2,1)}, bf16[128,2048]{1,0:T(8,128)(2,1)S(1)}, u32[]{:S(2)}, u32[]{:S(2)}) collective-permute-start(bf16[128,2048]{1,0:T(8,128)(2,1)} %convert_element_type.88), channel_id=1, source_target_pairs={{16,18},{17,19},{18,16},{19,17},{20,22},{21,23},{22,20},{23,21},{2... | collective-permute-start | bytes 1572872 | tf_op jit(solution)/shard_map/ppermute | solution.py:38
  68.3 14.5 %collective-permute-start.2 = (bf16[128,2048]{1,0:T(8,128)(2,1)}, bf16[128,2048]{1,0:T(8,128)(2,1)}, u32[]{:S(2)}, u32[]{:S(2)}) collective-permute-start(bf16[128,2048]{1,0:T(8,128)(2,1)} %convert_element_type.88), channel_id=1, source_target_pairs={{16,19},{17,16},{18,17},{19,18},{20,23},{21,20},{22,21},{23,22},{2... | collective-permute-start | bytes 1572872 | tf_op jit(solution)/shard_map/ppermute | solution.py:38
  74.6 16.7 %all-to-all-start.3 = ((f32[16,96,128]{2,1,0:T(8,128)}), f32[16,96,128]{2,1,0:T(8,128)}, u32[]{:S(2)}, u32[]{:S(2)}) async-start(f32[16,96,128]{2,1,0:T(8,128)} %broadcast_in_dim.137), calls=%async_computation.3 | async-start | bytes 1572864 | tf_op jit(solution)/shard_map/all_to_all | solution.py:57
  80.1 0.8 copy-start.12
  80.9 0.8 copy-start.13
  92.7 5.5 %collective-permute-start.5 = (f32[48,128]{1,0:T(8,128)S(1)}, f32[48,128]{1,0:T(8,128)S(1)}, u32[]{:S(2)}, u32[]{:S(2)}) collective-permute-start(f32[48,128]{1,0:T(8,128)S(1)} %constant_dynamic-slice_fusion), channel_id=1, source_target_pairs={{0,16},{16,0},{1,17},{17,1},{2,18},{18,2},{3,19},{19,3},{4,20},{20... | collective-permute-start | bytes 73736 | tf_op jit(solution)/shard_map/ppermute | solution.py:131
  95.7 18.5 %collective-permute-start.7 = (bf16[128,2048]{1,0:T(8,128)(2,1)}, bf16[128,2048]{1,0:T(8,128)(2,1)}, u32[]{:S(2)}, u32[]{:S(2)}) collective-permute-start(bf16[128,2048]{1,0:T(8,128)(2,1)} %copy-done.4), channel_id=1, source_target_pairs={{16,28},{17,29},{18,30},{19,31},{20,16},{21,17},{22,18},{23,19},{2... | collective-permute-start | bytes 1572872 | tf_op jit(solution)/shard_map/ppermute | solution.py:38
  98.9 14.6 %all-to-all-start.4 = ((f32[8,48,128]{2,1,0:T(8,128)}), f32[8,48,128]{2,1,0:T(8,128)S(1)}, u32[]{:S(2)}, u32[]{:S(2)}) async-start(f32[8,48,128]{2,1,0:T(8,128)} %broadcast_in_dim.138), calls=%async_computation.4 | async-start | bytes 393216 | tf_op jit(solution)/shard_map/all_to_all | solution.py:57
  104.0 19.6 %collective-permute-start.8 = (bf16[128,2048]{1,0:T(8,128)(2,1)}, bf16[128,2048]{1,0:T(8,128)(2,1)}, u32[]{:S(2)}, u32[]{:S(2)}) collective-permute-start(bf16[128,2048]{1,0:T(8,128)(2,1)} %copy-done.4), channel_id=1, source_target_pairs={{16,24},{17,25},{18,26},{19,27},{20,28},{21,29},{22,30},{23,31},{2... | collective-permute-start | bytes 1572872 | tf_op jit(solution)/shard_map/ppermute | solution.py:38
  105.9 19.6 %collective-permute-start.9 = (bf16[128,2048]{1,0:T(8,128)(2,1)}, bf16[128,2048]{1,0:T(8,128)(2,1)}, u32[]{:S(2)}, u32[]{:S(2)}) collective-permute-start(bf16[128,2048]{1,0:T(8,128)(2,1)} %copy-done.4), channel_id=1, source_target_pairs={{16,20},{17,21},{18,22},{19,23},{20,24},{21,25},{22,26},{23,27},{2... | collective-permute-start | bytes 1572872 | tf_op jit(solution)/shard_map/ppermute | solution.py:38
  114.2 19.1 %copy-start.8 = (bf16[1536,128]{1,0:T(8,128)(2,1)S(1)}, bf16[1536,128]{1,0:T(8,128)(2,1)}, u32[]{:S(2)}) copy-start(bf16[1536,128]{1,0:T(8,128)(2,1)} %copy-done.7) | copy-start | bytes 1179652
  114.2 2.0 %collective-permute-start.6 = (f32[48,128]{1,0:T(8,128)}, f32[48,128]{1,0:T(8,128)S(1)}, u32[]{:S(2)}, u32[]{:S(2)}) collective-permute-start(f32[48,128]{1,0:T(8,128)} %reduce_sum.70), channel_id=1, source_target_pairs={{0,16},{16,0},{1,17},{17,1},{2,18},{18,2},{3,19},{19,3},{4,20},{20... | collective-permute-start | bytes 73736 | tf_op jit(solution)/shard_map/ppermute | solution.py:132
  118.4 14.8 %all-to-all-start.5 = ((bf16[16,96,128]{2,1,0:T(8,128)(2,1)}), bf16[16,96,128]{2,1,0:T(8,128)(2,1)}, u32[]{:S(2)}, u32[]{:S(2)}) async-start(bf16[16,96,128]{2,1,0:T(8,128)(2,1)} %broadcast_in_dim.139), calls=%async_computation.5 | async-start | bytes 786432 | tf_op jit(solution)/shard_map/all_to_all | solution.py:57
  134.5 0.6 copy-start.9
  135.9 8.9 %all-to-all-start.6 = ((f32[4,128,128]{2,1,0:T(8,128)}), f32[4,128,128]{2,1,0:T(8,128)S(1)}, u32[]{:S(2)}, u32[]{:S(2)}) async-start(f32[4,128,128]{2,1,0:T(8,128)} %broadcast_in_dim.141), calls=%async_computation.6 | async-start | bytes 524288 | tf_op jit(solution)/shard_map/all_to_all | solution.py:139
  145.6 1.6 copy-start.3
  147.9 15.4 %copy-start.2 = (f32[1,128,2048]{2,1,0:T(8,128)S(1)}, f32[1,128,2048]{2,1,0:T(8,128)}, u32[]{:S(2)}) copy-start(f32[1,128,2048]{2,1,0:T(8,128)} %param.10) | copy-start | bytes 3145732
  147.9 15.4 %copy-start.10 = (f32[128,128]{1,0:T(8,128)S(1)}, f32[128,128]{1,0:T(8,128)}, u32[]{:S(2)}) copy-start(f32[128,128]{1,0:T(8,128)} %copy-done.9) | copy-start | bytes 196612
  156.7 6.5 %collective-permute-start.10 = (f32[128,128]{1,0:T(8,128)S(1)}, f32[128,128]{1,0:T(8,128)S(1)}, u32[]{:S(2)}, u32[]{:S(2)}) collective-permute-start(f32[128,128]{1,0:T(8,128)S(1)} %reduce_sum.71), channel_id=1, source_target_pairs={{16,0},{17,1},{18,2},{19,3},{20,4},{21,5},{22,6},{23,7},{24,8},{25... | collective-permute-start | bytes 196616 | tf_op jit(solution)/shard_map/ppermute | solution.py:148
  165.1 14.6 %all-to-all-start.8 = ((bf16[16,128,128]{2,1,0:T(8,128)(2,1)}), bf16[16,128,128]{2,1,0:T(8,128)(2,1)S(1)}, u32[]{:S(2)}, u32[]{:S(2)}) async-start(bf16[16,128,128]{2,1,0:T(8,128)(2,1)} %bitcast.20), calls=%async_computation.8 | async-start | bytes 1048576 | tf_op jit(solution)/shard_map/all_to_all | solution.py:151

commit v7 on v1

v7 whole, which is shorter than its diff:
```python
import jax
import jax.numpy as jnp
from jax import lax
from jax.sharding import PartitionSpec as P

BLOCK = 256
PANEL = 2048
SEPARATOR = 1536
COLS = 16
SUBS = 8

f32 = jnp.float32
bf16 = jnp.bfloat16
fine = lax.Precision.HIGH
first_axes = (((0,), (0,)), ((), ()))


def mul(left, right, **kw):
    return jnp.dot(left, right, preferred_element_type=f32, **kw)


def mul_t(left, right, **kw):
    return lax.dot_general(left, right, first_axes, preferred_element_type=f32, **kw)


def after(value, other):
    return lax.optimization_barrier((value, other))[0]


def sum_scatter(partial, axes, count):
    parts = partial.reshape(count, -1, partial.shape[-1])
    return lax.all_to_all(parts, axes, 0, 0).astype(f32).sum(0)


def gather(chunk, axes, count):
    spread = jnp.broadcast_to(chunk[None], (count,) + chunk.shape)
    return lax.all_to_all(spread, axes, 0, 0)


def shards(
    factor_cols,
    block_pattern,
    diag_inverse,
    coupling_cols,
    separator_rows,
    root_inverse,
    right_side,
    root_right,
):
    table = block_pattern[0]
    inverse = diag_inverse[0]
    couple = coupling_cols[0, 0]
    rows_sep = separator_rows[0]
    row_id = lax.axis_index("row")
    col_id = lax.axis_index("col")
    sources = right_side.shape[-1]
    factor = factor_cols[0, 0]
    width = factor.shape[0]
    half = PANEL // 2
    swap = [(0, 1), (1, 0)]
    up, down = [(0, 1)], [(1, 0)]
    on_first = row_id == 0

    count = half // BLOCK
    blocks = lax.dynamic_slice(
        table, (PANEL // BLOCK + row_id * count, col_id // 2), (count, 1)
    )
    lower = jnp.where(on_first, lax.ppermute(factor[:, :half], "row", down), factor[:, half:])
    lower = lower * jnp.repeat(blocks[:, 0], BLOCK)[None, :].astype(bf16)

    own = mul(inverse, right_side[0], precision=fine)
    low = own.astype(bf16)
    low = jnp.where(on_first, low, lax.ppermute(low, "row", up))
    partial = mul_t(lower, low).astype(bf16)
    total = sum_scatter(partial, "col", COLS).astype(bf16)

    flipped = lax.optimization_barrier(after(inverse, partial).T)
    flipped_own = lax.dynamic_slice_in_dim(flipped, col_id * width, width, 0)
    flipped_half = jnp.where(
        on_first, lax.ppermute(flipped[:half], "row", down), flipped[half:]
    )
    onehot = (jnp.arange(SEPARATOR)[:, None] == after(rows_sep, partial)[None, :]).astype(bf16)
    couple_sep = lax.dot_general(
        onehot, couple, (((1,), (1,)), ((), ())), preferred_element_type=f32
    ).astype(bf16)
    rows = SEPARATOR // (2 * COLS)
    pairs = [
        (core * COLS + chip, (chip // 8) * COLS + 2 * (chip % 8) + core)
        for core in range(2)
        for chip in range(COLS)
    ]
    root_rows = lax.dynamic_slice_in_dim(after(root_right, partial), row_id * rows, rows, 0)
    root_rows = lax.ppermute(root_rows, ("row", "col"), pairs)
    sep_half = SEPARATOR // 2
    root_half = lax.dynamic_slice_in_dim(after(root_inverse, partial), row_id * sep_half, sep_half, 1)

    total = gather(total, "col", COLS).reshape(half, sources).astype(f32)
    terms = mul_t(flipped_half, total, precision=fine)
    solved = own - jnp.where(on_first, 0.0, terms) - lax.ppermute(terms, "row", up)

    updates = sum_scatter(
        mul(couple_sep, solved.astype(bf16)).astype(bf16), ("row", "col"), COLS * 2
    )
    updates = gather(updates, "sub", SUBS).sum(0)
    rhs = gather(root_rows - updates, "col", COLS).reshape(sep_half, sources)
    inner = mul(root_half, rhs, precision=fine)
    inner = inner + lax.ppermute(inner, "row", swap)
    root_rows = sum_scatter(mul_t(root_half, inner, precision=fine), "col", COLS)
    root_low = gather(root_rows.astype(bf16), "col", COLS).reshape(sep_half, sources)
    other_low = lax.ppermute(root_low, "row", swap)
    mine = lax.dynamic_slice_in_dim(couple_sep, row_id * sep_half, sep_half, 0)
    others = lax.dynamic_slice_in_dim(couple_sep, (1 - row_id) * sep_half, sep_half, 0)
    value = solved - mul_t(mine, root_low) - mul_t(others, other_low)

    later = jnp.where(on_first, lax.ppermute(value, "row", down), value)
    later = sum_scatter(mul(flipped_half, later, precision=fine), "col", COLS).astype(bf16)
    later = gather(later, "col", COLS).reshape(half, sources)
    terms = mul(lower, later)
    value = value - jnp.where(on_first, terms, 0.0) - lax.ppermute(terms, "row", down)

    shares = mul(flipped, value, precision=fine).astype(bf16).reshape(COLS, width, sources)
    shares = lax.all_to_all(shares, "col", 0, 0).astype(f32)
    chips = lax.broadcasted_iota(jnp.int32, (COLS, 1, 1), 0)
    value = jnp.where(chips == col_id, mul(flipped_own, value, precision=fine), shares).sum(0)

    root_rows = lax.ppermute(root_rows, ("row", "col"), [(j, i) for i, j in pairs])
    theirs = lax.ppermute(root_rows, "row", swap)
    root_part = jnp.where(
        on_first,
        jnp.concatenate([root_rows, theirs], 0),
        jnp.concatenate([theirs, root_rows], 0),
    )
    return value[None], root_part


def solution(mesh):
    return jax.shard_map(
        shards,
        mesh=mesh,
        in_specs=(
            P("sub", None, "col", "row"),
            P("sub", None, None),
            P("sub", ("row", "col"), None),
            P("sub", "row", "col", None),
            P("sub", None),
            P("col", None),
            P("sub", "row", None),
            P("col", None),
        ),
        out_specs=(P("sub", ("row", "col"), None), P("col", None)),
        check_vma=False,
    )
```

time: 189 us -> 177 us (0.937)
  blocking collectives: 134 us -> 73.8 us
  starting transfers between devices: 19.3 us -> 52.4 us
  waiting for transfers between devices: 21.9 us -> 31.9 us
  matrix products: 6.8 us -> 9.59 us
  other arithmetic: 0.54 us -> 2.54 us
    all_to_all x5 -> x4, blocking collectives: 90.2 us -> 52.9 us  [sum_scatter(): return lax.all_to_all(parts, axes, 0, 0).astype(f32).sum(0)]
    ppermute x2 -> x11, starting transfers between devices: 7.5 us -> 32 us  [the longest x1 5.44 us: shards(): lax.ppermute(terms, 'row', down)]
    all_to_all x3 -> x2, blocking collectives: 44.2 us -> 21 us  [gather(): return lax.all_to_all(spread, axes, 0, 0)]
    ppermute x2 -> x11, waiting for transfers between devices: 4.5 us -> 10.4 us  [the longest x1 3.66 us: shards(): lax.ppermute(root_rows, ('row', 'col'), [(j, i) for i, j in pairs])]
    all_to_all x2 -> x3, starting transfers between devices: 11.8 us -> 16.9 us  [gather(): return lax.all_to_all(spread, axes, 0, 0)]
    all_to_all x2 -> x3, waiting for transfers between devices: 17.4 us -> 21.5 us  [gather(): return lax.all_to_all(spread, axes, 0, 0)]
    all_to_all x0 -> x1, starting transfers between devices: none -> 3.57 us  [shards(): shares = lax.all_to_all(shares, 'col', 0, 0).astype(f32)]
    dot_general x6 -> x7, matrix products: 4.5 us -> 4.96 us  [mul(): return jnp.dot(left, right, preferred_element_type=f32, **kw)]
  transfers between devices with their start and end apart: 4 -> 15, of which waited for: 4 -> 11; matrix products, arithmetic and copies ran while one was open for 1% -> 3% of each run, Pallas kernels for 0% -> 0%
where the time goes in v7:
time: 177 us; the launch traced here: 175 us
  blocking collectives  73.8 us (42%)
  starting transfers between devices  52.4 us (30%)
  waiting for transfers between devices  31.9 us (18%)
  matrix products  9.59 us (5%)
  local copies, waits for them, and re-layouts  4.11 us (2%)
  other arithmetic  2.54 us (1%)
    all_to_all x4, blocking collectives, sum_scatter(): return lax.all_to_all(parts, axes, 0, 0).astype(f32).sum(0)  52.9 us
    all_to_all x3, waiting for transfers between devices, gather(): return lax.all_to_all(spread, axes, 0, 0)  21.5 us
    all_to_all x2, blocking collectives, gather(): return lax.all_to_all(spread, axes, 0, 0)  21 us
    all_to_all x3, starting transfers between devices, gather(): return lax.all_to_all(spread, axes, 0, 0)  16.9 us
    ppermute x1, starting transfers between devices, shards(): lax.ppermute(terms, 'row', down)  5.44 us
    ppermute x1, starting transfers between devices, shards(): lax.ppermute(root_rows, ('row', 'col'), [(j, i) for i, j in pairs])  5.21 us
    ppermute x1, starting transfers between devices, shards(): lax.ppermute(factor[:, :half], 'row', down)  5.16 us
    dot_general x7, matrix products, mul(): return jnp.dot(left, right, preferred_element_type=f32, **kw)  4.96 us
  transfers between devices with their start and end apart: 15, of which 11 were waited for; matrix products, arithmetic and copies ran while one was open for 3% of the time, Pallas kernels for 0%

profile of v7, /device:TPU:1, one launch (start us, length us, event | category | flops | bytes accessed | tf_op | source)
XLA Modules:
  0.0 175.4 jit_solution(4417529281668982293)
XLA Ops:
  0.6 0.0 copy-start
  0.6 0.0 copy-start.1
  0.7 1.2 slice_bitcast_fusion
  1.9 5.2 %collective-permute-start = (bf16[128,1024]{1,0:T(8,128)(2,1)S(1)}, bf16[128,1024]{1,0:T(8,128)(2,1)S(1)}, u32[]{:S(2)}, u32[]{:S(2)}) collective-permute-start(bf16[128,1024]{1,0:T(8,128)(2,1)S(1)} %slice.20), channel_id=1, source_target_pairs={{16,0},{17,1},{18,2},{19,3},{20,4},{21,5},{22,6},{23,7},{24,8},{25... | collective-permute-start | bytes 786440 | tf_op jit(solution)/shard_map/ppermute | solution.py:68
  7.1 0.6 fusion.35
  7.7 1.3 collective-permute-start.1
  9.1 0.9 fusion.33
  9.9 0.1 broadcast_bitcast_fusion
  10.0 0.8 collective-permute-done.1
  10.8 0.0 collective-permute-done
  10.9 0.3 convolution_convert_fusion.2
  11.1 0.4 copy-done.6
  11.6 2.2 %collective-permute-start.2 = (f32[1024,128]{0,1:T(8,128)S(1)}, f32[1024,128]{0,1:T(8,128)S(1)}, u32[]{:S(2)}, u32[]{:S(2)}) collective-permute-start(f32[1024,128]{0,1:T(8,128)S(1)} %slice.22), channel_id=1, source_target_pairs={{16,0},{17,1},{18,2},{19,3},{20,4},{21,5},{22,6},{23,7},{24,8},{25... | collective-permute-start | bytes 1572872 | tf_op jit(solution)/shard_map/ppermute | solution.py:80
  13.9 14.0 %all_to_all.50 = bf16[16,64,128]{2,1,0:T(8,128)(2,1)S(1)} all-to-all(bf16[16,64,128]{2,1,0:T(8,128)(2,1)S(1)} %bitcast.51), channel_id=1, replica_groups=mesh['sub'=8,'row'=2,'col'=16] {'col'}, dimensions={0} | all-to-all | bytes 524288 | tf_op jit(solution)/shard_map/all_to_all | solution.py:32
  27.9 0.0 copy-start.7
  27.9 0.7 broadcast_in_dim.35
  28.7 3.5 %all-to-all-start.1 = ((bf16[16,64,128]{2,1,0:T(8,128)(2,1)}), bf16[16,64,128]{2,1,0:T(8,128)(2,1)S(1)}, u32[]{:S(2)}, u32[]{:S(2)}) async-start(bf16[16,64,128]{2,1,0:T(8,128)(2,1)} %broadcast_in_dim.35), calls=%async_computation.1 | async-start | bytes 524288 | tf_op jit(solution)/shard_map/all_to_all | solution.py:37
  32.2 8.3 %all-to-all-done.1 = bf16[16,64,128]{2,1,0:T(8,128)(2,1)S(1)} async-done(((bf16[16,64,128]{2,1,0:T(8,128)(2,1)}), bf16[16,64,128]{2,1,0:T(8,128)(2,1)S(1)}, u32[]{:S(2)}, u32[]{:S(2)}) %all-to-all-start.1) | async-done | bytes 262176 | tf_op jit(solution)/shard_map/all_to_all | solution.py:37
  40.5 0.0 collective-permute-done.2
  40.5 0.3 fusion.13
  40.8 1.3 collective-permute-start.3
  42.1 1.2 fusion.2
  43.3 0.9 collective-permute-done.3
  44.1 0.2 convolution_convert_fusion.1
  44.4 0.0 copy-start.4
  44.4 13.1 %all_to_all.51 = bf16[32,48,128]{2,1,0:T(8,128)(2,1)S(1)} all-to-all(bf16[32,48,128]{2,1,0:T(8,128)(2,1)S(1)} %bitcast.47), channel_id=1, replica_groups=mesh['sub'=8,'row'=2,'col'=16] {'row','col'}, dimensions={0} | all-to-all | bytes 786432 | tf_op jit(solution)/shard_map/all_to_all | solution.py:32
  57.5 0.1 convert_reduce_fusion
  57.6 0.7 broadcast_in_dim.60
  58.3 8.2 %all-to-all-start.3 = ((f32[8,48,128]{2,1,0:T(8,128)}), f32[8,48,128]{2,1,0:T(8,128)S(1)}, u32[]{:S(2)}, u32[]{:S(2)}) async-start(f32[8,48,128]{2,1,0:T(8,128)} %broadcast_in_dim.60), calls=%async_computation.3 | async-start | bytes 393216 | tf_op jit(solution)/shard_map/all_to_all | solution.py:37
  66.5 3.4 %collective-permute-start.4 = (f32[48,128]{1,0:T(8,128)S(1)}, f32[48,128]{1,0:T(8,128)S(1)}, u32[]{:S(2)}, u32[]{:S(2)}) collective-permute-start(f32[48,128]{1,0:T(8,128)S(1)} %constant_dynamic-slice_fusion), channel_id=1, source_target_pairs={{0,0},{1,2},{2,4},{3,6},{4,8},{5,10},{6,12},{7,14},{8,16},{9,18},{... | collective-permute-start | bytes 73736 | tf_op jit(solution)/shard_map/ppermute | solution.py:93
  69.9 5.0 %all-to-all-done.3 = f32[8,48,128]{2,1,0:T(8,128)S(1)} async-done(((f32[8,48,128]{2,1,0:T(8,128)}), f32[8,48,128]{2,1,0:T(8,128)S(1)}, u32[]{:S(2)}, u32[]{:S(2)}) %all-to-all-start.3) | async-done | bytes 196640 | tf_op jit(solution)/shard_map/all_to_all | solution.py:37
  75.0 0.0 collective-permute-done.4
  75.0 0.8 broadcast_in_dim.61
  75.8 5.2 %all-to-all-start.4 = ((f32[16,48,128]{2,1,0:T(8,128)}), f32[16,48,128]{2,1,0:T(8,128)S(1)}, u32[]{:S(2)}, u32[]{:S(2)}) async-start(f32[16,48,128]{2,1,0:T(8,128)} %broadcast_in_dim.61), calls=%async_computation.4 | async-start | bytes 786432 | tf_op jit(solution)/shard_map/all_to_all | solution.py:37
  80.9 8.2 %all-to-all-done.4 = f32[16,48,128]{2,1,0:T(8,128)S(1)} async-done(((f32[16,48,128]{2,1,0:T(8,128)}), f32[16,48,128]{2,1,0:T(8,128)S(1)}, u32[]{:S(2)}, u32[]{:S(2)}) %all-to-all-start.4) | async-done | bytes 393248 | tf_op jit(solution)/shard_map/all_to_all | solution.py:37
  89.2 1.2 fusion.8
  90.4 3.1 %collective-permute-start.5 = (f32[96,128]{1,0:T(8,128)S(1)}, f32[96,128]{1,0:T(8,128)S(1)}, u32[]{:S(2)}, u32[]{:S(2)}) collective-permute-start(f32[96,128]{1,0:T(8,128)S(1)} %fusion.8), channel_id=1, source_target_pairs={{0,16},{16,0},{1,17},{17,1},{2,18},{18,2},{3,19},{19,3},{4,20},{20... | collective-permute-start | bytes 147464 | tf_op jit(solution)/shard_map/ppermute | solution.py:107
  93.5 0.9 collective-permute-done.5
  94.4 1.5 fusion.6
  95.8 12.2 %all_to_all.52 = f32[16,48,128]{2,1,0:T(8,128)S(1)} all-to-all(f32[16,48,128]{2,1,0:T(8,128)S(1)} %bitcast.46), channel_id=1, replica_groups=mesh['sub'=8,'row'=2,'col'=16] {'col'}, dimensions={0} | all-to-all | bytes 786432 | tf_op jit(solution)/shard_map/all_to_all | solution.py:32
  108.1 10.2 %all_to_all.53 = bf16[16,48,128]{2,1,0:T(8,128)(2,1)S(1)} all-to-all(bf16[16,48,128]{2,1,0:T(8,128)(2,1)S(1)} %broadcast_in_dim.62), channel_id=1, replica_groups=mesh['sub'=8,'row'=2,'col'=16] {'col'}, dimensions={0} | all-to-all | bytes 393216 | tf_op jit(solution)/shard_map/all_to_all | solution.py:37
  118.2 2.6 %collective-permute-start.6 = (bf16[768,128]{1,0:T(8,128)(2,1)S(1)}, bf16[768,128]{1,0:T(8,128)(2,1)}, u32[]{:S(2)}, u32[]{:S(2)}) collective-permute-start(bf16[768,128]{1,0:T(8,128)(2,1)S(1)} %bitcast.49), channel_id=1, source_target_pairs={{0,16},{16,0},{1,17},{17,1},{2,18},{18,2},{3,19},{19,3},{4,20},{20... | collective-permute-start | bytes 589832 | tf_op jit(solution)/shard_map/ppermute | solution.py:110
  120.8 1.2 collective-permute-done.6
  122.0 1.2 fusion.14
  123.2 0.3 fusion.3
  123.5 2.3 %collective-permute-start.7 = (f32[128,128]{1,0:T(8,128)S(1)}, f32[128,128]{1,0:T(8,128)S(1)}, u32[]{:S(2)}, u32[]{:S(2)}) collective-permute-start(f32[128,128]{1,0:T(8,128)S(1)} %fusion.3), channel_id=1, source_target_pairs={{16,0},{17,1},{18,2},{19,3},{20,4},{21,5},{22,6},{23,7},{24,8},{25... | collective-permute-start | bytes 196616 | tf_op jit(solution)/shard_map/ppermute | solution.py:115
  125.8 0.9 collective-permute-done.7
  126.6 0.6 fusion.12
  127.2 13.6 %all_to_all.54 = f32[16,64,128]{2,1,0:T(8,128)S(1)} all-to-all(f32[16,64,128]{2,1,0:T(8,128)S(1)} %bitcast.44), channel_id=1, replica_groups=mesh['sub'=8,'row'=2,'col'=16] {'col'}, dimensions={0} | all-to-all | bytes 1048576 | tf_op jit(solution)/shard_map/all_to_all | solution.py:32
  140.9 10.8 %all_to_all.55 = bf16[16,64,128]{2,1,0:T(8,128)(2,1)S(1)} all-to-all(bf16[16,64,128]{2,1,0:T(8,128)(2,1)S(1)} %broadcast_in_dim.63), channel_id=1, replica_groups=mesh['sub'=8,'row'=2,'col'=16] {'col'}, dimensions={0} | all-to-all | bytes 524288 | tf_op jit(solution)/shard_map/all_to_all | solution.py:37
  151.7 0.0 copy-done.3
  151.7 0.2 fusion.21
  151.9 5.4 %collective-permute-start.8 = (f32[128,128]{1,0:T(8,128)S(1)}, f32[128,128]{1,0:T(8,128)S(1)}, u32[]{:S(2)}, u32[]{:S(2)}) collective-permute-start(f32[128,128]{1,0:T(8,128)S(1)} %fusion.21), channel_id=1, source_target_pairs={{16,0},{17,1},{18,2},{19,3},{20,4},{21,5},{22,6},{23,7},{24,8},{25... | collective-permute-start | bytes 196616 | tf_op jit(solution)/shard_map/ppermute | solution.py:119
  157.4 0.9 collective-permute-done.8
  158.3 1.8 %convolution_convert_fusion = bf16[2048,128]{1,0:T(8,128)(2,1)} fusion(f32[2048,128]{0,1:T(8,128)S(1)} %bitcast.42, f32[128,128]{1,0:T(8,128)S(1)} %subtract_subtract_fusion), kind=kOutput, calls=%fused_computation.4 | convolution fusion | flops 201588736 | bytes 1638400 | tf_op jit(solution)/shard_map/dot_general | solution.py:19
  160.1 3.6 %all-to-all-start.9 = ((bf16[16,128,128]{2,1,0:T(8,128)(2,1)}), bf16[16,128,128]{2,1,0:T(8,128)(2,1)S(1)}, u32[]{:S(2)}, u32[]{:S(2)}) async-start(bf16[16,128,128]{2,1,0:T(8,128)(2,1)} %bitcast.14), calls=%async_computation.9 | async-start | bytes 1048576 | tf_op jit(solution)/shard_map/all_to_all | solution.py:122
  163.7 5.2 %collective-permute-start.9 = (f32[48,128]{1,0:T(8,128)S(1)}, f32[48,128]{1,0:T(8,128)S(1)}, u32[]{:S(2)}, u32[]{:S(2)}) collective-permute-start(f32[48,128]{1,0:T(8,128)S(1)} %reduce_sum.60), channel_id=1, source_target_pairs={{0,0},{2,1},{4,2},{6,3},{8,4},{10,5},{12,6},{14,7},{16,8},{18,9},{... | collective-permute-start | bytes 73736 | tf_op jit(solution)/shard_map/ppermute | solution.py:126
  168.9 3.7 %collective-permute-done.9 = f32[48,128]{1,0:T(8,128)S(1)} collective-permute-done((f32[48,128]{1,0:T(8,128)S(1)}, f32[48,128]{1,0:T(8,128)S(1)}, u32[]{:S(2)}, u32[]{:S(2)}) %collective-permute-start.9) | collective-permute-done | bytes 24608 | tf_op jit(solution)/shard_map/ppermute | solution.py:126
  172.5 0.0 collective-permute-start.10
  172.5 1.2 collective-permute-done.10
  173.7 0.6 maximum_select_fusion
  174.4 0.3 fusion.18
  174.6 0.0 all-to-all-done.9
  174.6 0.8 select_reduce_fusion
  (25 shorter events, 0.3 us)
Async XLA Ops:
  0.6 6.5 %copy-start = (f32[1,2048,128]{2,1,0:T(8,128)S(1)}, f32[1,2048,128]{2,1,0:T(8,128)}, u32[]{:S(2)}) copy-start(f32[1,2048,128]{2,1,0:T(8,128)} %param.14) | copy-start | bytes 3145732
  0.6 6.5 %copy-start.1 = (f32[1,128,2048]{2,1,0:T(8,128)S(1)}, f32[1,128,2048]{2,1,0:T(8,128)}, u32[]{:S(2)}) copy-start(f32[1,128,2048]{2,1,0:T(8,128)} %param.10) | copy-start | bytes 3145732
  1.9 9.0 %copy-start.2 = (bf16[128,2048]{1,0:T(8,128)(2,1)}, bf16[128,2048]{1,0:T(8,128)(2,1)S(1)}, u32[]{:S(2)}) copy-start(bf16[128,2048]{1,0:T(8,128)(2,1)S(1)} %slice_bitcast_fusion) | copy-start | bytes 1572868
  1.9 8.9 %collective-permute-start = (bf16[128,1024]{1,0:T(8,128)(2,1)S(1)}, bf16[128,1024]{1,0:T(8,128)(2,1)S(1)}, u32[]{:S(2)}, u32[]{:S(2)}) collective-permute-start(bf16[128,1024]{1,0:T(8,128)(2,1)S(1)} %slice.20), channel_id=1, source_target_pairs={{16,0},{17,1},{18,2},{19,3},{20,4},{21,5},{22,6},{23,7},{24,8},{25... | collective-permute-start | bytes 786440 | tf_op jit(solution)/shard_map/ppermute | solution.py:68
  7.7 3.1 %collective-permute-start.1 = (bf16[128,128]{1,0:T(8,128)(2,1)S(1)}, bf16[128,128]{1,0:T(8,128)(2,1)S(1)}, u32[]{:S(2)}, u32[]{:S(2)}) collective-permute-start(bf16[128,128]{1,0:T(8,128)(2,1)S(1)} %get-tuple-element.10), channel_id=1, source_target_pairs={{0,16},{1,17},{2,18},{3,19},{4,20},{5,21},{6,22},{7,23},{8,24},{9,... | collective-permute-start | bytes 98312 | tf_op jit(solution)/shard_map/ppermute | solution.py:73
  10.8 0.7 copy-start.6
  11.6 28.9 %collective-permute-start.2 = (f32[1024,128]{0,1:T(8,128)S(1)}, f32[1024,128]{0,1:T(8,128)S(1)}, u32[]{:S(2)}, u32[]{:S(2)}) collective-permute-start(f32[1024,128]{0,1:T(8,128)S(1)} %slice.22), channel_id=1, source_target_pairs={{16,0},{17,1},{18,2},{19,3},{20,4},{21,5},{22,6},{23,7},{24,8},{25... | collective-permute-start | bytes 1572872 | tf_op jit(solution)/shard_map/ppermute | solution.py:80
  27.9 14.2 %copy-start.7 = (s32[1,1024]{1,0:T(1,128)S(1)}, s32[1,1024]{1,0:T(1,128)}, u32[]{:S(2)}) copy-start(s32[1,1024]{1,0:T(1,128)} %param.12) | copy-start | bytes 12292
  28.7 11.8 %all-to-all-start.1 = ((bf16[16,64,128]{2,1,0:T(8,128)(2,1)}), bf16[16,64,128]{2,1,0:T(8,128)(2,1)S(1)}, u32[]{:S(2)}, u32[]{:S(2)}) async-start(bf16[16,64,128]{2,1,0:T(8,128)(2,1)} %broadcast_in_dim.35), calls=%async_computation.1 | async-start | bytes 524288 | tf_op jit(solution)/shard_map/all_to_all | solution.py:37
  40.5 1.6 copy-start.5
  40.8 3.4 %collective-permute-start.3 = (f32[128,128]{1,0:T(8,128)S(1)}, f32[128,128]{1,0:T(8,128)S(1)}, u32[]{:S(2)}, u32[]{:S(2)}) collective-permute-start(f32[128,128]{1,0:T(8,128)S(1)} %fusion.13), channel_id=1, source_target_pairs={{0,16},{1,17},{2,18},{3,19},{4,20},{5,21},{6,22},{7,23},{8,24},{9,... | collective-permute-start | bytes 196616 | tf_op jit(solution)/shard_map/ppermute | solution.py:99
  44.4 22.1 %copy-start.4 = (f32[96,128]{1,0:T(8,128)S(1)}, f32[96,128]{1,0:T(8,128)}, u32[]{:S(2)}) copy-start(f32[96,128]{1,0:T(8,128)} %param.15) | copy-start | bytes 147460
  58.3 16.6 %all-to-all-start.3 = ((f32[8,48,128]{2,1,0:T(8,128)}), f32[8,48,128]{2,1,0:T(8,128)S(1)}, u32[]{:S(2)}, u32[]{:S(2)}) async-start(f32[8,48,128]{2,1,0:T(8,128)} %broadcast_in_dim.60), calls=%async_computation.3 | async-start | bytes 393216 | tf_op jit(solution)/shard_map/all_to_all | solution.py:37
  66.5 8.5 %collective-permute-start.4 = (f32[48,128]{1,0:T(8,128)S(1)}, f32[48,128]{1,0:T(8,128)S(1)}, u32[]{:S(2)}, u32[]{:S(2)}) collective-permute-start(f32[48,128]{1,0:T(8,128)S(1)} %constant_dynamic-slice_fusion), channel_id=1, source_target_pairs={{0,0},{1,2},{2,4},{3,6},{4,8},{5,10},{6,12},{7,14},{8,16},{9,18},{... | collective-permute-start | bytes 73736 | tf_op jit(solution)/shard_map/ppermute | solution.py:93
  75.8 13.4 %all-to-all-start.4 = ((f32[16,48,128]{2,1,0:T(8,128)}), f32[16,48,128]{2,1,0:T(8,128)S(1)}, u32[]{:S(2)}, u32[]{:S(2)}) async-start(f32[16,48,128]{2,1,0:T(8,128)} %broadcast_in_dim.61), calls=%async_computation.4 | async-start | bytes 786432 | tf_op jit(solution)/shard_map/all_to_all | solution.py:37
  90.4 4.0 %collective-permute-start.5 = (f32[96,128]{1,0:T(8,128)S(1)}, f32[96,128]{1,0:T(8,128)S(1)}, u32[]{:S(2)}, u32[]{:S(2)}) collective-permute-start(f32[96,128]{1,0:T(8,128)S(1)} %fusion.8), channel_id=1, source_target_pairs={{0,16},{16,0},{1,17},{17,1},{2,18},{18,2},{3,19},{19,3},{4,20},{20... | collective-permute-start | bytes 147464 | tf_op jit(solution)/shard_map/ppermute | solution.py:107
  118.2 3.8 %collective-permute-start.6 = (bf16[768,128]{1,0:T(8,128)(2,1)S(1)}, bf16[768,128]{1,0:T(8,128)(2,1)}, u32[]{:S(2)}, u32[]{:S(2)}) collective-permute-start(bf16[768,128]{1,0:T(8,128)(2,1)S(1)} %bitcast.49), channel_id=1, source_target_pairs={{0,16},{16,0},{1,17},{17,1},{2,18},{18,2},{3,19},{19,3},{4,20},{20... | collective-permute-start | bytes 589832 | tf_op jit(solution)/shard_map/ppermute | solution.py:110
  123.5 3.2 %collective-permute-start.7 = (f32[128,128]{1,0:T(8,128)S(1)}, f32[128,128]{1,0:T(8,128)S(1)}, u32[]{:S(2)}, u32[]{:S(2)}) collective-permute-start(f32[128,128]{1,0:T(8,128)S(1)} %fusion.3), channel_id=1, source_target_pairs={{16,0},{17,1},{18,2},{19,3},{20,4},{21,5},{22,6},{23,7},{24,8},{25... | collective-permute-start | bytes 196616 | tf_op jit(solution)/shard_map/ppermute | solution.py:115
  127.2 24.5 %copy-start.3 = (bf16[128,2048]{1,0:T(8,128)(2,1)S(1)}, bf16[128,2048]{1,0:T(8,128)(2,1)}, u32[]{:S(2)}) copy-start(bf16[128,2048]{1,0:T(8,128)(2,1)} %copy-done.2) | copy-start | bytes 1572868
  151.9 6.3 %collective-permute-start.8 = (f32[128,128]{1,0:T(8,128)S(1)}, f32[128,128]{1,0:T(8,128)S(1)}, u32[]{:S(2)}, u32[]{:S(2)}) collective-permute-start(f32[128,128]{1,0:T(8,128)S(1)} %fusion.21), channel_id=1, source_target_pairs={{16,0},{17,1},{18,2},{19,3},{20,4},{21,5},{22,6},{23,7},{24,8},{25... | collective-permute-start | bytes 196616 | tf_op jit(solution)/shard_map/ppermute | solution.py:119
  160.1 14.6 %all-to-all-start.9 = ((bf16[16,128,128]{2,1,0:T(8,128)(2,1)}), bf16[16,128,128]{2,1,0:T(8,128)(2,1)S(1)}, u32[]{:S(2)}, u32[]{:S(2)}) async-start(bf16[16,128,128]{2,1,0:T(8,128)(2,1)} %bitcast.14), calls=%async_computation.9 | async-start | bytes 1048576 | tf_op jit(solution)/shard_map/all_to_all | solution.py:122
  163.7 8.9 %collective-permute-start.9 = (f32[48,128]{1,0:T(8,128)S(1)}, f32[48,128]{1,0:T(8,128)S(1)}, u32[]{:S(2)}, u32[]{:S(2)}) collective-permute-start(f32[48,128]{1,0:T(8,128)S(1)} %reduce_sum.60), channel_id=1, source_target_pairs={{0,0},{2,1},{4,2},{6,3},{8,4},{10,5},{12,6},{14,7},{16,8},{18,9},{... | collective-permute-start | bytes 73736 | tf_op jit(solution)/shard_map/ppermute | solution.py:126
  172.5 1.2 collective-permute-start.10

commit v8 on v5

--- a/solution.py
+++ b/solution.py
@@ -58,7 +58,7 @@
     row_id = lax.axis_index("row")
     col_id = lax.axis_index("col")
     sources = right_side.shape[-1]
-    band_id = lax.axis_index(("sub", "row"))
+    sub_id = lax.axis_index("sub")
 
     blocks = lax.dynamic_slice(table, (PANEL // BLOCK, col_id // 2), (PANEL // BLOCK, 1))
     lower = factor_cols[0, 0] * jnp.repeat(blocks[:, 0], BLOCK)[None, :].astype(bf16)
@@ -71,46 +71,69 @@
     total = total.astype(f32).sum(0).astype(bf16)
 
     share = root_inverse.shape[0]
-    band = SEPARATOR // (2 * SUBS)
+    chunk = share // 2
+    half = SEPARATOR // 2
     root_inverse = after(root_inverse, partial)
-    gram = mul_t(
-        root_inverse,
-        lax.dynamic_slice_in_dim(root_inverse, band_id * band, band, 1),
-        precision=fine,
-    ).reshape(COLS, share, band)
+    rows_half = lax.dynamic_slice_in_dim(root_inverse, row_id * half, half, 1)
+    gram = [
+        mul_t(
+            rows_half,
+            lax.dynamic_slice_in_dim(root_inverse, (2 * sub_id + k) * share, share, 1),
+            precision=fine,
+        ).reshape(COLS, chunk, share)
+        for k in range(2)
+    ]
+    gram = jnp.concatenate(gram, 1)
     own_gram = lax.dynamic_index_in_dim(gram, col_id, 0)
-    gram = jnp.pad(gram.astype(bf16), ((0, 0), (0, 0), (0, sources - band)))
+    gram = jnp.pad(gram.astype(bf16), ((0, 0), (0, 0), (0, sources - share)))
 
     both = jnp.concatenate([jnp.broadcast_to(total[None], (COLS,) + total.shape), gram], 1)
     both = lax.all_to_all(both, "col", 0, 0)
     total = both[:, :width].reshape(PANEL, sources)
     solved = own - mul(inverse, total.astype(f32), precision=fine)
     chips = lax.broadcasted_iota(jnp.int32, (COLS, 1, 1), 0)
-    gram = jnp.where(chips == col_id, own_gram, both[:, width:, :band].astype(f32)).sum(0)
+    gram = jnp.where(chips == col_id, own_gram, both[:, width:, :share].astype(f32)).sum(0)
 
     onehot = (jnp.arange(SEPARATOR)[:, None] == rows_sep[None, :]).astype(bf16)
     couple_sep = lax.dot_general(
         onehot, couple, (((1,), (1,)), ((), ())), preferred_element_type=f32
     ).astype(bf16)
 
-    updates = mul(couple_sep, solved.astype(bf16)).astype(bf16).reshape(2 * SUBS, band, sources)
-    updates = lax.all_to_all(updates, ("sub", "row"), 0, 0).astype(f32).sum(0)
-    here = (band_id == col_id).astype(f32)
-    rhs = gather(here * root_right - updates, "col", COLS).sum(0)
-    applied = mul(gram, rhs, precision=fine)
-    half = share // 2
-    kept = lax.dynamic_slice_in_dim(applied, row_id * half, half, 0)
-    sent = lax.dynamic_slice_in_dim(applied, (1 - row_id) * half, half, 0)
     swap = [(0, 1), (1, 0)]
-    kept = gather(kept + lax.ppermute(sent, "row", swap), "sub", SUBS).sum(0)
-    other = lax.ppermute(kept, "row", swap)
-    root_part = jnp.where(
-        row_id == 0, jnp.concatenate([kept, other], 0), jnp.concatenate([other, kept], 0)
+    pairs = [
+        (core * COLS + chip, (chip // 8) * COLS + 2 * (chip % 8) + core)
+        for core in range(2)
+        for chip in range(COLS)
+    ]
+    root_rows = lax.dynamic_slice_in_dim(after(root_right, partial), row_id * chunk, chunk, 0)
+    root_rows = lax.ppermute(root_rows, ("row", "col"), pairs)
+
+    updates = mul(couple_sep, solved.astype(bf16)).astype(bf16).reshape(2 * COLS, chunk, sources)
+    updates = lax.all_to_all(updates, ("row", "col"), 0, 0).astype(f32).sum(0)
+    gram = jnp.pad(gram, ((0, 0), (0, sources - share)))
+    both = gather(jnp.concatenate([updates, gram], 0), "sub", SUBS)
+    rhs = root_rows - both[:, :chunk].sum(0)
+    gram = both[:, chunk:, :share].reshape(2 * SUBS, chunk, share)
+    applied = lax.dot_general(
+        gram,
+        jnp.broadcast_to(rhs[None], (2 * SUBS,) + rhs.shape),
+        (((1,), (1,)), ((0,), (0,))),
+        precision=fine,
+        preferred_element_type=f32,
     )
-    root_full = gather(root_part.astype(bf16), "col", COLS).reshape(SEPARATOR, sources)
-    value = solved - mul_t(couple_sep, root_full)
+    root_rows = sum_scatter(applied.reshape(SEPARATOR, sources), ("row", "col"), 2 * COLS)
+    root_full = gather(root_rows.astype(bf16), ("row", "col"), 2 * COLS)
+    value = solved - mul_t(couple_sep, root_full.reshape(SEPARATOR, sources))
 
     value = sum_scatter(mul_t(inverse, value, precision=fine), "col", COLS)
+    root_rows = lax.ppermute(root_rows, ("row", "col"), [(j, i) for i, j in pairs])
+    theirs = lax.ppermute(root_rows, "row", swap)
+    root_part = jnp.where(
+        row_id == 0,
+        jnp.concatenate([root_rows, theirs], 0),
+        jnp.concatenate([theirs, root_rows], 0),
+    )
+    value = after(value, root_part)
     later_low = gather(value.astype(bf16), "col", COLS).reshape(PANEL, sources)
     terms = lax.ppermute(mul(lower, later_low), "row", [(1, 0)])
     value = value - sum_scatter(mul_t(inverse, terms, precision=fine), "col", COLS)

time: 174 us -> 179 us (1.029)
  starting transfers between devices: 39.4 us -> 51.2 us
  blocking collectives: 37.4 us -> 31 us
  waiting for transfers between devices: 78.8 us -> 74.6 us
    ppermute x2 -> x3, starting transfers between devices: 1.81 us -> 9.25 us  [the longest x1 5.9 us: shards(): lax.ppermute(root_rows, ('row', 'col'), [(j, i) for i, j in pairs])]
    all_to_all x3 -> x2, blocking collectives: 37.4 us -> 31 us  [gather(): return lax.all_to_all(spread, axes, 0, 0)]
    all_to_all x2 -> x3, starting transfers between devices: 7.14 us -> 13.2 us  [sum_scatter(): others = lax.all_to_all(parts.astype(bf16), axes, 0, 0).astype(f32)]
    all_to_all x1, waiting for transfers between devices: 14.5 us -> 9.41 us  [shards(): updates = lax.all_to_all(updates, ('row', 'col'), 0, 0).astype(f32).sum(0)]
    all_to_all x1, starting transfers between devices: 11.2 us -> 6.41 us  [shards(): updates = lax.all_to_all(updates, ('row', 'col'), 0, 0).astype(f32).sum(0)]
    all_to_all x1, starting transfers between devices: 3.61 us -> 8.19 us  [gather(): return lax.all_to_all(spread, axes, 0, 0)]
    ppermute x2 -> x3, waiting for transfers between devices: 1.7 us -> 4.29 us  [the longest x1 3.1 us: shards(): lax.ppermute(root_rows, ('row', 'col'), [(j, i) for i, j in pairs])]
    dot_general x4 -> x6, matrix products: 2.68 us -> 3.74 us  [mul_t(): lax.dot_general(left, right, first_axes, preferred_element_type=f32, **kw)]
  transfers between devices with their start and end apart: 10 -> 12, of which waited for: 10 -> 10; matrix products, arithmetic and copies ran while one was open for 2% -> 3% of each run, Pallas kernels for 0% -> 0%
where the time goes in v8:
time: 179 us; the launch traced here: 178 us
  waiting for transfers between devices  74.6 us (42%)
  starting transfers between devices  51.2 us (29%)
  blocking collectives  31 us (17%)
  matrix products  10.2 us (6%)
  local copies, waits for them, and re-layouts  6.26 us (3%)
  other arithmetic  3.62 us (2%)
    all_to_all x2, blocking collectives, gather(): return lax.all_to_all(spread, axes, 0, 0)  31 us
    all_to_all x3, waiting for transfers between devices, sum_scatter(): others = lax.all_to_all(parts.astype(bf16), axes, 0, 0).astype(f32)  20.2 us
    all_to_all x1, waiting for transfers between devices, gather(): return lax.all_to_all(spread, axes, 0, 0)  14.7 us
    all_to_all x3, starting transfers between devices, sum_scatter(): others = lax.all_to_all(parts.astype(bf16), axes, 0, 0).astype(f32)  13.2 us
    all_to_all x1, waiting for transfers between devices, shards(): both = lax.all_to_all(both, 'col', 0, 0)  11.8 us
    all_to_all x1, waiting for transfers between devices, shards(): total = lax.all_to_all(partial.reshape(COLS, width, sources), 'col', 0, 0)  9.71 us
    all_to_all x1, waiting for transfers between devices, shards(): updates = lax.all_to_all(updates, ('row', 'col'), 0, 0).astype(f32).sum(0)  9.41 us
    all_to_all x1, starting transfers between devices, gather(): return lax.all_to_all(spread, axes, 0, 0)  8.19 us
  transfers between devices with their start and end apart: 12, of which 10 were waited for; matrix products, arithmetic and copies ran while one was open for 3% of the time, Pallas kernels for 0%

profile of v8, /device:TPU:1, one launch (start us, length us, event | category | flops | bytes accessed | tf_op | source)
XLA Modules:
  0.0 178.0 jit_solution(15176787554425754333)
XLA Ops:
  0.6 0.0 copy-start
  0.7 0.0 copy-start.4
  0.7 1.2 copy-done
  1.9 1.8 %fusion.37 = (bf16[128,128]{1,0:T(8,128)(2,1)S(1)}, f32[128,128]{1,0:T(8,128)S(1)}) fusion(f32[1,2048,128]{2,1,0:T(8,128)} %param.14, f32[1,128,2048]{2,1,0:T(8,128)S(1)} %copy-done), kind=kOutput, calls=%fused_computation.67 | convolution fusion | flops 201342976 | bytes 2195456 | tf_op jit(solution)/shard_map/dot_general | solution.py:19
  3.7 1.3 collective-permute-start
  5.0 0.2 fusion.36
  5.2 0.1 broadcast_bitcast_fusion
  5.3 3.6 %collective-permute-done = bf16[128,128]{1,0:T(8,128)(2,1)S(1)} collective-permute-done((bf16[128,128]{1,0:T(8,128)(2,1)S(1)}, bf16[128,128]{1,0:T(8,128)(2,1)S(1)}, u32[]{:S(2)}, u32[]{:S(2)}) %collective-permute-start) | collective-permute-done | bytes 32800 | tf_op jit(solution)/shard_map/ppermute | solution.py:68
  8.9 1.1 convolution_convert_fusion.1
  10.1 5.5 %all-to-all-start = ((bf16[16,128,128]{2,1,0:T(8,128)(2,1)}), bf16[16,128,128]{2,1,0:T(8,128)(2,1)S(1)}, u32[]{:S(2)}, u32[]{:S(2)}) async-start(bf16[16,128,128]{2,1,0:T(8,128)(2,1)} %bitcast.3), calls=%async_computation | async-start | bytes 1048576 | tf_op jit(solution)/shard_map/all_to_all | solution.py:70
  15.5 0.5 fusion.20
  16.1 0.5 fusion.22
  16.6 0.1 fusion.14
  16.7 9.7 %all-to-all-done = bf16[16,128,128]{2,1,0:T(8,128)(2,1)S(1)} async-done(((bf16[16,128,128]{2,1,0:T(8,128)(2,1)}), bf16[16,128,128]{2,1,0:T(8,128)(2,1)S(1)}, u32[]{:S(2)}, u32[]{:S(2)}) %all-to-all-start) | async-done | bytes 524320 | tf_op jit(solution)/shard_map/all_to_all | solution.py:70
  26.4 0.1 reduce_sum.66
  26.5 0.1 broadcast_in_dim.103
  26.6 1.1 fusion.13
  27.7 3.8 %all-to-all-start.1 = ((bf16[16,224,128]{2,1,0:T(8,128)(2,1)}), bf16[16,224,128]{2,1,0:T(8,128)(2,1)S(1)}, u32[]{:S(2)}, u32[]{:S(2)}) async-start(bf16[16,224,128]{2,1,0:T(8,128)(2,1)} %fusion.13), calls=%async_computation.1 | async-start | bytes 1835008 | tf_op jit(solution)/shard_map/all_to_all | solution.py:91
  31.5 2.1 %fusion.2 = bf16[1536,128]{1,0:T(8,128)(2,1)S(1)} fusion(s32[1024]{0:T(1024)S(1)} %bitcast.98, bf16[1,1,128,1024]{3,2,1,0:T(8,128)(2,1)} %param.11), kind=kOutput, calls=%fused_computation.3 | convolution fusion | flops 404422656 | bytes 659456 | tf_op jit(solution)/shard_map/dot_general | solution.py:98
  33.6 11.8 %all-to-all-done.1 = bf16[16,224,128]{2,1,0:T(8,128)(2,1)S(1)} async-done(((bf16[16,224,128]{2,1,0:T(8,128)(2,1)}), bf16[16,224,128]{2,1,0:T(8,128)(2,1)S(1)}, u32[]{:S(2)}, u32[]{:S(2)}) %all-to-all-start.1) | async-done | bytes 917536 | tf_op jit(solution)/shard_map/all_to_all | solution.py:91
  45.5 0.4 fusion.4
  45.9 0.0 copy-start.2
  45.9 0.6 copy-done.2
  46.5 1.0 convolution_convert_fusion
  47.5 6.4 %all-to-all-start.2 = ((bf16[32,48,128]{2,1,0:T(8,128)(2,1)}), bf16[32,48,128]{2,1,0:T(8,128)(2,1)S(1)}, u32[]{:S(2)}, u32[]{:S(2)}) async-start(bf16[32,48,128]{2,1,0:T(8,128)(2,1)} %bitcast.89), calls=%async_computation.2 | async-start | bytes 786432 | tf_op jit(solution)/shard_map/all_to_all | solution.py:112
  54.0 0.2 select_reduce_fusion.3
  54.2 9.4 %all-to-all-done.2 = bf16[32,48,128]{2,1,0:T(8,128)(2,1)S(1)} async-done(((bf16[32,48,128]{2,1,0:T(8,128)(2,1)}), bf16[32,48,128]{2,1,0:T(8,128)(2,1)S(1)}, u32[]{:S(2)}, u32[]{:S(2)}) %all-to-all-start.2) | async-done | bytes 393248 | tf_op jit(solution)/shard_map/all_to_all | solution.py:112
  63.6 0.1 convert_reduce_fusion
  63.7 0.9 broadcast_in_dim.108
  64.5 8.2 %all-to-all-start.3 = ((f32[8,144,128]{2,1,0:T(8,128)}), f32[8,144,128]{2,1,0:T(8,128)S(1)}, u32[]{:S(2)}, u32[]{:S(2)}) async-start(f32[8,144,128]{2,1,0:T(8,128)} %broadcast_in_dim.108), calls=%async_computation.3 | async-start | bytes 1179648 | tf_op jit(solution)/shard_map/all_to_all | solution.py:41
  72.7 3.3 %collective-permute-start.1 = (f32[48,128]{1,0:T(8,128)S(1)}, f32[48,128]{1,0:T(8,128)S(1)}, u32[]{:S(2)}, u32[]{:S(2)}) collective-permute-start(f32[48,128]{1,0:T(8,128)S(1)} %constant_dynamic-slice_fusion.1), channel_id=1, source_target_pairs={{0,0},{1,2},{2,4},{3,6},{4,8},{5,10},{6,12},{7,14},{8,16},{9,18},{... | collective-permute-start | bytes 73736 | tf_op jit(solution)/shard_map/ppermute | solution.py:109
  76.1 14.7 %all-to-all-done.3 = f32[8,144,128]{2,1,0:T(8,128)S(1)} async-done(((f32[8,144,128]{2,1,0:T(8,128)}), f32[8,144,128]{2,1,0:T(8,128)S(1)}, u32[]{:S(2)}, u32[]{:S(2)}) %all-to-all-start.3) | async-done | bytes 589856 | tf_op jit(solution)/shard_map/all_to_all | solution.py:41
  90.9 0.8 fusion.27
  91.7 0.8 convert_element_type.86
  92.5 5.8 %all-to-all-start.4 = ((bf16[32,48,128]{2,1,0:T(8,128)(2,1)}), bf16[32,48,128]{2,1,0:T(8,128)(2,1)S(1)}, u32[]{:S(2)}, u32[]{:S(2)}) async-start(bf16[32,48,128]{2,1,0:T(8,128)(2,1)} %convert_element_type.86), calls=%async_computation.4 | async-start | bytes 786432 | tf_op jit(solution)/shard_map/all_to_all | solution.py:34
  98.4 9.5 %all-to-all-done.4 = bf16[32,48,128]{2,1,0:T(8,128)(2,1)S(1)} async-done(((bf16[32,48,128]{2,1,0:T(8,128)(2,1)}), bf16[32,48,128]{2,1,0:T(8,128)(2,1)S(1)}, u32[]{:S(2)}, u32[]{:S(2)}) %all-to-all-start.4) | async-done | bytes 393248 | tf_op jit(solution)/shard_map/all_to_all | solution.py:34
  107.8 0.1 select_reduce_fusion.2
  108.0 0.1 broadcast_in_dim.112
  108.1 13.7 %all_to_all.45 = bf16[32,48,128]{2,1,0:T(8,128)(2,1)S(1)} all-to-all(bf16[32,48,128]{2,1,0:T(8,128)(2,1)S(1)} %broadcast_in_dim.112), channel_id=1, replica_groups=mesh['sub'=8,'row'=2,'col'=16] {'row','col'}, dimensions={0} | all-to-all | bytes 786432 | tf_op jit(solution)/shard_map/all_to_all | solution.py:41
  121.7 0.3 convolution_subtract_fusion
  122.1 0.6 fusion.9
  122.7 0.9 bitcast_convert_fusion.1
  123.6 3.8 %all-to-all-start.6 = ((bf16[16,128,128]{1,2,0:T(8,128)(2,1)}), bf16[16,128,128]{1,2,0:T(8,128)(2,1)S(1)}, u32[]{:S(2)}, u32[]{:S(2)}) async-start(bf16[16,128,128]{1,2,0:T(8,128)(2,1)} %bitcast_convert_fusion.1), calls=%async_computation.6 | async-start | bytes 1048576 | tf_op jit(solution)/shard_map/all_to_all | solution.py:34
  127.3 5.9 %collective-permute-start.2 = (f32[48,128]{1,0:T(8,128)S(1)}, f32[48,128]{1,0:T(8,128)S(1)}, u32[]{:S(2)}, u32[]{:S(2)}) collective-permute-start(f32[48,128]{1,0:T(8,128)S(1)} %select_reduce_fusion.2), channel_id=1, source_target_pairs={{0,0},{2,1},{4,2},{6,3},{8,4},{10,5},{12,6},{14,7},{16,8},{18,9},{... | collective-permute-start | bytes 73736 | tf_op jit(solution)/shard_map/ppermute | solution.py:129
  133.2 3.1 %collective-permute-done.2 = f32[48,128]{1,0:T(8,128)S(1)} collective-permute-done((f32[48,128]{1,0:T(8,128)S(1)}, f32[48,128]{1,0:T(8,128)S(1)}, u32[]{:S(2)}, u32[]{:S(2)}) %collective-permute-start.2) | collective-permute-done | bytes 24608 | tf_op jit(solution)/shard_map/ppermute | solution.py:129
  136.3 1.2 collective-permute-done.3
  137.5 0.6 maximum_select_fusion
  138.2 0.2 copy.41
  138.3 0.1 constant_dynamic-slice_fusion
  138.4 0.2 select_reduce_fusion.1
  138.6 0.1 copy.29
  138.7 0.1 broadcast_in_dim.115
  138.8 17.3 %all_to_all.46 = bf16[16,128,128]{2,1,0:T(8,128)(2,1)S(1)} all-to-all(bf16[16,128,128]{2,1,0:T(8,128)(2,1)S(1)} %broadcast_in_dim.115), channel_id=1, replica_groups=mesh['sub'=8,'row'=2,'col'=16] {'col'}, dimensions={0} | all-to-all | bytes 1048576 | tf_op jit(solution)/shard_map/all_to_all | solution.py:41
  156.2 0.3 fusion.15
  156.5 3.7 %collective-permute-start.4 = (f32[128,128]{1,0:T(8,128)S(1)}, f32[128,128]{1,0:T(8,128)S(1)}, u32[]{:S(2)}, u32[]{:S(2)}) collective-permute-start(f32[128,128]{1,0:T(8,128)S(1)} %fusion.15), channel_id=1, source_target_pairs={{16,0},{17,1},{18,2},{19,3},{20,4},{21,5},{22,6},{23,7},{24,8},{25... | collective-permute-start | bytes 196616 | tf_op jit(solution)/shard_map/ppermute | solution.py:138
  160.1 0.9 collective-permute-done.4
  161.0 0.6 fusion.7
  161.6 0.9 bitcast_convert_fusion
  162.5 3.6 %all-to-all-start.8 = ((bf16[16,128,128]{1,2,0:T(8,128)(2,1)}), bf16[16,128,128]{1,2,0:T(8,128)(2,1)S(1)}, u32[]{:S(2)}, u32[]{:S(2)}) async-start(bf16[16,128,128]{1,2,0:T(8,128)(2,1)} %bitcast_convert_fusion), calls=%async_computation.8 | async-start | bytes 1048576 | tf_op jit(solution)/shard_map/all_to_all | solution.py:34
  166.1 0.2 copy.42
  166.3 0.1 constant_dynamic-slice_fusion.2
  166.4 10.7 %all-to-all-done.8 = bf16[16,128,128]{1,2,0:T(8,128)(2,1)S(1)} async-done(((bf16[16,128,128]{1,2,0:T(8,128)(2,1)}), bf16[16,128,128]{1,2,0:T(8,128)(2,1)S(1)}, u32[]{:S(2)}, u32[]{:S(2)}) %all-to-all-start.8) | async-done | bytes 524320 | tf_op jit(solution)/shard_map/all_to_all | solution.py:34
  177.1 0.2 select_reduce_fusion
  177.3 0.7 copy.32
  (30 shorter events, 0.2 us)
Async XLA Ops:
  0.6 1.2 copy-start
  0.6 4.4 %copy-start.7 = (s32[1,16,16]{2,1,0:T(8,128)S(1)}, s32[1,16,16]{2,1,0:T(8,128)}, u32[]{:S(2)}) copy-start(s32[1,16,16]{2,1,0:T(8,128)} %param.9) | copy-start | bytes 3076
  0.7 8.3 %copy-start.4 = (bf16[1,2,128,2048]{3,2,1,0:T(8,128)(2,1)S(1)}, bf16[1,2,128,2048]{3,2,1,0:T(8,128)(2,1)}, u32[]{:S(2)}) copy-start(bf16[1,2,128,2048]{3,2,1,0:T(8,128)(2,1)} %param.8) | copy-start | bytes 3145732
  3.7 5.2 %collective-permute-start = (bf16[128,128]{1,0:T(8,128)(2,1)S(1)}, bf16[128,128]{1,0:T(8,128)(2,1)S(1)}, u32[]{:S(2)}, u32[]{:S(2)}) collective-permute-start(bf16[128,128]{1,0:T(8,128)(2,1)S(1)} %get-tuple-element.12), channel_id=1, source_target_pairs={{0,16},{1,17},{2,18},{3,19},{4,20},{5,21},{6,22},{7,23},{8,24},{9,... | collective-permute-start | bytes 98312 | tf_op jit(solution)/shard_map/ppermute | solution.py:68
  8.9 6.6 %copy-start.1 = (f32[96,1536]{1,0:T(8,128)S(1)}, f32[96,1536]{1,0:T(8,128)}, u32[]{:S(2)}) copy-start(f32[96,1536]{1,0:T(8,128)} %param.13) | copy-start | bytes 1769476
  10.1 16.4 %all-to-all-start = ((bf16[16,128,128]{2,1,0:T(8,128)(2,1)}), bf16[16,128,128]{2,1,0:T(8,128)(2,1)S(1)}, u32[]{:S(2)}, u32[]{:S(2)}) async-start(bf16[16,128,128]{2,1,0:T(8,128)(2,1)} %bitcast.3), calls=%async_computation | async-start | bytes 1048576 | tf_op jit(solution)/shard_map/all_to_all | solution.py:70
  27.7 3.8 %copy-start.8 = (s32[1,1024]{1,0:T(1,128)S(1)}, s32[1,1024]{1,0:T(1,128)}, u32[]{:S(2)}) copy-start(s32[1,1024]{1,0:T(1,128)} %param.12) | copy-start | bytes 12292
  27.7 17.8 %all-to-all-start.1 = ((bf16[16,224,128]{2,1,0:T(8,128)(2,1)}), bf16[16,224,128]{2,1,0:T(8,128)(2,1)S(1)}, u32[]{:S(2)}, u32[]{:S(2)}) async-start(bf16[16,224,128]{2,1,0:T(8,128)(2,1)} %fusion.13), calls=%async_computation.1 | async-start | bytes 1835008 | tf_op jit(solution)/shard_map/all_to_all | solution.py:91
  45.9 0.6 copy-start.2
  47.5 16.0 %all-to-all-start.2 = ((bf16[32,48,128]{2,1,0:T(8,128)(2,1)}), bf16[32,48,128]{2,1,0:T(8,128)(2,1)S(1)}, u32[]{:S(2)}, u32[]{:S(2)}) async-start(bf16[32,48,128]{2,1,0:T(8,128)(2,1)} %bitcast.89), calls=%async_computation.2 | async-start | bytes 786432 | tf_op jit(solution)/shard_map/all_to_all | solution.py:112
  63.6 9.1 %copy-start.6 = (f32[96,128]{1,0:T(8,128)S(1)}, f32[96,128]{1,0:T(8,128)}, u32[]{:S(2)}) copy-start(f32[96,128]{1,0:T(8,128)} %param.15) | copy-start | bytes 147460
  64.5 26.2 %all-to-all-start.3 = ((f32[8,144,128]{2,1,0:T(8,128)}), f32[8,144,128]{2,1,0:T(8,128)S(1)}, u32[]{:S(2)}, u32[]{:S(2)}) async-start(f32[8,144,128]{2,1,0:T(8,128)} %broadcast_in_dim.108), calls=%async_computation.3 | async-start | bytes 1179648 | tf_op jit(solution)/shard_map/all_to_all | solution.py:41
  72.7 18.1 %collective-permute-start.1 = (f32[48,128]{1,0:T(8,128)S(1)}, f32[48,128]{1,0:T(8,128)S(1)}, u32[]{:S(2)}, u32[]{:S(2)}) collective-permute-start(f32[48,128]{1,0:T(8,128)S(1)} %constant_dynamic-slice_fusion.1), channel_id=1, source_target_pairs={{0,0},{1,2},{2,4},{3,6},{4,8},{5,10},{6,12},{7,14},{8,16},{9,18},{... | collective-permute-start | bytes 73736 | tf_op jit(solution)/shard_map/ppermute | solution.py:109
  92.5 15.4 %all-to-all-start.4 = ((bf16[32,48,128]{2,1,0:T(8,128)(2,1)}), bf16[32,48,128]{2,1,0:T(8,128)(2,1)S(1)}, u32[]{:S(2)}, u32[]{:S(2)}) async-start(bf16[32,48,128]{2,1,0:T(8,128)(2,1)} %convert_element_type.86), calls=%async_computation.4 | async-start | bytes 786432 | tf_op jit(solution)/shard_map/all_to_all | solution.py:34
  98.3 23.4 %copy-start.3 = (f32[128,128]{1,0:T(8,128)S(1)}, f32[128,128]{1,0:T(8,128)}, u32[]{:S(2)}) copy-start(f32[128,128]{1,0:T(8,128)} %copy-done.2) | copy-start | bytes 196612
  123.6 14.8 %all-to-all-start.6 = ((bf16[16,128,128]{1,2,0:T(8,128)(2,1)}), bf16[16,128,128]{1,2,0:T(8,128)(2,1)S(1)}, u32[]{:S(2)}, u32[]{:S(2)}) async-start(bf16[16,128,128]{1,2,0:T(8,128)(2,1)} %bitcast_convert_fusion.1), calls=%async_computation.6 | async-start | bytes 1048576 | tf_op jit(solution)/shard_map/all_to_all | solution.py:34
  127.3 9.0 %collective-permute-start.2 = (f32[48,128]{1,0:T(8,128)S(1)}, f32[48,128]{1,0:T(8,128)S(1)}, u32[]{:S(2)}, u32[]{:S(2)}) collective-permute-start(f32[48,128]{1,0:T(8,128)S(1)} %select_reduce_fusion.2), channel_id=1, source_target_pairs={{0,0},{2,1},{4,2},{6,3},{8,4},{10,5},{12,6},{14,7},{16,8},{18,9},{... | collective-permute-start | bytes 73736 | tf_op jit(solution)/shard_map/ppermute | solution.py:129
  136.3 1.2 collective-permute-start.3
  138.6 17.6 %copy-start.5 = (bf16[1,2,128,2048]{3,2,1,0:T(8,128)(2,1)S(1)}, bf16[1,2,128,2048]{3,2,1,0:T(8,128)(2,1)}, u32[]{:S(2)}) copy-start(bf16[1,2,128,2048]{3,2,1,0:T(8,128)(2,1)} %param.8) | copy-start | bytes 3145732
  156.5 4.5 %collective-permute-start.4 = (f32[128,128]{1,0:T(8,128)S(1)}, f32[128,128]{1,0:T(8,128)S(1)}, u32[]{:S(2)}, u32[]{:S(2)}) collective-permute-start(f32[128,128]{1,0:T(8,128)S(1)} %fusion.15), channel_id=1, source_target_pairs={{16,0},{17,1},{18,2},{19,3},{20,4},{21,5},{22,6},{23,7},{24,8},{25... | collective-permute-start | bytes 196616 | tf_op jit(solution)/shard_map/ppermute | solution.py:138
  162.5 14.6 %all-to-all-start.8 = ((bf16[16,128,128]{1,2,0:T(8,128)(2,1)}), bf16[16,128,128]{1,2,0:T(8,128)(2,1)S(1)}, u32[]{:S(2)}, u32[]{:S(2)}) async-start(bf16[16,128,128]{1,2,0:T(8,128)(2,1)} %bitcast_convert_fusion), calls=%async_computation.8 | async-start | bytes 1048576 | tf_op jit(solution)/shard_map/all_to_all | solution.py:34

commit v9 on v5

--- a/solution.py
+++ b/solution.py
@@ -96,7 +96,8 @@
     updates = mul(couple_sep, solved.astype(bf16)).astype(bf16).reshape(2 * SUBS, band, sources)
     updates = lax.all_to_all(updates, ("sub", "row"), 0, 0).astype(f32).sum(0)
     here = (band_id == col_id).astype(f32)
-    rhs = gather(here * root_right - updates, "col", COLS).sum(0)
+    low = (here * root_right - updates).astype(bf16)
+    rhs = jnp.where(chips == col_id, here * root_right - updates, gather(low, "col", COLS)).sum(0)
     applied = mul(gram, rhs, precision=fine)
     half = share // 2
     kept = lax.dynamic_slice_in_dim(applied, row_id * half, half, 0)
@@ -112,7 +113,7 @@
 
     value = sum_scatter(mul_t(inverse, value, precision=fine), "col", COLS)
     later_low = gather(value.astype(bf16), "col", COLS).reshape(PANEL, sources)
-    terms = lax.ppermute(mul(lower, later_low), "row", [(1, 0)])
+    terms = lax.all_gather(mul(lower, later_low), "row")[1] * (row_id == 0).astype(f32)
     value = value - sum_scatter(mul_t(inverse, terms, precision=fine), "col", COLS)
     return value[None], root_part
 

time: 174 us -> 172 us (0.989)
  blocking collectives: 37.4 us -> 29 us
  waiting for transfers between devices: 78.8 us -> 81.3 us
  other arithmetic: 2.69 us -> 4.99 us
    all_to_all x3 -> x2, blocking collectives: 37.4 us -> 24.3 us  [gather(): return lax.all_to_all(spread, axes, 0, 0)]
    ppermute x1 -> x0, starting transfers between devices: 5.07 us -> none  [shards(): terms = lax.ppermute(mul(lower, later_low), 'row', [(1, 0)])]
    all_gather x0 -> x1, blocking collectives: none -> 4.72 us  [shards(): lax.all_gather(mul(lower, later_low), 'row')[1] * (row_id == 0).astype(f32)]
    all_to_all x1 -> x2, waiting for transfers between devices: 14.7 us -> 19.1 us  [gather(): return lax.all_to_all(spread, axes, 0, 0)]
    all_to_all x1 -> x2, starting transfers between devices: 3.61 us -> 7.12 us  [gather(): return lax.all_to_all(spread, axes, 0, 0)]
where the time goes in v9:
time: 172 us; the launch traced here: 171 us
  waiting for transfers between devices  81.3 us (47%)
  starting transfers between devices  38.6 us (22%)
  blocking collectives  29 us (17%)
  matrix products  9.35 us (5%)
  local copies, waits for them, and re-layouts  7.01 us (4%)
  other arithmetic  4.99 us (3%)
    all_to_all x2, blocking collectives, gather(): return lax.all_to_all(spread, axes, 0, 0)  24.3 us
    all_to_all x2, waiting for transfers between devices, sum_scatter(): others = lax.all_to_all(parts.astype(bf16), axes, 0, 0).astype(f32)  20.5 us
    all_to_all x2, waiting for transfers between devices, gather(): return lax.all_to_all(spread, axes, 0, 0)  19.1 us
    all_to_all x1, waiting for transfers between devices, shards(): updates = lax.all_to_all(updates, ('sub', 'row'), 0, 0).astype(f32).sum(0)  14.5 us
    all_to_all x1, waiting for transfers between devices, shards(): both = lax.all_to_all(both, 'col', 0, 0)  11.8 us
    all_to_all x1, starting transfers between devices, shards(): updates = lax.all_to_all(updates, ('sub', 'row'), 0, 0).astype(f32).sum(0)  11.3 us
    all_to_all x1, waiting for transfers between devices, shards(): total = lax.all_to_all(partial.reshape(COLS, width, sources), 'col', 0, 0)  9.98 us
    all_to_all x2, starting transfers between devices, sum_scatter(): others = lax.all_to_all(parts.astype(bf16), axes, 0, 0).astype(f32)  7.14 us
  transfers between devices with their start and end apart: 10, of which 10 were waited for; matrix products, arithmetic and copies ran while one was open for 2% of the time, Pallas kernels for 0%

profile of v9, /device:TPU:1, one launch (start us, length us, event | category | flops | bytes accessed | tf_op | source)
XLA Modules:
  0.0 171.3 jit_solution(2331888354576356789)
XLA Ops:
  0.6 0.0 copy-start
  0.7 0.0 copy-start.4
  0.7 1.2 copy-done
  1.9 1.8 %fusion.30 = (bf16[128,128]{1,0:T(8,128)(2,1)S(1)}, f32[128,128]{1,0:T(8,128)S(1)}) fusion(f32[1,2048,128]{2,1,0:T(8,128)} %param.14, f32[1,128,2048]{2,1,0:T(8,128)S(1)} %copy-done), kind=kOutput, calls=%fused_computation.56 | convolution fusion | flops 201342976 | bytes 2195456 | tf_op jit(solution)/shard_map/dot_general | solution.py:19
  3.7 1.3 collective-permute-start
  5.0 0.2 fusion.26
  5.2 0.1 broadcast_bitcast_fusion
  5.3 3.6 %collective-permute-done = bf16[128,128]{1,0:T(8,128)(2,1)S(1)} collective-permute-done((bf16[128,128]{1,0:T(8,128)(2,1)S(1)}, bf16[128,128]{1,0:T(8,128)(2,1)S(1)}, u32[]{:S(2)}, u32[]{:S(2)}) %collective-permute-start) | collective-permute-done | bytes 32800 | tf_op jit(solution)/shard_map/ppermute | solution.py:68
  8.9 1.1 convolution_convert_fusion.1
  10.1 5.5 %all-to-all-start = ((bf16[16,128,128]{2,1,0:T(8,128)(2,1)}), bf16[16,128,128]{2,1,0:T(8,128)(2,1)S(1)}, u32[]{:S(2)}, u32[]{:S(2)}) async-start(bf16[16,128,128]{2,1,0:T(8,128)(2,1)} %bitcast.3), calls=%async_computation | async-start | bytes 1048576 | tf_op jit(solution)/shard_map/all_to_all | solution.py:70
  15.6 0.8 fusion.22
  16.4 0.1 convert_element_type.89
  16.5 10.0 %all-to-all-done = bf16[16,128,128]{2,1,0:T(8,128)(2,1)S(1)} async-done(((bf16[16,128,128]{2,1,0:T(8,128)(2,1)}), bf16[16,128,128]{2,1,0:T(8,128)(2,1)S(1)}, u32[]{:S(2)}, u32[]{:S(2)}) %all-to-all-start) | async-done | bytes 524320 | tf_op jit(solution)/shard_map/all_to_all | solution.py:70
  26.4 0.1 reduce_sum.66
  26.5 0.1 broadcast_in_dim.95
  26.6 1.0 fusion.13
  27.7 3.8 %all-to-all-start.1 = ((bf16[16,224,128]{2,1,0:T(8,128)(2,1)}), bf16[16,224,128]{2,1,0:T(8,128)(2,1)S(1)}, u32[]{:S(2)}, u32[]{:S(2)}) async-start(bf16[16,224,128]{2,1,0:T(8,128)(2,1)} %fusion.13), calls=%async_computation.1 | async-start | bytes 1835008 | tf_op jit(solution)/shard_map/all_to_all | solution.py:85
  31.5 2.1 %fusion.2 = bf16[1536,128]{1,0:T(8,128)(2,1)S(1)} fusion(s32[1024]{0:T(1024)S(1)} %bitcast.89, bf16[1,1,128,1024]{3,2,1,0:T(8,128)(2,1)} %param.11), kind=kOutput, calls=%fused_computation.3 | convolution fusion | flops 404422656 | bytes 659456 | tf_op jit(solution)/shard_map/dot_general | solution.py:92
  33.6 11.8 %all-to-all-done.1 = bf16[16,224,128]{2,1,0:T(8,128)(2,1)S(1)} async-done(((bf16[16,224,128]{2,1,0:T(8,128)(2,1)}), bf16[16,224,128]{2,1,0:T(8,128)(2,1)S(1)}, u32[]{:S(2)}, u32[]{:S(2)}) %all-to-all-start.1) | async-done | bytes 917536 | tf_op jit(solution)/shard_map/all_to_all | solution.py:85
  45.5 0.4 fusion.4
  45.9 0.0 copy-start.2
  45.9 0.6 copy-done.2
  46.5 1.0 convolution_convert_fusion
  47.5 11.3 %all-to-all-start.2 = ((bf16[16,96,128]{2,1,0:T(8,128)(2,1)}), bf16[16,96,128]{2,1,0:T(8,128)(2,1)S(1)}, u32[]{:S(2)}, u32[]{:S(2)}) async-start(bf16[16,96,128]{2,1,0:T(8,128)(2,1)} %bitcast.81), calls=%async_computation.2 | async-start | bytes 786432 | tf_op jit(solution)/shard_map/all_to_all | solution.py:97
  58.8 14.5 %all-to-all-done.2 = bf16[16,96,128]{2,1,0:T(8,128)(2,1)S(1)} async-done(((bf16[16,96,128]{2,1,0:T(8,128)(2,1)}), bf16[16,96,128]{2,1,0:T(8,128)(2,1)S(1)}, u32[]{:S(2)}, u32[]{:S(2)}) %all-to-all-start.2) | async-done | bytes 393248 | tf_op jit(solution)/shard_map/all_to_all | solution.py:97
  73.3 0.1 convert_reduce_fusion
  73.4 1.4 fusion.29
  74.8 0.8 broadcast_in_dim.101
  75.6 3.6 %all-to-all-start.3 = ((bf16[16,96,128]{2,1,0:T(8,128)(2,1)}), bf16[16,96,128]{2,1,0:T(8,128)(2,1)S(1)}, u32[]{:S(2)}, u32[]{:S(2)}) async-start(bf16[16,96,128]{2,1,0:T(8,128)(2,1)} %broadcast_in_dim.101), calls=%async_computation.3 | async-start | bytes 786432 | tf_op jit(solution)/shard_map/all_to_all | solution.py:41
  79.2 0.2 select_reduce_fusion.3
  79.4 9.8 %all-to-all-done.3 = bf16[16,96,128]{2,1,0:T(8,128)(2,1)S(1)} async-done(((bf16[16,96,128]{2,1,0:T(8,128)(2,1)}), bf16[16,96,128]{2,1,0:T(8,128)(2,1)S(1)}, u32[]{:S(2)}, u32[]{:S(2)}) %all-to-all-start.3) | async-done | bytes 393248 | tf_op jit(solution)/shard_map/all_to_all | solution.py:41
  89.2 0.9 select_reduce_fusion.2
  90.2 0.2 fusion.31
  90.4 0.5 collective-permute-start.1
  90.9 0.8 collective-permute-done.1
  91.7 12.0 %all_to_all.45 = f32[8,48,128]{2,1,0:T(8,128)S(1)} all-to-all(f32[8,48,128]{2,1,0:T(8,128)S(1)} %broadcast_in_dim.102), channel_id=1, replica_groups=mesh['sub'=8,'row'=2,'col'=16] {'sub'}, dimensions={0} | all-to-all | bytes 393216 | tf_op jit(solution)/shard_map/all_to_all | solution.py:41
  103.8 2.0 %collective-permute-start.2 = (f32[48,128]{1,0:T(8,128)S(1)}, f32[48,128]{1,0:T(8,128)S(1)}, u32[]{:S(2)}, u32[]{:S(2)}) collective-permute-start(f32[48,128]{1,0:T(8,128)S(1)} %reduce_sum.70), channel_id=1, source_target_pairs={{0,16},{16,0},{1,17},{17,1},{2,18},{18,2},{3,19},{19,3},{4,20},{20... | collective-permute-start | bytes 73736 | tf_op jit(solution)/shard_map/ppermute | solution.py:107
  105.8 0.8 collective-permute-done.2
  106.7 0.6 fusion.28
  107.3 0.1 broadcast_in_dim.103
  107.3 12.3 %all_to_all.46 = bf16[16,96,128]{2,1,0:T(8,128)(2,1)S(1)} all-to-all(bf16[16,96,128]{2,1,0:T(8,128)(2,1)S(1)} %broadcast_in_dim.103), channel_id=1, replica_groups=mesh['sub'=8,'row'=2,'col'=16] {'col'}, dimensions={0} | all-to-all | bytes 786432 | tf_op jit(solution)/shard_map/all_to_all | solution.py:41
  119.7 0.3 convolution_subtract_fusion
  120.0 0.6 fusion.9
  120.6 0.9 bitcast_convert_fusion.1
  121.5 3.6 %all-to-all-start.6 = ((bf16[16,128,128]{1,2,0:T(8,128)(2,1)}), bf16[16,128,128]{1,2,0:T(8,128)(2,1)S(1)}, u32[]{:S(2)}, u32[]{:S(2)}) async-start(bf16[16,128,128]{1,2,0:T(8,128)(2,1)} %bitcast_convert_fusion.1), calls=%async_computation.6 | async-start | bytes 1048576 | tf_op jit(solution)/shard_map/all_to_all | solution.py:34
  125.1 0.2 copy.40
  125.3 0.1 constant_dynamic-slice_fusion.1
  125.3 9.8 %all-to-all-done.6 = bf16[16,128,128]{1,2,0:T(8,128)(2,1)S(1)} async-done(((bf16[16,128,128]{1,2,0:T(8,128)(2,1)}), bf16[16,128,128]{1,2,0:T(8,128)(2,1)S(1)}, u32[]{:S(2)}, u32[]{:S(2)}) %all-to-all-start.6) | async-done | bytes 524320 | tf_op jit(solution)/shard_map/all_to_all | solution.py:34
  135.2 0.2 select_reduce_fusion.1
  135.3 0.0 copy-start.5
  135.4 0.1 copy.29
  135.5 0.9 broadcast_in_dim.106
  136.4 3.6 %all-to-all-start.7 = ((bf16[16,128,128]{2,1,0:T(8,128)(2,1)}), bf16[16,128,128]{2,1,0:T(8,128)(2,1)S(1)}, u32[]{:S(2)}, u32[]{:S(2)}) async-start(bf16[16,128,128]{2,1,0:T(8,128)(2,1)} %broadcast_in_dim.106), calls=%async_computation.7 | async-start | bytes 1048576 | tf_op jit(solution)/shard_map/all_to_all | solution.py:41
  140.0 9.3 %all-to-all-done.7 = bf16[16,128,128]{2,1,0:T(8,128)(2,1)S(1)} async-done(((bf16[16,128,128]{2,1,0:T(8,128)(2,1)}), bf16[16,128,128]{2,1,0:T(8,128)(2,1)S(1)}, u32[]{:S(2)}, u32[]{:S(2)}) %all-to-all-start.7) | async-done | bytes 524320 | tf_op jit(solution)/shard_map/all_to_all | solution.py:41
  149.2 0.3 fusion.14
  149.5 4.7 %all-gather = f32[256,128]{1,0:T(8,128)S(1)} all-gather(f32[128,128]{1,0:T(8,128)S(1)} %fusion.14), channel_id=2, replica_groups=mesh['sub'=8,'row'=2,'col'=16] {'row'}, dimensions={0}, use_global_device_ids=true | all-gather | bytes 196608 | tf_op jit(solution)/shard_map/all_gather | solution.py:116
  154.3 0.6 fusion.7
  154.9 0.9 bitcast_convert_fusion
  155.8 3.6 %all-to-all-start.8 = ((bf16[16,128,128]{1,2,0:T(8,128)(2,1)}), bf16[16,128,128]{1,2,0:T(8,128)(2,1)S(1)}, u32[]{:S(2)}, u32[]{:S(2)}) async-start(bf16[16,128,128]{1,2,0:T(8,128)(2,1)} %bitcast_convert_fusion), calls=%async_computation.8 | async-start | bytes 1048576 | tf_op jit(solution)/shard_map/all_to_all | solution.py:34
  159.4 0.2 copy.41
  159.6 0.1 constant_dynamic-slice_fusion
  159.6 10.7 %all-to-all-done.8 = bf16[16,128,128]{1,2,0:T(8,128)(2,1)S(1)} async-done(((bf16[16,128,128]{1,2,0:T(8,128)(2,1)}), bf16[16,128,128]{1,2,0:T(8,128)(2,1)S(1)}, u32[]{:S(2)}, u32[]{:S(2)}) %all-to-all-start.8) | async-done | bytes 524320 | tf_op jit(solution)/shard_map/all_to_all | solution.py:34
  170.3 0.2 select_reduce_fusion
  170.5 0.7 copy.32
  (20 shorter events, 0.2 us)
Async XLA Ops:
  0.6 1.2 copy-start
  0.6 4.4 %copy-start.6 = (s32[1,16,16]{2,1,0:T(8,128)S(1)}, s32[1,16,16]{2,1,0:T(8,128)}, u32[]{:S(2)}) copy-start(s32[1,16,16]{2,1,0:T(8,128)} %param.9) | copy-start | bytes 3076
  0.7 8.3 %copy-start.4 = (bf16[1,2,128,2048]{3,2,1,0:T(8,128)(2,1)S(1)}, bf16[1,2,128,2048]{3,2,1,0:T(8,128)(2,1)}, u32[]{:S(2)}) copy-start(bf16[1,2,128,2048]{3,2,1,0:T(8,128)(2,1)} %param.8) | copy-start | bytes 3145732
  3.7 5.2 %collective-permute-start = (bf16[128,128]{1,0:T(8,128)(2,1)S(1)}, bf16[128,128]{1,0:T(8,128)(2,1)S(1)}, u32[]{:S(2)}, u32[]{:S(2)}) collective-permute-start(bf16[128,128]{1,0:T(8,128)(2,1)S(1)} %get-tuple-element.12), channel_id=1, source_target_pairs={{0,16},{1,17},{2,18},{3,19},{4,20},{5,21},{6,22},{7,23},{8,24},{9,... | collective-permute-start | bytes 98312 | tf_op jit(solution)/shard_map/ppermute | solution.py:68
  8.9 6.6 %copy-start.1 = (f32[96,1536]{1,0:T(8,128)S(1)}, f32[96,1536]{1,0:T(8,128)}, u32[]{:S(2)}) copy-start(f32[96,1536]{1,0:T(8,128)} %param.13) | copy-start | bytes 1769476
  10.1 16.4 %all-to-all-start = ((bf16[16,128,128]{2,1,0:T(8,128)(2,1)}), bf16[16,128,128]{2,1,0:T(8,128)(2,1)S(1)}, u32[]{:S(2)}, u32[]{:S(2)}) async-start(bf16[16,128,128]{2,1,0:T(8,128)(2,1)} %bitcast.3), calls=%async_computation | async-start | bytes 1048576 | tf_op jit(solution)/shard_map/all_to_all | solution.py:70
  27.7 3.8 %copy-start.7 = (s32[1,1024]{1,0:T(1,128)S(1)}, s32[1,1024]{1,0:T(1,128)}, u32[]{:S(2)}) copy-start(s32[1,1024]{1,0:T(1,128)} %param.12) | copy-start | bytes 12292
  27.7 17.8 %all-to-all-start.1 = ((bf16[16,224,128]{2,1,0:T(8,128)(2,1)}), bf16[16,224,128]{2,1,0:T(8,128)(2,1)S(1)}, u32[]{:S(2)}, u32[]{:S(2)}) async-start(bf16[16,224,128]{2,1,0:T(8,128)(2,1)} %fusion.13), calls=%async_computation.1 | async-start | bytes 1835008 | tf_op jit(solution)/shard_map/all_to_all | solution.py:85
  45.9 0.6 copy-start.2
  47.5 25.8 %all-to-all-start.2 = ((bf16[16,96,128]{2,1,0:T(8,128)(2,1)}), bf16[16,96,128]{2,1,0:T(8,128)(2,1)S(1)}, u32[]{:S(2)}, u32[]{:S(2)}) async-start(bf16[16,96,128]{2,1,0:T(8,128)(2,1)} %bitcast.81), calls=%async_computation.2 | async-start | bytes 786432 | tf_op jit(solution)/shard_map/all_to_all | solution.py:97
  75.6 13.6 %all-to-all-start.3 = ((bf16[16,96,128]{2,1,0:T(8,128)(2,1)}), bf16[16,96,128]{2,1,0:T(8,128)(2,1)S(1)}, u32[]{:S(2)}, u32[]{:S(2)}) async-start(bf16[16,96,128]{2,1,0:T(8,128)(2,1)} %broadcast_in_dim.101), calls=%async_computation.3 | async-start | bytes 786432 | tf_op jit(solution)/shard_map/all_to_all | solution.py:41
  90.4 1.3 collective-permute-start.1
  91.7 27.9 %copy-start.3 = (f32[128,128]{1,0:T(8,128)S(1)}, f32[128,128]{1,0:T(8,128)}, u32[]{:S(2)}) copy-start(f32[128,128]{1,0:T(8,128)} %copy-done.2) | copy-start | bytes 196612
  103.8 2.9 %collective-permute-start.2 = (f32[48,128]{1,0:T(8,128)S(1)}, f32[48,128]{1,0:T(8,128)S(1)}, u32[]{:S(2)}, u32[]{:S(2)}) collective-permute-start(f32[48,128]{1,0:T(8,128)S(1)} %reduce_sum.70), channel_id=1, source_target_pairs={{0,16},{16,0},{1,17},{17,1},{2,18},{18,2},{3,19},{19,3},{4,20},{20... | collective-permute-start | bytes 73736 | tf_op jit(solution)/shard_map/ppermute | solution.py:107
  121.5 13.7 %all-to-all-start.6 = ((bf16[16,128,128]{1,2,0:T(8,128)(2,1)}), bf16[16,128,128]{1,2,0:T(8,128)(2,1)S(1)}, u32[]{:S(2)}, u32[]{:S(2)}) async-start(bf16[16,128,128]{1,2,0:T(8,128)(2,1)} %bitcast_convert_fusion.1), calls=%async_computation.6 | async-start | bytes 1048576 | tf_op jit(solution)/shard_map/all_to_all | solution.py:34
  135.3 13.9 %copy-start.5 = (bf16[1,2,128,2048]{3,2,1,0:T(8,128)(2,1)S(1)}, bf16[1,2,128,2048]{3,2,1,0:T(8,128)(2,1)}, u32[]{:S(2)}) copy-start(bf16[1,2,128,2048]{3,2,1,0:T(8,128)(2,1)} %param.8) | copy-start | bytes 3145732
  136.4 12.9 %all-to-all-start.7 = ((bf16[16,128,128]{2,1,0:T(8,128)(2,1)}), bf16[16,128,128]{2,1,0:T(8,128)(2,1)S(1)}, u32[]{:S(2)}, u32[]{:S(2)}) async-start(bf16[16,128,128]{2,1,0:T(8,128)(2,1)} %broadcast_in_dim.106), calls=%async_computation.7 | async-start | bytes 1048576 | tf_op jit(solution)/shard_map/all_to_all | solution.py:41
  155.8 14.6 %all-to-all-start.8 = ((bf16[16,128,128]{1,2,0:T(8,128)(2,1)}), bf16[16,128,128]{1,2,0:T(8,128)(2,1)S(1)}, u32[]{:S(2)}, u32[]{:S(2)}) async-start(bf16[16,128,128]{1,2,0:T(8,128)(2,1)} %bitcast_convert_fusion), calls=%async_computation.8 | async-start | bytes 1048576 | tf_op jit(solution)/shard_map/all_to_all | solution.py:34

commit v10 on v9

--- a/solution.py
+++ b/solution.py
@@ -58,7 +58,8 @@
     row_id = lax.axis_index("row")
     col_id = lax.axis_index("col")
     sources = right_side.shape[-1]
-    band_id = lax.axis_index(("sub", "row"))
+    band_id = lax.axis_index(("row", "sub"))
+    sub_id = lax.axis_index("sub")
 
     blocks = lax.dynamic_slice(table, (PANEL // BLOCK, col_id // 2), (PANEL // BLOCK, 1))
     lower = factor_cols[0, 0] * jnp.repeat(blocks[:, 0], BLOCK)[None, :].astype(bf16)
@@ -81,10 +82,18 @@
     own_gram = lax.dynamic_index_in_dim(gram, col_id, 0)
     gram = jnp.pad(gram.astype(bf16), ((0, 0), (0, 0), (0, sources - band)))
 
+    chunk = share // 2
+    pairs = [
+        (core * COLS + chip, (chip // 8) * COLS + 2 * (chip % 8) + core)
+        for core in range(2)
+        for chip in range(COLS)
+    ]
+    root_rows = lax.dynamic_slice_in_dim(after(root_right, partial), row_id * chunk, chunk, 0)
+    root_rows = lax.ppermute(root_rows, ("row", "col"), pairs)
     both = jnp.concatenate([jnp.broadcast_to(total[None], (COLS,) + total.shape), gram], 1)
     both = lax.all_to_all(both, "col", 0, 0)
     total = both[:, :width].reshape(PANEL, sources)
-    solved = own - mul(inverse, total.astype(f32), precision=fine)
+    solved = after(own, root_rows) - mul(inverse, total.astype(f32), precision=fine)
     chips = lax.broadcasted_iota(jnp.int32, (COLS, 1, 1), 0)
     gram = jnp.where(chips == col_id, own_gram, both[:, width:, :band].astype(f32)).sum(0)
 
@@ -93,21 +102,25 @@
         onehot, couple, (((1,), (1,)), ((), ())), preferred_element_type=f32
     ).astype(bf16)
 
-    updates = mul(couple_sep, solved.astype(bf16)).astype(bf16).reshape(2 * SUBS, band, sources)
-    updates = lax.all_to_all(updates, ("sub", "row"), 0, 0).astype(f32).sum(0)
-    here = (band_id == col_id).astype(f32)
-    low = (here * root_right - updates).astype(bf16)
-    rhs = jnp.where(chips == col_id, here * root_right - updates, gather(low, "col", COLS)).sum(0)
-    applied = mul(gram, rhs, precision=fine)
-    half = share // 2
-    kept = lax.dynamic_slice_in_dim(applied, row_id * half, half, 0)
-    sent = lax.dynamic_slice_in_dim(applied, (1 - row_id) * half, half, 0)
-    swap = [(0, 1), (1, 0)]
-    kept = gather(kept + lax.ppermute(sent, "row", swap), "sub", SUBS).sum(0)
-    other = lax.ppermute(kept, "row", swap)
-    root_part = jnp.where(
-        row_id == 0, jnp.concatenate([kept, other], 0), jnp.concatenate([other, kept], 0)
-    )
+    gram = gram.T
+    for step in (1, 2, 4):
+        if step == 2:
+            gram_pair = gram
+        if step == 4:
+            root_rows = after(root_rows, gram)
+        other = lax.ppermute(gram, "sub", [(i, i ^ step) for i in range(SUBS)])
+        gram = jnp.where(
+            sub_id & step == 0,
+            jnp.concatenate([gram, other], 0),
+            jnp.concatenate([other, gram], 0),
+        )
+
+    updates = mul(couple_sep, solved.astype(bf16)).astype(bf16).reshape(2 * COLS, chunk, sources)
+    updates = after(lax.all_to_all(updates, ("row", "col"), 0, 0), gram_pair)
+    updates = updates.astype(f32).sum(0)
+    updates = gather(updates, "sub", SUBS).sum(0)
+    rhs = gather(root_rows - updates, "col", COLS).reshape(SEPARATOR // 2, sources)
+    root_part = lax.all_gather(mul_t(gram, rhs, precision=fine), "row").sum(0)
     root_full = gather(root_part.astype(bf16), "col", COLS).reshape(SEPARATOR, sources)
     value = solved - mul_t(couple_sep, root_full)
 

time: 172 us -> 172 us (level)
  starting transfers between devices: 38.6 us -> 53.7 us
  waiting for transfers between devices: 81.3 us -> 72.1 us
  blocking collectives: 29 us -> 24.6 us
  other arithmetic: 4.99 us -> 2.25 us
    ppermute x2 -> x4, waiting for transfers between devices: 1.7 us -> 23 us  [the longest x3 15.9 us: shards(): other = lax.ppermute(gram, 'sub', [(i, i ^ step) for i in range(SUBS)])]
    all_to_all x1, waiting for transfers between devices: 11.8 us -> 0.01 us  [shards(): both = lax.all_to_all(both, 'col', 0, 0)]
    ppermute x2 -> x4, starting transfers between devices: 2.52 us -> 12.8 us  [the longest x3 7.93 us: shards(): other = lax.ppermute(gram, 'sub', [(i, i ^ step) for i in range(SUBS)])]
    all_to_all x2 -> x3, starting transfers between devices: 7.12 us -> 17 us  [gather(): return lax.all_to_all(spread, axes, 0, 0)]
    all_to_all x2 -> x3, waiting for transfers between devices: 19.1 us -> 9.27 us  [gather(): return lax.all_to_all(spread, axes, 0, 0)]
    all_to_all x1, waiting for transfers between devices: 14.5 us -> 5.64 us  [shards(): updates = after(lax.all_to_all(updates, ('row', 'col'), 0, 0), gram_pair)]
    all_to_all x2 -> x1, blocking collectives: 24.3 us -> 15.4 us  [gather(): return lax.all_to_all(spread, axes, 0, 0)]
    all_to_all x1, starting transfers between devices: 11.3 us -> 6.16 us  [shards(): updates = after(lax.all_to_all(updates, ('row', 'col'), 0, 0), gram_pair)]
  transfers between devices with their start and end apart: 10 -> 13, of which waited for: 10 -> 10; matrix products, arithmetic and copies ran while one was open for 2% -> 2% of each run, Pallas kernels for 0% -> 0%
where the time goes in v10:
time: 172 us; the launch traced here: 171 us
  waiting for transfers between devices  72.1 us (42%)
  starting transfers between devices  53.7 us (31%)
  blocking collectives  24.6 us (14%)
  matrix products  9.47 us (6%)
  local copies, waits for them, and re-layouts  8.22 us (5%)
  other arithmetic  2.25 us (1%)
    all_to_all x2, waiting for transfers between devices, sum_scatter(): others = lax.all_to_all(parts.astype(bf16), axes, 0, 0).astype(f32)  20.5 us
    all_to_all x3, starting transfers between devices, gather(): return lax.all_to_all(spread, axes, 0, 0)  17 us
    ppermute x3, waiting for transfers between devices, shards(): other = lax.ppermute(gram, 'sub', [(i, i ^ step) for i in range(SUBS)])  15.9 us
    all_to_all x1, blocking collectives, gather(): return lax.all_to_all(spread, axes, 0, 0)  15.4 us
    all_to_all x1, waiting for transfers between devices, shards(): total = lax.all_to_all(partial.reshape(COLS, width, sources), 'col', 0, 0)  9.98 us
    all_to_all x3, waiting for transfers between devices, gather(): return lax.all_to_all(spread, axes, 0, 0)  9.27 us
    ppermute x3, starting transfers between devices, shards(): other = lax.ppermute(gram, 'sub', [(i, i ^ step) for i in range(SUBS)])  7.93 us
    all_to_all x2, starting transfers between devices, sum_scatter(): others = lax.all_to_all(parts.astype(bf16), axes, 0, 0).astype(f32)  7.14 us
  transfers between devices with their start and end apart: 13, of which 10 were waited for; matrix products, arithmetic and copies ran while one was open for 2% of the time, Pallas kernels for 0%

profile of v10, /device:TPU:1, one launch (start us, length us, event | category | flops | bytes accessed | tf_op | source)
XLA Modules:
  0.0 171.4 jit_solution(2917971602871776407)
XLA Ops:
  0.7 1.2 copy-done
  1.9 1.8 %fusion.35 = (bf16[128,128]{1,0:T(8,128)(2,1)S(1)}, f32[128,128]{1,0:T(8,128)S(1)}) fusion(f32[1,2048,128]{2,1,0:T(8,128)} %param.14, f32[1,128,2048]{2,1,0:T(8,128)S(1)} %copy-done), kind=kOutput, calls=%fused_computation.60 | convolution fusion | flops 201342976 | bytes 2195456 | tf_op jit(solution)/shard_map/dot_general | solution.py:19
  3.7 1.3 collective-permute-start
  5.0 0.2 fusion.32
  5.2 0.1 broadcast_bitcast_fusion
  5.3 3.6 %collective-permute-done = bf16[128,128]{1,0:T(8,128)(2,1)S(1)} collective-permute-done((bf16[128,128]{1,0:T(8,128)(2,1)S(1)}, bf16[128,128]{1,0:T(8,128)(2,1)S(1)}, u32[]{:S(2)}, u32[]{:S(2)}) %collective-permute-start) | collective-permute-done | bytes 32800 | tf_op jit(solution)/shard_map/ppermute | solution.py:69
  8.9 1.1 convolution_convert_fusion.1
  10.1 5.5 %all-to-all-start = ((bf16[16,128,128]{2,1,0:T(8,128)(2,1)}), bf16[16,128,128]{2,1,0:T(8,128)(2,1)S(1)}, u32[]{:S(2)}, u32[]{:S(2)}) async-start(bf16[16,128,128]{2,1,0:T(8,128)(2,1)} %bitcast.3), calls=%async_computation | async-start | bytes 1048576 | tf_op jit(solution)/shard_map/all_to_all | solution.py:71
  15.6 0.8 fusion.28
  16.4 0.1 convert_element_type.79
  16.5 10.0 %all-to-all-done = bf16[16,128,128]{2,1,0:T(8,128)(2,1)S(1)} async-done(((bf16[16,128,128]{2,1,0:T(8,128)(2,1)}), bf16[16,128,128]{2,1,0:T(8,128)(2,1)S(1)}, u32[]{:S(2)}, u32[]{:S(2)}) %all-to-all-start) | async-done | bytes 524320 | tf_op jit(solution)/shard_map/all_to_all | solution.py:71
  26.4 0.1 reduce_sum.66
  26.5 0.1 broadcast_in_dim.83
  26.6 1.0 fusion.12
  27.7 3.8 %all-to-all-start.1 = ((bf16[16,224,128]{2,1,0:T(8,128)(2,1)}), bf16[16,224,128]{2,1,0:T(8,128)(2,1)S(1)}, u32[]{:S(2)}, u32[]{:S(2)}) async-start(bf16[16,224,128]{2,1,0:T(8,128)(2,1)} %fusion.12), calls=%async_computation.1 | async-start | bytes 1835008 | tf_op jit(solution)/shard_map/all_to_all | solution.py:94
  31.5 2.1 %fusion.2 = bf16[1536,128]{1,0:T(8,128)(2,1)S(1)} fusion(s32[1024]{0:T(1024)S(1)} %bitcast.93, bf16[1,1,128,1024]{3,2,1,0:T(8,128)(2,1)} %param.11), kind=kOutput, calls=%fused_computation.3 | convolution fusion | flops 404422656 | bytes 659456 | tf_op jit(solution)/shard_map/dot_general | solution.py:101
  33.6 4.9 %collective-permute-start.1 = (f32[48,128]{1,0:T(8,128)S(1)}, f32[48,128]{1,0:T(8,128)S(1)}, u32[]{:S(2)}, u32[]{:S(2)}) collective-permute-start(f32[48,128]{1,0:T(8,128)S(1)} %constant_dynamic-slice_fusion.2), channel_id=1, source_target_pairs={{0,0},{1,2},{2,4},{3,6},{4,8},{5,10},{6,12},{7,14},{8,16},{9,18},{... | collective-permute-start | bytes 73736 | tf_op jit(solution)/shard_map/ppermute | solution.py:92
  38.6 7.1 %collective-permute-done.1 = f32[48,128]{1,0:T(8,128)S(1)} collective-permute-done((f32[48,128]{1,0:T(8,128)S(1)}, f32[48,128]{1,0:T(8,128)S(1)}, u32[]{:S(2)}, u32[]{:S(2)}) %collective-permute-start.1) | collective-permute-done | bytes 24608 | tf_op jit(solution)/shard_map/ppermute | solution.py:92
  45.7 0.5 copy-done.7
  46.3 0.4 convolution_bitcast_fusion
  46.8 0.6 copy-done.2
  47.4 1.0 convolution_convert_fusion
  48.4 6.2 %all-to-all-start.2 = ((bf16[32,48,128]{2,1,0:T(8,128)(2,1)}), bf16[32,48,128]{2,1,0:T(8,128)(2,1)S(1)}, u32[]{:S(2)}, u32[]{:S(2)}) async-start(bf16[32,48,128]{2,1,0:T(8,128)(2,1)} %bitcast.82), calls=%async_computation.2 | async-start | bytes 786432 | tf_op jit(solution)/shard_map/all_to_all | solution.py:119
  54.6 0.2 select_reduce_fusion.2
  54.8 1.7 %collective-permute-start.2 = (f32[96,96]{0,1:T(8,128)S(1)}, f32[96,96]{0,1:T(8,128)S(1)}, u32[]{:S(2)}, u32[]{:S(2)}) collective-permute-start(f32[96,96]{0,1:T(8,128)S(1)} %bitcast.89), channel_id=1, source_target_pairs={{0,32},{32,0},{64,96},{96,64},{128,160},{160,128},{192,224},{224,1... | collective-permute-start | bytes 110600 | tf_op jit(solution)/shard_map/ppermute | solution.py:111
  56.5 1.9 %collective-permute-done.2 = f32[96,96]{0,1:T(8,128)S(1)} collective-permute-done((f32[96,96]{0,1:T(8,128)S(1)}, f32[96,96]{0,1:T(8,128)S(1)}, u32[]{:S(2)}, u32[]{:S(2)}) %collective-permute-start.2) | collective-permute-done | bytes 36896 | tf_op jit(solution)/shard_map/ppermute | solution.py:111
  58.3 0.1 maximum_select_fusion.3
  58.5 5.6 %all-to-all-done.2 = bf16[32,48,128]{2,1,0:T(8,128)(2,1)S(1)} async-done(((bf16[32,48,128]{2,1,0:T(8,128)(2,1)}), bf16[32,48,128]{2,1,0:T(8,128)(2,1)S(1)}, u32[]{:S(2)}, u32[]{:S(2)}) %all-to-all-start.2) | async-done | bytes 393248 | tf_op jit(solution)/shard_map/all_to_all | solution.py:119
  64.1 0.1 convert_reduce_fusion
  64.2 0.7 broadcast_in_dim.87
  64.8 8.2 %all-to-all-start.3 = ((f32[8,48,128]{2,1,0:T(8,128)}), f32[8,48,128]{2,1,0:T(8,128)S(1)}, u32[]{:S(2)}, u32[]{:S(2)}) async-start(f32[8,48,128]{2,1,0:T(8,128)} %broadcast_in_dim.87), calls=%async_computation.3 | async-start | bytes 393216 | tf_op jit(solution)/shard_map/all_to_all | solution.py:41
  73.0 2.4 %collective-permute-start.3 = (f32[192,96]{0,1:T(8,128)S(1)}, f32[192,96]{0,1:T(8,128)S(1)}, u32[]{:S(2)}, u32[]{:S(2)}) collective-permute-start(f32[192,96]{0,1:T(8,128)S(1)} %maximum_select_fusion.3), channel_id=1, source_target_pairs={{0,64},{32,96},{64,0},{96,32},{128,192},{160,224},{192,128},{224,1... | collective-permute-start | bytes 221192 | tf_op jit(solution)/shard_map/ppermute | solution.py:111
  75.4 7.5 %collective-permute-done.3 = f32[192,96]{0,1:T(8,128)S(1)} collective-permute-done((f32[192,96]{0,1:T(8,128)S(1)}, f32[192,96]{0,1:T(8,128)S(1)}, u32[]{:S(2)}, u32[]{:S(2)}) %collective-permute-start.3) | collective-permute-done | bytes 73760 | tf_op jit(solution)/shard_map/ppermute | solution.py:111
  82.8 0.1 maximum_select_fusion.2
  83.0 0.8 broadcast_in_dim.88
  83.8 5.3 %all-to-all-start.4 = ((f32[16,48,128]{2,1,0:T(8,128)}), f32[16,48,128]{2,1,0:T(8,128)S(1)}, u32[]{:S(2)}, u32[]{:S(2)}) async-start(f32[16,48,128]{2,1,0:T(8,128)} %broadcast_in_dim.88), calls=%async_computation.4 | async-start | bytes 786432 | tf_op jit(solution)/shard_map/all_to_all | solution.py:41
  89.1 3.8 %collective-permute-start.4 = (f32[384,96]{0,1:T(8,128)S(1)}, f32[384,96]{0,1:T(8,128)S(1)}, u32[]{:S(2)}, u32[]{:S(2)}) collective-permute-start(f32[384,96]{0,1:T(8,128)S(1)} %maximum_select_fusion.2), channel_id=1, source_target_pairs={{0,128},{32,160},{64,192},{96,224},{128,0},{160,32},{192,64},{224,... | collective-permute-start | bytes 442376 | tf_op jit(solution)/shard_map/ppermute | solution.py:111
  92.9 6.6 %collective-permute-done.4 = f32[384,96]{0,1:T(8,128)S(1)} collective-permute-done((f32[384,96]{0,1:T(8,128)S(1)}, f32[384,96]{0,1:T(8,128)S(1)}, u32[]{:S(2)}, u32[]{:S(2)}) %collective-permute-start.4) | collective-permute-done | bytes 147488 | tf_op jit(solution)/shard_map/ppermute | solution.py:111
  99.5 0.3 fusion.18
  99.8 4.4 %all-gather = f32[192,128]{1,0:T(8,128)S(1)} all-gather(f32[96,128]{1,0:T(8,128)S(1)} %fusion.18), channel_id=2, replica_groups=mesh['sub'=8,'row'=2,'col'=16] {'row'}, dimensions={0}, use_global_device_ids=true | all-gather | bytes 147456 | tf_op jit(solution)/shard_map/all_gather | solution.py:123
  104.3 0.1 broadcast_in_dim.89
  104.3 15.4 %all_to_all.45 = bf16[16,96,128]{2,1,0:T(8,128)(2,1)S(1)} all-to-all(bf16[16,96,128]{2,1,0:T(8,128)(2,1)S(1)} %broadcast_in_dim.89), channel_id=1, replica_groups=mesh['sub'=8,'row'=2,'col'=16] {'col'}, dimensions={0} | all-to-all | bytes 786432 | tf_op jit(solution)/shard_map/all_to_all | solution.py:41
  119.8 0.3 convolution_subtract_fusion
  120.1 0.6 fusion.8
  120.7 0.9 bitcast_convert_fusion.1
  121.6 3.6 %all-to-all-start.6 = ((bf16[16,128,128]{1,2,0:T(8,128)(2,1)}), bf16[16,128,128]{1,2,0:T(8,128)(2,1)S(1)}, u32[]{:S(2)}, u32[]{:S(2)}) async-start(bf16[16,128,128]{1,2,0:T(8,128)(2,1)} %bitcast_convert_fusion.1), calls=%async_computation.6 | async-start | bytes 1048576 | tf_op jit(solution)/shard_map/all_to_all | solution.py:34
  125.2 0.2 copy.40
  125.4 0.1 constant_dynamic-slice_fusion.1
  125.5 9.8 %all-to-all-done.6 = bf16[16,128,128]{1,2,0:T(8,128)(2,1)S(1)} async-done(((bf16[16,128,128]{1,2,0:T(8,128)(2,1)}), bf16[16,128,128]{1,2,0:T(8,128)(2,1)S(1)}, u32[]{:S(2)}, u32[]{:S(2)}) %all-to-all-start.6) | async-done | bytes 524320 | tf_op jit(solution)/shard_map/all_to_all | solution.py:34
  135.3 0.2 select_reduce_fusion.1
  135.5 0.1 copy.29
  135.6 0.9 broadcast_in_dim.92
  136.5 3.6 %all-to-all-start.7 = ((bf16[16,128,128]{2,1,0:T(8,128)(2,1)}), bf16[16,128,128]{2,1,0:T(8,128)(2,1)S(1)}, u32[]{:S(2)}, u32[]{:S(2)}) async-start(bf16[16,128,128]{2,1,0:T(8,128)(2,1)} %broadcast_in_dim.92), calls=%async_computation.7 | async-start | bytes 1048576 | tf_op jit(solution)/shard_map/all_to_all | solution.py:41
  140.1 9.3 %all-to-all-done.7 = bf16[16,128,128]{2,1,0:T(8,128)(2,1)S(1)} async-done(((bf16[16,128,128]{2,1,0:T(8,128)(2,1)}), bf16[16,128,128]{2,1,0:T(8,128)(2,1)S(1)}, u32[]{:S(2)}, u32[]{:S(2)}) %all-to-all-start.7) | async-done | bytes 524320 | tf_op jit(solution)/shard_map/all_to_all | solution.py:41
  149.4 0.3 fusion.13
  149.6 4.7 %all-gather.1 = f32[256,128]{1,0:T(8,128)S(1)} all-gather(f32[128,128]{1,0:T(8,128)S(1)} %fusion.13), channel_id=3, replica_groups=mesh['sub'=8,'row'=2,'col'=16] {'row'}, dimensions={0}, use_global_device_ids=true | all-gather | bytes 196608 | tf_op jit(solution)/shard_map/all_gather | solution.py:129
  154.4 0.6 fusion.6
  155.0 0.9 bitcast_convert_fusion
  155.9 3.6 %all-to-all-start.8 = ((bf16[16,128,128]{1,2,0:T(8,128)(2,1)}), bf16[16,128,128]{1,2,0:T(8,128)(2,1)S(1)}, u32[]{:S(2)}, u32[]{:S(2)}) async-start(bf16[16,128,128]{1,2,0:T(8,128)(2,1)} %bitcast_convert_fusion), calls=%async_computation.8 | async-start | bytes 1048576 | tf_op jit(solution)/shard_map/all_to_all | solution.py:34
  159.5 0.2 copy.41
  159.7 0.1 constant_dynamic-slice_fusion
  159.7 10.7 %all-to-all-done.8 = bf16[16,128,128]{1,2,0:T(8,128)(2,1)S(1)} async-done(((bf16[16,128,128]{1,2,0:T(8,128)(2,1)}), bf16[16,128,128]{1,2,0:T(8,128)(2,1)S(1)}, u32[]{:S(2)}, u32[]{:S(2)}) %all-to-all-start.8) | async-done | bytes 524320 | tf_op jit(solution)/shard_map/all_to_all | solution.py:34
  170.4 0.2 select_reduce_fusion
  170.6 0.7 copy.32
  (36 shorter events, 0.2 us)
Async XLA Ops:
  0.6 1.2 copy-start
  0.6 4.4 %copy-start.10 = (s32[1,16,16]{2,1,0:T(8,128)S(1)}, s32[1,16,16]{2,1,0:T(8,128)}, u32[]{:S(2)}) copy-start(s32[1,16,16]{2,1,0:T(8,128)} %param.9) | copy-start | bytes 3076
  0.7 8.3 %copy-start.4 = (bf16[1,2,128,2048]{3,2,1,0:T(8,128)(2,1)S(1)}, bf16[1,2,128,2048]{3,2,1,0:T(8,128)(2,1)}, u32[]{:S(2)}) copy-start(bf16[1,2,128,2048]{3,2,1,0:T(8,128)(2,1)} %param.8) | copy-start | bytes 3145732
  3.7 5.2 %collective-permute-start = (bf16[128,128]{1,0:T(8,128)(2,1)S(1)}, bf16[128,128]{1,0:T(8,128)(2,1)S(1)}, u32[]{:S(2)}, u32[]{:S(2)}) collective-permute-start(bf16[128,128]{1,0:T(8,128)(2,1)S(1)} %get-tuple-element.16), channel_id=1, source_target_pairs={{0,16},{1,17},{2,18},{3,19},{4,20},{5,21},{6,22},{7,23},{8,24},{9,... | collective-permute-start | bytes 98312 | tf_op jit(solution)/shard_map/ppermute | solution.py:69
  8.9 6.6 %copy-start.1 = (f32[96,1536]{1,0:T(8,128)S(1)}, f32[96,1536]{1,0:T(8,128)}, u32[]{:S(2)}) copy-start(f32[96,1536]{1,0:T(8,128)} %param.13) | copy-start | bytes 1769476
  10.1 16.4 %all-to-all-start = ((bf16[16,128,128]{2,1,0:T(8,128)(2,1)}), bf16[16,128,128]{2,1,0:T(8,128)(2,1)S(1)}, u32[]{:S(2)}, u32[]{:S(2)}) async-start(bf16[16,128,128]{2,1,0:T(8,128)(2,1)} %bitcast.3), calls=%async_computation | async-start | bytes 1048576 | tf_op jit(solution)/shard_map/all_to_all | solution.py:71
  27.7 3.8 %copy-start.11 = (s32[1,1024]{1,0:T(1,128)S(1)}, s32[1,1024]{1,0:T(1,128)}, u32[]{:S(2)}) copy-start(s32[1,1024]{1,0:T(1,128)} %param.12) | copy-start | bytes 12292
  27.7 18.0 %all-to-all-start.1 = ((bf16[16,224,128]{2,1,0:T(8,128)(2,1)}), bf16[16,224,128]{2,1,0:T(8,128)(2,1)S(1)}, u32[]{:S(2)}, u32[]{:S(2)}) async-start(bf16[16,224,128]{2,1,0:T(8,128)(2,1)} %fusion.12), calls=%async_computation.1 | async-start | bytes 1835008 | tf_op jit(solution)/shard_map/all_to_all | solution.py:94
  31.5 2.2 %copy-start.9 = (f32[96,128]{1,0:T(8,128)S(1)}, f32[96,128]{1,0:T(8,128)}, u32[]{:S(2)}) copy-start(f32[96,128]{1,0:T(8,128)} %param.15) | copy-start | bytes 147460
  33.6 12.1 %collective-permute-start.1 = (f32[48,128]{1,0:T(8,128)S(1)}, f32[48,128]{1,0:T(8,128)S(1)}, u32[]{:S(2)}, u32[]{:S(2)}) collective-permute-start(f32[48,128]{1,0:T(8,128)S(1)} %constant_dynamic-slice_fusion.2), channel_id=1, source_target_pairs={{0,0},{1,2},{2,4},{3,6},{4,8},{5,10},{6,12},{7,14},{8,16},{9,18},{... | collective-permute-start | bytes 73736 | tf_op jit(solution)/shard_map/ppermute | solution.py:92
  45.7 0.6 copy-start.7
  46.7 0.6 copy-start.2
  48.4 15.7 %all-to-all-start.2 = ((bf16[32,48,128]{2,1,0:T(8,128)(2,1)}), bf16[32,48,128]{2,1,0:T(8,128)(2,1)S(1)}, u32[]{:S(2)}, u32[]{:S(2)}) async-start(bf16[32,48,128]{2,1,0:T(8,128)(2,1)} %bitcast.82), calls=%async_computation.2 | async-start | bytes 786432 | tf_op jit(solution)/shard_map/all_to_all | solution.py:119
  54.6 28.4 %copy-start.8 = (f32[48,128]{1,0:T(8,128)S(1)}, f32[48,128]{1,0:T(8,128)}, u32[]{:S(2)}) copy-start(f32[48,128]{1,0:T(8,128)} %copy-done.7) | copy-start | bytes 73732
  54.8 3.6 %collective-permute-start.2 = (f32[96,96]{0,1:T(8,128)S(1)}, f32[96,96]{0,1:T(8,128)S(1)}, u32[]{:S(2)}, u32[]{:S(2)}) collective-permute-start(f32[96,96]{0,1:T(8,128)S(1)} %bitcast.89), channel_id=1, source_target_pairs={{0,32},{32,0},{64,96},{96,64},{128,160},{160,128},{192,224},{224,1... | collective-permute-start | bytes 110600 | tf_op jit(solution)/shard_map/ppermute | solution.py:111
  64.8 18.1 %all-to-all-start.3 = ((f32[8,48,128]{2,1,0:T(8,128)}), f32[8,48,128]{2,1,0:T(8,128)S(1)}, u32[]{:S(2)}, u32[]{:S(2)}) async-start(f32[8,48,128]{2,1,0:T(8,128)} %broadcast_in_dim.87), calls=%async_computation.3 | async-start | bytes 393216 | tf_op jit(solution)/shard_map/all_to_all | solution.py:41
  73.0 9.8 %collective-permute-start.3 = (f32[192,96]{0,1:T(8,128)S(1)}, f32[192,96]{0,1:T(8,128)S(1)}, u32[]{:S(2)}, u32[]{:S(2)}) collective-permute-start(f32[192,96]{0,1:T(8,128)S(1)} %maximum_select_fusion.3), channel_id=1, source_target_pairs={{0,64},{32,96},{64,0},{96,32},{128,192},{160,224},{192,128},{224,1... | collective-permute-start | bytes 221192 | tf_op jit(solution)/shard_map/ppermute | solution.py:111
  83.8 15.7 %all-to-all-start.4 = ((f32[16,48,128]{2,1,0:T(8,128)}), f32[16,48,128]{2,1,0:T(8,128)S(1)}, u32[]{:S(2)}, u32[]{:S(2)}) async-start(f32[16,48,128]{2,1,0:T(8,128)} %broadcast_in_dim.88), calls=%async_computation.4 | async-start | bytes 786432 | tf_op jit(solution)/shard_map/all_to_all | solution.py:41
  89.1 10.4 %collective-permute-start.4 = (f32[384,96]{0,1:T(8,128)S(1)}, f32[384,96]{0,1:T(8,128)S(1)}, u32[]{:S(2)}, u32[]{:S(2)}) collective-permute-start(f32[384,96]{0,1:T(8,128)S(1)} %maximum_select_fusion.2), channel_id=1, source_target_pairs={{0,128},{32,160},{64,192},{96,224},{128,0},{160,32},{192,64},{224,... | collective-permute-start | bytes 442376 | tf_op jit(solution)/shard_map/ppermute | solution.py:111
  99.5 20.2 %copy-start.3 = (f32[128,128]{1,0:T(8,128)S(1)}, f32[128,128]{1,0:T(8,128)}, u32[]{:S(2)}) copy-start(f32[128,128]{1,0:T(8,128)} %copy-done.2) | copy-start | bytes 196612
  104.3 15.8 %copy-start.6 = (f32[96,128]{1,0:T(8,128)}, f32[96,128]{1,0:T(8,128)S(1)}, u32[]{:S(2)}) copy-start(f32[96,128]{1,0:T(8,128)S(1)} %reduce_sum.70) | copy-start | bytes 147460
  121.6 13.7 %all-to-all-start.6 = ((bf16[16,128,128]{1,2,0:T(8,128)(2,1)}), bf16[16,128,128]{1,2,0:T(8,128)(2,1)S(1)}, u32[]{:S(2)}, u32[]{:S(2)}) async-start(bf16[16,128,128]{1,2,0:T(8,128)(2,1)} %bitcast_convert_fusion.1), calls=%async_computation.6 | async-start | bytes 1048576 | tf_op jit(solution)/shard_map/all_to_all | solution.py:34
  135.4 13.9 %copy-start.5 = (bf16[1,2,128,2048]{3,2,1,0:T(8,128)(2,1)S(1)}, bf16[1,2,128,2048]{3,2,1,0:T(8,128)(2,1)}, u32[]{:S(2)}) copy-start(bf16[1,2,128,2048]{3,2,1,0:T(8,128)(2,1)} %param.8) | copy-start | bytes 3145732
  136.5 12.9 %all-to-all-start.7 = ((bf16[16,128,128]{2,1,0:T(8,128)(2,1)}), bf16[16,128,128]{2,1,0:T(8,128)(2,1)S(1)}, u32[]{:S(2)}, u32[]{:S(2)}) async-start(bf16[16,128,128]{2,1,0:T(8,128)(2,1)} %broadcast_in_dim.92), calls=%async_computation.7 | async-start | bytes 1048576 | tf_op jit(solution)/shard_map/all_to_all | solution.py:41
  155.9 14.6 %all-to-all-start.8 = ((bf16[16,128,128]{1,2,0:T(8,128)(2,1)}), bf16[16,128,128]{1,2,0:T(8,128)(2,1)S(1)}, u32[]{:S(2)}, u32[]{:S(2)}) async-start(bf16[16,128,128]{1,2,0:T(8,128)(2,1)} %bitcast_convert_fusion), calls=%async_computation.8 | async-start | bytes 1048576 | tf_op jit(solution)/shard_map/all_to_all | solution.py:34

commit v11 on v10

--- a/solution.py
+++ b/solution.py
@@ -58,8 +58,8 @@
     row_id = lax.axis_index("row")
     col_id = lax.axis_index("col")
     sources = right_side.shape[-1]
-    band_id = lax.axis_index(("row", "sub"))
     sub_id = lax.axis_index("sub")
+    band_id = row_id * SUBS + sub_id % 2 * 4 + sub_id // 2 % 2 * 2 + sub_id // 4
 
     blocks = lax.dynamic_slice(table, (PANEL // BLOCK, col_id // 2), (PANEL // BLOCK, 1))
     lower = factor_cols[0, 0] * jnp.repeat(blocks[:, 0], BLOCK)[None, :].astype(bf16)
@@ -89,11 +89,11 @@
         for chip in range(COLS)
     ]
     root_rows = lax.dynamic_slice_in_dim(after(root_right, partial), row_id * chunk, chunk, 0)
-    root_rows = lax.ppermute(root_rows, ("row", "col"), pairs)
+    root_rows = root_rows_sent = lax.ppermute(root_rows, ("row", "col"), pairs)
     both = jnp.concatenate([jnp.broadcast_to(total[None], (COLS,) + total.shape), gram], 1)
     both = lax.all_to_all(both, "col", 0, 0)
     total = both[:, :width].reshape(PANEL, sources)
-    solved = after(own, root_rows) - mul(inverse, total.astype(f32), precision=fine)
+    solved = own - mul(inverse, total.astype(f32), precision=fine)
     chips = lax.broadcasted_iota(jnp.int32, (COLS, 1, 1), 0)
     gram = jnp.where(chips == col_id, own_gram, both[:, width:, :band].astype(f32)).sum(0)
 
@@ -103,10 +103,10 @@
     ).astype(bf16)
 
     gram = gram.T
-    for step in (1, 2, 4):
+    for step in (4, 2, 1):
         if step == 2:
             gram_pair = gram
-        if step == 4:
+        if step == 1:
             root_rows = after(root_rows, gram)
         other = lax.ppermute(gram, "sub", [(i, i ^ step) for i in range(SUBS)])
         gram = jnp.where(
@@ -116,7 +116,7 @@
         )
 
     updates = mul(couple_sep, solved.astype(bf16)).astype(bf16).reshape(2 * COLS, chunk, sources)
-    updates = after(lax.all_to_all(updates, ("row", "col"), 0, 0), gram_pair)
+    updates = after(lax.all_to_all(updates, ("row", "col"), 0, 0), (gram_pair, root_rows_sent))
     updates = updates.astype(f32).sum(0)
     updates = gather(updates, "sub", SUBS).sum(0)
     rhs = gather(root_rows - updates, "col", COLS).reshape(SEPARATOR // 2, sources)

time: 172 us -> 169 us (0.983)
  starting transfers between devices: 53.7 us -> 51.1 us
  blocking collectives: 24.6 us -> 22.3 us
    all_to_all x1, waiting for transfers between devices: 0.01 us -> 11.8 us  [shards(): both = lax.all_to_all(both, 'col', 0, 0)]
    all_to_all x1, waiting for transfers between devices: 5.64 us -> 0.01 us  [shards(): lax.all_to_all(updates, ('row', 'col'), 0, 0)]
    ppermute x3, waiting for transfers between devices: 15.9 us -> 11.4 us  [shards(): other = lax.ppermute(gram, 'sub', [(i, i ^ step) for i in range(SUBS)])]
    ppermute x1, waiting for transfers between devices: 7.13 us -> 2.91 us  [shards(): root_rows = root_rows_sent = lax.ppermute(root_rows, ('row', 'col'), pairs)]
    all_to_all x3, waiting for transfers between devices: 9.27 us -> 13.4 us  [gather(): return lax.all_to_all(spread, axes, 0, 0)]
    all_to_all x1, blocking collectives: 15.4 us -> 12.2 us  [gather(): return lax.all_to_all(spread, axes, 0, 0)]
    all_to_all x3, starting transfers between devices: 17 us -> 14 us  [gather(): return lax.all_to_all(spread, axes, 0, 0)]
    unnamed x29 -> x23, local copies, waits for them, and re-layouts: 3.61 us -> 3.04 us
  transfers between devices with their start and end apart: 13 -> 13, of which waited for: 10 -> 10; matrix products, arithmetic and copies ran while one was open for 2% -> 3% of each run, Pallas kernels for 0% -> 0%
where the time goes in v11:
time: 169 us; the launch traced here: 168 us
  waiting for transfers between devices  73.7 us (44%)
  starting transfers between devices  51.1 us (30%)
  blocking collectives  22.3 us (13%)
  matrix products  9.46 us (6%)
  local copies, waits for them, and re-layouts  8.36 us (5%)
  other arithmetic  2.26 us (1%)
    all_to_all x2, waiting for transfers between devices, sum_scatter(): others = lax.all_to_all(parts.astype(bf16), axes, 0, 0).astype(f32)  20.5 us
    all_to_all x3, starting transfers between devices, gather(): return lax.all_to_all(spread, axes, 0, 0)  14 us
    all_to_all x3, waiting for transfers between devices, gather(): return lax.all_to_all(spread, axes, 0, 0)  13.4 us
    all_to_all x1, blocking collectives, gather(): return lax.all_to_all(spread, axes, 0, 0)  12.2 us
    all_to_all x1, waiting for transfers between devices, shards(): both = lax.all_to_all(both, 'col', 0, 0)  11.8 us
    ppermute x3, waiting for transfers between devices, shards(): other = lax.ppermute(gram, 'sub', [(i, i ^ step) for i in range(SUBS)])  11.4 us
    all_to_all x1, waiting for transfers between devices, shards(): total = lax.all_to_all(partial.reshape(COLS, width, sources), 'col', 0, 0)  9.94 us
    ppermute x3, starting transfers between devices, shards(): other = lax.ppermute(gram, 'sub', [(i, i ^ step) for i in range(SUBS)])  9.36 us
  transfers between devices with their start and end apart: 13, of which 10 were waited for; matrix products, arithmetic and copies ran while one was open for 3% of the time, Pallas kernels for 0%

profile of v11, /device:TPU:1, one launch (start us, length us, event | category | flops | bytes accessed | tf_op | source)
XLA Modules:
  0.0 168.2 jit_solution(7841662208595131265)
XLA Ops:
  0.7 1.2 copy-done
  1.9 1.8 %fusion.36 = (bf16[128,128]{1,0:T(8,128)(2,1)S(1)}, f32[128,128]{1,0:T(8,128)S(1)}) fusion(f32[1,2048,128]{2,1,0:T(8,128)} %param.14, f32[1,128,2048]{2,1,0:T(8,128)S(1)} %copy-done), kind=kOutput, calls=%fused_computation.61 | convolution fusion | flops 201342976 | bytes 2195456 | tf_op jit(solution)/shard_map/dot_general | solution.py:19
  3.7 1.3 collective-permute-start
  5.0 0.2 fusion.33
  5.2 0.1 broadcast_bitcast_fusion
  5.3 3.6 %collective-permute-done = bf16[128,128]{1,0:T(8,128)(2,1)S(1)} collective-permute-done((bf16[128,128]{1,0:T(8,128)(2,1)S(1)}, bf16[128,128]{1,0:T(8,128)(2,1)S(1)}, u32[]{:S(2)}, u32[]{:S(2)}) %collective-permute-start) | collective-permute-done | bytes 32800 | tf_op jit(solution)/shard_map/ppermute | solution.py:69
  8.9 1.1 convolution_convert_fusion.1
  10.1 5.5 %all-to-all-start = ((bf16[16,128,128]{2,1,0:T(8,128)(2,1)}), bf16[16,128,128]{2,1,0:T(8,128)(2,1)S(1)}, u32[]{:S(2)}, u32[]{:S(2)}) async-start(bf16[16,128,128]{2,1,0:T(8,128)(2,1)} %bitcast.3), calls=%async_computation | async-start | bytes 1048576 | tf_op jit(solution)/shard_map/all_to_all | solution.py:71
  15.6 0.8 fusion.29
  16.4 0.1 convert_element_type.79
  16.5 9.9 %all-to-all-done = bf16[16,128,128]{2,1,0:T(8,128)(2,1)S(1)} async-done(((bf16[16,128,128]{2,1,0:T(8,128)(2,1)}), bf16[16,128,128]{2,1,0:T(8,128)(2,1)S(1)}, u32[]{:S(2)}, u32[]{:S(2)}) %all-to-all-start) | async-done | bytes 524320 | tf_op jit(solution)/shard_map/all_to_all | solution.py:71
  26.4 0.1 reduce_sum.66
  26.5 0.1 broadcast_in_dim.83
  26.6 1.1 fusion.13
  27.7 3.8 %all-to-all-start.1 = ((bf16[16,224,128]{2,1,0:T(8,128)(2,1)}), bf16[16,224,128]{2,1,0:T(8,128)(2,1)S(1)}, u32[]{:S(2)}, u32[]{:S(2)}) async-start(bf16[16,224,128]{2,1,0:T(8,128)(2,1)} %fusion.13), calls=%async_computation.1 | async-start | bytes 1835008 | tf_op jit(solution)/shard_map/all_to_all | solution.py:94
  31.5 2.1 %fusion.2 = bf16[1536,128]{1,0:T(8,128)(2,1)S(1)} fusion(s32[1024]{0:T(1024)S(1)} %bitcast.95, bf16[1,1,128,1024]{3,2,1,0:T(8,128)(2,1)} %param.11), kind=kOutput, calls=%fused_computation.3 | convolution fusion | flops 404422656 | bytes 659456 | tf_op jit(solution)/shard_map/dot_general | solution.py:101
  33.6 11.8 %all-to-all-done.1 = bf16[16,224,128]{2,1,0:T(8,128)(2,1)S(1)} async-done(((bf16[16,224,128]{2,1,0:T(8,128)(2,1)}), bf16[16,224,128]{2,1,0:T(8,128)(2,1)S(1)}, u32[]{:S(2)}, u32[]{:S(2)}) %all-to-all-start.1) | async-done | bytes 917536 | tf_op jit(solution)/shard_map/all_to_all | solution.py:94
  45.5 0.4 fusion.4
  45.9 0.6 copy-done.2
  46.6 1.0 convolution_convert_fusion
  47.6 6.4 %all-to-all-start.2 = ((bf16[32,48,128]{2,1,0:T(8,128)(2,1)}), bf16[32,48,128]{2,1,0:T(8,128)(2,1)S(1)}, u32[]{:S(2)}, u32[]{:S(2)}) async-start(bf16[32,48,128]{2,1,0:T(8,128)(2,1)} %bitcast.84), calls=%async_computation.2 | async-start | bytes 786432 | tf_op jit(solution)/shard_map/all_to_all | solution.py:119
  54.0 0.2 select_reduce_fusion.2
  54.2 7.0 %collective-permute-start.1 = (f32[96,96]{0,1:T(8,128)S(1)}, f32[96,96]{0,1:T(8,128)S(1)}, u32[]{:S(2)}, u32[]{:S(2)}) collective-permute-start(f32[96,96]{0,1:T(8,128)S(1)} %bitcast.91), channel_id=1, source_target_pairs={{0,128},{32,160},{64,192},{96,224},{128,0},{160,32},{192,64},{224,... | collective-permute-start | bytes 110600 | tf_op jit(solution)/shard_map/ppermute | solution.py:111
  61.2 0.7 constant_dynamic-slice_fusion.2
  61.9 3.7 %collective-permute-start.4 = (f32[48,128]{1,0:T(8,128)S(1)}, f32[48,128]{1,0:T(8,128)S(1)}, u32[]{:S(2)}, u32[]{:S(2)}) collective-permute-start(f32[48,128]{1,0:T(8,128)S(1)} %constant_dynamic-slice_fusion.2), channel_id=1, source_target_pairs={{0,0},{1,2},{2,4},{3,6},{4,8},{5,10},{6,12},{7,14},{8,16},{9,18},{... | collective-permute-start | bytes 73736 | tf_op jit(solution)/shard_map/ppermute | solution.py:92
  65.6 0.1 maximum_select_fusion.3
  65.8 2.9 %collective-permute-done.4 = f32[48,128]{1,0:T(8,128)S(1)} collective-permute-done((f32[48,128]{1,0:T(8,128)S(1)}, f32[48,128]{1,0:T(8,128)S(1)}, u32[]{:S(2)}, u32[]{:S(2)}) %collective-permute-start.4) | collective-permute-done | bytes 24608 | tf_op jit(solution)/shard_map/ppermute | solution.py:92
  68.7 0.1 convert_reduce_fusion
  68.7 0.7 broadcast_in_dim.87
  69.4 3.4 %all-to-all-start.3 = ((f32[8,48,128]{2,1,0:T(8,128)}), f32[8,48,128]{2,1,0:T(8,128)S(1)}, u32[]{:S(2)}, u32[]{:S(2)}) async-start(f32[8,48,128]{2,1,0:T(8,128)} %broadcast_in_dim.87), calls=%async_computation.3 | async-start | bytes 393216 | tf_op jit(solution)/shard_map/all_to_all | solution.py:41
  72.8 2.3 %collective-permute-start.2 = (f32[192,96]{0,1:T(8,128)S(1)}, f32[192,96]{0,1:T(8,128)S(1)}, u32[]{:S(2)}, u32[]{:S(2)}) collective-permute-start(f32[192,96]{0,1:T(8,128)S(1)} %maximum_select_fusion.3), channel_id=1, source_target_pairs={{0,64},{32,96},{64,0},{96,32},{128,192},{160,224},{192,128},{224,1... | collective-permute-start | bytes 221192 | tf_op jit(solution)/shard_map/ppermute | solution.py:111
  75.1 7.5 %collective-permute-done.2 = f32[192,96]{0,1:T(8,128)S(1)} collective-permute-done((f32[192,96]{0,1:T(8,128)S(1)}, f32[192,96]{0,1:T(8,128)S(1)}, u32[]{:S(2)}, u32[]{:S(2)}) %collective-permute-start.2) | collective-permute-done | bytes 73760 | tf_op jit(solution)/shard_map/ppermute | solution.py:111
  82.5 0.1 maximum_select_fusion.2
  82.7 0.8 broadcast_in_dim.88
  83.5 7.0 %all-to-all-start.4 = ((f32[16,48,128]{2,1,0:T(8,128)}), f32[16,48,128]{2,1,0:T(8,128)S(1)}, u32[]{:S(2)}, u32[]{:S(2)}) async-start(f32[16,48,128]{2,1,0:T(8,128)} %broadcast_in_dim.88), calls=%async_computation.4 | async-start | bytes 786432 | tf_op jit(solution)/shard_map/all_to_all | solution.py:41
  90.5 0.1 collective-permute-start.3
  90.6 4.0 %collective-permute-done.3 = f32[384,96]{0,1:T(8,128)S(1)} collective-permute-done((f32[384,96]{0,1:T(8,128)S(1)}, f32[384,96]{0,1:T(8,128)S(1)}, u32[]{:S(2)}, u32[]{:S(2)}) %collective-permute-start.3) | collective-permute-done | bytes 147488 | tf_op jit(solution)/shard_map/ppermute | solution.py:111
  94.6 4.2 %all-to-all-done.4 = f32[16,48,128]{2,1,0:T(8,128)S(1)} async-done(((f32[16,48,128]{2,1,0:T(8,128)}), f32[16,48,128]{2,1,0:T(8,128)S(1)}, u32[]{:S(2)}, u32[]{:S(2)}) %all-to-all-start.4) | async-done | bytes 393248 | tf_op jit(solution)/shard_map/all_to_all | solution.py:41
  98.7 0.3 fusion.19
  99.0 5.4 %all-gather = f32[192,128]{1,0:T(8,128)S(1)} all-gather(f32[96,128]{1,0:T(8,128)S(1)} %fusion.19), channel_id=2, replica_groups=mesh['sub'=8,'row'=2,'col'=16] {'row'}, dimensions={0}, use_global_device_ids=true | all-gather | bytes 147456 | tf_op jit(solution)/shard_map/all_gather | solution.py:123
  104.4 0.1 broadcast_in_dim.89
  104.5 12.2 %all_to_all.45 = bf16[16,96,128]{2,1,0:T(8,128)(2,1)S(1)} all-to-all(bf16[16,96,128]{2,1,0:T(8,128)(2,1)S(1)} %broadcast_in_dim.89), channel_id=1, replica_groups=mesh['sub'=8,'row'=2,'col'=16] {'col'}, dimensions={0} | all-to-all | bytes 786432 | tf_op jit(solution)/shard_map/all_to_all | solution.py:41
  116.7 0.3 convolution_subtract_fusion
  117.0 0.6 fusion.9
  117.6 0.9 bitcast_convert_fusion.1
  118.5 3.6 %all-to-all-start.6 = ((bf16[16,128,128]{1,2,0:T(8,128)(2,1)}), bf16[16,128,128]{1,2,0:T(8,128)(2,1)S(1)}, u32[]{:S(2)}, u32[]{:S(2)}) async-start(bf16[16,128,128]{1,2,0:T(8,128)(2,1)} %bitcast_convert_fusion.1), calls=%async_computation.6 | async-start | bytes 1048576 | tf_op jit(solution)/shard_map/all_to_all | solution.py:34
  122.1 0.2 copy.40
  122.3 0.1 constant_dynamic-slice_fusion.1
  122.3 9.8 %all-to-all-done.6 = bf16[16,128,128]{1,2,0:T(8,128)(2,1)S(1)} async-done(((bf16[16,128,128]{1,2,0:T(8,128)(2,1)}), bf16[16,128,128]{1,2,0:T(8,128)(2,1)S(1)}, u32[]{:S(2)}, u32[]{:S(2)}) %all-to-all-start.6) | async-done | bytes 524320 | tf_op jit(solution)/shard_map/all_to_all | solution.py:34
  132.2 0.2 select_reduce_fusion.1
  132.4 0.1 copy.29
  132.5 0.9 broadcast_in_dim.92
  133.4 3.6 %all-to-all-start.7 = ((bf16[16,128,128]{2,1,0:T(8,128)(2,1)}), bf16[16,128,128]{2,1,0:T(8,128)(2,1)S(1)}, u32[]{:S(2)}, u32[]{:S(2)}) async-start(bf16[16,128,128]{2,1,0:T(8,128)(2,1)} %broadcast_in_dim.92), calls=%async_computation.7 | async-start | bytes 1048576 | tf_op jit(solution)/shard_map/all_to_all | solution.py:41
  137.0 9.3 %all-to-all-done.7 = bf16[16,128,128]{2,1,0:T(8,128)(2,1)S(1)} async-done(((bf16[16,128,128]{2,1,0:T(8,128)(2,1)}), bf16[16,128,128]{2,1,0:T(8,128)(2,1)S(1)}, u32[]{:S(2)}, u32[]{:S(2)}) %all-to-all-start.7) | async-done | bytes 524320 | tf_op jit(solution)/shard_map/all_to_all | solution.py:41
  146.2 0.3 fusion.14
  146.5 4.7 %all-gather.1 = f32[256,128]{1,0:T(8,128)S(1)} all-gather(f32[128,128]{1,0:T(8,128)S(1)} %fusion.14), channel_id=3, replica_groups=mesh['sub'=8,'row'=2,'col'=16] {'row'}, dimensions={0}, use_global_device_ids=true | all-gather | bytes 196608 | tf_op jit(solution)/shard_map/all_gather | solution.py:129
  151.2 0.6 fusion.7
  151.9 0.9 bitcast_convert_fusion
  152.8 3.6 %all-to-all-start.8 = ((bf16[16,128,128]{1,2,0:T(8,128)(2,1)}), bf16[16,128,128]{1,2,0:T(8,128)(2,1)S(1)}, u32[]{:S(2)}, u32[]{:S(2)}) async-start(bf16[16,128,128]{1,2,0:T(8,128)(2,1)} %bitcast_convert_fusion), calls=%async_computation.8 | async-start | bytes 1048576 | tf_op jit(solution)/shard_map/all_to_all | solution.py:34
  156.3 0.2 copy.41
  156.5 0.1 constant_dynamic-slice_fusion
  156.6 10.7 %all-to-all-done.8 = bf16[16,128,128]{1,2,0:T(8,128)(2,1)S(1)} async-done(((bf16[16,128,128]{1,2,0:T(8,128)(2,1)}), bf16[16,128,128]{1,2,0:T(8,128)(2,1)S(1)}, u32[]{:S(2)}, u32[]{:S(2)}) %all-to-all-start.8) | async-done | bytes 524320 | tf_op jit(solution)/shard_map/all_to_all | solution.py:34
  167.3 0.2 select_reduce_fusion
  167.5 0.7 copy.32
  (29 shorter events, 0.2 us)
Async XLA Ops:
  0.6 1.2 copy-start
  0.6 4.4 %copy-start.7 = (s32[1,16,16]{2,1,0:T(8,128)S(1)}, s32[1,16,16]{2,1,0:T(8,128)}, u32[]{:S(2)}) copy-start(s32[1,16,16]{2,1,0:T(8,128)} %param.9) | copy-start | bytes 3076
  0.7 8.3 %copy-start.4 = (bf16[1,2,128,2048]{3,2,1,0:T(8,128)(2,1)S(1)}, bf16[1,2,128,2048]{3,2,1,0:T(8,128)(2,1)}, u32[]{:S(2)}) copy-start(bf16[1,2,128,2048]{3,2,1,0:T(8,128)(2,1)} %param.8) | copy-start | bytes 3145732
  3.7 5.2 %collective-permute-start = (bf16[128,128]{1,0:T(8,128)(2,1)S(1)}, bf16[128,128]{1,0:T(8,128)(2,1)S(1)}, u32[]{:S(2)}, u32[]{:S(2)}) collective-permute-start(bf16[128,128]{1,0:T(8,128)(2,1)S(1)} %get-tuple-element.14), channel_id=1, source_target_pairs={{0,16},{1,17},{2,18},{3,19},{4,20},{5,21},{6,22},{7,23},{8,24},{9,... | collective-permute-start | bytes 98312 | tf_op jit(solution)/shard_map/ppermute | solution.py:69
  8.9 6.7 %copy-start.1 = (f32[96,1536]{1,0:T(8,128)S(1)}, f32[96,1536]{1,0:T(8,128)}, u32[]{:S(2)}) copy-start(f32[96,1536]{1,0:T(8,128)} %param.13) | copy-start | bytes 1769476
  10.1 16.4 %all-to-all-start = ((bf16[16,128,128]{2,1,0:T(8,128)(2,1)}), bf16[16,128,128]{2,1,0:T(8,128)(2,1)S(1)}, u32[]{:S(2)}, u32[]{:S(2)}) async-start(bf16[16,128,128]{2,1,0:T(8,128)(2,1)} %bitcast.3), calls=%async_computation | async-start | bytes 1048576 | tf_op jit(solution)/shard_map/all_to_all | solution.py:71
  27.7 3.8 %copy-start.8 = (s32[1,1024]{1,0:T(1,128)S(1)}, s32[1,1024]{1,0:T(1,128)}, u32[]{:S(2)}) copy-start(s32[1,1024]{1,0:T(1,128)} %param.12) | copy-start | bytes 12292
  27.7 17.8 %all-to-all-start.1 = ((bf16[16,224,128]{2,1,0:T(8,128)(2,1)}), bf16[16,224,128]{2,1,0:T(8,128)(2,1)S(1)}, u32[]{:S(2)}, u32[]{:S(2)}) async-start(bf16[16,224,128]{2,1,0:T(8,128)(2,1)} %fusion.13), calls=%async_computation.1 | async-start | bytes 1835008 | tf_op jit(solution)/shard_map/all_to_all | solution.py:94
  45.9 0.6 copy-start.2
  47.6 21.1 %all-to-all-start.2 = ((bf16[32,48,128]{2,1,0:T(8,128)(2,1)}), bf16[32,48,128]{2,1,0:T(8,128)(2,1)S(1)}, u32[]{:S(2)}, u32[]{:S(2)}) async-start(bf16[32,48,128]{2,1,0:T(8,128)(2,1)} %bitcast.84), calls=%async_computation.2 | async-start | bytes 786432 | tf_op jit(solution)/shard_map/all_to_all | solution.py:119
  54.2 11.5 %collective-permute-start.1 = (f32[96,96]{0,1:T(8,128)S(1)}, f32[96,96]{0,1:T(8,128)S(1)}, u32[]{:S(2)}, u32[]{:S(2)}) collective-permute-start(f32[96,96]{0,1:T(8,128)S(1)} %bitcast.91), channel_id=1, source_target_pairs={{0,128},{32,160},{64,192},{96,224},{128,0},{160,32},{192,64},{224,... | collective-permute-start | bytes 110600 | tf_op jit(solution)/shard_map/ppermute | solution.py:111
  61.9 6.8 %collective-permute-start.4 = (f32[48,128]{1,0:T(8,128)S(1)}, f32[48,128]{1,0:T(8,128)S(1)}, u32[]{:S(2)}, u32[]{:S(2)}) collective-permute-start(f32[48,128]{1,0:T(8,128)S(1)} %constant_dynamic-slice_fusion.2), channel_id=1, source_target_pairs={{0,0},{1,2},{2,4},{3,6},{4,8},{5,10},{6,12},{7,14},{8,16},{9,18},{... | collective-permute-start | bytes 73736 | tf_op jit(solution)/shard_map/ppermute | solution.py:92
  69.4 13.2 %all-to-all-start.3 = ((f32[8,48,128]{2,1,0:T(8,128)}), f32[8,48,128]{2,1,0:T(8,128)S(1)}, u32[]{:S(2)}, u32[]{:S(2)}) async-start(f32[8,48,128]{2,1,0:T(8,128)} %broadcast_in_dim.87), calls=%async_computation.3 | async-start | bytes 393216 | tf_op jit(solution)/shard_map/all_to_all | solution.py:41
  72.8 9.7 %collective-permute-start.2 = (f32[192,96]{0,1:T(8,128)S(1)}, f32[192,96]{0,1:T(8,128)S(1)}, u32[]{:S(2)}, u32[]{:S(2)}) collective-permute-start(f32[192,96]{0,1:T(8,128)S(1)} %maximum_select_fusion.3), channel_id=1, source_target_pairs={{0,64},{32,96},{64,0},{96,32},{128,192},{160,224},{192,128},{224,1... | collective-permute-start | bytes 221192 | tf_op jit(solution)/shard_map/ppermute | solution.py:111
  83.5 15.2 %all-to-all-start.4 = ((f32[16,48,128]{2,1,0:T(8,128)}), f32[16,48,128]{2,1,0:T(8,128)S(1)}, u32[]{:S(2)}, u32[]{:S(2)}) async-start(f32[16,48,128]{2,1,0:T(8,128)} %broadcast_in_dim.88), calls=%async_computation.4 | async-start | bytes 786432 | tf_op jit(solution)/shard_map/all_to_all | solution.py:41
  90.5 4.1 %collective-permute-start.3 = (f32[384,96]{0,1:T(8,128)S(1)}, f32[384,96]{0,1:T(8,128)S(1)}, u32[]{:S(2)}, u32[]{:S(2)}) collective-permute-start(f32[384,96]{0,1:T(8,128)S(1)} %maximum_select_fusion.2), channel_id=1, source_target_pairs={{0,32},{32,0},{64,96},{96,64},{128,160},{160,128},{192,224},{224,1... | collective-permute-start | bytes 442376 | tf_op jit(solution)/shard_map/ppermute | solution.py:111
  98.7 17.9 %copy-start.3 = (f32[128,128]{1,0:T(8,128)S(1)}, f32[128,128]{1,0:T(8,128)}, u32[]{:S(2)}) copy-start(f32[128,128]{1,0:T(8,128)} %copy-done.2) | copy-start | bytes 196612
  104.4 12.6 %copy-start.6 = (f32[96,128]{1,0:T(8,128)}, f32[96,128]{1,0:T(8,128)S(1)}, u32[]{:S(2)}) copy-start(f32[96,128]{1,0:T(8,128)S(1)} %reduce_sum.70) | copy-start | bytes 147460
  118.5 13.7 %all-to-all-start.6 = ((bf16[16,128,128]{1,2,0:T(8,128)(2,1)}), bf16[16,128,128]{1,2,0:T(8,128)(2,1)S(1)}, u32[]{:S(2)}, u32[]{:S(2)}) async-start(bf16[16,128,128]{1,2,0:T(8,128)(2,1)} %bitcast_convert_fusion.1), calls=%async_computation.6 | async-start | bytes 1048576 | tf_op jit(solution)/shard_map/all_to_all | solution.py:34
  132.3 13.9 %copy-start.5 = (bf16[1,2,128,2048]{3,2,1,0:T(8,128)(2,1)S(1)}, bf16[1,2,128,2048]{3,2,1,0:T(8,128)(2,1)}, u32[]{:S(2)}) copy-start(bf16[1,2,128,2048]{3,2,1,0:T(8,128)(2,1)} %param.8) | copy-start | bytes 3145732
  133.4 12.9 %all-to-all-start.7 = ((bf16[16,128,128]{2,1,0:T(8,128)(2,1)}), bf16[16,128,128]{2,1,0:T(8,128)(2,1)S(1)}, u32[]{:S(2)}, u32[]{:S(2)}) async-start(bf16[16,128,128]{2,1,0:T(8,128)(2,1)} %broadcast_in_dim.92), calls=%async_computation.7 | async-start | bytes 1048576 | tf_op jit(solution)/shard_map/all_to_all | solution.py:41
  152.8 14.6 %all-to-all-start.8 = ((bf16[16,128,128]{1,2,0:T(8,128)(2,1)}), bf16[16,128,128]{1,2,0:T(8,128)(2,1)S(1)}, u32[]{:S(2)}, u32[]{:S(2)}) async-start(bf16[16,128,128]{1,2,0:T(8,128)(2,1)} %bitcast_convert_fusion), calls=%async_computation.8 | async-start | bytes 1048576 | tf_op jit(solution)/shard_map/all_to_all | solution.py:34

commit v12 on v11

--- a/solution.py
+++ b/solution.py
@@ -25,6 +25,15 @@
 
 def after(value, other):
     return lax.optimization_barrier((value, other))[0]
+
+
+def collect(blocks, step, sub_id):
+    other = lax.ppermute(blocks, "sub", [(i, i ^ step) for i in range(SUBS)])
+    return jnp.where(
+        sub_id & step == 0,
+        jnp.concatenate([blocks, other], 0),
+        jnp.concatenate([other, blocks], 0),
+    )
 
 
 def sum_scatter(partial, axes, count):
@@ -89,7 +98,7 @@
         for chip in range(COLS)
     ]
     root_rows = lax.dynamic_slice_in_dim(after(root_right, partial), row_id * chunk, chunk, 0)
-    root_rows = root_rows_sent = lax.ppermute(root_rows, ("row", "col"), pairs)
+    root_rows = lax.ppermute(root_rows, ("row", "col"), pairs)
     both = jnp.concatenate([jnp.broadcast_to(total[None], (COLS,) + total.shape), gram], 1)
     both = lax.all_to_all(both, "col", 0, 0)
     total = both[:, :width].reshape(PANEL, sources)
@@ -102,23 +111,12 @@
         onehot, couple, (((1,), (1,)), ((), ())), preferred_element_type=f32
     ).astype(bf16)
 
-    gram = gram.T
-    for step in (4, 2, 1):
-        if step == 2:
-            gram_pair = gram
-        if step == 1:
-            root_rows = after(root_rows, gram)
-        other = lax.ppermute(gram, "sub", [(i, i ^ step) for i in range(SUBS)])
-        gram = jnp.where(
-            sub_id & step == 0,
-            jnp.concatenate([gram, other], 0),
-            jnp.concatenate([other, gram], 0),
-        )
-
+    gram = collect(gram.T, 4, sub_id)
     updates = mul(couple_sep, solved.astype(bf16)).astype(bf16).reshape(2 * COLS, chunk, sources)
-    updates = after(lax.all_to_all(updates, ("row", "col"), 0, 0), (gram_pair, root_rows_sent))
+    updates = after(lax.all_to_all(updates, ("row", "col"), 0, 0), (gram, root_rows))
     updates = updates.astype(f32).sum(0)
     updates = gather(updates, "sub", SUBS).sum(0)
+    gram = collect(collect(after(gram, updates), 2, sub_id), 1, sub_id)
     rhs = gather(root_rows - updates, "col", COLS).reshape(SEPARATOR // 2, sources)
     root_part = lax.all_gather(mul_t(gram, rhs, precision=fine), "row").sum(0)
     root_full = gather(root_part.astype(bf16), "col", COLS).reshape(SEPARATOR, sources)

time: 169 us -> 174 us (1.030)
  blocking collectives: 22.3 us -> 38.1 us
  starting transfers between devices: 51.1 us -> 45.8 us
  waiting for transfers between devices: 73.7 us -> 68.4 us
    all_to_all x1 -> x2, blocking collectives: 12.2 us -> 27.6 us  [gather(): return lax.all_to_all(spread, axes, 0, 0)]
    all_to_all x3 -> x2, waiting for transfers between devices: 13.4 us -> 9.27 us  [gather(): return lax.all_to_all(spread, axes, 0, 0)]
    all_to_all x3 -> x2, starting transfers between devices: 14 us -> 10.8 us  [gather(): return lax.all_to_all(spread, axes, 0, 0)]
    ppermute x4, starting transfers between devices: 13.1 us -> 10.9 us  [the longest x3 7.2 us: collect(): other = lax.ppermute(blocks, 'sub', [(i, i ^ step) for i in range(SUBS)])]
  transfers between devices with their start and end apart: 13 -> 12, of which waited for: 10 -> 9; matrix products, arithmetic and copies ran while one was open for 3% -> 3% of each run, Pallas kernels for 0% -> 0%
where the time goes in v12:
time: 174 us; the launch traced here: 173 us
  waiting for transfers between devices  68.4 us (39%)
  starting transfers between devices  45.8 us (26%)
  blocking collectives  38.1 us (22%)
  matrix products  9.44 us (5%)
  local copies, waits for them, and re-layouts  7.68 us (4%)
  other arithmetic  2.25 us (1%)
    all_to_all x2, blocking collectives, gather(): return lax.all_to_all(spread, axes, 0, 0)  27.6 us
    all_to_all x2, waiting for transfers between devices, sum_scatter(): others = lax.all_to_all(parts.astype(bf16), axes, 0, 0).astype(f32)  20.5 us
    all_to_all x1, waiting for transfers between devices, shards(): both = lax.all_to_all(both, 'col', 0, 0)  11.8 us
    all_to_all x2, starting transfers between devices, gather(): return lax.all_to_all(spread, axes, 0, 0)  10.8 us
    ppermute x3, waiting for transfers between devices, collect(): other = lax.ppermute(blocks, 'sub', [(i, i ^ step) for i in range(SUBS)])  10.3 us
    all_to_all x1, waiting for transfers between devices, shards(): total = lax.all_to_all(partial.reshape(COLS, width, sources), 'col', 0, 0)  9.94 us
    all_to_all x2, waiting for transfers between devices, gather(): return lax.all_to_all(spread, axes, 0, 0)  9.27 us
    ppermute x3, starting transfers between devices, collect(): other = lax.ppermute(blocks, 'sub', [(i, i ^ step) for i in range(SUBS)])  7.2 us
  transfers between devices with their start and end apart: 12, of which 9 were waited for; matrix products, arithmetic and copies ran while one was open for 3% of the time, Pallas kernels for 0%

profile of v12, /device:TPU:1, one launch (start us, length us, event | category | flops | bytes accessed | tf_op | source)
XLA Modules:
  0.0 172.8 jit_solution(8195299617236029701)
XLA Ops:
  0.6 0.0 copy-start
  0.7 1.2 copy-done
  1.9 1.8 %fusion.36 = (bf16[128,128]{1,0:T(8,128)(2,1)S(1)}, f32[128,128]{1,0:T(8,128)S(1)}) fusion(f32[1,2048,128]{2,1,0:T(8,128)} %param.14, f32[1,128,2048]{2,1,0:T(8,128)S(1)} %copy-done), kind=kOutput, calls=%fused_computation.61 | convolution fusion | flops 201342976 | bytes 2195456 | tf_op jit(solution)/shard_map/dot_general | solution.py:19
  3.7 1.3 collective-permute-start
  5.0 0.2 fusion.33
  5.2 0.1 broadcast_bitcast_fusion
  5.3 3.6 %collective-permute-done = bf16[128,128]{1,0:T(8,128)(2,1)S(1)} collective-permute-done((bf16[128,128]{1,0:T(8,128)(2,1)S(1)}, bf16[128,128]{1,0:T(8,128)(2,1)S(1)}, u32[]{:S(2)}, u32[]{:S(2)}) %collective-permute-start) | collective-permute-done | bytes 32800 | tf_op jit(solution)/shard_map/ppermute | solution.py:78
  8.9 1.1 convolution_convert_fusion.1
  10.1 5.5 %all-to-all-start = ((bf16[16,128,128]{2,1,0:T(8,128)(2,1)}), bf16[16,128,128]{2,1,0:T(8,128)(2,1)S(1)}, u32[]{:S(2)}, u32[]{:S(2)}) async-start(bf16[16,128,128]{2,1,0:T(8,128)(2,1)} %bitcast.3), calls=%async_computation | async-start | bytes 1048576 | tf_op jit(solution)/shard_map/all_to_all | solution.py:80
  15.6 0.8 fusion.29
  16.4 0.1 convert_element_type.79
  16.5 9.9 %all-to-all-done = bf16[16,128,128]{2,1,0:T(8,128)(2,1)S(1)} async-done(((bf16[16,128,128]{2,1,0:T(8,128)(2,1)}), bf16[16,128,128]{2,1,0:T(8,128)(2,1)S(1)}, u32[]{:S(2)}, u32[]{:S(2)}) %all-to-all-start) | async-done | bytes 524320 | tf_op jit(solution)/shard_map/all_to_all | solution.py:80
  26.4 0.1 reduce_sum.66
  26.5 0.1 broadcast_in_dim.83
  26.6 1.1 fusion.13
  27.7 3.8 %all-to-all-start.1 = ((bf16[16,224,128]{2,1,0:T(8,128)(2,1)}), bf16[16,224,128]{2,1,0:T(8,128)(2,1)S(1)}, u32[]{:S(2)}, u32[]{:S(2)}) async-start(bf16[16,224,128]{2,1,0:T(8,128)(2,1)} %fusion.13), calls=%async_computation.1 | async-start | bytes 1835008 | tf_op jit(solution)/shard_map/all_to_all | solution.py:103
  31.5 2.1 %fusion.2 = bf16[1536,128]{1,0:T(8,128)(2,1)S(1)} fusion(s32[1024]{0:T(1024)S(1)} %bitcast.95, bf16[1,1,128,1024]{3,2,1,0:T(8,128)(2,1)} %param.11), kind=kOutput, calls=%fused_computation.3 | convolution fusion | flops 404422656 | bytes 659456 | tf_op jit(solution)/shard_map/dot_general | solution.py:110
  33.6 11.8 %all-to-all-done.1 = bf16[16,224,128]{2,1,0:T(8,128)(2,1)S(1)} async-done(((bf16[16,224,128]{2,1,0:T(8,128)(2,1)}), bf16[16,224,128]{2,1,0:T(8,128)(2,1)S(1)}, u32[]{:S(2)}, u32[]{:S(2)}) %all-to-all-start.1) | async-done | bytes 917536 | tf_op jit(solution)/shard_map/all_to_all | solution.py:103
  45.5 0.4 fusion.4
  45.9 0.0 copy-start.2
  45.9 0.6 copy-done.2
  46.5 1.0 convolution_convert_fusion
  47.5 6.4 %all-to-all-start.2 = ((bf16[32,48,128]{2,1,0:T(8,128)(2,1)}), bf16[32,48,128]{2,1,0:T(8,128)(2,1)S(1)}, u32[]{:S(2)}, u32[]{:S(2)}) async-start(bf16[32,48,128]{2,1,0:T(8,128)(2,1)} %bitcast.84), calls=%async_computation.2 | async-start | bytes 786432 | tf_op jit(solution)/shard_map/all_to_all | solution.py:116
  54.0 0.2 select_reduce_fusion.2
  54.1 7.0 %collective-permute-start.1 = (f32[96,96]{0,1:T(8,128)S(1)}, f32[96,96]{0,1:T(8,128)S(1)}, u32[]{:S(2)}, u32[]{:S(2)}) collective-permute-start(f32[96,96]{0,1:T(8,128)S(1)} %bitcast.91), channel_id=1, source_target_pairs={{0,128},{32,160},{64,192},{96,224},{128,0},{160,32},{192,64},{224,... | collective-permute-start | bytes 110600 | tf_op jit(solution)/shard_map/ppermute | solution.py:31
  61.1 0.7 constant_dynamic-slice_fusion.2
  61.9 3.7 %collective-permute-start.2 = (f32[48,128]{1,0:T(8,128)S(1)}, f32[48,128]{1,0:T(8,128)S(1)}, u32[]{:S(2)}, u32[]{:S(2)}) collective-permute-start(f32[48,128]{1,0:T(8,128)S(1)} %constant_dynamic-slice_fusion.2), channel_id=1, source_target_pairs={{0,0},{1,2},{2,4},{3,6},{4,8},{5,10},{6,12},{7,14},{8,16},{9,18},{... | collective-permute-start | bytes 73736 | tf_op jit(solution)/shard_map/ppermute | solution.py:101
  65.6 0.1 maximum_select_fusion.3
  65.7 2.9 %collective-permute-done.2 = f32[48,128]{1,0:T(8,128)S(1)} collective-permute-done((f32[48,128]{1,0:T(8,128)S(1)}, f32[48,128]{1,0:T(8,128)S(1)}, u32[]{:S(2)}, u32[]{:S(2)}) %collective-permute-start.2) | collective-permute-done | bytes 24608 | tf_op jit(solution)/shard_map/ppermute | solution.py:101
  68.7 0.1 convert_reduce_fusion
  68.7 11.4 %all_to_all.45 = f32[8,48,128]{2,1,0:T(8,128)S(1)} all-to-all(f32[8,48,128]{2,1,0:T(8,128)S(1)} %broadcast_in_dim.87), channel_id=1, replica_groups=mesh['sub'=8,'row'=2,'col'=16] {'sub'}, dimensions={0} | all-to-all | bytes 393216 | tf_op jit(solution)/shard_map/all_to_all | solution.py:50
  80.1 0.8 broadcast_in_dim.88
  80.9 7.2 %all-to-all-start.4 = ((f32[16,48,128]{2,1,0:T(8,128)}), f32[16,48,128]{2,1,0:T(8,128)S(1)}, u32[]{:S(2)}, u32[]{:S(2)}) async-start(f32[16,48,128]{2,1,0:T(8,128)} %broadcast_in_dim.88), calls=%async_computation.4 | async-start | bytes 786432 | tf_op jit(solution)/shard_map/all_to_all | solution.py:50
  88.2 0.1 collective-permute-start.3
  88.3 5.4 %collective-permute-done.3 = f32[192,96]{0,1:T(8,128)S(1)} collective-permute-done((f32[192,96]{0,1:T(8,128)S(1)}, f32[192,96]{0,1:T(8,128)S(1)}, u32[]{:S(2)}, u32[]{:S(2)}) %collective-permute-start.3) | collective-permute-done | bytes 73760 | tf_op jit(solution)/shard_map/ppermute | solution.py:31
  93.7 0.1 maximum_select_fusion.2
  93.8 0.1 collective-permute-start.4
  93.9 4.9 %collective-permute-done.4 = f32[384,96]{0,1:T(8,128)S(1)} collective-permute-done((f32[384,96]{0,1:T(8,128)S(1)}, f32[384,96]{0,1:T(8,128)S(1)}, u32[]{:S(2)}, u32[]{:S(2)}) %collective-permute-start.4) | collective-permute-done | bytes 147488 | tf_op jit(solution)/shard_map/ppermute | solution.py:31
  98.8 0.3 fusion.19
  99.1 5.8 %all-gather = f32[192,128]{1,0:T(8,128)S(1)} all-gather(f32[96,128]{1,0:T(8,128)S(1)} %fusion.19), channel_id=2, replica_groups=mesh['sub'=8,'row'=2,'col'=16] {'row'}, dimensions={0}, use_global_device_ids=true | all-gather | bytes 147456 | tf_op jit(solution)/shard_map/all_gather | solution.py:121
  104.9 0.1 broadcast_in_dim.89
  105.0 16.2 %all_to_all.46 = bf16[16,96,128]{2,1,0:T(8,128)(2,1)S(1)} all-to-all(bf16[16,96,128]{2,1,0:T(8,128)(2,1)S(1)} %broadcast_in_dim.89), channel_id=1, replica_groups=mesh['sub'=8,'row'=2,'col'=16] {'col'}, dimensions={0} | all-to-all | bytes 786432 | tf_op jit(solution)/shard_map/all_to_all | solution.py:50
  121.2 0.3 convolution_subtract_fusion
  121.5 0.6 fusion.9
  122.1 0.9 bitcast_convert_fusion.1
  123.0 3.6 %all-to-all-start.6 = ((bf16[16,128,128]{1,2,0:T(8,128)(2,1)}), bf16[16,128,128]{1,2,0:T(8,128)(2,1)S(1)}, u32[]{:S(2)}, u32[]{:S(2)}) async-start(bf16[16,128,128]{1,2,0:T(8,128)(2,1)} %bitcast_convert_fusion.1), calls=%async_computation.6 | async-start | bytes 1048576 | tf_op jit(solution)/shard_map/all_to_all | solution.py:43
  126.6 0.2 copy.40
  126.8 0.1 constant_dynamic-slice_fusion.1
  126.9 9.8 %all-to-all-done.6 = bf16[16,128,128]{1,2,0:T(8,128)(2,1)S(1)} async-done(((bf16[16,128,128]{1,2,0:T(8,128)(2,1)}), bf16[16,128,128]{1,2,0:T(8,128)(2,1)S(1)}, u32[]{:S(2)}, u32[]{:S(2)}) %all-to-all-start.6) | async-done | bytes 524320 | tf_op jit(solution)/shard_map/all_to_all | solution.py:43
  136.7 0.2 select_reduce_fusion.1
  136.9 0.1 copy.29
  137.0 0.9 broadcast_in_dim.92
  137.9 3.6 %all-to-all-start.7 = ((bf16[16,128,128]{2,1,0:T(8,128)(2,1)}), bf16[16,128,128]{2,1,0:T(8,128)(2,1)S(1)}, u32[]{:S(2)}, u32[]{:S(2)}) async-start(bf16[16,128,128]{2,1,0:T(8,128)(2,1)} %broadcast_in_dim.92), calls=%async_computation.7 | async-start | bytes 1048576 | tf_op jit(solution)/shard_map/all_to_all | solution.py:50
  141.5 9.3 %all-to-all-done.7 = bf16[16,128,128]{2,1,0:T(8,128)(2,1)S(1)} async-done(((bf16[16,128,128]{2,1,0:T(8,128)(2,1)}), bf16[16,128,128]{2,1,0:T(8,128)(2,1)S(1)}, u32[]{:S(2)}, u32[]{:S(2)}) %all-to-all-start.7) | async-done | bytes 524320 | tf_op jit(solution)/shard_map/all_to_all | solution.py:50
  150.7 0.3 fusion.14
  151.0 4.7 %all-gather.1 = f32[256,128]{1,0:T(8,128)S(1)} all-gather(f32[128,128]{1,0:T(8,128)S(1)} %fusion.14), channel_id=3, replica_groups=mesh['sub'=8,'row'=2,'col'=16] {'row'}, dimensions={0}, use_global_device_ids=true | all-gather | bytes 196608 | tf_op jit(solution)/shard_map/all_gather | solution.py:127
  155.8 0.6 fusion.7
  156.4 0.9 bitcast_convert_fusion
  157.3 3.6 %all-to-all-start.8 = ((bf16[16,128,128]{1,2,0:T(8,128)(2,1)}), bf16[16,128,128]{1,2,0:T(8,128)(2,1)S(1)}, u32[]{:S(2)}, u32[]{:S(2)}) async-start(bf16[16,128,128]{1,2,0:T(8,128)(2,1)} %bitcast_convert_fusion), calls=%async_computation.8 | async-start | bytes 1048576 | tf_op jit(solution)/shard_map/all_to_all | solution.py:43
  160.9 0.2 copy.41
  161.1 0.1 constant_dynamic-slice_fusion
  161.1 10.7 %all-to-all-done.8 = bf16[16,128,128]{1,2,0:T(8,128)(2,1)S(1)} async-done(((bf16[16,128,128]{1,2,0:T(8,128)(2,1)}), bf16[16,128,128]{1,2,0:T(8,128)(2,1)S(1)}, u32[]{:S(2)}, u32[]{:S(2)}) %all-to-all-start.8) | async-done | bytes 524320 | tf_op jit(solution)/shard_map/all_to_all | solution.py:43
  171.8 0.2 select_reduce_fusion
  172.0 0.7 copy.32
  (28 shorter events, 0.2 us)
Async XLA Ops:
  0.6 1.2 copy-start
  0.6 4.4 %copy-start.7 = (s32[1,16,16]{2,1,0:T(8,128)S(1)}, s32[1,16,16]{2,1,0:T(8,128)}, u32[]{:S(2)}) copy-start(s32[1,16,16]{2,1,0:T(8,128)} %param.9) | copy-start | bytes 3076
  0.7 8.3 %copy-start.4 = (bf16[1,2,128,2048]{3,2,1,0:T(8,128)(2,1)S(1)}, bf16[1,2,128,2048]{3,2,1,0:T(8,128)(2,1)}, u32[]{:S(2)}) copy-start(bf16[1,2,128,2048]{3,2,1,0:T(8,128)(2,1)} %param.8) | copy-start | bytes 3145732
  3.7 5.2 %collective-permute-start = (bf16[128,128]{1,0:T(8,128)(2,1)S(1)}, bf16[128,128]{1,0:T(8,128)(2,1)S(1)}, u32[]{:S(2)}, u32[]{:S(2)}) collective-permute-start(bf16[128,128]{1,0:T(8,128)(2,1)S(1)} %get-tuple-element.14), channel_id=1, source_target_pairs={{0,16},{1,17},{2,18},{3,19},{4,20},{5,21},{6,22},{7,23},{8,24},{9,... | collective-permute-start | bytes 98312 | tf_op jit(solution)/shard_map/ppermute | solution.py:78
  8.9 6.7 %copy-start.1 = (f32[96,1536]{1,0:T(8,128)S(1)}, f32[96,1536]{1,0:T(8,128)}, u32[]{:S(2)}) copy-start(f32[96,1536]{1,0:T(8,128)} %param.13) | copy-start | bytes 1769476
  10.1 16.4 %all-to-all-start = ((bf16[16,128,128]{2,1,0:T(8,128)(2,1)}), bf16[16,128,128]{2,1,0:T(8,128)(2,1)S(1)}, u32[]{:S(2)}, u32[]{:S(2)}) async-start(bf16[16,128,128]{2,1,0:T(8,128)(2,1)} %bitcast.3), calls=%async_computation | async-start | bytes 1048576 | tf_op jit(solution)/shard_map/all_to_all | solution.py:80
  27.7 3.8 %copy-start.8 = (s32[1,1024]{1,0:T(1,128)S(1)}, s32[1,1024]{1,0:T(1,128)}, u32[]{:S(2)}) copy-start(s32[1,1024]{1,0:T(1,128)} %param.12) | copy-start | bytes 12292
  27.7 17.8 %all-to-all-start.1 = ((bf16[16,224,128]{2,1,0:T(8,128)(2,1)}), bf16[16,224,128]{2,1,0:T(8,128)(2,1)S(1)}, u32[]{:S(2)}, u32[]{:S(2)}) async-start(bf16[16,224,128]{2,1,0:T(8,128)(2,1)} %fusion.13), calls=%async_computation.1 | async-start | bytes 1835008 | tf_op jit(solution)/shard_map/all_to_all | solution.py:103
  45.9 0.6 copy-start.2
  47.5 21.1 %all-to-all-start.2 = ((bf16[32,48,128]{2,1,0:T(8,128)(2,1)}), bf16[32,48,128]{2,1,0:T(8,128)(2,1)S(1)}, u32[]{:S(2)}, u32[]{:S(2)}) async-start(bf16[32,48,128]{2,1,0:T(8,128)(2,1)} %bitcast.84), calls=%async_computation.2 | async-start | bytes 786432 | tf_op jit(solution)/shard_map/all_to_all | solution.py:116
  54.1 11.5 %collective-permute-start.1 = (f32[96,96]{0,1:T(8,128)S(1)}, f32[96,96]{0,1:T(8,128)S(1)}, u32[]{:S(2)}, u32[]{:S(2)}) collective-permute-start(f32[96,96]{0,1:T(8,128)S(1)} %bitcast.91), channel_id=1, source_target_pairs={{0,128},{32,160},{64,192},{96,224},{128,0},{160,32},{192,64},{224,... | collective-permute-start | bytes 110600 | tf_op jit(solution)/shard_map/ppermute | solution.py:31
  61.9 6.8 %collective-permute-start.2 = (f32[48,128]{1,0:T(8,128)S(1)}, f32[48,128]{1,0:T(8,128)S(1)}, u32[]{:S(2)}, u32[]{:S(2)}) collective-permute-start(f32[48,128]{1,0:T(8,128)S(1)} %constant_dynamic-slice_fusion.2), channel_id=1, source_target_pairs={{0,0},{1,2},{2,4},{3,6},{4,8},{5,10},{6,12},{7,14},{8,16},{9,18},{... | collective-permute-start | bytes 73736 | tf_op jit(solution)/shard_map/ppermute | solution.py:101
  80.9 17.9 %all-to-all-start.4 = ((f32[16,48,128]{2,1,0:T(8,128)}), f32[16,48,128]{2,1,0:T(8,128)S(1)}, u32[]{:S(2)}, u32[]{:S(2)}) async-start(f32[16,48,128]{2,1,0:T(8,128)} %broadcast_in_dim.88), calls=%async_computation.4 | async-start | bytes 786432 | tf_op jit(solution)/shard_map/all_to_all | solution.py:50
  88.2 5.5 %collective-permute-start.3 = (f32[192,96]{0,1:T(8,128)S(1)}, f32[192,96]{0,1:T(8,128)S(1)}, u32[]{:S(2)}, u32[]{:S(2)}) collective-permute-start(f32[192,96]{0,1:T(8,128)S(1)} %maximum_select_fusion.3), channel_id=1, source_target_pairs={{0,64},{32,96},{64,0},{96,32},{128,192},{160,224},{192,128},{224,1... | collective-permute-start | bytes 221192 | tf_op jit(solution)/shard_map/ppermute | solution.py:31
  93.8 5.0 %collective-permute-start.4 = (f32[384,96]{0,1:T(8,128)S(1)}, f32[384,96]{0,1:T(8,128)S(1)}, u32[]{:S(2)}, u32[]{:S(2)}) collective-permute-start(f32[384,96]{0,1:T(8,128)S(1)} %maximum_select_fusion.2), channel_id=1, source_target_pairs={{0,32},{32,0},{64,96},{96,64},{128,160},{160,128},{192,224},{224,1... | collective-permute-start | bytes 442376 | tf_op jit(solution)/shard_map/ppermute | solution.py:31
  98.8 22.4 %copy-start.3 = (f32[128,128]{1,0:T(8,128)S(1)}, f32[128,128]{1,0:T(8,128)}, u32[]{:S(2)}) copy-start(f32[128,128]{1,0:T(8,128)} %copy-done.2) | copy-start | bytes 196612
  104.9 16.6 %copy-start.6 = (f32[96,128]{1,0:T(8,128)}, f32[96,128]{1,0:T(8,128)S(1)}, u32[]{:S(2)}) copy-start(f32[96,128]{1,0:T(8,128)S(1)} %reduce_sum.70) | copy-start | bytes 147460
  123.0 13.7 %all-to-all-start.6 = ((bf16[16,128,128]{1,2,0:T(8,128)(2,1)}), bf16[16,128,128]{1,2,0:T(8,128)(2,1)S(1)}, u32[]{:S(2)}, u32[]{:S(2)}) async-start(bf16[16,128,128]{1,2,0:T(8,128)(2,1)} %bitcast_convert_fusion.1), calls=%async_computation.6 | async-start | bytes 1048576 | tf_op jit(solution)/shard_map/all_to_all | solution.py:43
  136.8 13.9 %copy-start.5 = (bf16[1,2,128,2048]{3,2,1,0:T(8,128)(2,1)S(1)}, bf16[1,2,128,2048]{3,2,1,0:T(8,128)(2,1)}, u32[]{:S(2)}) copy-start(bf16[1,2,128,2048]{3,2,1,0:T(8,128)(2,1)} %param.8) | copy-start | bytes 3145732
  137.9 12.9 %all-to-all-start.7 = ((bf16[16,128,128]{2,1,0:T(8,128)(2,1)}), bf16[16,128,128]{2,1,0:T(8,128)(2,1)S(1)}, u32[]{:S(2)}, u32[]{:S(2)}) async-start(bf16[16,128,128]{2,1,0:T(8,128)(2,1)} %broadcast_in_dim.92), calls=%async_computation.7 | async-start | bytes 1048576 | tf_op jit(solution)/shard_map/all_to_all | solution.py:50
  157.3 14.6 %all-to-all-start.8 = ((bf16[16,128,128]{1,2,0:T(8,128)(2,1)}), bf16[16,128,128]{1,2,0:T(8,128)(2,1)S(1)}, u32[]{:S(2)}, u32[]{:S(2)}) async-start(bf16[16,128,128]{1,2,0:T(8,128)(2,1)} %bitcast_convert_fusion), calls=%async_computation.8 | async-start | bytes 1048576 | tf_op jit(solution)/shard_map/all_to_all | solution.py:43

commit v13 on v12

--- a/solution.py
+++ b/solution.py
@@ -77,12 +77,9 @@
     own = mul(inverse, right_side[0], precision=fine)
     first_low = lax.ppermute(own.astype(bf16), "row", [(0, 1)])
     partial = mul_t(lower, first_low).astype(bf16)
-    total = lax.all_to_all(partial.reshape(COLS, width, sources), "col", 0, 0)
-    total = total.astype(f32).sum(0).astype(bf16)
 
     share = root_inverse.shape[0]
     band = SEPARATOR // (2 * SUBS)
-    root_inverse = after(root_inverse, partial)
     gram = mul_t(
         root_inverse,
         lax.dynamic_slice_in_dim(root_inverse, band_id * band, band, 1),
@@ -90,6 +87,13 @@
     ).reshape(COLS, share, band)
     own_gram = lax.dynamic_index_in_dim(gram, col_id, 0)
     gram = jnp.pad(gram.astype(bf16), ((0, 0), (0, 0), (0, sources - band)))
+
+    both = jnp.concatenate([partial.reshape(COLS, width, sources), gram], 1)
+    both = lax.all_to_all(both, "col", 0, 0)
+    total = both[:, :width].astype(f32).sum(0).astype(bf16)
+    chips = lax.broadcasted_iota(jnp.int32, (COLS, 1, 1), 0)
+    gram = jnp.where(chips == col_id, own_gram, both[:, width:, :band].astype(f32)).sum(0)
+    gram = collect(gram.T, 4, sub_id)
 
     chunk = share // 2
     pairs = [
@@ -99,24 +103,21 @@
     ]
     root_rows = lax.dynamic_slice_in_dim(after(root_right, partial), row_id * chunk, chunk, 0)
     root_rows = lax.ppermute(root_rows, ("row", "col"), pairs)
-    both = jnp.concatenate([jnp.broadcast_to(total[None], (COLS,) + total.shape), gram], 1)
-    both = lax.all_to_all(both, "col", 0, 0)
-    total = both[:, :width].reshape(PANEL, sources)
+
+    total = after(gather(total, "col", COLS), gram).reshape(PANEL, sources)
     solved = own - mul(inverse, total.astype(f32), precision=fine)
-    chips = lax.broadcasted_iota(jnp.int32, (COLS, 1, 1), 0)
-    gram = jnp.where(chips == col_id, own_gram, both[:, width:, :band].astype(f32)).sum(0)
 
     onehot = (jnp.arange(SEPARATOR)[:, None] == rows_sep[None, :]).astype(bf16)
     couple_sep = lax.dot_general(
         onehot, couple, (((1,), (1,)), ((), ())), preferred_element_type=f32
     ).astype(bf16)
 
-    gram = collect(gram.T, 4, sub_id)
+    gram = collect(gram, 2, sub_id)
     updates = mul(couple_sep, solved.astype(bf16)).astype(bf16).reshape(2 * COLS, chunk, sources)
     updates = after(lax.all_to_all(updates, ("row", "col"), 0, 0), (gram, root_rows))
     updates = updates.astype(f32).sum(0)
     updates = gather(updates, "sub", SUBS).sum(0)
-    gram = collect(collect(after(gram, updates), 2, sub_id), 1, sub_id)
+    gram = collect(after(gram, updates), 1, sub_id)
     rhs = gather(root_rows - updates, "col", COLS).reshape(SEPARATOR // 2, sources)
     root_part = lax.all_gather(mul_t(gram, rhs, precision=fine), "row").sum(0)
     root_full = gather(root_part.astype(bf16), "col", COLS).reshape(SEPARATOR, sources)

time: 174 us -> 167 us (0.960)
  waiting for transfers between devices: 68.4 us -> 60.3 us
  starting transfers between devices: 45.8 us -> 51.1 us
  blocking collectives: 38.1 us -> 36 us
  matrix products: 9.44 us -> 7.39 us
    all_to_all x1 -> x0, waiting for transfers between devices: 9.94 us -> none  [shards(): total = lax.all_to_all(partial.reshape(COLS, width, sources), 'col', 0, 0)]
    all_to_all x2 -> x3, waiting for transfers between devices: 9.27 us -> 14.9 us  [gather(): return lax.all_to_all(spread, axes, 0, 0)]
    all_to_all x1 -> x0, starting transfers between devices: 5.47 us -> none  [shards(): total = lax.all_to_all(partial.reshape(COLS, width, sources), 'col', 0, 0)]
    ppermute x3, waiting for transfers between devices: 10.3 us -> 5.37 us  [collect(): other = lax.ppermute(blocks, 'sub', [(i, i ^ step) for i in range(SUBS)])]
    all_to_all x2 -> x3, starting transfers between devices: 10.8 us -> 14.7 us  [gather(): return lax.all_to_all(spread, axes, 0, 0)]
    all_to_all x1, starting transfers between devices: 6.4 us -> 8.69 us  [shards(): lax.all_to_all(updates, ('row', 'col'), 0, 0)]
    all_to_all x1, waiting for transfers between devices: 11.8 us -> 14.1 us  [shards(): both = lax.all_to_all(both, 'col', 0, 0)]
    all_to_all x1, starting transfers between devices: 3.76 us -> 6.04 us  [shards(): both = lax.all_to_all(both, 'col', 0, 0)]
  transfers between devices with their start and end apart: 12 -> 12, of which waited for: 9 -> 11; matrix products, arithmetic and copies ran while one was open for 3% -> 2% of each run, Pallas kernels for 0% -> 0%
where the time goes in v13:
time: 167 us; the launch traced here: 166 us
  waiting for transfers between devices  60.3 us (36%)
  starting transfers between devices  51.1 us (31%)
  blocking collectives  36 us (22%)
  matrix products  7.39 us (4%)
  local copies, waits for them, and re-layouts  7.34 us (4%)
  other arithmetic  2.24 us (1%)
    all_to_all x2, blocking collectives, gather(): return lax.all_to_all(spread, axes, 0, 0)  26.8 us
    all_to_all x2, waiting for transfers between devices, sum_scatter(): others = lax.all_to_all(parts.astype(bf16), axes, 0, 0).astype(f32)  20.5 us
    all_to_all x3, waiting for transfers between devices, gather(): return lax.all_to_all(spread, axes, 0, 0)  14.9 us
    all_to_all x3, starting transfers between devices, gather(): return lax.all_to_all(spread, axes, 0, 0)  14.7 us
    all_to_all x1, waiting for transfers between devices, shards(): both = lax.all_to_all(both, 'col', 0, 0)  14.1 us
    ppermute x3, starting transfers between devices, collect(): other = lax.ppermute(blocks, 'sub', [(i, i ^ step) for i in range(SUBS)])  9.44 us
    all_to_all x1, starting transfers between devices, shards(): lax.all_to_all(updates, ('row', 'col'), 0, 0)  8.69 us
    all_to_all x2, starting transfers between devices, sum_scatter(): others = lax.all_to_all(parts.astype(bf16), axes, 0, 0).astype(f32)  7.14 us
  transfers between devices with their start and end apart: 12, of which 11 were waited for; matrix products, arithmetic and copies ran while one was open for 2% of the time, Pallas kernels for 0%

profile of v13, /device:TPU:1, one launch (start us, length us, event | category | flops | bytes accessed | tf_op | source)
XLA Modules:
  0.0 165.5 jit_solution(10418459853551454964)
XLA Ops:
  0.6 0.0 copy-start
  0.7 1.2 copy-done
  1.9 1.8 %fusion.35 = (bf16[128,128]{1,0:T(8,128)(2,1)S(1)}, f32[128,128]{1,0:T(8,128)S(1)}) fusion(f32[1,2048,128]{2,1,0:T(8,128)} %param.14, f32[1,128,2048]{2,1,0:T(8,128)S(1)} %copy-done), kind=kOutput, calls=%fused_computation.62 | convolution fusion | flops 201342976 | bytes 2195456 | tf_op jit(solution)/shard_map/dot_general | solution.py:19
  3.7 1.3 collective-permute-start
  5.1 0.2 fusion.32
  5.3 0.5 convolution_bitcast_fusion
  5.8 0.1 broadcast_bitcast_fusion
  5.9 0.3 copy.34
  6.2 0.1 convert_element_type.79
  6.2 2.7 %collective-permute-done = bf16[128,128]{1,0:T(8,128)(2,1)S(1)} collective-permute-done((bf16[128,128]{1,0:T(8,128)(2,1)S(1)}, bf16[128,128]{1,0:T(8,128)(2,1)S(1)}, u32[]{:S(2)}, u32[]{:S(2)}) %collective-permute-start) | collective-permute-done | bytes 32800 | tf_op jit(solution)/shard_map/ppermute | solution.py:78
  8.9 0.3 convolution_convert_fusion.1
  9.3 1.1 fusion.13
  10.3 6.0 %all-to-all-start = ((bf16[16,224,128]{2,1,0:T(8,128)(2,1)}), bf16[16,224,128]{2,1,0:T(8,128)(2,1)S(1)}, u32[]{:S(2)}, u32[]{:S(2)}) async-start(bf16[16,224,128]{2,1,0:T(8,128)(2,1)} %fusion.13), calls=%async_computation | async-start | bytes 1835008 | tf_op jit(solution)/shard_map/all_to_all | solution.py:92
  16.4 14.1 %all-to-all-done = bf16[16,224,128]{2,1,0:T(8,128)(2,1)S(1)} async-done(((bf16[16,224,128]{2,1,0:T(8,128)(2,1)}), bf16[16,224,128]{2,1,0:T(8,128)(2,1)S(1)}, u32[]{:S(2)}, u32[]{:S(2)}) %all-to-all-start) | async-done | bytes 917536 | tf_op jit(solution)/shard_map/all_to_all | solution.py:92
  30.5 0.1 slice_reduce_fusion
  30.6 0.9 broadcast_in_dim.83
  31.5 4.5 %all-to-all-start.1 = ((bf16[16,128,128]{2,1,0:T(8,128)(2,1)}), bf16[16,128,128]{2,1,0:T(8,128)(2,1)S(1)}, u32[]{:S(2)}, u32[]{:S(2)}) async-start(bf16[16,128,128]{2,1,0:T(8,128)(2,1)} %broadcast_in_dim.83), calls=%async_computation.1 | async-start | bytes 1048576 | tf_op jit(solution)/shard_map/all_to_all | solution.py:50
  36.0 0.2 select_reduce_fusion.2
  36.2 7.0 %collective-permute-start.1 = (f32[96,96]{0,1:T(8,128)S(1)}, f32[96,96]{0,1:T(8,128)S(1)}, u32[]{:S(2)}, u32[]{:S(2)}) collective-permute-start(f32[96,96]{0,1:T(8,128)S(1)} %bitcast.93), channel_id=1, source_target_pairs={{0,128},{32,160},{64,192},{96,224},{128,0},{160,32},{192,64},{224,... | collective-permute-start | bytes 110600 | tf_op jit(solution)/shard_map/ppermute | solution.py:31
  43.2 1.2 fusion.2
  44.4 0.3 collective-permute-done.1
  44.7 0.1 maximum_select_fusion.3
  44.8 1.3 all-to-all-done.1
  46.1 0.4 fusion.4
  46.5 1.0 convolution_convert_fusion
  47.5 8.7 %all-to-all-start.2 = ((bf16[32,48,128]{2,1,0:T(8,128)(2,1)}), bf16[32,48,128]{2,1,0:T(8,128)(2,1)S(1)}, u32[]{:S(2)}, u32[]{:S(2)}) async-start(bf16[32,48,128]{2,1,0:T(8,128)(2,1)} %bitcast.11), calls=%async_computation.2 | async-start | bytes 786432 | tf_op jit(solution)/shard_map/all_to_all | solution.py:117
  56.2 2.3 %collective-permute-start.2 = (f32[192,96]{0,1:T(8,128)S(1)}, f32[192,96]{0,1:T(8,128)S(1)}, u32[]{:S(2)}, u32[]{:S(2)}) collective-permute-start(f32[192,96]{0,1:T(8,128)S(1)} %maximum_select_fusion.3), channel_id=1, source_target_pairs={{0,64},{32,96},{64,0},{96,32},{128,192},{160,224},{192,128},{224,1... | collective-permute-start | bytes 221192 | tf_op jit(solution)/shard_map/ppermute | solution.py:31
  58.6 3.8 %collective-permute-start.3 = (f32[48,128]{1,0:T(8,128)S(1)}, f32[48,128]{1,0:T(8,128)S(1)}, u32[]{:S(2)}, u32[]{:S(2)}) collective-permute-start(f32[48,128]{1,0:T(8,128)S(1)} %constant_dynamic-slice_fusion.2), channel_id=1, source_target_pairs={{0,0},{1,2},{2,4},{3,6},{4,8},{5,10},{6,12},{7,14},{8,16},{9,18},{... | collective-permute-start | bytes 73736 | tf_op jit(solution)/shard_map/ppermute | solution.py:105
  62.4 1.1 collective-permute-done.2
  63.5 0.1 maximum_select_fusion.2
  63.6 2.7 %collective-permute-done.3 = f32[48,128]{1,0:T(8,128)S(1)} collective-permute-done((f32[48,128]{1,0:T(8,128)S(1)}, f32[48,128]{1,0:T(8,128)S(1)}, u32[]{:S(2)}, u32[]{:S(2)}) %collective-permute-start.3) | collective-permute-done | bytes 24608 | tf_op jit(solution)/shard_map/ppermute | solution.py:105
  66.3 0.1 convert_reduce_fusion
  66.4 14.6 %all_to_all.45 = f32[8,48,128]{2,1,0:T(8,128)S(1)} all-to-all(f32[8,48,128]{2,1,0:T(8,128)S(1)} %broadcast_in_dim.87), channel_id=1, replica_groups=mesh['sub'=8,'row'=2,'col'=16] {'sub'}, dimensions={0} | all-to-all | bytes 393216 | tf_op jit(solution)/shard_map/all_to_all | solution.py:50
  81.0 0.8 broadcast_in_dim.88
  81.8 6.6 %all-to-all-start.4 = ((f32[16,48,128]{2,1,0:T(8,128)}), f32[16,48,128]{2,1,0:T(8,128)S(1)}, u32[]{:S(2)}, u32[]{:S(2)}) async-start(f32[16,48,128]{2,1,0:T(8,128)} %broadcast_in_dim.88), calls=%async_computation.4 | async-start | bytes 786432 | tf_op jit(solution)/shard_map/all_to_all | solution.py:50
  88.5 0.1 collective-permute-start.4
  88.6 4.0 %collective-permute-done.4 = f32[384,96]{0,1:T(8,128)S(1)} collective-permute-done((f32[384,96]{0,1:T(8,128)S(1)}, f32[384,96]{0,1:T(8,128)S(1)}, u32[]{:S(2)}, u32[]{:S(2)}) %collective-permute-start.4) | collective-permute-done | bytes 147488 | tf_op jit(solution)/shard_map/ppermute | solution.py:31
  92.5 4.4 %all-to-all-done.4 = f32[16,48,128]{2,1,0:T(8,128)S(1)} async-done(((f32[16,48,128]{2,1,0:T(8,128)}), f32[16,48,128]{2,1,0:T(8,128)S(1)}, u32[]{:S(2)}, u32[]{:S(2)}) %all-to-all-start.4) | async-done | bytes 393248 | tf_op jit(solution)/shard_map/all_to_all | solution.py:50
  96.9 0.3 fusion.19
  97.2 4.5 %all-gather = f32[192,128]{1,0:T(8,128)S(1)} all-gather(f32[96,128]{1,0:T(8,128)S(1)} %fusion.19), channel_id=2, replica_groups=mesh['sub'=8,'row'=2,'col'=16] {'row'}, dimensions={0}, use_global_device_ids=true | all-gather | bytes 147456 | tf_op jit(solution)/shard_map/all_gather | solution.py:122
  101.7 0.1 broadcast_in_dim.89
  101.8 12.2 %all_to_all.46 = bf16[16,96,128]{2,1,0:T(8,128)(2,1)S(1)} all-to-all(bf16[16,96,128]{2,1,0:T(8,128)(2,1)S(1)} %broadcast_in_dim.89), channel_id=1, replica_groups=mesh['sub'=8,'row'=2,'col'=16] {'col'}, dimensions={0} | all-to-all | bytes 786432 | tf_op jit(solution)/shard_map/all_to_all | solution.py:50
  114.0 0.3 convolution_subtract_fusion
  114.3 0.6 fusion.9
  114.9 0.9 bitcast_convert_fusion.1
  115.8 3.6 %all-to-all-start.6 = ((bf16[16,128,128]{1,2,0:T(8,128)(2,1)}), bf16[16,128,128]{1,2,0:T(8,128)(2,1)S(1)}, u32[]{:S(2)}, u32[]{:S(2)}) async-start(bf16[16,128,128]{1,2,0:T(8,128)(2,1)} %bitcast_convert_fusion.1), calls=%async_computation.6 | async-start | bytes 1048576 | tf_op jit(solution)/shard_map/all_to_all | solution.py:43
  119.4 0.2 copy.40
  119.6 0.1 constant_dynamic-slice_fusion.1
  119.6 9.8 %all-to-all-done.6 = bf16[16,128,128]{1,2,0:T(8,128)(2,1)S(1)} async-done(((bf16[16,128,128]{1,2,0:T(8,128)(2,1)}), bf16[16,128,128]{1,2,0:T(8,128)(2,1)S(1)}, u32[]{:S(2)}, u32[]{:S(2)}) %all-to-all-start.6) | async-done | bytes 524320 | tf_op jit(solution)/shard_map/all_to_all | solution.py:43
  129.5 0.2 select_reduce_fusion.1
  129.7 0.1 copy.29
  129.8 0.9 broadcast_in_dim.92
  130.7 3.6 %all-to-all-start.7 = ((bf16[16,128,128]{2,1,0:T(8,128)(2,1)}), bf16[16,128,128]{2,1,0:T(8,128)(2,1)S(1)}, u32[]{:S(2)}, u32[]{:S(2)}) async-start(bf16[16,128,128]{2,1,0:T(8,128)(2,1)} %broadcast_in_dim.92), calls=%async_computation.7 | async-start | bytes 1048576 | tf_op jit(solution)/shard_map/all_to_all | solution.py:50
  134.3 9.3 %all-to-all-done.7 = bf16[16,128,128]{2,1,0:T(8,128)(2,1)S(1)} async-done(((bf16[16,128,128]{2,1,0:T(8,128)(2,1)}), bf16[16,128,128]{2,1,0:T(8,128)(2,1)S(1)}, u32[]{:S(2)}, u32[]{:S(2)}) %all-to-all-start.7) | async-done | bytes 524320 | tf_op jit(solution)/shard_map/all_to_all | solution.py:50
  143.5 0.3 fusion.14
  143.8 4.7 %all-gather.1 = f32[256,128]{1,0:T(8,128)S(1)} all-gather(f32[128,128]{1,0:T(8,128)S(1)} %fusion.14), channel_id=3, replica_groups=mesh['sub'=8,'row'=2,'col'=16] {'row'}, dimensions={0}, use_global_device_ids=true | all-gather | bytes 196608 | tf_op jit(solution)/shard_map/all_gather | solution.py:128
  148.5 0.6 fusion.7
  149.2 0.9 bitcast_convert_fusion
  150.1 3.6 %all-to-all-start.8 = ((bf16[16,128,128]{1,2,0:T(8,128)(2,1)}), bf16[16,128,128]{1,2,0:T(8,128)(2,1)S(1)}, u32[]{:S(2)}, u32[]{:S(2)}) async-start(bf16[16,128,128]{1,2,0:T(8,128)(2,1)} %bitcast_convert_fusion), calls=%async_computation.8 | async-start | bytes 1048576 | tf_op jit(solution)/shard_map/all_to_all | solution.py:43
  153.6 0.2 copy.41
  153.8 0.1 constant_dynamic-slice_fusion
  153.9 10.7 %all-to-all-done.8 = bf16[16,128,128]{1,2,0:T(8,128)(2,1)S(1)} async-done(((bf16[16,128,128]{1,2,0:T(8,128)(2,1)}), bf16[16,128,128]{1,2,0:T(8,128)(2,1)S(1)}, u32[]{:S(2)}, u32[]{:S(2)}) %all-to-all-start.8) | async-done | bytes 524320 | tf_op jit(solution)/shard_map/all_to_all | solution.py:43
  164.6 0.2 select_reduce_fusion
  164.8 0.7 copy.32
  (28 shorter events, 0.1 us)
Async XLA Ops:
  0.6 1.2 copy-start
  0.6 4.4 %copy-start.6 = (s32[1,16,16]{2,1,0:T(8,128)S(1)}, s32[1,16,16]{2,1,0:T(8,128)}, u32[]{:S(2)}) copy-start(s32[1,16,16]{2,1,0:T(8,128)} %param.9) | copy-start | bytes 3076
  0.7 4.6 %copy-start.1 = (f32[96,1536]{1,0:T(8,128)S(1)}, f32[96,1536]{1,0:T(8,128)}, u32[]{:S(2)}) copy-start(f32[96,1536]{1,0:T(8,128)} %param.13) | copy-start | bytes 1769476
  3.7 5.2 %collective-permute-start = (bf16[128,128]{1,0:T(8,128)(2,1)S(1)}, bf16[128,128]{1,0:T(8,128)(2,1)S(1)}, u32[]{:S(2)}, u32[]{:S(2)}) collective-permute-start(bf16[128,128]{1,0:T(8,128)(2,1)S(1)} %get-tuple-element.14), channel_id=1, source_target_pairs={{0,16},{1,17},{2,18},{3,19},{4,20},{5,21},{6,22},{7,23},{8,24},{9,... | collective-permute-start | bytes 98312 | tf_op jit(solution)/shard_map/ppermute | solution.py:78
  6.1 2.8 %copy-start.2 = (bf16[1,2,128,2048]{3,2,1,0:T(8,128)(2,1)S(1)}, bf16[1,2,128,2048]{3,2,1,0:T(8,128)(2,1)}, u32[]{:S(2)}) copy-start(bf16[1,2,128,2048]{3,2,1,0:T(8,128)(2,1)} %param.8) | copy-start | bytes 3145732
  10.3 20.2 %all-to-all-start = ((bf16[16,224,128]{2,1,0:T(8,128)(2,1)}), bf16[16,224,128]{2,1,0:T(8,128)(2,1)S(1)}, u32[]{:S(2)}, u32[]{:S(2)}) async-start(bf16[16,224,128]{2,1,0:T(8,128)(2,1)} %fusion.13), calls=%async_computation | async-start | bytes 1835008 | tf_op jit(solution)/shard_map/all_to_all | solution.py:92
  30.6 12.6 %copy-start.7 = (bf16[1,1,128,1024]{3,2,1,0:T(8,128)(2,1)S(1)}, bf16[1,1,128,1024]{3,2,1,0:T(8,128)(2,1)}, u32[]{:S(2)}) copy-start(bf16[1,1,128,1024]{3,2,1,0:T(8,128)(2,1)} %param.11) | copy-start | bytes 786436
  30.6 12.6 %copy-start.8 = (s32[1,1024]{1,0:T(1,128)S(1)}, s32[1,1024]{1,0:T(1,128)}, u32[]{:S(2)}) copy-start(s32[1,1024]{1,0:T(1,128)} %param.12) | copy-start | bytes 12292
  31.5 14.6 %all-to-all-start.1 = ((bf16[16,128,128]{2,1,0:T(8,128)(2,1)}), bf16[16,128,128]{2,1,0:T(8,128)(2,1)S(1)}, u32[]{:S(2)}, u32[]{:S(2)}) async-start(bf16[16,128,128]{2,1,0:T(8,128)(2,1)} %broadcast_in_dim.83), calls=%async_computation.1 | async-start | bytes 1048576 | tf_op jit(solution)/shard_map/all_to_all | solution.py:50
  36.2 8.5 %collective-permute-start.1 = (f32[96,96]{0,1:T(8,128)S(1)}, f32[96,96]{0,1:T(8,128)S(1)}, u32[]{:S(2)}, u32[]{:S(2)}) collective-permute-start(f32[96,96]{0,1:T(8,128)S(1)} %bitcast.93), channel_id=1, source_target_pairs={{0,128},{32,160},{64,192},{96,224},{128,0},{160,32},{192,64},{224,... | collective-permute-start | bytes 110600 | tf_op jit(solution)/shard_map/ppermute | solution.py:31
  46.5 12.1 %copy-start.5 = (f32[96,128]{1,0:T(8,128)S(1)}, f32[96,128]{1,0:T(8,128)}, u32[]{:S(2)}) copy-start(f32[96,128]{1,0:T(8,128)} %param.15) | copy-start | bytes 147460
  47.5 18.8 %all-to-all-start.2 = ((bf16[32,48,128]{2,1,0:T(8,128)(2,1)}), bf16[32,48,128]{2,1,0:T(8,128)(2,1)S(1)}, u32[]{:S(2)}, u32[]{:S(2)}) async-start(bf16[32,48,128]{2,1,0:T(8,128)(2,1)} %bitcast.11), calls=%async_computation.2 | async-start | bytes 786432 | tf_op jit(solution)/shard_map/all_to_all | solution.py:117
  56.2 7.3 %collective-permute-start.2 = (f32[192,96]{0,1:T(8,128)S(1)}, f32[192,96]{0,1:T(8,128)S(1)}, u32[]{:S(2)}, u32[]{:S(2)}) collective-permute-start(f32[192,96]{0,1:T(8,128)S(1)} %maximum_select_fusion.3), channel_id=1, source_target_pairs={{0,64},{32,96},{64,0},{96,32},{128,192},{160,224},{192,128},{224,1... | collective-permute-start | bytes 221192 | tf_op jit(solution)/shard_map/ppermute | solution.py:31
  58.6 7.7 %collective-permute-start.3 = (f32[48,128]{1,0:T(8,128)S(1)}, f32[48,128]{1,0:T(8,128)S(1)}, u32[]{:S(2)}, u32[]{:S(2)}) collective-permute-start(f32[48,128]{1,0:T(8,128)S(1)} %constant_dynamic-slice_fusion.2), channel_id=1, source_target_pairs={{0,0},{1,2},{2,4},{3,6},{4,8},{5,10},{6,12},{7,14},{8,16},{9,18},{... | collective-permute-start | bytes 73736 | tf_op jit(solution)/shard_map/ppermute | solution.py:105
  81.8 15.1 %all-to-all-start.4 = ((f32[16,48,128]{2,1,0:T(8,128)}), f32[16,48,128]{2,1,0:T(8,128)S(1)}, u32[]{:S(2)}, u32[]{:S(2)}) async-start(f32[16,48,128]{2,1,0:T(8,128)} %broadcast_in_dim.88), calls=%async_computation.4 | async-start | bytes 786432 | tf_op jit(solution)/shard_map/all_to_all | solution.py:50
  88.5 4.1 %collective-permute-start.4 = (f32[384,96]{0,1:T(8,128)S(1)}, f32[384,96]{0,1:T(8,128)S(1)}, u32[]{:S(2)}, u32[]{:S(2)}) collective-permute-start(f32[384,96]{0,1:T(8,128)S(1)} %maximum_select_fusion.2), channel_id=1, source_target_pairs={{0,32},{32,0},{64,96},{96,64},{128,160},{160,128},{192,224},{224,1... | collective-permute-start | bytes 442376 | tf_op jit(solution)/shard_map/ppermute | solution.py:31
  101.7 12.6 %copy-start.4 = (f32[96,128]{1,0:T(8,128)}, f32[96,128]{1,0:T(8,128)S(1)}, u32[]{:S(2)}) copy-start(f32[96,128]{1,0:T(8,128)S(1)} %reduce_sum.70) | copy-start | bytes 147460
  115.8 13.7 %all-to-all-start.6 = ((bf16[16,128,128]{1,2,0:T(8,128)(2,1)}), bf16[16,128,128]{1,2,0:T(8,128)(2,1)S(1)}, u32[]{:S(2)}, u32[]{:S(2)}) async-start(bf16[16,128,128]{1,2,0:T(8,128)(2,1)} %bitcast_convert_fusion.1), calls=%async_computation.6 | async-start | bytes 1048576 | tf_op jit(solution)/shard_map/all_to_all | solution.py:43
  129.6 13.9 %copy-start.3 = (bf16[1,2,128,2048]{3,2,1,0:T(8,128)(2,1)S(1)}, bf16[1,2,128,2048]{3,2,1,0:T(8,128)(2,1)}, u32[]{:S(2)}) copy-start(bf16[1,2,128,2048]{3,2,1,0:T(8,128)(2,1)} %param.8) | copy-start | bytes 3145732
  130.7 12.9 %all-to-all-start.7 = ((bf16[16,128,128]{2,1,0:T(8,128)(2,1)}), bf16[16,128,128]{2,1,0:T(8,128)(2,1)S(1)}, u32[]{:S(2)}, u32[]{:S(2)}) async-start(bf16[16,128,128]{2,1,0:T(8,128)(2,1)} %broadcast_in_dim.92), calls=%async_computation.7 | async-start | bytes 1048576 | tf_op jit(solution)/shard_map/all_to_all | solution.py:50
  150.1 14.6 %all-to-all-start.8 = ((bf16[16,128,128]{1,2,0:T(8,128)(2,1)}), bf16[16,128,128]{1,2,0:T(8,128)(2,1)S(1)}, u32[]{:S(2)}, u32[]{:S(2)}) async-start(bf16[16,128,128]{1,2,0:T(8,128)(2,1)} %bitcast_convert_fusion), calls=%async_computation.8 | async-start | bytes 1048576 | tf_op jit(solution)/shard_map/all_to_all | solution.py:43

commit v14 on v13

--- a/solution.py
+++ b/solution.py
@@ -40,7 +40,8 @@
     parts = partial.reshape(count, -1, partial.shape[-1])
     here = lax.axis_index(axes)
     own = lax.dynamic_index_in_dim(parts, here, 0)
-    others = lax.all_to_all(parts.astype(bf16), axes, 0, 0).astype(f32)
+    low, own = lax.optimization_barrier((parts.astype(bf16), own))
+    others = lax.all_to_all(low, axes, 0, 0).astype(f32)
     index = lax.broadcasted_iota(jnp.int32, (count, 1, 1), 0)
     return jnp.where(index == here, own, others).sum(0)
 
@@ -118,6 +119,7 @@
     updates = updates.astype(f32).sum(0)
     updates = gather(updates, "sub", SUBS).sum(0)
     gram = collect(after(gram, updates), 1, sub_id)
+    gram, first = lax.optimization_barrier((gram, (row_id == 0).astype(f32)))
     rhs = gather(root_rows - updates, "col", COLS).reshape(SEPARATOR // 2, sources)
     root_part = lax.all_gather(mul_t(gram, rhs, precision=fine), "row").sum(0)
     root_full = gather(root_part.astype(bf16), "col", COLS).reshape(SEPARATOR, sources)
@@ -125,7 +127,7 @@
 
     value = sum_scatter(mul_t(inverse, value, precision=fine), "col", COLS)
     later_low = gather(value.astype(bf16), "col", COLS).reshape(PANEL, sources)
-    terms = lax.all_gather(mul(lower, later_low), "row")[1] * (row_id == 0).astype(f32)
+    terms = lax.all_gather(mul(lower, later_low), "row")[1] * first
     value = value - sum_scatter(mul_t(inverse, terms, precision=fine), "col", COLS)
     return value[None], root_part
 

time: 167 us -> 162 us (0.970)
  blocking collectives: 36 us -> 74.8 us
  waiting for transfers between devices: 60.3 us -> 30.5 us
  starting transfers between devices: 51.1 us -> 40.4 us
  local copies, waits for them, and re-layouts: 7.34 us -> 4.95 us
    all_to_all x0 -> x2, blocking collectives: none -> 26.4 us  [sum_scatter(): others = lax.all_to_all(low, axes, 0, 0).astype(f32)]
    all_to_all x2 -> x0, waiting for transfers between devices: 20.5 us -> none  [sum_scatter(): others = lax.all_to_all(parts.astype(bf16), axes, 0, 0).astype(f32)]
    all_to_all x2 -> x3, blocking collectives: 26.8 us -> 39.1 us  [gather(): return lax.all_to_all(spread, axes, 0, 0)]
    all_to_all x3 -> x2, waiting for transfers between devices: 14.9 us -> 5.63 us  [gather(): return lax.all_to_all(spread, axes, 0, 0)]
    all_to_all x2 -> x0, starting transfers between devices: 7.14 us -> none  [sum_scatter(): others = lax.all_to_all(parts.astype(bf16), axes, 0, 0).astype(f32)]
    all_to_all x3 -> x2, starting transfers between devices: 14.7 us -> 11.2 us  [gather(): return lax.all_to_all(spread, axes, 0, 0)]
  transfers between devices with their start and end apart: 12 -> 9, of which waited for: 11 -> 8; matrix products, arithmetic and copies ran while one was open for 2% -> 2% of each run, Pallas kernels for 0% -> 0%
where the time goes in v14:
time: 162 us; the launch traced here: 161 us
  blocking collectives  74.8 us (46%)
  starting transfers between devices  40.4 us (25%)
  waiting for transfers between devices  30.5 us (19%)
  matrix products  7.38 us (5%)
  local copies, waits for them, and re-layouts  4.95 us (3%)
  other arithmetic  2.25 us (1%)
    all_to_all x3, blocking collectives, gather(): return lax.all_to_all(spread, axes, 0, 0)  39.1 us
    all_to_all x2, blocking collectives, sum_scatter(): others = lax.all_to_all(low, axes, 0, 0).astype(f32)  26.4 us
    all_to_all x1, waiting for transfers between devices, shards(): both = lax.all_to_all(both, 'col', 0, 0)  14.1 us
    all_to_all x2, starting transfers between devices, gather(): return lax.all_to_all(spread, axes, 0, 0)  11.2 us
    ppermute x3, starting transfers between devices, collect(): other = lax.ppermute(blocks, 'sub', [(i, i ^ step) for i in range(SUBS)])  9.44 us
    all_to_all x1, starting transfers between devices, shards(): lax.all_to_all(updates, ('row', 'col'), 0, 0)  8.69 us
    all_to_all x1, starting transfers between devices, shards(): both = lax.all_to_all(both, 'col', 0, 0)  6.04 us
    all_to_all x2, waiting for transfers between devices, gather(): return lax.all_to_all(spread, axes, 0, 0)  5.63 us
  transfers between devices with their start and end apart: 9, of which 8 were waited for; matrix products, arithmetic and copies ran while one was open for 2% of the time, Pallas kernels for 0%

profile of v14, /device:TPU:1, one launch (start us, length us, event | category | flops | bytes accessed | tf_op | source)
XLA Modules:
  0.0 161.4 jit_solution(17258352434284535749)
XLA Ops:
  0.6 0.0 copy-start
  0.7 1.2 copy-done
  1.9 1.8 %fusion.27 = (bf16[128,128]{1,0:T(8,128)(2,1)S(1)}, f32[128,128]{1,0:T(8,128)S(1)}) fusion(f32[1,2048,128]{2,1,0:T(8,128)} %param.14, f32[1,128,2048]{2,1,0:T(8,128)S(1)} %copy-done), kind=kOutput, calls=%fused_computation.54 | convolution fusion | flops 201342976 | bytes 2195456 | tf_op jit(solution)/shard_map/dot_general | solution.py:19
  3.7 1.3 collective-permute-start
  5.1 0.2 fusion.25
  5.3 0.5 convolution_bitcast_fusion
  5.8 0.1 broadcast_bitcast_fusion
  5.9 0.3 copy.34
  6.1 0.0 copy-start.2
  6.2 0.1 convert_element_type.79
  6.2 2.7 %collective-permute-done = bf16[128,128]{1,0:T(8,128)(2,1)S(1)} collective-permute-done((bf16[128,128]{1,0:T(8,128)(2,1)S(1)}, bf16[128,128]{1,0:T(8,128)(2,1)S(1)}, u32[]{:S(2)}, u32[]{:S(2)}) %collective-permute-start) | collective-permute-done | bytes 32800 | tf_op jit(solution)/shard_map/ppermute | solution.py:79
  8.9 0.3 convolution_convert_fusion.1
  9.3 1.0 fusion.13
  10.3 6.0 %all-to-all-start = ((bf16[16,224,128]{2,1,0:T(8,128)(2,1)}), bf16[16,224,128]{2,1,0:T(8,128)(2,1)S(1)}, u32[]{:S(2)}, u32[]{:S(2)}) async-start(bf16[16,224,128]{2,1,0:T(8,128)(2,1)} %fusion.13), calls=%async_computation | async-start | bytes 1835008 | tf_op jit(solution)/shard_map/all_to_all | solution.py:93
  16.4 14.1 %all-to-all-done = bf16[16,224,128]{2,1,0:T(8,128)(2,1)S(1)} async-done(((bf16[16,224,128]{2,1,0:T(8,128)(2,1)}), bf16[16,224,128]{2,1,0:T(8,128)(2,1)S(1)}, u32[]{:S(2)}, u32[]{:S(2)}) %all-to-all-start) | async-done | bytes 917536 | tf_op jit(solution)/shard_map/all_to_all | solution.py:93
  30.5 0.1 slice_reduce_fusion
  30.6 0.0 copy-start.7
  30.6 0.9 broadcast_in_dim.83
  31.5 4.5 %all-to-all-start.1 = ((bf16[16,128,128]{2,1,0:T(8,128)(2,1)}), bf16[16,128,128]{2,1,0:T(8,128)(2,1)S(1)}, u32[]{:S(2)}, u32[]{:S(2)}) async-start(bf16[16,128,128]{2,1,0:T(8,128)(2,1)} %broadcast_in_dim.83), calls=%async_computation.1 | async-start | bytes 1048576 | tf_op jit(solution)/shard_map/all_to_all | solution.py:51
  36.0 0.2 select_reduce_fusion.2
  36.2 7.0 %collective-permute-start.1 = (f32[96,96]{0,1:T(8,128)S(1)}, f32[96,96]{0,1:T(8,128)S(1)}, u32[]{:S(2)}, u32[]{:S(2)}) collective-permute-start(f32[96,96]{0,1:T(8,128)S(1)} %bitcast.94), channel_id=1, source_target_pairs={{0,128},{32,160},{64,192},{96,224},{128,0},{160,32},{192,64},{224,... | collective-permute-start | bytes 110600 | tf_op jit(solution)/shard_map/ppermute | solution.py:31
  43.2 1.2 fusion.2
  44.4 0.3 collective-permute-done.1
  44.7 0.1 maximum_select_fusion.2
  44.8 1.3 all-to-all-done.1
  46.1 0.4 fusion.4
  46.5 0.0 copy-start.5
  46.5 1.0 convolution_convert_fusion
  47.5 8.7 %all-to-all-start.2 = ((bf16[32,48,128]{2,1,0:T(8,128)(2,1)}), bf16[32,48,128]{2,1,0:T(8,128)(2,1)S(1)}, u32[]{:S(2)}, u32[]{:S(2)}) async-start(bf16[32,48,128]{2,1,0:T(8,128)(2,1)} %bitcast.11), calls=%async_computation.2 | async-start | bytes 786432 | tf_op jit(solution)/shard_map/all_to_all | solution.py:118
  56.2 2.3 %collective-permute-start.2 = (f32[192,96]{0,1:T(8,128)S(1)}, f32[192,96]{0,1:T(8,128)S(1)}, u32[]{:S(2)}, u32[]{:S(2)}) collective-permute-start(f32[192,96]{0,1:T(8,128)S(1)} %maximum_select_fusion.2), channel_id=1, source_target_pairs={{0,64},{32,96},{64,0},{96,32},{128,192},{160,224},{192,128},{224,1... | collective-permute-start | bytes 221192 | tf_op jit(solution)/shard_map/ppermute | solution.py:31
  58.6 3.8 %collective-permute-start.3 = (f32[48,128]{1,0:T(8,128)S(1)}, f32[48,128]{1,0:T(8,128)S(1)}, u32[]{:S(2)}, u32[]{:S(2)}) collective-permute-start(f32[48,128]{1,0:T(8,128)S(1)} %constant_dynamic-slice_fusion.2), channel_id=1, source_target_pairs={{0,0},{1,2},{2,4},{3,6},{4,8},{5,10},{6,12},{7,14},{8,16},{9,18},{... | collective-permute-start | bytes 73736 | tf_op jit(solution)/shard_map/ppermute | solution.py:106
  62.4 1.1 collective-permute-done.2
  63.5 0.1 maximum_select_fusion.1
  63.6 2.7 %collective-permute-done.3 = f32[48,128]{1,0:T(8,128)S(1)} collective-permute-done((f32[48,128]{1,0:T(8,128)S(1)}, f32[48,128]{1,0:T(8,128)S(1)}, u32[]{:S(2)}, u32[]{:S(2)}) %collective-permute-start.3) | collective-permute-done | bytes 24608 | tf_op jit(solution)/shard_map/ppermute | solution.py:106
  66.3 0.1 convert_reduce_fusion
  66.4 14.6 %all_to_all.45 = f32[8,48,128]{2,1,0:T(8,128)S(1)} all-to-all(f32[8,48,128]{2,1,0:T(8,128)S(1)} %broadcast_in_dim.87), channel_id=1, replica_groups=mesh['sub'=8,'row'=2,'col'=16] {'sub'}, dimensions={0} | all-to-all | bytes 393216 | tf_op jit(solution)/shard_map/all_to_all | solution.py:51
  81.0 0.8 broadcast_in_dim.88
  81.8 6.7 %all-to-all-start.4 = ((f32[16,48,128]{2,1,0:T(8,128)}), f32[16,48,128]{2,1,0:T(8,128)S(1)}, u32[]{:S(2)}, u32[]{:S(2)}) async-start(f32[16,48,128]{2,1,0:T(8,128)} %broadcast_in_dim.88), calls=%async_computation.4 | async-start | bytes 786432 | tf_op jit(solution)/shard_map/all_to_all | solution.py:51
  88.4 0.1 collective-permute-start.4
  88.6 4.0 %collective-permute-done.4 = f32[384,96]{0,1:T(8,128)S(1)} collective-permute-done((f32[384,96]{0,1:T(8,128)S(1)}, f32[384,96]{0,1:T(8,128)S(1)}, u32[]{:S(2)}, u32[]{:S(2)}) %collective-permute-start.4) | collective-permute-done | bytes 147488 | tf_op jit(solution)/shard_map/ppermute | solution.py:31
  92.5 4.3 %all-to-all-done.4 = f32[16,48,128]{2,1,0:T(8,128)S(1)} async-done(((f32[16,48,128]{2,1,0:T(8,128)}), f32[16,48,128]{2,1,0:T(8,128)S(1)}, u32[]{:S(2)}, u32[]{:S(2)}) %all-to-all-start.4) | async-done | bytes 393248 | tf_op jit(solution)/shard_map/all_to_all | solution.py:51
  96.9 0.3 fusion.28
  97.2 4.5 %all-gather = f32[192,128]{1,0:T(8,128)S(1)} all-gather(f32[96,128]{1,0:T(8,128)S(1)} %fusion.28), channel_id=2, replica_groups=mesh['sub'=8,'row'=2,'col'=16] {'row'}, dimensions={0}, use_global_device_ids=true | all-gather | bytes 147456 | tf_op jit(solution)/shard_map/all_gather | solution.py:124
  101.7 0.1 broadcast_in_dim.89
  101.8 12.2 %all_to_all.46 = bf16[16,96,128]{2,1,0:T(8,128)(2,1)S(1)} all-to-all(bf16[16,96,128]{2,1,0:T(8,128)(2,1)S(1)} %broadcast_in_dim.89), channel_id=1, replica_groups=mesh['sub'=8,'row'=2,'col'=16] {'col'}, dimensions={0} | all-to-all | bytes 786432 | tf_op jit(solution)/shard_map/all_to_all | solution.py:51
  113.9 0.3 convolution_subtract_fusion
  114.3 0.6 fusion.9
  114.9 0.1 bitcast_convert_fusion.1
  115.0 0.2 copy.40
  115.2 0.1 constant_dynamic-slice_fusion.1
  115.3 13.0 %all_to_all.47 = bf16[16,128,128]{1,2,0:T(8,128)(2,1)S(1)} all-to-all(bf16[16,128,128]{1,2,0:T(8,128)(2,1)S(1)} %bitcast_convert_fusion.1), channel_id=1, replica_groups=mesh['sub'=8,'row'=2,'col'=16] {'col'}, dimensions={0} | all-to-all | bytes 1048576 | tf_op jit(solution)/shard_map/all_to_all | solution.py:44
  128.3 0.2 select_reduce_fusion.1
  128.5 0.1 copy.29
  128.6 0.1 broadcast_in_dim.92
  128.7 12.4 %all_to_all.48 = bf16[16,128,128]{2,1,0:T(8,128)(2,1)S(1)} all-to-all(bf16[16,128,128]{2,1,0:T(8,128)(2,1)S(1)} %broadcast_in_dim.92), channel_id=1, replica_groups=mesh['sub'=8,'row'=2,'col'=16] {'col'}, dimensions={0} | all-to-all | bytes 1048576 | tf_op jit(solution)/shard_map/all_to_all | solution.py:51
  141.0 0.3 fusion.14
  141.3 4.7 %all-gather.1 = f32[256,128]{1,0:T(8,128)S(1)} all-gather(f32[128,128]{1,0:T(8,128)S(1)} %fusion.14), channel_id=3, replica_groups=mesh['sub'=8,'row'=2,'col'=16] {'row'}, dimensions={0}, use_global_device_ids=true | all-gather | bytes 196608 | tf_op jit(solution)/shard_map/all_gather | solution.py:130
  146.1 0.6 fusion.7
  146.7 0.1 bitcast_convert_fusion
  146.8 0.2 copy.41
  147.0 0.1 constant_dynamic-slice_fusion
  147.0 13.5 %all_to_all.49 = bf16[16,128,128]{1,2,0:T(8,128)(2,1)S(1)} all-to-all(bf16[16,128,128]{1,2,0:T(8,128)(2,1)S(1)} %bitcast_convert_fusion), channel_id=1, replica_groups=mesh['sub'=8,'row'=2,'col'=16] {'col'}, dimensions={0} | all-to-all | bytes 1048576 | tf_op jit(solution)/shard_map/all_to_all | solution.py:44
  160.5 0.2 select_reduce_fusion
  160.7 0.7 copy.32
  (26 shorter events, 0.2 us)
Async XLA Ops:
  0.6 1.2 copy-start
  0.6 4.4 %copy-start.6 = (s32[1,16,16]{2,1,0:T(8,128)S(1)}, s32[1,16,16]{2,1,0:T(8,128)}, u32[]{:S(2)}) copy-start(s32[1,16,16]{2,1,0:T(8,128)} %param.9) | copy-start | bytes 3076
  0.7 4.6 %copy-start.1 = (f32[96,1536]{1,0:T(8,128)S(1)}, f32[96,1536]{1,0:T(8,128)}, u32[]{:S(2)}) copy-start(f32[96,1536]{1,0:T(8,128)} %param.13) | copy-start | bytes 1769476
  3.7 5.2 %collective-permute-start = (bf16[128,128]{1,0:T(8,128)(2,1)S(1)}, bf16[128,128]{1,0:T(8,128)(2,1)S(1)}, u32[]{:S(2)}, u32[]{:S(2)}) collective-permute-start(bf16[128,128]{1,0:T(8,128)(2,1)S(1)} %get-tuple-element.26), channel_id=1, source_target_pairs={{0,16},{1,17},{2,18},{3,19},{4,20},{5,21},{6,22},{7,23},{8,24},{9,... | collective-permute-start | bytes 98312 | tf_op jit(solution)/shard_map/ppermute | solution.py:79
  6.1 2.8 %copy-start.2 = (bf16[1,2,128,2048]{3,2,1,0:T(8,128)(2,1)S(1)}, bf16[1,2,128,2048]{3,2,1,0:T(8,128)(2,1)}, u32[]{:S(2)}) copy-start(bf16[1,2,128,2048]{3,2,1,0:T(8,128)(2,1)} %param.8) | copy-start | bytes 3145732
  10.3 20.2 %all-to-all-start = ((bf16[16,224,128]{2,1,0:T(8,128)(2,1)}), bf16[16,224,128]{2,1,0:T(8,128)(2,1)S(1)}, u32[]{:S(2)}, u32[]{:S(2)}) async-start(bf16[16,224,128]{2,1,0:T(8,128)(2,1)} %fusion.13), calls=%async_computation | async-start | bytes 1835008 | tf_op jit(solution)/shard_map/all_to_all | solution.py:93
  30.6 12.6 %copy-start.7 = (bf16[1,1,128,1024]{3,2,1,0:T(8,128)(2,1)S(1)}, bf16[1,1,128,1024]{3,2,1,0:T(8,128)(2,1)}, u32[]{:S(2)}) copy-start(bf16[1,1,128,1024]{3,2,1,0:T(8,128)(2,1)} %param.11) | copy-start | bytes 786436
  30.6 12.6 %copy-start.8 = (s32[1,1024]{1,0:T(1,128)S(1)}, s32[1,1024]{1,0:T(1,128)}, u32[]{:S(2)}) copy-start(s32[1,1024]{1,0:T(1,128)} %param.12) | copy-start | bytes 12292
  31.5 14.6 %all-to-all-start.1 = ((bf16[16,128,128]{2,1,0:T(8,128)(2,1)}), bf16[16,128,128]{2,1,0:T(8,128)(2,1)S(1)}, u32[]{:S(2)}, u32[]{:S(2)}) async-start(bf16[16,128,128]{2,1,0:T(8,128)(2,1)} %broadcast_in_dim.83), calls=%async_computation.1 | async-start | bytes 1048576 | tf_op jit(solution)/shard_map/all_to_all | solution.py:51
  36.2 8.5 %collective-permute-start.1 = (f32[96,96]{0,1:T(8,128)S(1)}, f32[96,96]{0,1:T(8,128)S(1)}, u32[]{:S(2)}, u32[]{:S(2)}) collective-permute-start(f32[96,96]{0,1:T(8,128)S(1)} %bitcast.94), channel_id=1, source_target_pairs={{0,128},{32,160},{64,192},{96,224},{128,0},{160,32},{192,64},{224,... | collective-permute-start | bytes 110600 | tf_op jit(solution)/shard_map/ppermute | solution.py:31
  46.5 12.1 %copy-start.5 = (f32[96,128]{1,0:T(8,128)S(1)}, f32[96,128]{1,0:T(8,128)}, u32[]{:S(2)}) copy-start(f32[96,128]{1,0:T(8,128)} %param.15) | copy-start | bytes 147460
  47.5 18.8 %all-to-all-start.2 = ((bf16[32,48,128]{2,1,0:T(8,128)(2,1)}), bf16[32,48,128]{2,1,0:T(8,128)(2,1)S(1)}, u32[]{:S(2)}, u32[]{:S(2)}) async-start(bf16[32,48,128]{2,1,0:T(8,128)(2,1)} %bitcast.11), calls=%async_computation.2 | async-start | bytes 786432 | tf_op jit(solution)/shard_map/all_to_all | solution.py:118
  56.2 7.3 %collective-permute-start.2 = (f32[192,96]{0,1:T(8,128)S(1)}, f32[192,96]{0,1:T(8,128)S(1)}, u32[]{:S(2)}, u32[]{:S(2)}) collective-permute-start(f32[192,96]{0,1:T(8,128)S(1)} %maximum_select_fusion.2), channel_id=1, source_target_pairs={{0,64},{32,96},{64,0},{96,32},{128,192},{160,224},{192,128},{224,1... | collective-permute-start | bytes 221192 | tf_op jit(solution)/shard_map/ppermute | solution.py:31
  58.6 7.7 %collective-permute-start.3 = (f32[48,128]{1,0:T(8,128)S(1)}, f32[48,128]{1,0:T(8,128)S(1)}, u32[]{:S(2)}, u32[]{:S(2)}) collective-permute-start(f32[48,128]{1,0:T(8,128)S(1)} %constant_dynamic-slice_fusion.2), channel_id=1, source_target_pairs={{0,0},{1,2},{2,4},{3,6},{4,8},{5,10},{6,12},{7,14},{8,16},{9,18},{... | collective-permute-start | bytes 73736 | tf_op jit(solution)/shard_map/ppermute | solution.py:106
  81.8 15.1 %all-to-all-start.4 = ((f32[16,48,128]{2,1,0:T(8,128)}), f32[16,48,128]{2,1,0:T(8,128)S(1)}, u32[]{:S(2)}, u32[]{:S(2)}) async-start(f32[16,48,128]{2,1,0:T(8,128)} %broadcast_in_dim.88), calls=%async_computation.4 | async-start | bytes 786432 | tf_op jit(solution)/shard_map/all_to_all | solution.py:51
  88.4 4.1 %collective-permute-start.4 = (f32[384,96]{0,1:T(8,128)S(1)}, f32[384,96]{0,1:T(8,128)S(1)}, u32[]{:S(2)}, u32[]{:S(2)}) collective-permute-start(f32[384,96]{0,1:T(8,128)S(1)} %maximum_select_fusion.1), channel_id=1, source_target_pairs={{0,32},{32,0},{64,96},{96,64},{128,160},{160,128},{192,224},{224,1... | collective-permute-start | bytes 442376 | tf_op jit(solution)/shard_map/ppermute | solution.py:31
  101.7 12.6 %copy-start.4 = (f32[96,128]{1,0:T(8,128)}, f32[96,128]{1,0:T(8,128)S(1)}, u32[]{:S(2)}) copy-start(f32[96,128]{1,0:T(8,128)S(1)} %reduce_sum.70) | copy-start | bytes 147460
  128.4 12.6 %copy-start.3 = (bf16[1,2,128,2048]{3,2,1,0:T(8,128)(2,1)S(1)}, bf16[1,2,128,2048]{3,2,1,0:T(8,128)(2,1)}, u32[]{:S(2)}) copy-start(bf16[1,2,128,2048]{3,2,1,0:T(8,128)(2,1)} %param.8) | copy-start | bytes 3145732

commit v15 on v14

--- a/solution.py
+++ b/solution.py
@@ -86,14 +86,16 @@
         lax.dynamic_slice_in_dim(root_inverse, band_id * band, band, 1),
         precision=fine,
     ).reshape(COLS, share, band)
-    own_gram = lax.dynamic_index_in_dim(gram, col_id, 0)
+    own_gram = gram
     gram = jnp.pad(gram.astype(bf16), ((0, 0), (0, 0), (0, sources - band)))
 
     both = jnp.concatenate([partial.reshape(COLS, width, sources), gram], 1)
     both = lax.all_to_all(both, "col", 0, 0)
     total = both[:, :width].astype(f32).sum(0).astype(bf16)
+    here, own_gram = after((col_id, own_gram), total)
+    own_gram = lax.dynamic_index_in_dim(own_gram, here, 0)
     chips = lax.broadcasted_iota(jnp.int32, (COLS, 1, 1), 0)
-    gram = jnp.where(chips == col_id, own_gram, both[:, width:, :band].astype(f32)).sum(0)
+    gram = jnp.where(chips == here, own_gram, both[:, width:, :band].astype(f32)).sum(0)
     gram = collect(gram.T, 4, sub_id)
 
     chunk = share // 2

time: 162 us -> 166 us (1.025)
  blocking collectives: 74.8 us -> 69.7 us
  waiting for transfers between devices: 30.5 us -> 34.1 us
  local copies, waits for them, and re-layouts: 4.95 us -> 7.93 us
    all_to_all x0 -> x1, blocking collectives: none -> 20 us  [shards(): both = lax.all_to_all(both, 'col', 0, 0)]
    all_to_all x2 -> x1, blocking collectives: 26.4 us -> 13.5 us  [sum_scatter(): others = lax.all_to_all(low, axes, 0, 0).astype(f32)]
    all_to_all x3 -> x2, blocking collectives: 39.1 us -> 27 us  [gather(): return lax.all_to_all(spread, axes, 0, 0)]
    all_to_all x2 -> x3, waiting for transfers between devices: 5.63 us -> 13.9 us  [gather(): return lax.all_to_all(spread, axes, 0, 0)]
    all_to_all x1, waiting for transfers between devices: 14.1 us -> 10.1 us  [sum_scatter(): others = lax.all_to_all(low, axes, 0, 0).astype(f32)]
    all_to_all x2 -> x3, starting transfers between devices: 11.2 us -> 13.8 us  [gather(): return lax.all_to_all(spread, axes, 0, 0)]
    all_to_all x1, starting transfers between devices: 6.04 us -> 3.58 us  [sum_scatter(): others = lax.all_to_all(low, axes, 0, 0).astype(f32)]
  transfers between devices with their start and end apart: 9 -> 10, of which waited for: 8 -> 7; matrix products, arithmetic and copies ran while one was open for 2% -> 2% of each run, Pallas kernels for 0% -> 0%
where the time goes in v15:
time: 166 us; the launch traced here: 165 us
  blocking collectives  69.7 us (42%)
  starting transfers between devices  41.7 us (25%)
  waiting for transfers between devices  34.1 us (21%)
  matrix products  8.98 us (5%)
  local copies, waits for them, and re-layouts  7.93 us (5%)
  other arithmetic  1.88 us (1%)
    all_to_all x2, blocking collectives, gather(): return lax.all_to_all(spread, axes, 0, 0)  27 us
    all_to_all x1, blocking collectives, shards(): both = lax.all_to_all(both, 'col', 0, 0)  20 us
    all_to_all x3, waiting for transfers between devices, gather(): return lax.all_to_all(spread, axes, 0, 0)  13.9 us
    all_to_all x3, starting transfers between devices, gather(): return lax.all_to_all(spread, axes, 0, 0)  13.8 us
    all_to_all x1, blocking collectives, sum_scatter(): others = lax.all_to_all(low, axes, 0, 0).astype(f32)  13.5 us
    all_to_all x1, waiting for transfers between devices, sum_scatter(): others = lax.all_to_all(low, axes, 0, 0).astype(f32)  10.1 us
    all_to_all x1, starting transfers between devices, shards(): lax.all_to_all(updates, ('row', 'col'), 0, 0)  9.81 us
    ppermute x3, starting transfers between devices, collect(): other = lax.ppermute(blocks, 'sub', [(i, i ^ step) for i in range(SUBS)])  9.42 us
  transfers between devices with their start and end apart: 10, of which 7 were waited for; matrix products, arithmetic and copies ran while one was open for 2% of the time, Pallas kernels for 0%

profile of v15, /device:TPU:1, one launch (start us, length us, event | category | flops | bytes accessed | tf_op | source)
XLA Modules:
  0.0 165.4 jit_solution(2829740458158349290)
XLA Ops:
  0.6 0.0 copy-start
  0.7 1.2 copy-done
  1.9 2.5 %fusion.27 = (bf16[128,128]{1,0:T(8,128)(2,1)S(1)}, f32[128,128]{1,0:T(8,128)}) fusion(f32[1,2048,128]{2,1,0:T(8,128)} %param.14, f32[1,128,2048]{2,1,0:T(8,128)S(1)} %copy-done), kind=kOutput, calls=%fused_computation.55 | convolution fusion | flops 201342976 | bytes 2195456 | tf_op jit(solution)/shard_map/dot_general | solution.py:19
  4.3 1.3 collective-permute-start
  5.7 0.2 fusion.25
  5.9 0.5 convolution_bitcast_fusion
  6.4 0.1 broadcast_bitcast_fusion
  6.5 0.3 reshape.82
  6.8 0.4 copy.24
  7.1 2.4 %collective-permute-done = bf16[128,128]{1,0:T(8,128)(2,1)S(1)} collective-permute-done((bf16[128,128]{1,0:T(8,128)(2,1)S(1)}, bf16[128,128]{1,0:T(8,128)(2,1)S(1)}, u32[]{:S(2)}, u32[]{:S(2)}) %collective-permute-start) | collective-permute-done | bytes 32800 | tf_op jit(solution)/shard_map/ppermute | solution.py:79
  9.5 0.3 convolution_convert_fusion.1
  9.9 0.1 fusion.13
  10.0 20.0 %all_to_all.45 = bf16[16,224,128]{2,1,0:T(8,128)(2,1)S(1)} all-to-all(bf16[16,224,128]{2,1,0:T(8,128)(2,1)S(1)} %fusion.13), channel_id=1, replica_groups=mesh['sub'=8,'row'=2,'col'=16] {'col'}, dimensions={0} | all-to-all | bytes 1835008 | tf_op jit(solution)/shard_map/all_to_all | solution.py:93
  30.0 0.7 slice_reduce_fusion
  30.7 0.4 copy.25
  31.0 0.0 copy-start.8
  31.0 1.6 broadcast_in_dim.83
  32.7 3.6 %all-to-all-start.1 = ((bf16[16,128,128]{2,1,0:T(8,128)(2,1)}), bf16[16,128,128]{2,1,0:T(8,128)(2,1)S(1)}, u32[]{:S(2)}, u32[]{:S(2)}) async-start(bf16[16,128,128]{2,1,0:T(8,128)(2,1)} %broadcast_in_dim.83), calls=%async_computation.1 | async-start | bytes 1048576 | tf_op jit(solution)/shard_map/all_to_all | solution.py:51
  36.3 0.2 select_reduce_fusion.2
  36.5 7.0 %collective-permute-start.1 = (f32[96,96]{0,1:T(8,128)S(1)}, f32[96,96]{0,1:T(8,128)S(1)}, u32[]{:S(2)}, u32[]{:S(2)}) collective-permute-start(f32[96,96]{0,1:T(8,128)S(1)} %bitcast.93), channel_id=1, source_target_pairs={{0,128},{32,160},{64,192},{96,224},{128,0},{160,32},{192,64},{224,... | collective-permute-start | bytes 110600 | tf_op jit(solution)/shard_map/ppermute | solution.py:31
  43.5 2.2 %fusion.2 = bf16[1536,128]{1,0:T(8,128)(2,1)S(1)} fusion(s32[1024]{0:T(1024)S(1)} %bitcast.97, bf16[1,1,128,1024]{3,2,1,0:T(8,128)(2,1)} %param.11), kind=kOutput, calls=%fused_computation.3 | convolution fusion | flops 404422656 | bytes 659456 | tf_op jit(solution)/shard_map/dot_general | solution.py:114
  45.6 0.1 maximum_select_fusion.2
  45.8 0.4 fusion.4
  46.2 0.0 copy-start.6
  46.2 1.0 convolution_convert_fusion
  47.2 9.8 %all-to-all-start.2 = ((bf16[32,48,128]{2,1,0:T(8,128)(2,1)}), bf16[32,48,128]{2,1,0:T(8,128)(2,1)S(1)}, u32[]{:S(2)}, u32[]{:S(2)}) async-start(bf16[32,48,128]{2,1,0:T(8,128)(2,1)} %bitcast.11), calls=%async_computation.2 | async-start | bytes 786432 | tf_op jit(solution)/shard_map/all_to_all | solution.py:120
  57.0 2.3 %collective-permute-start.2 = (f32[192,96]{0,1:T(8,128)S(1)}, f32[192,96]{0,1:T(8,128)S(1)}, u32[]{:S(2)}, u32[]{:S(2)}) collective-permute-start(f32[192,96]{0,1:T(8,128)S(1)} %maximum_select_fusion.2), channel_id=1, source_target_pairs={{0,64},{32,96},{64,0},{96,32},{128,192},{160,224},{192,128},{224,1... | collective-permute-start | bytes 221192 | tf_op jit(solution)/shard_map/ppermute | solution.py:31
  59.4 3.8 %collective-permute-start.3 = (f32[48,128]{1,0:T(8,128)S(1)}, f32[48,128]{1,0:T(8,128)S(1)}, u32[]{:S(2)}, u32[]{:S(2)}) collective-permute-start(f32[48,128]{1,0:T(8,128)S(1)} %constant_dynamic-slice_fusion.2), channel_id=1, source_target_pairs={{0,0},{1,2},{2,4},{3,6},{4,8},{5,10},{6,12},{7,14},{8,16},{9,18},{... | collective-permute-start | bytes 73736 | tf_op jit(solution)/shard_map/ppermute | solution.py:108
  63.2 1.1 collective-permute-done.2
  64.3 0.1 maximum_select_fusion.1
  64.4 2.7 %collective-permute-done.3 = f32[48,128]{1,0:T(8,128)S(1)} collective-permute-done((f32[48,128]{1,0:T(8,128)S(1)}, f32[48,128]{1,0:T(8,128)S(1)}, u32[]{:S(2)}, u32[]{:S(2)}) %collective-permute-start.3) | collective-permute-done | bytes 24608 | tf_op jit(solution)/shard_map/ppermute | solution.py:108
  67.1 0.1 convert_reduce_fusion
  67.2 14.6 %all_to_all.46 = f32[8,48,128]{2,1,0:T(8,128)S(1)} all-to-all(f32[8,48,128]{2,1,0:T(8,128)S(1)} %broadcast_in_dim.87), channel_id=1, replica_groups=mesh['sub'=8,'row'=2,'col'=16] {'sub'}, dimensions={0} | all-to-all | bytes 393216 | tf_op jit(solution)/shard_map/all_to_all | solution.py:51
  81.9 0.8 broadcast_in_dim.88
  82.6 6.6 %all-to-all-start.4 = ((f32[16,48,128]{2,1,0:T(8,128)}), f32[16,48,128]{2,1,0:T(8,128)S(1)}, u32[]{:S(2)}, u32[]{:S(2)}) async-start(f32[16,48,128]{2,1,0:T(8,128)} %broadcast_in_dim.88), calls=%async_computation.4 | async-start | bytes 786432 | tf_op jit(solution)/shard_map/all_to_all | solution.py:51
  89.3 0.1 collective-permute-start.4
  89.4 4.0 %collective-permute-done.4 = f32[384,96]{0,1:T(8,128)S(1)} collective-permute-done((f32[384,96]{0,1:T(8,128)S(1)}, f32[384,96]{0,1:T(8,128)S(1)}, u32[]{:S(2)}, u32[]{:S(2)}) %collective-permute-start.4) | collective-permute-done | bytes 147488 | tf_op jit(solution)/shard_map/ppermute | solution.py:31
  93.4 4.3 %all-to-all-done.4 = f32[16,48,128]{2,1,0:T(8,128)S(1)} async-done(((f32[16,48,128]{2,1,0:T(8,128)}), f32[16,48,128]{2,1,0:T(8,128)S(1)}, u32[]{:S(2)}, u32[]{:S(2)}) %all-to-all-start.4) | async-done | bytes 393248 | tf_op jit(solution)/shard_map/all_to_all | solution.py:51
  97.7 0.3 fusion.28
  98.0 4.5 %all-gather = f32[192,128]{1,0:T(8,128)S(1)} all-gather(f32[96,128]{1,0:T(8,128)S(1)} %fusion.28), channel_id=2, replica_groups=mesh['sub'=8,'row'=2,'col'=16] {'row'}, dimensions={0}, use_global_device_ids=true | all-gather | bytes 147456 | tf_op jit(solution)/shard_map/all_gather | solution.py:126
  102.6 0.8 broadcast_in_dim.89
  103.4 3.6 %all-to-all-start.5 = ((bf16[16,96,128]{2,1,0:T(8,128)(2,1)}), bf16[16,96,128]{2,1,0:T(8,128)(2,1)S(1)}, u32[]{:S(2)}, u32[]{:S(2)}) async-start(bf16[16,96,128]{2,1,0:T(8,128)(2,1)} %broadcast_in_dim.89), calls=%async_computation.5 | async-start | bytes 786432 | tf_op jit(solution)/shard_map/all_to_all | solution.py:51
  106.9 9.5 %all-to-all-done.5 = bf16[16,96,128]{2,1,0:T(8,128)(2,1)S(1)} async-done(((bf16[16,96,128]{2,1,0:T(8,128)(2,1)}), bf16[16,96,128]{2,1,0:T(8,128)(2,1)S(1)}, u32[]{:S(2)}, u32[]{:S(2)}) %all-to-all-start.5) | async-done | bytes 393248 | tf_op jit(solution)/shard_map/all_to_all | solution.py:51
  116.4 0.3 convolution_subtract_fusion
  116.8 0.6 fusion.9
  117.4 0.9 bitcast_convert_fusion.1
  118.3 0.2 copy.39
  118.5 0.1 constant_dynamic-slice_fusion.1
  118.5 3.6 %all-to-all-start.6 = ((bf16[16,128,128]{1,2,0:T(8,128)(2,1)}), bf16[16,128,128]{1,2,0:T(8,128)(2,1)S(1)}, u32[]{:S(2)}, u32[]{:S(2)}) async-start(bf16[16,128,128]{1,2,0:T(8,128)(2,1)} %bitcast_convert_fusion.1), calls=%async_computation.6 | async-start | bytes 1048576 | tf_op jit(solution)/shard_map/all_to_all | solution.py:44
  122.1 10.1 %all-to-all-done.6 = bf16[16,128,128]{1,2,0:T(8,128)(2,1)S(1)} async-done(((bf16[16,128,128]{1,2,0:T(8,128)(2,1)}), bf16[16,128,128]{1,2,0:T(8,128)(2,1)S(1)}, u32[]{:S(2)}, u32[]{:S(2)}) %all-to-all-start.6) | async-done | bytes 524320 | tf_op jit(solution)/shard_map/all_to_all | solution.py:44
  132.2 0.2 select_reduce_fusion.1
  132.4 0.0 copy-start.3
  132.4 0.1 copy.29
  132.5 0.1 broadcast_in_dim.92
  132.6 12.4 %all_to_all.47 = bf16[16,128,128]{2,1,0:T(8,128)(2,1)S(1)} all-to-all(bf16[16,128,128]{2,1,0:T(8,128)(2,1)S(1)} %broadcast_in_dim.92), channel_id=1, replica_groups=mesh['sub'=8,'row'=2,'col'=16] {'col'}, dimensions={0} | all-to-all | bytes 1048576 | tf_op jit(solution)/shard_map/all_to_all | solution.py:51
  145.0 0.3 fusion.14
  145.3 4.7 %all-gather.1 = f32[256,128]{1,0:T(8,128)S(1)} all-gather(f32[128,128]{1,0:T(8,128)S(1)} %fusion.14), channel_id=3, replica_groups=mesh['sub'=8,'row'=2,'col'=16] {'row'}, dimensions={0}, use_global_device_ids=true | all-gather | bytes 196608 | tf_op jit(solution)/shard_map/all_gather | solution.py:132
  150.0 0.6 fusion.7
  150.7 0.1 bitcast_convert_fusion
  150.8 0.2 copy.40
  151.0 0.1 constant_dynamic-slice_fusion
  151.0 13.5 %all_to_all.48 = bf16[16,128,128]{1,2,0:T(8,128)(2,1)S(1)} all-to-all(bf16[16,128,128]{1,2,0:T(8,128)(2,1)S(1)} %bitcast_convert_fusion), channel_id=1, replica_groups=mesh['sub'=8,'row'=2,'col'=16] {'col'}, dimensions={0} | all-to-all | bytes 1048576 | tf_op jit(solution)/shard_map/all_to_all | solution.py:44
  164.5 0.2 select_reduce_fusion
  164.7 0.7 copy.32
  (29 shorter events, 0.2 us)
Async XLA Ops:
  0.6 1.2 copy-start
  0.6 5.0 %copy-start.7 = (s32[1,16,16]{2,1,0:T(8,128)S(1)}, s32[1,16,16]{2,1,0:T(8,128)}, u32[]{:S(2)}) copy-start(s32[1,16,16]{2,1,0:T(8,128)} %param.9) | copy-start | bytes 3076
  0.7 5.2 %copy-start.1 = (f32[96,1536]{1,0:T(8,128)S(1)}, f32[96,1536]{1,0:T(8,128)}, u32[]{:S(2)}) copy-start(f32[96,1536]{1,0:T(8,128)} %param.13) | copy-start | bytes 1769476
  4.3 5.2 %collective-permute-start = (bf16[128,128]{1,0:T(8,128)(2,1)S(1)}, bf16[128,128]{1,0:T(8,128)(2,1)S(1)}, u32[]{:S(2)}, u32[]{:S(2)}) collective-permute-start(bf16[128,128]{1,0:T(8,128)(2,1)S(1)} %get-tuple-element.30), channel_id=1, source_target_pairs={{0,16},{1,17},{2,18},{3,19},{4,20},{5,21},{6,22},{7,23},{8,24},{9,... | collective-permute-start | bytes 98312 | tf_op jit(solution)/shard_map/ppermute | solution.py:79
  6.5 3.0 %copy-start.2 = (bf16[1,2,128,2048]{3,2,1,0:T(8,128)(2,1)S(1)}, bf16[1,2,128,2048]{3,2,1,0:T(8,128)(2,1)}, u32[]{:S(2)}) copy-start(bf16[1,2,128,2048]{3,2,1,0:T(8,128)(2,1)} %param.8) | copy-start | bytes 3145732
  31.0 12.4 %copy-start.8 = (s32[1,1024]{1,0:T(1,128)S(1)}, s32[1,1024]{1,0:T(1,128)}, u32[]{:S(2)}) copy-start(s32[1,1024]{1,0:T(1,128)} %param.12) | copy-start | bytes 12292
  32.7 13.1 %all-to-all-start.1 = ((bf16[16,128,128]{2,1,0:T(8,128)(2,1)}), bf16[16,128,128]{2,1,0:T(8,128)(2,1)S(1)}, u32[]{:S(2)}, u32[]{:S(2)}) async-start(bf16[16,128,128]{2,1,0:T(8,128)(2,1)} %broadcast_in_dim.83), calls=%async_computation.1 | async-start | bytes 1048576 | tf_op jit(solution)/shard_map/all_to_all | solution.py:51
  36.5 9.2 %collective-permute-start.1 = (f32[96,96]{0,1:T(8,128)S(1)}, f32[96,96]{0,1:T(8,128)S(1)}, u32[]{:S(2)}, u32[]{:S(2)}) collective-permute-start(f32[96,96]{0,1:T(8,128)S(1)} %bitcast.93), channel_id=1, source_target_pairs={{0,128},{32,160},{64,192},{96,224},{128,0},{160,32},{192,64},{224,... | collective-permute-start | bytes 110600 | tf_op jit(solution)/shard_map/ppermute | solution.py:31
  43.5 2.3 %copy-start.4 = (f32[128,128]{1,0:T(8,128)S(1)}, f32[128,128]{1,0:T(8,128)}, u32[]{:S(2)}) copy-start(f32[128,128]{1,0:T(8,128)} %get-tuple-element.31) | copy-start | bytes 196612
  46.2 13.2 %copy-start.6 = (f32[96,128]{1,0:T(8,128)S(1)}, f32[96,128]{1,0:T(8,128)}, u32[]{:S(2)}) copy-start(f32[96,128]{1,0:T(8,128)} %param.15) | copy-start | bytes 147460
  47.2 19.9 %all-to-all-start.2 = ((bf16[32,48,128]{2,1,0:T(8,128)(2,1)}), bf16[32,48,128]{2,1,0:T(8,128)(2,1)S(1)}, u32[]{:S(2)}, u32[]{:S(2)}) async-start(bf16[32,48,128]{2,1,0:T(8,128)(2,1)} %bitcast.11), calls=%async_computation.2 | async-start | bytes 786432 | tf_op jit(solution)/shard_map/all_to_all | solution.py:120
  57.0 7.3 %collective-permute-start.2 = (f32[192,96]{0,1:T(8,128)S(1)}, f32[192,96]{0,1:T(8,128)S(1)}, u32[]{:S(2)}, u32[]{:S(2)}) collective-permute-start(f32[192,96]{0,1:T(8,128)S(1)} %maximum_select_fusion.2), channel_id=1, source_target_pairs={{0,64},{32,96},{64,0},{96,32},{128,192},{160,224},{192,128},{224,1... | collective-permute-start | bytes 221192 | tf_op jit(solution)/shard_map/ppermute | solution.py:31
  59.4 7.7 %collective-permute-start.3 = (f32[48,128]{1,0:T(8,128)S(1)}, f32[48,128]{1,0:T(8,128)S(1)}, u32[]{:S(2)}, u32[]{:S(2)}) collective-permute-start(f32[48,128]{1,0:T(8,128)S(1)} %constant_dynamic-slice_fusion.2), channel_id=1, source_target_pairs={{0,0},{1,2},{2,4},{3,6},{4,8},{5,10},{6,12},{7,14},{8,16},{9,18},{... | collective-permute-start | bytes 73736 | tf_op jit(solution)/shard_map/ppermute | solution.py:108
  82.6 15.1 %all-to-all-start.4 = ((f32[16,48,128]{2,1,0:T(8,128)}), f32[16,48,128]{2,1,0:T(8,128)S(1)}, u32[]{:S(2)}, u32[]{:S(2)}) async-start(f32[16,48,128]{2,1,0:T(8,128)} %broadcast_in_dim.88), calls=%async_computation.4 | async-start | bytes 786432 | tf_op jit(solution)/shard_map/all_to_all | solution.py:51
  89.3 4.1 %collective-permute-start.4 = (f32[384,96]{0,1:T(8,128)S(1)}, f32[384,96]{0,1:T(8,128)S(1)}, u32[]{:S(2)}, u32[]{:S(2)}) collective-permute-start(f32[384,96]{0,1:T(8,128)S(1)} %maximum_select_fusion.1), channel_id=1, source_target_pairs={{0,32},{32,0},{64,96},{96,64},{128,160},{160,128},{192,224},{224,1... | collective-permute-start | bytes 442376 | tf_op jit(solution)/shard_map/ppermute | solution.py:31
  102.5 14.2 %copy-start.5 = (f32[96,128]{1,0:T(8,128)}, f32[96,128]{1,0:T(8,128)S(1)}, u32[]{:S(2)}) copy-start(f32[96,128]{1,0:T(8,128)S(1)} %reduce_sum.70) | copy-start | bytes 147460
  103.4 13.1 %all-to-all-start.5 = ((bf16[16,96,128]{2,1,0:T(8,128)(2,1)}), bf16[16,96,128]{2,1,0:T(8,128)(2,1)S(1)}, u32[]{:S(2)}, u32[]{:S(2)}) async-start(bf16[16,96,128]{2,1,0:T(8,128)(2,1)} %broadcast_in_dim.89), calls=%async_computation.5 | async-start | bytes 786432 | tf_op jit(solution)/shard_map/all_to_all | solution.py:51
  118.5 13.7 %all-to-all-start.6 = ((bf16[16,128,128]{1,2,0:T(8,128)(2,1)}), bf16[16,128,128]{1,2,0:T(8,128)(2,1)S(1)}, u32[]{:S(2)}, u32[]{:S(2)}) async-start(bf16[16,128,128]{1,2,0:T(8,128)(2,1)} %bitcast_convert_fusion.1), calls=%async_computation.6 | async-start | bytes 1048576 | tf_op jit(solution)/shard_map/all_to_all | solution.py:44
  132.4 12.7 %copy-start.3 = (bf16[1,2,128,2048]{3,2,1,0:T(8,128)(2,1)S(1)}, bf16[1,2,128,2048]{3,2,1,0:T(8,128)(2,1)}, u32[]{:S(2)}) copy-start(bf16[1,2,128,2048]{3,2,1,0:T(8,128)(2,1)} %param.8) | copy-start | bytes 3145732

commit v16 on v14

--- a/solution.py
+++ b/solution.py
@@ -89,13 +89,6 @@
     own_gram = lax.dynamic_index_in_dim(gram, col_id, 0)
     gram = jnp.pad(gram.astype(bf16), ((0, 0), (0, 0), (0, sources - band)))
 
-    both = jnp.concatenate([partial.reshape(COLS, width, sources), gram], 1)
-    both = lax.all_to_all(both, "col", 0, 0)
-    total = both[:, :width].astype(f32).sum(0).astype(bf16)
-    chips = lax.broadcasted_iota(jnp.int32, (COLS, 1, 1), 0)
-    gram = jnp.where(chips == col_id, own_gram, both[:, width:, :band].astype(f32)).sum(0)
-    gram = collect(gram.T, 4, sub_id)
-
     chunk = share // 2
     pairs = [
         (core * COLS + chip, (chip // 8) * COLS + 2 * (chip % 8) + core)
@@ -104,6 +97,13 @@
     ]
     root_rows = lax.dynamic_slice_in_dim(after(root_right, partial), row_id * chunk, chunk, 0)
     root_rows = lax.ppermute(root_rows, ("row", "col"), pairs)
+
+    both = jnp.concatenate([partial.reshape(COLS, width, sources), gram], 1)
+    both = after(lax.all_to_all(both, "col", 0, 0), root_rows)
+    total = both[:, :width].astype(f32).sum(0).astype(bf16)
+    chips = lax.broadcasted_iota(jnp.int32, (COLS, 1, 1), 0)
+    gram = jnp.where(chips == col_id, own_gram, both[:, width:, :band].astype(f32)).sum(0)
+    gram = collect(gram.T, 4, sub_id)
 
     total = after(gather(total, "col", COLS), gram).reshape(PANEL, sources)
     solved = own - mul(inverse, total.astype(f32), precision=fine)
@@ -115,7 +115,7 @@
 
     gram = collect(gram, 2, sub_id)
     updates = mul(couple_sep, solved.astype(bf16)).astype(bf16).reshape(2 * COLS, chunk, sources)
-    updates = after(lax.all_to_all(updates, ("row", "col"), 0, 0), (gram, root_rows))
+    updates = after(lax.all_to_all(updates, ("row", "col"), 0, 0), gram)
     updates = updates.astype(f32).sum(0)
     updates = gather(updates, "sub", SUBS).sum(0)
     gram = collect(after(gram, updates), 1, sub_id)

time: 162 us -> 162 us (level)
  waiting for transfers between devices: 30.5 us -> 28.6 us
  blocking collectives: 74.8 us -> 76.5 us
    all_to_all x2, waiting for transfers between devices: 14.1 us -> 2.3 us  [the longest x1 2.16 us: shards(): updates = after(lax.all_to_all(updates, ('row', 'col'), 0, 0), gram)]
    ppermute x1, waiting for transfers between devices: 2.68 us -> 9.09 us  [shards(): root_rows = lax.ppermute(root_rows, ('row', 'col'), pairs)]
    ppermute x3, waiting for transfers between devices: 5.36 us -> 9.05 us  [collect(): other = lax.ppermute(blocks, 'sub', [(i, i ^ step) for i in range(SUBS)])]
  transfers between devices with their start and end apart: 9 -> 9, of which waited for: 8 -> 9; matrix products, arithmetic and copies ran while one was open for 2% -> 2% of each run, Pallas kernels for 0% -> 0%
where the time goes in v16:
time: 162 us; the launch traced here: 161 us
  blocking collectives  76.5 us (47%)
  starting transfers between devices  40.1 us (25%)
  waiting for transfers between devices  28.6 us (18%)
  matrix products  7.38 us (5%)
  local copies, waits for them, and re-layouts  4.96 us (3%)
  other arithmetic  2.25 us (1%)
    all_to_all x3, blocking collectives, gather(): return lax.all_to_all(spread, axes, 0, 0)  39.7 us
    all_to_all x2, blocking collectives, sum_scatter(): others = lax.all_to_all(low, axes, 0, 0).astype(f32)  26.4 us
    all_to_all x2, starting transfers between devices, gather(): return lax.all_to_all(spread, axes, 0, 0)  9.94 us
    ppermute x3, starting transfers between devices, collect(): other = lax.ppermute(blocks, 'sub', [(i, i ^ step) for i in range(SUBS)])  9.88 us
    ppermute x1, waiting for transfers between devices, shards(): root_rows = lax.ppermute(root_rows, ('row', 'col'), pairs)  9.09 us
    ppermute x3, waiting for transfers between devices, collect(): other = lax.ppermute(blocks, 'sub', [(i, i ^ step) for i in range(SUBS)])  9.05 us
    all_to_all x1, starting transfers between devices, shards(): updates = after(lax.all_to_all(updates, ('row', 'col'), 0, 0), gram)  7.95 us
    all_to_all x1, starting transfers between devices, shards(): both = after(lax.all_to_all(both, 'col', 0, 0), root_rows)  6.17 us
  transfers between devices with their start and end apart: 9, of which 9 were waited for; matrix products, arithmetic and copies ran while one was open for 2% of the time, Pallas kernels for 0%

profile of v16, /device:TPU:1, one launch (start us, length us, event | category | flops | bytes accessed | tf_op | source)
XLA Modules:
  0.0 160.9 jit_solution(13802986234468517185)
XLA Ops:
  0.6 0.0 copy-start
  0.7 1.2 copy-done
  1.9 1.8 %fusion.27 = (bf16[128,128]{1,0:T(8,128)(2,1)S(1)}, f32[128,128]{1,0:T(8,128)S(1)}) fusion(f32[1,2048,128]{2,1,0:T(8,128)} %param.14, f32[1,128,2048]{2,1,0:T(8,128)S(1)} %copy-done), kind=kOutput, calls=%fused_computation.54 | convolution fusion | flops 201342976 | bytes 2195456 | tf_op jit(solution)/shard_map/dot_general | solution.py:19
  3.7 1.3 collective-permute-start
  5.1 0.2 fusion.25
  5.3 0.5 convolution_bitcast_fusion
  5.8 0.1 broadcast_bitcast_fusion
  5.9 0.3 copy.34
  6.1 0.0 copy-start.2
  6.2 0.1 convert_element_type.79
  6.2 2.7 %collective-permute-done = bf16[128,128]{1,0:T(8,128)(2,1)S(1)} collective-permute-done((bf16[128,128]{1,0:T(8,128)(2,1)S(1)}, bf16[128,128]{1,0:T(8,128)(2,1)S(1)}, u32[]{:S(2)}, u32[]{:S(2)}) %collective-permute-start) | collective-permute-done | bytes 32800 | tf_op jit(solution)/shard_map/ppermute | solution.py:79
  8.9 0.3 convolution_convert_fusion.1
  9.3 1.0 fusion.13
  10.3 6.2 %all-to-all-start = ((bf16[16,224,128]{2,1,0:T(8,128)(2,1)}), bf16[16,224,128]{2,1,0:T(8,128)(2,1)S(1)}, u32[]{:S(2)}, u32[]{:S(2)}) async-start(bf16[16,224,128]{2,1,0:T(8,128)(2,1)} %fusion.13), calls=%async_computation | async-start | bytes 1835008 | tf_op jit(solution)/shard_map/all_to_all | solution.py:102
  16.5 4.8 %collective-permute-start.1 = (f32[48,128]{1,0:T(8,128)S(1)}, f32[48,128]{1,0:T(8,128)S(1)}, u32[]{:S(2)}, u32[]{:S(2)}) collective-permute-start(f32[48,128]{1,0:T(8,128)S(1)} %constant_dynamic-slice_fusion.2), channel_id=1, source_target_pairs={{0,0},{1,2},{2,4},{3,6},{4,8},{5,10},{6,12},{7,14},{8,16},{9,18},{... | collective-permute-start | bytes 73736 | tf_op jit(solution)/shard_map/ppermute | solution.py:99
  21.4 9.1 %collective-permute-done.1 = f32[48,128]{1,0:T(8,128)S(1)} collective-permute-done((f32[48,128]{1,0:T(8,128)S(1)}, f32[48,128]{1,0:T(8,128)S(1)}, u32[]{:S(2)}, u32[]{:S(2)}) %collective-permute-start.1) | collective-permute-done | bytes 24608 | tf_op jit(solution)/shard_map/ppermute | solution.py:99
  30.5 0.1 all-to-all-done
  30.6 0.1 slice_reduce_fusion
  30.7 0.0 copy-start.7
  30.7 0.9 broadcast_in_dim.83
  31.6 5.0 %all-to-all-start.1 = ((bf16[16,128,128]{2,1,0:T(8,128)(2,1)}), bf16[16,128,128]{2,1,0:T(8,128)(2,1)S(1)}, u32[]{:S(2)}, u32[]{:S(2)}) async-start(bf16[16,128,128]{2,1,0:T(8,128)(2,1)} %broadcast_in_dim.83), calls=%async_computation.1 | async-start | bytes 1048576 | tf_op jit(solution)/shard_map/all_to_all | solution.py:51
  36.6 0.2 select_reduce_fusion.2
  36.8 7.0 %collective-permute-start.2 = (f32[96,96]{0,1:T(8,128)S(1)}, f32[96,96]{0,1:T(8,128)S(1)}, u32[]{:S(2)}, u32[]{:S(2)}) collective-permute-start(f32[96,96]{0,1:T(8,128)S(1)} %bitcast.94), channel_id=1, source_target_pairs={{0,128},{32,160},{64,192},{96,224},{128,0},{160,32},{192,64},{224,... | collective-permute-start | bytes 110600 | tf_op jit(solution)/shard_map/ppermute | solution.py:31
  43.8 1.2 fusion.2
  45.0 0.6 collective-permute-done.2
  45.6 0.1 maximum_select_fusion.2
  45.7 1.3 all-to-all-done.1
  47.0 0.4 fusion.4
  47.4 1.0 convolution_convert_fusion
  48.4 8.0 %all-to-all-start.2 = ((bf16[32,48,128]{2,1,0:T(8,128)(2,1)}), bf16[32,48,128]{2,1,0:T(8,128)(2,1)S(1)}, u32[]{:S(2)}, u32[]{:S(2)}) async-start(bf16[32,48,128]{2,1,0:T(8,128)(2,1)} %bitcast.11), calls=%async_computation.2 | async-start | bytes 786432 | tf_op jit(solution)/shard_map/all_to_all | solution.py:118
  56.4 2.3 %collective-permute-start.3 = (f32[192,96]{0,1:T(8,128)S(1)}, f32[192,96]{0,1:T(8,128)S(1)}, u32[]{:S(2)}, u32[]{:S(2)}) collective-permute-start(f32[192,96]{0,1:T(8,128)S(1)} %maximum_select_fusion.2), channel_id=1, source_target_pairs={{0,64},{32,96},{64,0},{96,32},{128,192},{160,224},{192,128},{224,1... | collective-permute-start | bytes 221192 | tf_op jit(solution)/shard_map/ppermute | solution.py:31
  58.7 4.9 %collective-permute-done.3 = f32[192,96]{0,1:T(8,128)S(1)} collective-permute-done((f32[192,96]{0,1:T(8,128)S(1)}, f32[192,96]{0,1:T(8,128)S(1)}, u32[]{:S(2)}, u32[]{:S(2)}) %collective-permute-start.3) | collective-permute-done | bytes 73760 | tf_op jit(solution)/shard_map/ppermute | solution.py:31
  63.6 0.1 maximum_select_fusion.1
  63.8 2.2 %all-to-all-done.2 = bf16[32,48,128]{2,1,0:T(8,128)(2,1)S(1)} async-done(((bf16[32,48,128]{2,1,0:T(8,128)(2,1)}), bf16[32,48,128]{2,1,0:T(8,128)(2,1)S(1)}, u32[]{:S(2)}, u32[]{:S(2)}) %all-to-all-start.2) | async-done | bytes 393248 | tf_op jit(solution)/shard_map/all_to_all | solution.py:118
  65.9 0.1 convert_reduce_fusion
  66.0 15.2 %all_to_all.45 = f32[8,48,128]{2,1,0:T(8,128)S(1)} all-to-all(f32[8,48,128]{2,1,0:T(8,128)S(1)} %broadcast_in_dim.87), channel_id=1, replica_groups=mesh['sub'=8,'row'=2,'col'=16] {'sub'}, dimensions={0} | all-to-all | bytes 393216 | tf_op jit(solution)/shard_map/all_to_all | solution.py:51
  81.2 0.8 broadcast_in_dim.88
  81.9 4.9 %all-to-all-start.4 = ((f32[16,48,128]{2,1,0:T(8,128)}), f32[16,48,128]{2,1,0:T(8,128)S(1)}, u32[]{:S(2)}, u32[]{:S(2)}) async-start(f32[16,48,128]{2,1,0:T(8,128)} %broadcast_in_dim.88), calls=%async_computation.4 | async-start | bytes 786432 | tf_op jit(solution)/shard_map/all_to_all | solution.py:51
  86.9 0.5 collective-permute-start.4
  87.4 3.5 %collective-permute-done.4 = f32[384,96]{0,1:T(8,128)S(1)} collective-permute-done((f32[384,96]{0,1:T(8,128)S(1)}, f32[384,96]{0,1:T(8,128)S(1)}, u32[]{:S(2)}, u32[]{:S(2)}) %collective-permute-start.4) | collective-permute-done | bytes 147488 | tf_op jit(solution)/shard_map/ppermute | solution.py:31
  91.0 4.2 %all-to-all-done.4 = f32[16,48,128]{2,1,0:T(8,128)S(1)} async-done(((f32[16,48,128]{2,1,0:T(8,128)}), f32[16,48,128]{2,1,0:T(8,128)S(1)}, u32[]{:S(2)}, u32[]{:S(2)}) %all-to-all-start.4) | async-done | bytes 393248 | tf_op jit(solution)/shard_map/all_to_all | solution.py:51
  95.2 0.3 fusion.28
  95.5 5.6 %all-gather = f32[192,128]{1,0:T(8,128)S(1)} all-gather(f32[96,128]{1,0:T(8,128)S(1)} %fusion.28), channel_id=2, replica_groups=mesh['sub'=8,'row'=2,'col'=16] {'row'}, dimensions={0}, use_global_device_ids=true | all-gather | bytes 147456 | tf_op jit(solution)/shard_map/all_gather | solution.py:124
  101.2 0.1 broadcast_in_dim.89
  101.2 12.2 %all_to_all.46 = bf16[16,96,128]{2,1,0:T(8,128)(2,1)S(1)} all-to-all(bf16[16,96,128]{2,1,0:T(8,128)(2,1)S(1)} %broadcast_in_dim.89), channel_id=1, replica_groups=mesh['sub'=8,'row'=2,'col'=16] {'col'}, dimensions={0} | all-to-all | bytes 786432 | tf_op jit(solution)/shard_map/all_to_all | solution.py:51
  113.4 0.3 convolution_subtract_fusion
  113.7 0.6 fusion.9
  114.3 0.1 bitcast_convert_fusion.1
  114.5 0.2 copy.40
  114.6 0.1 constant_dynamic-slice_fusion.1
  114.7 13.0 %all_to_all.47 = bf16[16,128,128]{1,2,0:T(8,128)(2,1)S(1)} all-to-all(bf16[16,128,128]{1,2,0:T(8,128)(2,1)S(1)} %bitcast_convert_fusion.1), channel_id=1, replica_groups=mesh['sub'=8,'row'=2,'col'=16] {'col'}, dimensions={0} | all-to-all | bytes 1048576 | tf_op jit(solution)/shard_map/all_to_all | solution.py:44
  127.7 0.2 select_reduce_fusion.1
  127.9 0.1 copy.29
  128.0 0.1 broadcast_in_dim.92
  128.1 12.4 %all_to_all.48 = bf16[16,128,128]{2,1,0:T(8,128)(2,1)S(1)} all-to-all(bf16[16,128,128]{2,1,0:T(8,128)(2,1)S(1)} %broadcast_in_dim.92), channel_id=1, replica_groups=mesh['sub'=8,'row'=2,'col'=16] {'col'}, dimensions={0} | all-to-all | bytes 1048576 | tf_op jit(solution)/shard_map/all_to_all | solution.py:51
  140.5 0.3 fusion.14
  140.8 4.7 %all-gather.1 = f32[256,128]{1,0:T(8,128)S(1)} all-gather(f32[128,128]{1,0:T(8,128)S(1)} %fusion.14), channel_id=3, replica_groups=mesh['sub'=8,'row'=2,'col'=16] {'row'}, dimensions={0}, use_global_device_ids=true | all-gather | bytes 196608 | tf_op jit(solution)/shard_map/all_gather | solution.py:130
  145.5 0.6 fusion.7
  146.1 0.1 bitcast_convert_fusion
  146.2 0.2 copy.41
  146.4 0.1 constant_dynamic-slice_fusion
  146.5 13.5 %all_to_all.49 = bf16[16,128,128]{1,2,0:T(8,128)(2,1)S(1)} all-to-all(bf16[16,128,128]{1,2,0:T(8,128)(2,1)S(1)} %bitcast_convert_fusion), channel_id=1, replica_groups=mesh['sub'=8,'row'=2,'col'=16] {'col'}, dimensions={0} | all-to-all | bytes 1048576 | tf_op jit(solution)/shard_map/all_to_all | solution.py:44
  160.0 0.2 select_reduce_fusion
  160.1 0.7 copy.32
  (26 shorter events, 0.2 us)
Async XLA Ops:
  0.6 1.2 copy-start
  0.6 4.4 %copy-start.6 = (s32[1,16,16]{2,1,0:T(8,128)S(1)}, s32[1,16,16]{2,1,0:T(8,128)}, u32[]{:S(2)}) copy-start(s32[1,16,16]{2,1,0:T(8,128)} %param.9) | copy-start | bytes 3076
  0.7 4.6 %copy-start.1 = (f32[96,1536]{1,0:T(8,128)S(1)}, f32[96,1536]{1,0:T(8,128)}, u32[]{:S(2)}) copy-start(f32[96,1536]{1,0:T(8,128)} %param.13) | copy-start | bytes 1769476
  3.7 5.2 %collective-permute-start = (bf16[128,128]{1,0:T(8,128)(2,1)S(1)}, bf16[128,128]{1,0:T(8,128)(2,1)S(1)}, u32[]{:S(2)}, u32[]{:S(2)}) collective-permute-start(bf16[128,128]{1,0:T(8,128)(2,1)S(1)} %get-tuple-element.28), channel_id=1, source_target_pairs={{0,16},{1,17},{2,18},{3,19},{4,20},{5,21},{6,22},{7,23},{8,24},{9,... | collective-permute-start | bytes 98312 | tf_op jit(solution)/shard_map/ppermute | solution.py:79
  6.1 2.8 %copy-start.2 = (bf16[1,2,128,2048]{3,2,1,0:T(8,128)(2,1)S(1)}, bf16[1,2,128,2048]{3,2,1,0:T(8,128)(2,1)}, u32[]{:S(2)}) copy-start(bf16[1,2,128,2048]{3,2,1,0:T(8,128)(2,1)} %param.8) | copy-start | bytes 3145732
  10.3 6.2 %copy-start.5 = (f32[96,128]{1,0:T(8,128)S(1)}, f32[96,128]{1,0:T(8,128)}, u32[]{:S(2)}) copy-start(f32[96,128]{1,0:T(8,128)} %param.15) | copy-start | bytes 147460
  10.3 20.3 %all-to-all-start = ((bf16[16,224,128]{2,1,0:T(8,128)(2,1)}), bf16[16,224,128]{2,1,0:T(8,128)(2,1)S(1)}, u32[]{:S(2)}, u32[]{:S(2)}) async-start(bf16[16,224,128]{2,1,0:T(8,128)(2,1)} %fusion.13), calls=%async_computation | async-start | bytes 1835008 | tf_op jit(solution)/shard_map/all_to_all | solution.py:102
  16.5 13.9 %collective-permute-start.1 = (f32[48,128]{1,0:T(8,128)S(1)}, f32[48,128]{1,0:T(8,128)S(1)}, u32[]{:S(2)}, u32[]{:S(2)}) collective-permute-start(f32[48,128]{1,0:T(8,128)S(1)} %constant_dynamic-slice_fusion.2), channel_id=1, source_target_pairs={{0,0},{1,2},{2,4},{3,6},{4,8},{5,10},{6,12},{7,14},{8,16},{9,18},{... | collective-permute-start | bytes 73736 | tf_op jit(solution)/shard_map/ppermute | solution.py:99
  30.7 13.1 %copy-start.7 = (bf16[1,1,128,1024]{3,2,1,0:T(8,128)(2,1)S(1)}, bf16[1,1,128,1024]{3,2,1,0:T(8,128)(2,1)}, u32[]{:S(2)}) copy-start(bf16[1,1,128,1024]{3,2,1,0:T(8,128)(2,1)} %param.11) | copy-start | bytes 786436
  30.7 13.1 %copy-start.8 = (s32[1,1024]{1,0:T(1,128)S(1)}, s32[1,1024]{1,0:T(1,128)}, u32[]{:S(2)}) copy-start(s32[1,1024]{1,0:T(1,128)} %param.12) | copy-start | bytes 12292
  31.6 15.4 %all-to-all-start.1 = ((bf16[16,128,128]{2,1,0:T(8,128)(2,1)}), bf16[16,128,128]{2,1,0:T(8,128)(2,1)S(1)}, u32[]{:S(2)}, u32[]{:S(2)}) async-start(bf16[16,128,128]{2,1,0:T(8,128)(2,1)} %broadcast_in_dim.83), calls=%async_computation.1 | async-start | bytes 1048576 | tf_op jit(solution)/shard_map/all_to_all | solution.py:51
  36.8 8.8 %collective-permute-start.2 = (f32[96,96]{0,1:T(8,128)S(1)}, f32[96,96]{0,1:T(8,128)S(1)}, u32[]{:S(2)}, u32[]{:S(2)}) collective-permute-start(f32[96,96]{0,1:T(8,128)S(1)} %bitcast.94), channel_id=1, source_target_pairs={{0,128},{32,160},{64,192},{96,224},{128,0},{160,32},{192,64},{224,... | collective-permute-start | bytes 110600 | tf_op jit(solution)/shard_map/ppermute | solution.py:31
  48.4 17.5 %all-to-all-start.2 = ((bf16[32,48,128]{2,1,0:T(8,128)(2,1)}), bf16[32,48,128]{2,1,0:T(8,128)(2,1)S(1)}, u32[]{:S(2)}, u32[]{:S(2)}) async-start(bf16[32,48,128]{2,1,0:T(8,128)(2,1)} %bitcast.11), calls=%async_computation.2 | async-start | bytes 786432 | tf_op jit(solution)/shard_map/all_to_all | solution.py:118
  56.4 7.3 %collective-permute-start.3 = (f32[192,96]{0,1:T(8,128)S(1)}, f32[192,96]{0,1:T(8,128)S(1)}, u32[]{:S(2)}, u32[]{:S(2)}) collective-permute-start(f32[192,96]{0,1:T(8,128)S(1)} %maximum_select_fusion.2), channel_id=1, source_target_pairs={{0,64},{32,96},{64,0},{96,32},{128,192},{160,224},{192,128},{224,1... | collective-permute-start | bytes 221192 | tf_op jit(solution)/shard_map/ppermute | solution.py:31
  81.9 13.3 %all-to-all-start.4 = ((f32[16,48,128]{2,1,0:T(8,128)}), f32[16,48,128]{2,1,0:T(8,128)S(1)}, u32[]{:S(2)}, u32[]{:S(2)}) async-start(f32[16,48,128]{2,1,0:T(8,128)} %broadcast_in_dim.88), calls=%async_computation.4 | async-start | bytes 786432 | tf_op jit(solution)/shard_map/all_to_all | solution.py:51
  86.9 4.1 %collective-permute-start.4 = (f32[384,96]{0,1:T(8,128)S(1)}, f32[384,96]{0,1:T(8,128)S(1)}, u32[]{:S(2)}, u32[]{:S(2)}) collective-permute-start(f32[384,96]{0,1:T(8,128)S(1)} %maximum_select_fusion.1), channel_id=1, source_target_pairs={{0,32},{32,0},{64,96},{96,64},{128,160},{160,128},{192,224},{224,1... | collective-permute-start | bytes 442376 | tf_op jit(solution)/shard_map/ppermute | solution.py:31
  101.1 12.6 %copy-start.4 = (f32[96,128]{1,0:T(8,128)}, f32[96,128]{1,0:T(8,128)S(1)}, u32[]{:S(2)}) copy-start(f32[96,128]{1,0:T(8,128)S(1)} %reduce_sum.70) | copy-start | bytes 147460
  127.9 12.6 %copy-start.3 = (bf16[1,2,128,2048]{3,2,1,0:T(8,128)(2,1)S(1)}, bf16[1,2,128,2048]{3,2,1,0:T(8,128)(2,1)}, u32[]{:S(2)}) copy-start(bf16[1,2,128,2048]{3,2,1,0:T(8,128)(2,1)} %param.8) | copy-start | bytes 3145732

commit v17 on v16

--- a/solution.py
+++ b/solution.py
@@ -98,8 +98,13 @@
     root_rows = lax.dynamic_slice_in_dim(after(root_right, partial), row_id * chunk, chunk, 0)
     root_rows = lax.ppermute(root_rows, ("row", "col"), pairs)
 
+    onehot = (jnp.arange(SEPARATOR)[:, None] == after(rows_sep, partial)[None, :]).astype(bf16)
+    couple_sep = lax.dot_general(
+        onehot, couple, (((1,), (1,)), ((), ())), preferred_element_type=f32
+    ).astype(bf16)
+
     both = jnp.concatenate([partial.reshape(COLS, width, sources), gram], 1)
-    both = after(lax.all_to_all(both, "col", 0, 0), root_rows)
+    both = after(lax.all_to_all(both, "col", 0, 0), (root_rows, couple_sep))
     total = both[:, :width].astype(f32).sum(0).astype(bf16)
     chips = lax.broadcasted_iota(jnp.int32, (COLS, 1, 1), 0)
     gram = jnp.where(chips == col_id, own_gram, both[:, width:, :band].astype(f32)).sum(0)
@@ -107,11 +112,6 @@
 
     total = after(gather(total, "col", COLS), gram).reshape(PANEL, sources)
     solved = own - mul(inverse, total.astype(f32), precision=fine)
-
-    onehot = (jnp.arange(SEPARATOR)[:, None] == rows_sep[None, :]).astype(bf16)
-    couple_sep = lax.dot_general(
-        onehot, couple, (((1,), (1,)), ((), ())), preferred_element_type=f32
-    ).astype(bf16)
 
     gram = collect(gram, 2, sub_id)
     updates = mul(couple_sep, solved.astype(bf16)).astype(bf16).reshape(2 * COLS, chunk, sources)

time: 162 us -> 163 us (level)
  matrix products: 7.38 us -> 9.52 us
    ppermute x1, waiting for transfers between devices: 9.09 us -> 7.1 us  [shards(): root_rows = lax.ppermute(root_rows, ('row', 'col'), pairs)]
  transfers between devices with their start and end apart: 9 -> 9, of which waited for: 9 -> 8; matrix products, arithmetic and copies ran while one was open for 2% -> 2% of each run, Pallas kernels for 0% -> 0%
where the time goes in v17:
time: 163 us; the launch traced here: 162 us
  blocking collectives  76.5 us (47%)
  starting transfers between devices  39.9 us (24%)
  waiting for transfers between devices  28.1 us (17%)
  matrix products  9.52 us (6%)
  local copies, waits for them, and re-layouts  4.95 us (3%)
  other arithmetic  2.26 us (1%)
    all_to_all x3, blocking collectives, gather(): return lax.all_to_all(spread, axes, 0, 0)  39.7 us
    all_to_all x2, blocking collectives, sum_scatter(): others = lax.all_to_all(low, axes, 0, 0).astype(f32)  26.5 us
    ppermute x3, waiting for transfers between devices, collect(): other = lax.ppermute(blocks, 'sub', [(i, i ^ step) for i in range(SUBS)])  10.2 us
    all_to_all x2, starting transfers between devices, gather(): return lax.all_to_all(spread, axes, 0, 0)  9.92 us
    ppermute x3, starting transfers between devices, collect(): other = lax.ppermute(blocks, 'sub', [(i, i ^ step) for i in range(SUBS)])  9.87 us
    all_to_all x1, starting transfers between devices, shards(): updates = after(lax.all_to_all(updates, ('row', 'col'), 0, 0), gram)  7.9 us
    ppermute x1, waiting for transfers between devices, shards(): root_rows = lax.ppermute(root_rows, ('row', 'col'), pairs)  7.1 us
    all_gather x1, blocking collectives, shards(): root_part = lax.all_gather(mul_t(gram, rhs, precision=fine), 'row').sum(0)  5.65 us
  transfers between devices with their start and end apart: 9, of which 8 were waited for; matrix products, arithmetic and copies ran while one was open for 2% of the time, Pallas kernels for 0%

profile of v17, /device:TPU:1, one launch (start us, length us, event | category | flops | bytes accessed | tf_op | source)
XLA Modules:
  0.0 162.2 jit_solution(9979273535822334188)
XLA Ops:
  0.6 0.0 copy-start
  0.7 1.2 copy-done
  1.9 2.5 %fusion.27 = (bf16[128,128]{1,0:T(8,128)(2,1)}, f32[128,128]{1,0:T(8,128)S(1)}) fusion(f32[1,2048,128]{2,1,0:T(8,128)} %param.14, f32[1,128,2048]{2,1,0:T(8,128)S(1)} %copy-done), kind=kOutput, calls=%fused_computation.54 | convolution fusion | flops 201342976 | bytes 2195456 | tf_op jit(solution)/shard_map/dot_general | solution.py:19
  4.3 1.3 collective-permute-start
  5.7 0.2 fusion.25
  5.9 0.0 copy-done.2
  5.9 0.5 convolution_bitcast_fusion
  6.4 0.1 broadcast_bitcast_fusion
  6.5 0.3 copy.34
  6.8 0.1 convert_element_type.79
  6.8 3.0 %collective-permute-done = bf16[128,128]{1,0:T(8,128)(2,1)} collective-permute-done((bf16[128,128]{1,0:T(8,128)(2,1)}, bf16[128,128]{1,0:T(8,128)(2,1)}, u32[]{:S(2)}, u32[]{:S(2)}) %collective-permute-start) | collective-permute-done | bytes 32800 | tf_op jit(solution)/shard_map/ppermute | solution.py:79
  9.9 1.1 convolution_convert_fusion.1
  11.0 1.0 fusion.13
  12.0 5.6 %all-to-all-start = ((bf16[16,224,128]{2,1,0:T(8,128)(2,1)}), bf16[16,224,128]{2,1,0:T(8,128)(2,1)S(1)}, u32[]{:S(2)}, u32[]{:S(2)}) async-start(bf16[16,224,128]{2,1,0:T(8,128)(2,1)} %fusion.13), calls=%async_computation | async-start | bytes 1835008 | tf_op jit(solution)/shard_map/all_to_all | solution.py:107
  17.7 5.3 %collective-permute-start.1 = (f32[48,128]{1,0:T(8,128)S(1)}, f32[48,128]{1,0:T(8,128)S(1)}, u32[]{:S(2)}, u32[]{:S(2)}) collective-permute-start(f32[48,128]{1,0:T(8,128)S(1)} %constant_dynamic-slice_fusion.2), channel_id=1, source_target_pairs={{0,0},{1,2},{2,4},{3,6},{4,8},{5,10},{6,12},{7,14},{8,16},{9,18},{... | collective-permute-start | bytes 73736 | tf_op jit(solution)/shard_map/ppermute | solution.py:99
  23.0 1.9 %fusion.2 = bf16[1536,128]{1,0:T(8,128)(2,1)} fusion(s32[1024]{0:T(1024)S(1)} %bitcast.98, bf16[1,1,128,1024]{3,2,1,0:T(8,128)(2,1)S(1)} %copy-done.8), kind=kOutput, calls=%fused_computation.3 | convolution fusion | flops 404422656 | bytes 659456 | tf_op jit(solution)/shard_map/dot_general | solution.py:102
  24.9 7.1 %collective-permute-done.1 = f32[48,128]{1,0:T(8,128)S(1)} collective-permute-done((f32[48,128]{1,0:T(8,128)S(1)}, f32[48,128]{1,0:T(8,128)S(1)}, u32[]{:S(2)}, u32[]{:S(2)}) %collective-permute-start.1) | collective-permute-done | bytes 24608 | tf_op jit(solution)/shard_map/ppermute | solution.py:99
  32.1 0.0 all-to-all-done
  32.1 0.1 slice_reduce_fusion
  32.1 0.9 broadcast_in_dim.84
  33.0 5.0 %all-to-all-start.1 = ((bf16[16,128,128]{2,1,0:T(8,128)(2,1)}), bf16[16,128,128]{2,1,0:T(8,128)(2,1)S(1)}, u32[]{:S(2)}, u32[]{:S(2)}) async-start(bf16[16,128,128]{2,1,0:T(8,128)(2,1)} %broadcast_in_dim.84), calls=%async_computation.1 | async-start | bytes 1048576 | tf_op jit(solution)/shard_map/all_to_all | solution.py:51
  38.0 0.2 select_reduce_fusion.2
  38.2 7.0 %collective-permute-start.2 = (f32[96,96]{0,1:T(8,128)S(1)}, f32[96,96]{0,1:T(8,128)S(1)}, u32[]{:S(2)}, u32[]{:S(2)}) collective-permute-start(f32[96,96]{0,1:T(8,128)S(1)} %bitcast.94), channel_id=1, source_target_pairs={{0,128},{32,160},{64,192},{96,224},{128,0},{160,32},{192,64},{224,... | collective-permute-start | bytes 110600 | tf_op jit(solution)/shard_map/ppermute | solution.py:31
  45.2 1.8 %collective-permute-done.2 = f32[96,96]{0,1:T(8,128)S(1)} collective-permute-done((f32[96,96]{0,1:T(8,128)S(1)}, f32[96,96]{0,1:T(8,128)S(1)}, u32[]{:S(2)}, u32[]{:S(2)}) %collective-permute-start.2) | collective-permute-done | bytes 36896 | tf_op jit(solution)/shard_map/ppermute | solution.py:31
  47.0 0.1 maximum_select_fusion.2
  47.1 1.3 all-to-all-done.1
  48.4 0.4 fusion.4
  48.9 1.0 convolution_convert_fusion
  49.8 7.9 %all-to-all-start.2 = ((bf16[32,48,128]{2,1,0:T(8,128)(2,1)}), bf16[32,48,128]{2,1,0:T(8,128)(2,1)S(1)}, u32[]{:S(2)}, u32[]{:S(2)}) async-start(bf16[32,48,128]{2,1,0:T(8,128)(2,1)} %bitcast.11), calls=%async_computation.2 | async-start | bytes 786432 | tf_op jit(solution)/shard_map/all_to_all | solution.py:118
  57.7 2.3 %collective-permute-start.3 = (f32[192,96]{0,1:T(8,128)S(1)}, f32[192,96]{0,1:T(8,128)S(1)}, u32[]{:S(2)}, u32[]{:S(2)}) collective-permute-start(f32[192,96]{0,1:T(8,128)S(1)} %maximum_select_fusion.2), channel_id=1, source_target_pairs={{0,64},{32,96},{64,0},{96,32},{128,192},{160,224},{192,128},{224,1... | collective-permute-start | bytes 221192 | tf_op jit(solution)/shard_map/ppermute | solution.py:31
  60.1 4.9 %collective-permute-done.3 = f32[192,96]{0,1:T(8,128)S(1)} collective-permute-done((f32[192,96]{0,1:T(8,128)S(1)}, f32[192,96]{0,1:T(8,128)S(1)}, u32[]{:S(2)}, u32[]{:S(2)}) %collective-permute-start.3) | collective-permute-done | bytes 73760 | tf_op jit(solution)/shard_map/ppermute | solution.py:31
  65.0 0.1 maximum_select_fusion.1
  65.1 2.2 %all-to-all-done.2 = bf16[32,48,128]{2,1,0:T(8,128)(2,1)S(1)} async-done(((bf16[32,48,128]{2,1,0:T(8,128)(2,1)}), bf16[32,48,128]{2,1,0:T(8,128)(2,1)S(1)}, u32[]{:S(2)}, u32[]{:S(2)}) %all-to-all-start.2) | async-done | bytes 393248 | tf_op jit(solution)/shard_map/all_to_all | solution.py:118
  67.3 0.1 convert_reduce_fusion
  67.4 15.2 %all_to_all.45 = f32[8,48,128]{2,1,0:T(8,128)S(1)} all-to-all(f32[8,48,128]{2,1,0:T(8,128)S(1)} %broadcast_in_dim.88), channel_id=1, replica_groups=mesh['sub'=8,'row'=2,'col'=16] {'sub'}, dimensions={0} | all-to-all | bytes 393216 | tf_op jit(solution)/shard_map/all_to_all | solution.py:51
  82.6 0.8 broadcast_in_dim.89
  83.3 4.9 %all-to-all-start.4 = ((f32[16,48,128]{2,1,0:T(8,128)}), f32[16,48,128]{2,1,0:T(8,128)S(1)}, u32[]{:S(2)}, u32[]{:S(2)}) async-start(f32[16,48,128]{2,1,0:T(8,128)} %broadcast_in_dim.89), calls=%async_computation.4 | async-start | bytes 786432 | tf_op jit(solution)/shard_map/all_to_all | solution.py:51
  88.3 0.5 collective-permute-start.4
  88.8 3.5 %collective-permute-done.4 = f32[384,96]{0,1:T(8,128)S(1)} collective-permute-done((f32[384,96]{0,1:T(8,128)S(1)}, f32[384,96]{0,1:T(8,128)S(1)}, u32[]{:S(2)}, u32[]{:S(2)}) %collective-permute-start.4) | collective-permute-done | bytes 147488 | tf_op jit(solution)/shard_map/ppermute | solution.py:31
  92.4 4.2 %all-to-all-done.4 = f32[16,48,128]{2,1,0:T(8,128)S(1)} async-done(((f32[16,48,128]{2,1,0:T(8,128)}), f32[16,48,128]{2,1,0:T(8,128)S(1)}, u32[]{:S(2)}, u32[]{:S(2)}) %all-to-all-start.4) | async-done | bytes 393248 | tf_op jit(solution)/shard_map/all_to_all | solution.py:51
  96.6 0.3 fusion.28
  96.9 5.6 %all-gather = f32[192,128]{1,0:T(8,128)S(1)} all-gather(f32[96,128]{1,0:T(8,128)S(1)} %fusion.28), channel_id=2, replica_groups=mesh['sub'=8,'row'=2,'col'=16] {'row'}, dimensions={0}, use_global_device_ids=true | all-gather | bytes 147456 | tf_op jit(solution)/shard_map/all_gather | solution.py:124
  102.5 0.1 broadcast_in_dim.90
  102.6 12.2 %all_to_all.46 = bf16[16,96,128]{2,1,0:T(8,128)(2,1)S(1)} all-to-all(bf16[16,96,128]{2,1,0:T(8,128)(2,1)S(1)} %broadcast_in_dim.90), channel_id=1, replica_groups=mesh['sub'=8,'row'=2,'col'=16] {'col'}, dimensions={0} | all-to-all | bytes 786432 | tf_op jit(solution)/shard_map/all_to_all | solution.py:51
  114.8 0.3 convolution_subtract_fusion
  115.1 0.6 fusion.9
  115.7 0.1 bitcast_convert_fusion.1
  115.8 0.2 copy.40
  116.0 0.1 constant_dynamic-slice_fusion.1
  116.1 13.0 %all_to_all.47 = bf16[16,128,128]{1,2,0:T(8,128)(2,1)S(1)} all-to-all(bf16[16,128,128]{1,2,0:T(8,128)(2,1)S(1)} %bitcast_convert_fusion.1), channel_id=1, replica_groups=mesh['sub'=8,'row'=2,'col'=16] {'col'}, dimensions={0} | all-to-all | bytes 1048576 | tf_op jit(solution)/shard_map/all_to_all | solution.py:44
  129.1 0.2 select_reduce_fusion.1
  129.2 0.0 copy-start.4
  129.3 0.1 copy.29
  129.4 0.1 broadcast_in_dim.93
  129.5 12.4 %all_to_all.48 = bf16[16,128,128]{2,1,0:T(8,128)(2,1)S(1)} all-to-all(bf16[16,128,128]{2,1,0:T(8,128)(2,1)S(1)} %broadcast_in_dim.93), channel_id=1, replica_groups=mesh['sub'=8,'row'=2,'col'=16] {'col'}, dimensions={0} | all-to-all | bytes 1048576 | tf_op jit(solution)/shard_map/all_to_all | solution.py:51
  141.9 0.3 fusion.14
  142.2 4.7 %all-gather.1 = f32[256,128]{1,0:T(8,128)S(1)} all-gather(f32[128,128]{1,0:T(8,128)S(1)} %fusion.14), channel_id=3, replica_groups=mesh['sub'=8,'row'=2,'col'=16] {'row'}, dimensions={0}, use_global_device_ids=true | all-gather | bytes 196608 | tf_op jit(solution)/shard_map/all_gather | solution.py:130
  146.9 0.6 fusion.7
  147.5 0.1 bitcast_convert_fusion
  147.6 0.2 copy.41
  147.8 0.1 constant_dynamic-slice_fusion
  147.9 13.5 %all_to_all.49 = bf16[16,128,128]{1,2,0:T(8,128)(2,1)S(1)} all-to-all(bf16[16,128,128]{1,2,0:T(8,128)(2,1)S(1)} %bitcast_convert_fusion), channel_id=1, replica_groups=mesh['sub'=8,'row'=2,'col'=16] {'col'}, dimensions={0} | all-to-all | bytes 1048576 | tf_op jit(solution)/shard_map/all_to_all | solution.py:44
  161.3 0.2 select_reduce_fusion
  161.5 0.7 copy.32
  (28 shorter events, 0.2 us)
Async XLA Ops:
  0.6 1.2 copy-start
  0.6 5.0 %copy-start.7 = (s32[1,16,16]{2,1,0:T(8,128)S(1)}, s32[1,16,16]{2,1,0:T(8,128)}, u32[]{:S(2)}) copy-start(s32[1,16,16]{2,1,0:T(8,128)} %param.9) | copy-start | bytes 3076
  0.7 5.2 %copy-start.2 = (f32[96,1536]{1,0:T(8,128)S(1)}, f32[96,1536]{1,0:T(8,128)}, u32[]{:S(2)}) copy-start(f32[96,1536]{1,0:T(8,128)} %param.13) | copy-start | bytes 1769476
  4.3 5.5 %collective-permute-start = (bf16[128,128]{1,0:T(8,128)(2,1)}, bf16[128,128]{1,0:T(8,128)(2,1)}, u32[]{:S(2)}, u32[]{:S(2)}) collective-permute-start(bf16[128,128]{1,0:T(8,128)(2,1)} %get-tuple-element.30), channel_id=1, source_target_pairs={{0,16},{1,17},{2,18},{3,19},{4,20},{5,21},{6,22},{7,23},{8,24},{9,... | collective-permute-start | bytes 98312 | tf_op jit(solution)/shard_map/ppermute | solution.py:79
  6.5 3.4 %copy-start.3 = (bf16[1,2,128,2048]{3,2,1,0:T(8,128)(2,1)S(1)}, bf16[1,2,128,2048]{3,2,1,0:T(8,128)(2,1)}, u32[]{:S(2)}) copy-start(bf16[1,2,128,2048]{3,2,1,0:T(8,128)(2,1)} %param.8) | copy-start | bytes 3145732
  12.0 5.6 %copy-start.6 = (f32[96,128]{1,0:T(8,128)S(1)}, f32[96,128]{1,0:T(8,128)}, u32[]{:S(2)}) copy-start(f32[96,128]{1,0:T(8,128)} %param.15) | copy-start | bytes 147460
  12.0 11.0 %copy-start.8 = (bf16[1,1,128,1024]{3,2,1,0:T(8,128)(2,1)S(1)}, bf16[1,1,128,1024]{3,2,1,0:T(8,128)(2,1)}, u32[]{:S(2)}) copy-start(bf16[1,1,128,1024]{3,2,1,0:T(8,128)(2,1)} %param.11) | copy-start | bytes 786436
  12.0 11.0 %copy-start.9 = (s32[1,1024]{1,0:T(1,128)S(1)}, s32[1,1024]{1,0:T(1,128)}, u32[]{:S(2)}) copy-start(s32[1,1024]{1,0:T(1,128)} %param.12) | copy-start | bytes 12292
  12.0 20.0 %all-to-all-start = ((bf16[16,224,128]{2,1,0:T(8,128)(2,1)}), bf16[16,224,128]{2,1,0:T(8,128)(2,1)S(1)}, u32[]{:S(2)}, u32[]{:S(2)}) async-start(bf16[16,224,128]{2,1,0:T(8,128)(2,1)} %fusion.13), calls=%async_computation | async-start | bytes 1835008 | tf_op jit(solution)/shard_map/all_to_all | solution.py:107
  17.7 14.4 %collective-permute-start.1 = (f32[48,128]{1,0:T(8,128)S(1)}, f32[48,128]{1,0:T(8,128)S(1)}, u32[]{:S(2)}, u32[]{:S(2)}) collective-permute-start(f32[48,128]{1,0:T(8,128)S(1)} %constant_dynamic-slice_fusion.2), channel_id=1, source_target_pairs={{0,0},{1,2},{2,4},{3,6},{4,8},{5,10},{6,12},{7,14},{8,16},{9,18},{... | collective-permute-start | bytes 73736 | tf_op jit(solution)/shard_map/ppermute | solution.py:99
  33.0 15.4 %all-to-all-start.1 = ((bf16[16,128,128]{2,1,0:T(8,128)(2,1)}), bf16[16,128,128]{2,1,0:T(8,128)(2,1)S(1)}, u32[]{:S(2)}, u32[]{:S(2)}) async-start(bf16[16,128,128]{2,1,0:T(8,128)(2,1)} %broadcast_in_dim.84), calls=%async_computation.1 | async-start | bytes 1048576 | tf_op jit(solution)/shard_map/all_to_all | solution.py:51
  38.2 10.6 %copy-start.1 = (bf16[1536,128]{1,0:T(8,128)(2,1)S(1)}, bf16[1536,128]{1,0:T(8,128)(2,1)}, u32[]{:S(2)}) copy-start(bf16[1536,128]{1,0:T(8,128)(2,1)} %fusion.2) | copy-start | bytes 1179652
  38.2 8.8 %collective-permute-start.2 = (f32[96,96]{0,1:T(8,128)S(1)}, f32[96,96]{0,1:T(8,128)S(1)}, u32[]{:S(2)}, u32[]{:S(2)}) collective-permute-start(f32[96,96]{0,1:T(8,128)S(1)} %bitcast.94), channel_id=1, source_target_pairs={{0,128},{32,160},{64,192},{96,224},{128,0},{160,32},{192,64},{224,... | collective-permute-start | bytes 110600 | tf_op jit(solution)/shard_map/ppermute | solution.py:31
  49.8 17.4 %all-to-all-start.2 = ((bf16[32,48,128]{2,1,0:T(8,128)(2,1)}), bf16[32,48,128]{2,1,0:T(8,128)(2,1)S(1)}, u32[]{:S(2)}, u32[]{:S(2)}) async-start(bf16[32,48,128]{2,1,0:T(8,128)(2,1)} %bitcast.11), calls=%async_computation.2 | async-start | bytes 786432 | tf_op jit(solution)/shard_map/all_to_all | solution.py:118
  57.7 7.3 %collective-permute-start.3 = (f32[192,96]{0,1:T(8,128)S(1)}, f32[192,96]{0,1:T(8,128)S(1)}, u32[]{:S(2)}, u32[]{:S(2)}) collective-permute-start(f32[192,96]{0,1:T(8,128)S(1)} %maximum_select_fusion.2), channel_id=1, source_target_pairs={{0,64},{32,96},{64,0},{96,32},{128,192},{160,224},{192,128},{224,1... | collective-permute-start | bytes 221192 | tf_op jit(solution)/shard_map/ppermute | solution.py:31
  83.3 13.3 %all-to-all-start.4 = ((f32[16,48,128]{2,1,0:T(8,128)}), f32[16,48,128]{2,1,0:T(8,128)S(1)}, u32[]{:S(2)}, u32[]{:S(2)}) async-start(f32[16,48,128]{2,1,0:T(8,128)} %broadcast_in_dim.89), calls=%async_computation.4 | async-start | bytes 786432 | tf_op jit(solution)/shard_map/all_to_all | solution.py:51
  88.3 4.1 %collective-permute-start.4 = (f32[384,96]{0,1:T(8,128)S(1)}, f32[384,96]{0,1:T(8,128)S(1)}, u32[]{:S(2)}, u32[]{:S(2)}) collective-permute-start(f32[384,96]{0,1:T(8,128)S(1)} %maximum_select_fusion.1), channel_id=1, source_target_pairs={{0,32},{32,0},{64,96},{96,64},{128,160},{160,128},{192,224},{224,1... | collective-permute-start | bytes 442376 | tf_op jit(solution)/shard_map/ppermute | solution.py:31
  102.5 12.6 %copy-start.5 = (f32[96,128]{1,0:T(8,128)}, f32[96,128]{1,0:T(8,128)S(1)}, u32[]{:S(2)}) copy-start(f32[96,128]{1,0:T(8,128)S(1)} %reduce_sum.70) | copy-start | bytes 147460
  129.2 12.6 %copy-start.4 = (bf16[1,2,128,2048]{3,2,1,0:T(8,128)(2,1)S(1)}, bf16[1,2,128,2048]{3,2,1,0:T(8,128)(2,1)}, u32[]{:S(2)}) copy-start(bf16[1,2,128,2048]{3,2,1,0:T(8,128)(2,1)} %param.8) | copy-start | bytes 3145732
